TPU v7x, 256 devices: a whole 4x4x8 slice. The times are simulated.
256 devices in a mesh: section: 2 (over core), tile: 128 (over y, x, z).
Axes of the slice: x: 4, y: 4, z: 8, core: 2. Of those that a mesh axis runs over, the one named last changes fastest.
Arguments:
- aerial_patch_grid: bfloat16 [384, 384, 768], P('tile'), may hold values from -6 to 6
- patch_conv_weight: bfloat16 [3, 4, 4, 96], replicated, may hold values from -0.875 to 0.875
- patch_bias: float32 [96], replicated, may hold values from -3 to 3
- merging_conv_weight: bfloat16 [2, 2, 96, 192], replicated, may hold values from -0.3125 to 0.3125
- merge_bias: float32 [192], replicated, may hold values from -3 to 3
- down_weight: bfloat16 [3, 3, 192, 384], replicated, may hold values from -0.15625 to 0.15625
- down_bias: float32 [384], replicated, may hold values from -3 to 3
- norm_gain: float32 [384], replicated, may hold values from 0.1 to 1.9
- spectral_filter: bfloat16 [384, 2, 384, 384], P('tile'), may hold values from -6 to 6
Outputs:
- block_output: bfloat16 [384, 384, 384], P('section', 'tile')
All inputs are finite; a program needn't handle non-finite values.
Results may differ from a plain program's by a relative error of at most 0.015.
Values may be sent and summed in bfloat16 or wider, within the bound.
A program may use at most 64 MiB of HBM per device.

v0:
```python
import math

import jax
import jax.numpy as jnp
from jax import lax
from jax.sharding import PartitionSpec as P

EPSILON = 1e-05


def from_behind(block, axis, distance):
    devices = range(lax.axis_size(axis))
    route = [(i - distance, i) for i in devices if i - distance in devices]
    return lax.ppermute(block, axis, route)


def fourier_tables(length):
    indices = jnp.arange(length, dtype=jnp.int32)
    product = indices[:, None] * indices[None, :] % length
    angles = product.astype(jnp.float32) * (2.0 * math.pi / length)
    return (jnp.cos(angles).astype(jnp.bfloat16), jnp.sin(angles).astype(jnp.bfloat16))


def one_hot_rows(indices, width):
    return (indices[:, None] == jnp.arange(width, dtype=jnp.int32)[None, :]).astype(jnp.bfloat16)


def spread_kernel(weight_rows, row_pick, row_cell, col_cell, width, out_cols):
    picked = jnp.dot(
        one_hot_rows(row_pick, weight_rows.shape[0]), weight_rows,
        preferred_element_type=jnp.float32,
    ).astype(jnp.bfloat16)
    col = jnp.arange(out_cols, dtype=jnp.int32)
    repeat = one_hot_rows(col % width, width).T
    full = jnp.dot(picked, repeat, preferred_element_type=jnp.float32)
    mask = row_cell[:, None] == col_cell[None, :]
    return jnp.where(mask, full, 0.0).astype(jnp.bfloat16)


def patch_kernel_matrix(patch_conv_weight):
    band_count = patch_conv_weight.shape[0]
    width = patch_conv_weight.shape[3]
    row = jnp.arange(band_count * 256, dtype=jnp.int32)
    pick = (row // 256) * 16 + ((row // 16) % 4) * 4 + row % 4
    row_cell = ((row // 64) % 4) * 4 + (row // 4) % 4
    col = jnp.arange(16 * width, dtype=jnp.int32)
    col_cell = col // width
    weight_rows = patch_conv_weight.reshape(band_count * 16, width)
    return spread_kernel(weight_rows, pick, row_cell, col_cell, width, 16 * width)


def merging_kernel_matrix(merging_conv_weight):
    in_width = merging_conv_weight.shape[2]
    out_width = merging_conv_weight.shape[3]
    row = jnp.arange(16 * in_width, dtype=jnp.int32)
    pos = row // in_width
    pick = ((pos // 4) % 2 * 2 + pos % 2) * in_width + row % in_width
    row_cell = (pos // 8) * 2 + (pos // 2) % 2
    col = jnp.arange(4 * out_width, dtype=jnp.int32)
    col_cell = col // out_width
    weight_rows = merging_conv_weight.reshape(4 * in_width, out_width)
    return spread_kernel(weight_rows, pick, row_cell, col_cell, out_width, 4 * out_width)


def down_matrices(down_weight):
    nothing = jnp.zeros_like(down_weight[0, 0])
    in_width = down_weight.shape[2]
    out_width = down_weight.shape[3]

    def arrange(entries):
        return jnp.stack(
            [jnp.stack(entries[0], axis=0), jnp.stack(entries[1], axis=0)], axis=0
        ).reshape(4 * in_width, out_width)

    own_taps = arrange(
        [[down_weight[1, 1], down_weight[1, 2]], [down_weight[2, 1], down_weight[2, 2]]]
    )
    upper_taps = arrange([[nothing, nothing], [down_weight[0, 1], down_weight[0, 2]]])
    left_taps = arrange([[nothing, down_weight[1, 0]], [nothing, down_weight[2, 0]]])
    corner_taps = arrange([[nothing, nothing], [nothing, down_weight[0, 0]]])
    return (own_taps, upper_taps, left_taps, corner_taps)


def stem_layers(aerial_patch_grid, patch_conv_weight, patch_bias, merging_conv_weight, merge_bias):
    initial_layer = jnp.einsum(
        "zji,if->zjf",
        aerial_patch_grid,
        patch_kernel_matrix(patch_conv_weight),
        preferred_element_type=jnp.float32,
    )
    initial_layer = jax.nn.gelu(initial_layer + jnp.tile(patch_bias, 16), approximate=True).astype(
        jnp.bfloat16
    )
    layer_two = jnp.einsum(
        "zji,if->zjf",
        initial_layer,
        merging_kernel_matrix(merging_conv_weight),
        preferred_element_type=jnp.float32,
    )
    return jax.nn.gelu(layer_two + jnp.tile(merge_bias, 4), approximate=True).astype(jnp.bfloat16)


def rim_above(extended):
    return from_behind(extended[-1:], "tile", 1)


def down_conv(upper_rim, extended, down_weight, down_bias):
    stacked = jnp.concatenate([upper_rim, extended], axis=0)
    own_taps, upper_taps, left_taps, corner_taps = down_matrices(down_weight)
    summed = jnp.einsum(
        "rwk,kc->crw", stacked[1:, 1:], own_taps, preferred_element_type=jnp.float32
    )
    summed = summed + jnp.einsum(
        "rwk,kc->crw", stacked[:-1, 1:], upper_taps, preferred_element_type=jnp.float32
    )
    summed = summed + jnp.einsum(
        "rwk,kc->crw", stacked[1:, :-1], left_taps, preferred_element_type=jnp.float32
    )
    summed = summed + jnp.einsum(
        "rwk,kc->crw", stacked[:-1, :-1], corner_taps, preferred_element_type=jnp.float32
    )
    return (summed + down_bias[:, None, None]).astype(jnp.bfloat16)


def layer_norm(features, norm_gain):
    values = features.astype(jnp.float32)
    mean_value = jnp.mean(values, axis=0, keepdims=True)
    centered = values - mean_value
    variance = jnp.mean(centered * centered, axis=0, keepdims=True)
    return (norm_gain[:, None, None] * centered * lax.rsqrt(variance + EPSILON)).astype(
        jnp.bfloat16
    )


def filter_columns(row_spectrum, kernel, forward_h, inverse_h):
    spectrum = jnp.einsum(
        "puqh,chqw->cpuw", forward_h, row_spectrum, preferred_element_type=jnp.float32
    ).astype(jnp.bfloat16)
    spec_real = spectrum[:, 0].astype(jnp.float32)
    spec_imag = spectrum[:, 1].astype(jnp.float32)
    filter_real = kernel[:, 0].astype(jnp.float32)
    filter_imag = kernel[:, 1].astype(jnp.float32)
    weighted = jnp.stack(
        [
            filter_real * spec_real - filter_imag * spec_imag,
            filter_real * spec_imag + filter_imag * spec_real,
        ],
        axis=1,
    ).astype(jnp.bfloat16)
    return jnp.einsum(
        "qhpu,cpuw->chqw", inverse_h, weighted, preferred_element_type=jnp.float32
    ).astype(jnp.bfloat16)


def local(
    aerial_patch_grid,
    patch_conv_weight,
    patch_bias,
    merging_conv_weight,
    merge_bias,
    down_weight,
    down_bias,
    norm_gain,
    spectral_filter,
):
    section_index = lax.axis_index("section")
    field_cols = aerial_patch_grid.shape[1]
    channels = down_weight.shape[3]
    full_rows = spectral_filter.shape[2]
    half_channels = channels // 2
    cell_half = field_cols // 2
    image_part = lax.dynamic_slice_in_dim(
        aerial_patch_grid, section_index * cell_half, cell_half, 1
    )
    layer_two = stem_layers(
        image_part, patch_conv_weight, patch_bias, merging_conv_weight, merge_bias
    )
    left_column = from_behind(layer_two[:, -1:], "section", 1)
    extended = jnp.concatenate([left_column, layer_two], axis=1)
    upper_rim = rim_above(extended)
    feature_half = down_conv(upper_rim, extended, down_weight, down_bias)
    normed_half = layer_norm(feature_half, norm_gain)
    fields = lax.all_to_all(normed_half, "tile", split_axis=0, concat_axis=1, tiled=True)
    fields = lax.all_gather(fields, "section", axis=2, tiled=True)

    cos_h, sin_h = fourier_tables(full_rows)
    if full_rows == field_cols:
        cos_w, sin_w = cos_h, sin_h
    else:
        cos_w, sin_w = fourier_tables(field_cols)
    cos_part = lax.dynamic_slice_in_dim(cos_w, section_index * cell_half, cell_half, 1)
    sin_part = lax.dynamic_slice_in_dim(sin_w, section_index * cell_half, cell_half, 1)
    forward_table = jnp.stack([cos_part, -sin_part], axis=1)
    inverse_table = jnp.stack([cos_part, -sin_part], axis=0)
    forward_h = jnp.stack(
        [jnp.stack([cos_h, sin_h], axis=1), jnp.stack([-sin_h, cos_h], axis=1)], axis=0
    )
    inverse_h = jnp.stack(
        [jnp.stack([cos_h, -sin_h], axis=1), jnp.stack([sin_h, cos_h], axis=1)], axis=0
    )
    norm_scale = 1.0 / (full_rows * field_cols)
    kernel_part = lax.dynamic_slice_in_dim(
        spectral_filter, section_index * cell_half, cell_half, 3
    )
    frequency_rows = jnp.einsum(
        "chx,xqw->chqw", fields, forward_table, preferred_element_type=jnp.float32
    ).astype(jnp.bfloat16)
    back_rows = filter_columns(frequency_rows, kernel_part, forward_h, inverse_h)
    back_rows = lax.all_gather(back_rows, "section", axis=3, tiled=True)
    result = jnp.einsum(
        "chqw,qwv->chv", back_rows, inverse_table, preferred_element_type=jnp.float32
    )
    filtered_fields = (result * norm_scale).astype(jnp.bfloat16)
    rows_back = lax.all_to_all(filtered_fields, "tile", split_axis=1, concat_axis=0, tiled=True)
    summed = (feature_half.astype(jnp.float32) + rows_back.astype(jnp.float32)).astype(
        jnp.bfloat16
    )
    kept = lax.dynamic_slice_in_dim(summed, section_index * half_channels, half_channels, 0)
    sent = lax.dynamic_slice_in_dim(
        summed, (1 - section_index) * half_channels, half_channels, 0
    )
    received = lax.ppermute(sent, "section", [(0, 1), (1, 0)])
    return jnp.where(
        section_index == 0,
        jnp.concatenate([kept, received], axis=2),
        jnp.concatenate([received, kept], axis=2),
    )


def solution(mesh):
    return jax.shard_map(
        local,
        mesh=mesh,
        in_specs=(
            P("tile", None, None),
            P(),
            P(),
            P(),
            P(),
            P(),
            P(),
            P(),
            P("tile", None, None, None),
        ),
        out_specs=P("section", "tile", None),
        check_vma=False,
    )
```

profile of v0, /device:TPU:1, one launch (start us, length us, event | category | flops | bytes accessed | tf_op | source)
XLA Modules:
  0.0 175.3 jit_solution(6050538914939704282)
XLA Ops:
  6.6 0.8 tile.4
  7.5 0.7 tile.5
  8.3 2.5 %convolution_convert_fusion = bf16[1536,192]{0,1:T(8,128)(2,1)} fusion(bf16[384,192]{1,0:T(8,128)(2,1)} %bitcast.142, s32[1536]{0:T(1024)S(1)} %fusion.101), kind=kOutput, calls=%fused_computation.14 | convolution fusion | flops 227377152 | bytes 743424 | tf_op jit(solution)/shard_map/dot_general | solution.py:29
  10.8 3.5 %fusion.8 = bf16[768,1536,1]{1,0,2:T(8,128)(2,1)} fusion(s32[1536]{0:T(1024)S(1)} %get-tuple-element.41, s32[768]{0:T(1024)S(1)} %get-tuple-element.42, bf16[48,96]{1,0:T(8,128)(2,1)} %bitcast.143, s32[1536]{0:T(1024)S(1)} %get-tuple-element.40, s32[768]{0:T(1024)S(1)} %get-tuple-element.43), kind=kOutput, calls=%fused_computation.11 | convolution fusion | flops 237367296 | bytes 2386944 | tf_op jit(solution)/shard_map/dot_general | solution.py:35
  14.3 5.0 %fusion.7 = bf16[3,192,1536]{2,1,0:T(8,128)(2,1)} fusion(bf16[768,1536,1]{1,0,2:T(8,128)(2,1)} %fusion.8, f32[1536]{0:T(1024)S(1)} %add.318, bf16[3,384,768]{2,1,0:T(8,128)(2,1)S(1)} %copy-done, s32[]{:T(128)S(6)} %select_n.229), kind=kOutput, calls=%fused_computation.10 | convolution fusion | flops 1367801856 | bytes 5021700 | tf_op jit(solution)/shard_map/zji,if->zjf/dot_general | solution.py:85
  19.3 4.3 %fusion.17 = bf16[3,192,768]{2,1,0:T(8,128)(2,1)S(1)} fusion(bf16[3,192,1536]{2,1,0:T(8,128)(2,1)} %fusion.7, bf16[1536,192]{0,1:T(8,128)(2,1)} %convolution_convert_fusion, s32[768]{0:T(1024)S(1)} %get-tuple-element.45, s32[1536]{0:T(1024)S(1)} %fusion.94, f32[768]{0:T(1024)S(1)} %add.331, s32[768]{0:T(1024)S(1)} %get-tuple-element.44), kind=kOutput, calls=%fused_computation.23 | convolution fusion | flops 1820049408 | bytes 3259392 | tf_op jit(solution)/shard_map/zji,if->zjf/dot_general | solution.py:94
  23.6 1.3 collective-permute-start
  24.9 1.5 slice_bitcast_fusion.2
  26.5 0.9 pad_maximum_fusion.6
  27.5 0.9 pad_maximum_fusion.7
  28.9 4.0 %collective-permute-start.1 = (bf16[1,193,768]{2,1,0:T(8,128)(2,1)S(1)}, bf16[1,193,768]{2,1,0:T(8,128)(2,1)S(1)}, u32[]{:S(2)}, u32[]{:S(2)}) collective-permute-start(bf16[1,193,768]{2,1,0:T(8,128)(2,1)S(1)} %pad_maximum_fusion.8), channel_id=1, source_target_pairs={{0,1},{1,2},{2,3},{3,4},{4,5},{5,6},{6,7},{7,8},{8,9},{9,10},{10,1... | collective-permute-start | bytes 889352 | tf_op jit(solution)/shard_map/ppermute | solution.py:14
  32.9 0.9 stack.117
  33.8 0.9 stack.125
  34.7 1.7 fusion.135
  36.4 1.9 %collective-permute-done.1 = bf16[1,193,768]{2,1,0:T(8,128)(2,1)S(1)} collective-permute-done((bf16[1,193,768]{2,1,0:T(8,128)(2,1)S(1)}, bf16[1,193,768]{2,1,0:T(8,128)(2,1)S(1)}, u32[]{:S(2)}, u32[]{:S(2)}) %collective-permute-start.1) | collective-permute-done | bytes 296480 | tf_op jit(solution)/shard_map/ppermute | solution.py:14
  40.3 0.8 convert_reduce_fusion
  41.7 1.4 copy.31
  43.1 17.3 %all-to-all-start = ((bf16[384,3,192]{2,1,0:T(4,128)(2,1)}), bf16[384,3,192]{2,1,0:T(4,128)(2,1)S(1)}, u32[]{:S(2)}, u32[]{:S(2)}) async-start(bf16[384,3,192]{2,1,0:T(4,128)(2,1)} %copy.31), calls=%async_computation | async-start | bytes 1572864 | tf_op jit(solution)/shard_map/all_to_all | solution.py:183
  60.4 2.8 %constant_dynamic-slice_fusion = (bf16[3,1,384,192]{3,2,1,0:T(8,128)(2,1)}, bf16[3,1,384,192]{3,2,1,0:T(8,128)(2,1)}) fusion(bf16[3,2,384,384]{3,2,1,0:T(8,128)(2,1)} %param.17, s32[]{:T(128)S(6)} %select_n.229, s32[]{:T(128)S(6)} %add.349), kind=kLoop, calls=%fused_computation.233 | loop fusion | bytes 1769480 | tf_op jit(solution)/shard_map/slice | solution.py:141
  63.2 2.1 %copy.50 = bf16[3,1,384,192]{2,3,1,0:T(8,128)(2,1)} copy(bf16[3,1,384,192]{3,2,1,0:T(8,128)(2,1)} %get-tuple-element.7) | data formatting | bytes 884736
  65.3 2.1 %copy.51 = bf16[3,1,384,192]{2,3,1,0:T(8,128)(2,1)} copy(bf16[3,1,384,192]{3,2,1,0:T(8,128)(2,1)} %get-tuple-element.8) | data formatting | bytes 884736
  67.7 1.6 fusion.79
  69.3 1.6 fusion.80
  71.0 2.3 %fusion.77 = bf16[384,1,384]{2,0,1:T(8,128)(2,1)S(1)} fusion(), kind=kLoop, calls=%fused_computation.132 | loop fusion | flops 1916928 | bytes 294912 | tf_op jit(solution)/shard_map/neg | solution.py:196
  73.3 2.6 %sine_convert_fusion = (bf16[384,1,384]{2,0,1:T(8,128)(2,1)S(1)}, bf16[384,1,384]{2,0,1:T(8,128)(2,1)S(1)}) fusion(), kind=kLoop, calls=%fused_computation.93 | loop fusion | flops 1622016 | bytes 589824 | tf_op jit(solution)/shard_map/convert_element_type | solution.py:21
  75.9 1.5 fusion.53
  77.4 6.4 %all-to-all-done = bf16[384,3,192]{2,1,0:T(4,128)(2,1)S(1)} async-done(((bf16[384,3,192]{2,1,0:T(4,128)(2,1)}), bf16[384,3,192]{2,1,0:T(4,128)(2,1)S(1)}, u32[]{:S(2)}, u32[]{:S(2)}) %all-to-all-start) | async-done | bytes 442400 | tf_op jit(solution)/shard_map/all_to_all | solution.py:183
  83.8 1.2 copy.33
  85.0 1.5 all_to_all.23
  86.8 6.0 %all_gather.6 = bf16[3,384,384]{1,2,0:T(8,128)(2,1)} all-gather(bf16[3,384,192]{1,2,0:T(8,128)(2,1)S(1)} %copy.34), channel_id=1, replica_groups=mesh['section'=2,'tile'=128] {'section'}, dimensions={2}, use_global_device_ids=true | all-gather | bytes 1327104 | tf_op jit(solution)/shard_map/all_gather | solution.py:184
  92.8 4.1 %fusion.21 = bf16[3,2,384,192]{2,3,1,0:T(8,128)(2,1)} fusion(bf16[1,384,2,384]{3,1,2,0:T(8,128)(2,1)} %get-tuple-element.29, bf16[1,384,2,384]{3,1,2,0:T(8,128)(2,1)} %get-tuple-element.22, bf16[3,384,384]{1,2,0:T(8,128)(2,1)} %all_gather.6, bf16[384,1,192]{0,2,1:T(8,128)(2,1)} %get-tuple-element.21, bf16[384,1,192]{0,2,1:T(8,128)(2,1)} %get-tuple-element.19), kind=kOutput, calls=%fused_computation.35 | convolution fusion | flops 1023049728 | bytes 3244032 | tf_op jit(solution)/shard_map/puqh,chqw->cpuw/dot_general | solution.py:136
  96.9 1.6 fusion.37
  98.5 1.8 %fusion.22 = bf16[3,384,2,192]{1,3,2,0:T(8,128)(2,1)} fusion(bf16[1,384,2,384]{3,1,2,0:T(8,128)(2,1)S(1)} %copy-done.6, bf16[1,384,2,384]{3,1,2,0:T(8,128)(2,1)S(1)} %copy-done.7, bf16[3,1,384,192]{2,3,1,0:T(8,128)(2,1)S(1)} %get-tuple-element.6, bf16[3,1,384,192]{2,3,1,0:T(8,128)(2,1)S(1)} %get-tuple-element.5), kind=kOutput, calls=%fused_computation.36 | convolution fusion | flops 684048384 | bytes 2949120 | tf_op jit(solution)/shard_map/qhpu,cpuw->chqw/dot_general | solution.py:150
  100.4 9.3 %all-gather.2.cloned.1.call-done = bf16[3,384,2,384]{1,3,2,0:T(8,128)(2,1)} async-done(((bf16[3,384,2,192]{1,3,2,0:T(8,128)(2,1)}), bf16[3,384,2,384]{1,3,2,0:T(8,128)(2,1)}) %all-gather.2.cloned.1.call-update) | async-done | bytes 1769488 | tf_op jit(solution)/shard_map/all_gather | solution.py:209
  109.6 2.0 %fusion.24 = bf16[3,384,192]{1,2,0:T(8,128)(2,1)S(1)} fusion(bf16[3,384,2,384]{1,3,2,0:T(8,128)(2,1)} %all-gather.2.cloned.1.call-done, bf16[1,384,192]{1,2,0:T(8,128)(2,1)S(1)} %get-tuple-element.20, bf16[1,384,192]{1,2,0:T(8,128)(2,1)S(1)} %get-tuple-element.18), kind=kOutput, calls=%fused_computation.39 | convolution fusion | flops 340770816 | bytes 2506752 | tf_op jit(solution)/shard_map/chqw,qwv->chv/dot_general | solution.py:210
  111.7 1.4 copy.35
  113.1 13.6 %all-to-all-start.1 = ((bf16[3,384,192]{2,0,1:T(4,128)(2,1)}), bf16[3,384,192]{2,0,1:T(4,128)(2,1)S(1)}, u32[]{:S(2)}, u32[]{:S(2)}) async-start(bf16[3,384,192]{2,0,1:T(4,128)(2,1)} %copy.35), calls=%async_computation.1 | async-start | bytes 1572864 | tf_op jit(solution)/shard_map/all_to_all | solution.py:214
  126.7 25.4 %all-to-all-done.1 = bf16[3,384,192]{2,0,1:T(4,128)(2,1)S(1)} async-done(((bf16[3,384,192]{2,0,1:T(4,128)(2,1)}), bf16[3,384,192]{2,0,1:T(4,128)(2,1)S(1)}, u32[]{:S(2)}, u32[]{:S(2)}) %all-to-all-start.1) | async-done | bytes 442400 | tf_op jit(solution)/shard_map/all_to_all | solution.py:214
  152.0 1.4 copy.36
  153.4 1.2 copy.37
  154.7 1.5 reshape.334
  156.2 3.4 %copy.38 = f32[128,3,3,192]{3,1,0,2:T(4,128)} copy(f32[128,3,3,192]{3,2,0,1:T(4,128)} %bitcast.136) | data formatting | bytes 1769472 | tf_op jit(solution)/shard_map/convert_element_type | solution.py:215
  159.5 1.8 reshape.333
  161.3 1.3 copy.39
  162.6 1.2 fusion.40
  164.1 1.9 %collective-permute-start.2 = (bf16[192,3,192]{0,2,1:T(8,128)(2,1)S(1)}, bf16[192,3,192]{0,2,1:T(8,128)(2,1)S(1)}, u32[]{:S(2)}, u32[]{:S(2)}) collective-permute-start(bf16[192,3,192]{0,2,1:T(8,128)(2,1)S(1)} %get-tuple-element.27), channel_id=1, source_target_pairs={{0,128},{128,0},{1,129},{129,1},{2,130},{130,2},{3,131},{131,3},{4... | collective-permute-start | bytes 663560 | tf_op jit(solution)/shard_map/ppermute | solution.py:222
  166.0 1.2 collective-permute-done.2
  167.5 1.0 copy.40
  (46 shorter events, 4.7 us)
Async XLA Ops:
  6.5 7.8 %copy-start = (bf16[3,384,768]{2,1,0:T(8,128)(2,1)S(1)}, bf16[3,384,768]{2,1,0:T(8,128)(2,1)}, u32[]{:S(2)}) copy-start(bf16[3,384,768]{2,1,0:T(8,128)(2,1)} %param.9) | copy-start | bytes 5308420
  23.6 5.2 %collective-permute-start = (bf16[3,1,768]{2,1,0:T(2,128)(2,1)S(1)}, bf16[3,1,768]{2,1,0:T(2,128)(2,1)S(1)}, u32[]{:S(2)}, u32[]{:S(2)}) collective-permute-start(bf16[3,1,768]{2,1,0:T(2,128)(2,1)S(1)} %slice.72), channel_id=1, source_target_pairs={{0,128},{1,129},{2,130},{3,131},{4,132},{5,133},{6,134},{7,135},{8... | collective-permute-start | bytes 13832 | tf_op jit(solution)/shard_map/ppermute | solution.py:14
  28.9 9.4 %collective-permute-start.1 = (bf16[1,193,768]{2,1,0:T(8,128)(2,1)S(1)}, bf16[1,193,768]{2,1,0:T(8,128)(2,1)S(1)}, u32[]{:S(2)}, u32[]{:S(2)}) collective-permute-start(bf16[1,193,768]{2,1,0:T(8,128)(2,1)S(1)} %pad_maximum_fusion.8), channel_id=1, source_target_pairs={{0,1},{1,2},{2,3},{3,4},{4,5},{5,6},{6,7},{7,8},{8,9},{9,10},{10,1... | collective-permute-start | bytes 889352 | tf_op jit(solution)/shard_map/ppermute | solution.py:14
  36.4 2.2 %copy-start.3 = (bf16[2,2,192,384]{3,2,1,0:T(8,128)(2,1)S(1)}, bf16[2,2,192,384]{3,2,1,0:T(8,128)(2,1)}, u32[]{:S(2)}) copy-start(bf16[2,2,192,384]{3,2,1,0:T(8,128)(2,1)} %stack.125) | copy-start | bytes 1769476
  38.5 1.1 copy-start.1
  39.2 1.1 copy-start.2
  39.2 1.1 copy-start.8
  40.3 1.2 copy-start.9
  43.1 40.7 %all-to-all-start = ((bf16[384,3,192]{2,1,0:T(4,128)(2,1)}), bf16[384,3,192]{2,1,0:T(4,128)(2,1)S(1)}, u32[]{:S(2)}, u32[]{:S(2)}) async-start(bf16[384,3,192]{2,1,0:T(4,128)(2,1)} %copy.31), calls=%async_computation | async-start | bytes 1572864 | tf_op jit(solution)/shard_map/all_to_all | solution.py:183
  60.4 49.3 %all-gather.2.cloned.1.call-start = ((), (), s32[]{:S(2)}) async-start(), calls=%async_computation.2 | async-start | bytes 2654208 | tf_op jit(solution)/shard_map/all_gather | solution.py:209
  92.8 4.1 %copy-start.4 = (bf16[3,1,384,192]{2,3,1,0:T(8,128)(2,1)S(1)}, bf16[3,1,384,192]{2,3,1,0:T(8,128)(2,1)}, u32[]{:S(2)}) copy-start(bf16[3,1,384,192]{2,3,1,0:T(8,128)(2,1)} %copy.50) | copy-start | bytes 1327108
  92.8 4.1 %copy-start.5 = (bf16[3,1,384,192]{2,3,1,0:T(8,128)(2,1)S(1)}, bf16[3,1,384,192]{2,3,1,0:T(8,128)(2,1)}, u32[]{:S(2)}) copy-start(bf16[3,1,384,192]{2,3,1,0:T(8,128)(2,1)} %copy.51) | copy-start | bytes 1327108
  96.9 1.6 copy-start.6
  96.9 1.6 copy-start.7
  113.1 39.0 %all-to-all-start.1 = ((bf16[3,384,192]{2,0,1:T(4,128)(2,1)}), bf16[3,384,192]{2,0,1:T(4,128)(2,1)S(1)}, u32[]{:S(2)}, u32[]{:S(2)}) async-start(bf16[3,384,192]{2,0,1:T(4,128)(2,1)} %copy.35), calls=%async_computation.1 | async-start | bytes 1572864 | tf_op jit(solution)/shard_map/all_to_all | solution.py:214
  164.1 3.2 %collective-permute-start.2 = (bf16[192,3,192]{0,2,1:T(8,128)(2,1)S(1)}, bf16[192,3,192]{0,2,1:T(8,128)(2,1)S(1)}, u32[]{:S(2)}, u32[]{:S(2)}) collective-permute-start(bf16[192,3,192]{0,2,1:T(8,128)(2,1)S(1)} %get-tuple-element.27), channel_id=1, source_target_pairs={{0,128},{128,0},{1,129},{129,1},{2,130},{130,2},{3,131},{131,3},{4... | collective-permute-start | bytes 663560 | tf_op jit(solution)/shard_map/ppermute | solution.py:222
Sparse Core Ops, SparseCore 0:
  100.5 9.1 all-gather.1
where the time goes:
time: 176 us; the launch traced here: 175 us
  waiting for transfers between devices  44.7 us (25%)
  starting transfers between devices  38.1 us (22%)
  local copies, waits for them, and re-layouts  29.9 us (17%)
  matrix products  27 us (15%)
  other arithmetic  15.9 us (9%)
  between operations  13.7 us (8%)
  blocking collectives  6.01 us (3%)
    all_to_all x1, waiting for transfers between devices, local(): lax.all_to_all(filtered_fields, 'tile', split_axis=1, concat_axis=0, tile...  25.4 us
    all_to_all x1, starting transfers between devices, local(): lax.all_to_all(normed_half, 'tile', split_axis=0, concat_axis=1, tiled=True)  17.3 us
    all_to_all x1, starting transfers between devices, local(): lax.all_to_all(filtered_fields, 'tile', split_axis=1, concat_axis=0, tile...  13.6 us
    all_gather x1, waiting for transfers between devices, local(): back_rows = lax.all_gather(back_rows, 'section', axis=3, tiled=True)  9.27 us
    convert_element_type x5, local copies, waits for them, and re-layouts, local(): rows_back.astype(jnp.float32)  9.11 us
    all_to_all x1, waiting for transfers between devices, local(): lax.all_to_all(normed_half, 'tile', split_axis=0, concat_axis=1, tiled=True)  6.44 us
    all_gather x1, blocking collectives, local(): fields = lax.all_gather(fields, 'section', axis=2, tiled=True)  6.01 us
    ppermute x2, starting transfers between devices, from_behind(): return lax.ppermute(block, axis, route)  5.25 us
  transfers between devices with their start and end apart: 6, of which 6 were waited for; matrix products, arithmetic and copies ran while one was open for 14% of the time, Pallas kernels for 0%

commit v1 on v0

--- a/solution.py
+++ b/solution.py
@@ -3,9 +3,72 @@
 import jax
 import jax.numpy as jnp
 from jax import lax
+from jax.experimental import pallas as pl
+from jax.experimental.pallas import tpu as pltpu
 from jax.sharding import PartitionSpec as P
 
 EPSILON = 1e-05
+MESH_ID = pl.DeviceIdType.MESH
+
+
+def exchange_kernel(x_ref, o_ref, send_sem, recv_sem, own_sem):
+    count = x_ref.shape[0]
+    me = lax.axis_index("tile")
+    section = lax.axis_index("section")
+    barrier = pltpu.get_barrier_semaphore()
+
+    def greet(step, carry):
+        peer = lax.rem(me + step, count)
+        pl.semaphore_signal(barrier, 1, device_id=(section, peer), device_id_type=MESH_ID)
+        return carry
+
+    lax.fori_loop(1, count, greet, 0)
+    pl.semaphore_wait(barrier, count - 1)
+    own = pltpu.make_async_copy(x_ref.at[pl.ds(me, 1)], o_ref.at[pl.ds(me, 1)], own_sem)
+    own.start()
+
+    def send(step, carry):
+        peer = lax.rem(me + step, count)
+        pltpu.make_async_remote_copy(
+            src_ref=x_ref.at[pl.ds(peer, 1)],
+            dst_ref=o_ref.at[pl.ds(me, 1)],
+            send_sem=send_sem,
+            recv_sem=recv_sem,
+            device_id=(section, peer),
+            device_id_type=MESH_ID,
+        ).start()
+        return carry
+
+    lax.fori_loop(1, count, send, 0)
+    every = pltpu.make_async_remote_copy(
+        src_ref=x_ref.at[pl.ds(0, count - 1)],
+        dst_ref=o_ref.at[pl.ds(0, count - 1)],
+        send_sem=send_sem,
+        recv_sem=recv_sem,
+        device_id=(section, lax.rem(me + 1, count)),
+        device_id_type=MESH_ID,
+    )
+    every.wait_send()
+    every.wait_recv()
+    own.wait()
+
+
+def exchange(chunks, collective_id):
+    return pl.pallas_call(
+        exchange_kernel,
+        out_shape=jax.ShapeDtypeStruct(chunks.shape, chunks.dtype),
+        in_specs=[pl.BlockSpec(memory_space=pl.ANY)],
+        out_specs=pl.BlockSpec(memory_space=pl.ANY),
+        scratch_shapes=[pltpu.SemaphoreType.DMA(())] * 3,
+        compiler_params=pltpu.CompilerParams(collective_id=collective_id, has_side_effects=True),
+    )(chunks)
+
+
+def exchange_chunks(chunks, collective_id):
+    count, length = chunks.shape
+    padded = -(-length // 2048) * 2048
+    slabs = jnp.pad(chunks, ((0, 0), (0, padded - length))).reshape(count, padded // 128, 128)
+    return exchange(slabs, collective_id).reshape(count, padded)[:, :length]
 
 
 def from_behind(block, axis, distance):
@@ -180,7 +243,14 @@
     upper_rim = rim_above(extended)
     feature_half = down_conv(upper_rim, extended, down_weight, down_bias)
     normed_half = layer_norm(feature_half, norm_gain)
-    fields = lax.all_to_all(normed_half, "tile", split_axis=0, concat_axis=1, tiled=True)
+    tiles = lax.axis_size("tile")
+    group_width, tile_rows = channels // tiles, normed_half.shape[1]
+    arrived = exchange_chunks(normed_half.reshape(tiles, -1), 0)
+    fields = (
+        arrived.reshape(tiles, group_width, tile_rows, cell_half)
+        .transpose(1, 0, 2, 3)
+        .reshape(group_width, tiles * tile_rows, cell_half)
+    )
     fields = lax.all_gather(fields, "section", axis=2, tiled=True)
 
     cos_h, sin_h = fourier_tables(full_rows)
@@ -211,7 +281,12 @@
         "chqw,qwv->chv", back_rows, inverse_table, preferred_element_type=jnp.float32
     )
     filtered_fields = (result * norm_scale).astype(jnp.bfloat16)
-    rows_back = lax.all_to_all(filtered_fields, "tile", split_axis=1, concat_axis=0, tiled=True)
+    outgoing = (
+        filtered_fields.reshape(group_width, tiles, tile_rows, cell_half)
+        .transpose(1, 0, 2, 3)
+        .reshape(tiles, -1)
+    )
+    rows_back = exchange_chunks(outgoing, 1).reshape(channels, tile_rows, cell_half)
     summed = (feature_half.astype(jnp.float32) + rows_back.astype(jnp.float32)).astype(
         jnp.bfloat16
     )

time: 176 us -> 163 us (0.926)
  Pallas kernels: 0 us -> 48.3 us
  starting transfers between devices: 38.1 us -> 6.87 us
  waiting for transfers between devices: 44.7 us -> 14.7 us
    pallas_call x0 -> x2, Pallas kernels: none -> 48.3 us  [exchange(): pl.pallas_call(exchange_kernel, out_shape=jax.ShapeDtypeStruct(chunks.sha...]
    all_to_all x2 -> x0, waiting for transfers between devices: 31.8 us -> none  [the longest x1 25.4 us: local(): lax.all_to_all(filtered_fields, 'tile', split_axis=1, concat_axis=0, tile...]
    all_to_all x2 -> x0, starting transfers between devices: 30.8 us -> none  [the longest x1 17.3 us: local(): lax.all_to_all(normed_half, 'tile', split_axis=0, concat_axis=1, tiled=True)]
    reshape x0 -> x6, local copies, waits for them, and re-layouts: none -> 7.04 us  [the longest x2 2.57 us: local(): fields = arrived.reshape(tiles, group_width, tile_rows, cell_half).transp...]
    convert_element_type x5 -> x2, local copies, waits for them, and re-layouts: 9.11 us -> 3.82 us  [local(): rows_back.astype(jnp.float32)]
    all_to_all x4 -> x0, local copies, waits for them, and re-layouts: 4.35 us -> none  [the longest x3 2.95 us: local(): lax.all_to_all(normed_half, 'tile', split_axis=0, concat_axis=1, tiled=True)]
    all_gather x1, waiting for transfers between devices: 9.27 us -> 13.4 us  [local(): back_rows = lax.all_gather(back_rows, 'section', axis=3, tiled=True)]
    unnamed x22 -> x51, local copies, waits for them, and re-layouts: 4.61 us -> 7.57 us
  transfers between devices with their start and end apart: 6 -> 4, of which waited for: 6 -> 2; matrix products, arithmetic and copies ran while one was open for 14% -> 15% of each run, Pallas kernels for 0% -> 0%
where the time goes in v1:
time: 163 us; the launch traced here: 162 us
  Pallas kernels  48.3 us (30%)
  local copies, waits for them, and re-layouts  29.8 us (18%)
  matrix products  26.9 us (17%)
  other arithmetic  17.5 us (11%)
  waiting for transfers between devices  14.7 us (9%)
  between operations  13.8 us (8%)
  starting transfers between devices  6.87 us (4%)
  blocking collectives  4.49 us (3%)
    pallas_call x2, Pallas kernels, exchange(): pl.pallas_call(exchange_kernel, out_shape=jax.ShapeDtypeStruct(chunks.sha...  48.3 us
    all_gather x1, waiting for transfers between devices, local(): back_rows = lax.all_gather(back_rows, 'section', axis=3, tiled=True)  13.4 us
    unnamed x51, local copies, waits for them, and re-layouts  7.57 us
    ppermute x2, starting transfers between devices, from_behind(): return lax.ppermute(block, axis, route)  5.85 us
    dot_general x1, matrix products, stem_layers(): jnp.einsum('zji,if->zjf', aerial_patch_grid, patch_kernel_matrix(patch_co...  5.08 us
    all_gather x1, blocking collectives, local(): fields = lax.all_gather(fields, 'section', axis=2, tiled=True)  4.49 us
    dot_general x1, matrix products, stem_layers(): jnp.einsum('zji,if->zjf', initial_layer, merging_kernel_matrix(merging_co...  4.26 us
    dot_general x1, matrix products, filter_columns(): jnp.einsum('puqh,chqw->cpuw', forward_h, row_spectrum, preferred_element_...  3.99 us
  transfers between devices with their start and end apart: 4, of which 2 were waited for; matrix products, arithmetic and copies ran while one was open for 15% of the time, Pallas kernels for 0%

profile of v1, /device:TPU:1, one launch (start us, length us, event | category | flops | bytes accessed | tf_op | source)
XLA Modules:
  0.0 162.4 jit_solution(3493580070187824602)
XLA Ops:
  6.6 0.8 tile.4
  8.3 2.5 %convolution_convert_fusion = bf16[1536,192]{0,1:T(8,128)(2,1)} fusion(bf16[384,192]{1,0:T(8,128)(2,1)} %bitcast.155, s32[1536]{0:T(1024)S(1)} %fusion.101), kind=kOutput, calls=%fused_computation.14 | convolution fusion | flops 227377152 | bytes 743424 | tf_op jit(solution)/shard_map/dot_general | solution.py:92
  10.8 3.5 %fusion.8 = bf16[768,1536,1]{1,0,2:T(8,128)(2,1)} fusion(s32[1536]{0:T(1024)S(1)} %get-tuple-element.41, s32[768]{0:T(1024)S(1)} %get-tuple-element.42, bf16[48,96]{1,0:T(8,128)(2,1)} %bitcast.156, s32[1536]{0:T(1024)S(1)} %get-tuple-element.40, s32[768]{0:T(1024)S(1)} %get-tuple-element.43), kind=kOutput, calls=%fused_computation.11 | convolution fusion | flops 237367296 | bytes 2386944 | tf_op jit(solution)/shard_map/dot_general | solution.py:98
  14.3 5.1 %fusion.7 = bf16[3,192,1536]{2,1,0:T(8,128)(2,1)} fusion(bf16[768,1536,1]{1,0,2:T(8,128)(2,1)} %fusion.8, f32[1536]{0:T(1024)S(1)} %add.322, bf16[3,384,768]{2,1,0:T(8,128)(2,1)S(1)} %copy-done, s32[]{:T(128)S(6)} %select_n.229), kind=kOutput, calls=%fused_computation.10 | convolution fusion | flops 1367801856 | bytes 5021700 | tf_op jit(solution)/shard_map/zji,if->zjf/dot_general | solution.py:148
  19.4 4.3 %fusion.17 = bf16[3,192,768]{2,1,0:T(8,128)(2,1)S(1)} fusion(bf16[3,192,1536]{2,1,0:T(8,128)(2,1)} %fusion.7, bf16[1536,192]{0,1:T(8,128)(2,1)} %convolution_convert_fusion, s32[768]{0:T(1024)S(1)} %get-tuple-element.45, s32[1536]{0:T(1024)S(1)} %fusion.94, f32[768]{0:T(1024)S(1)} %add.335, s32[768]{0:T(1024)S(1)} %get-tuple-element.44), kind=kOutput, calls=%fused_computation.23 | convolution fusion | flops 1820049408 | bytes 3259392 | tf_op jit(solution)/shard_map/zji,if->zjf/dot_general | solution.py:157
  24.2 1.3 collective-permute-start
  25.5 1.2 fusion.56
  26.7 2.5 %sine_convert_fusion = (bf16[384,1,384]{2,0,1:T(8,128)(2,1)S(1)}, bf16[384,1,384]{2,0,1:T(8,128)(2,1)S(1)}) fusion(), kind=kLoop, calls=%fused_computation.93 | loop fusion | flops 1622016 | bytes 589824 | tf_op jit(solution)/shard_map/convert_element_type | solution.py:84
  29.3 3.0 %fusion.77 = bf16[384,1,384]{2,0,1:T(8,128)(2,1)} fusion(), kind=kLoop, calls=%fused_computation.135 | loop fusion | flops 1916928 | bytes 294912 | tf_op jit(solution)/shard_map/neg | solution.py:266
  32.3 1.0 slice_bitcast_fusion.2
  33.3 1.1 maximum_bitcast_fusion.6
  34.4 0.9 pad_maximum_fusion.6
  35.4 0.9 pad_maximum_fusion.7
  36.3 1.5 constant_dynamic-slice_fusion
  38.0 1.5 fusion.53
  39.5 1.7 %fusion.79 = (bf16[1,384,192]{1,2,0:T(8,128)(2,1)}, bf16[384,1,192]{0,2,1:T(8,128)(2,1)}) fusion(f32[384,384]{0,1:T(8,128)S(1)} %copy-done.2, s32[]{:T(128)S(6)} %select_n.229), kind=kLoop, calls=%fused_computation.137 | loop fusion | flops 73728 | bytes 589828 | tf_op jit(solution)/shard_map/stack | solution.py:264
  41.2 4.6 %collective-permute-start.1 = (bf16[1,193,768]{2,1,0:T(8,128)(2,1)S(1)}, bf16[1,193,768]{2,1,0:T(8,128)(2,1)S(1)}, u32[]{:S(2)}, u32[]{:S(2)}) collective-permute-start(bf16[1,193,768]{2,1,0:T(8,128)(2,1)S(1)} %pad_maximum_fusion.8), channel_id=1, source_target_pairs={{0,1},{1,2},{2,3},{3,4},{4,5},{5,6},{6,7},{7,8},{8,9},{9,10},{10,1... | collective-permute-start | bytes 889352 | tf_op jit(solution)/shard_map/ppermute | solution.py:77
  45.8 1.7 %fusion.80 = (bf16[1,384,192]{1,2,0:T(8,128)(2,1)}, bf16[384,1,192]{0,2,1:T(8,128)(2,1)}) fusion(f32[384,384]{0,1:T(8,128)S(1)} %copy-done.2, s32[]{:T(128)S(6)} %select_n.229), kind=kLoop, calls=%fused_computation.138 | loop fusion | flops 294912 | bytes 589828 | tf_op jit(solution)/shard_map/stack | solution.py:264
  47.5 0.9 stack.117
  48.4 0.9 stack.125
  49.3 2.1 %copy.41 = bf16[3,1,384,192]{2,3,1,0:T(8,128)(2,1)} copy(bf16[3,1,384,192]{3,2,1,0:T(8,128)(2,1)} %get-tuple-element.7) | data formatting | bytes 884736
  51.3 2.1 %copy.42 = bf16[3,1,384,192]{2,3,1,0:T(8,128)(2,1)} copy(bf16[3,1,384,192]{3,2,1,0:T(8,128)(2,1)} %get-tuple-element.8) | data formatting | bytes 884736
  53.4 1.7 %fusion.135 = f32[384,3,192]{0,2,1:T(8,128)S(1)} fusion(bf16[768,384,1]{1,0,2:T(8,128)(2,1)} %bitcast.146, bf16[3,192,768]{2,1,0:T(8,128)(2,1)S(1)} %fusion.17), kind=kOutput, calls=%fused_computation.246 | convolution fusion | flops 339738624 | bytes 2359296 | tf_op jit(solution)/shard_map/rwk,kc->crw/dot_general | solution.py:173
  55.4 0.8 copy-done.4
  57.9 0.8 convert_reduce_fusion
  59.3 0.9 copy.23
  60.7 0.9 copy.43
  61.6 25.0 %shard_map.91 = bf16[128,16,128]{2,1,0:T(8,128)(2,1)} custom-call(bf16[128,16,128]{2,1,0:T(8,128)(2,1)} %bitcast.149), custom_call_target="tpu_custom_call" | custom-call | tf_op jit(solution)/shard_map/pallas_call | solution.py:57
  86.6 1.5 copy.38
  88.9 1.2 reshape.363
  90.2 1.3 copy.26
  91.5 4.5 %all_gather.6 = bf16[3,384,384]{1,2,0:T(8,128)(2,1)} all-gather(bf16[3,384,192]{1,2,0:T(8,128)(2,1)S(1)} %copy.26), channel_id=1, replica_groups=mesh['section'=2,'tile'=128] {'section'}, dimensions={2}, use_global_device_ids=true | all-gather | bytes 1327104 | tf_op jit(solution)/shard_map/all_gather | solution.py:254
  96.0 4.0 %fusion.21 = bf16[3,2,384,192]{2,3,1,0:T(8,128)(2,1)} fusion(bf16[1,384,2,384]{3,1,2,0:T(8,128)(2,1)} %get-tuple-element.29, bf16[1,384,2,384]{3,1,2,0:T(8,128)(2,1)} %get-tuple-element.22, bf16[3,384,384]{1,2,0:T(8,128)(2,1)} %all_gather.6, bf16[384,1,192]{0,2,1:T(8,128)(2,1)S(1)} %copy-done.20, bf16[384,1,192]{0,2,1:T(8,128)(2,1)S(1)} %copy-done.19), kind=kOutput, calls=%fused_computation.35 | convolution fusion | flops 1023049728 | bytes 3244032 | tf_op jit(solution)/shard_map/puqh,chqw->cpuw/dot_general | solution.py:199
  100.0 1.6 fusion.37
  101.6 1.8 %fusion.22 = bf16[3,384,2,192]{1,3,2,0:T(8,128)(2,1)} fusion(bf16[1,384,2,384]{3,1,2,0:T(8,128)(2,1)S(1)} %copy-done.10, bf16[1,384,2,384]{3,1,2,0:T(8,128)(2,1)S(1)} %copy-done.11, bf16[3,1,384,192]{2,3,1,0:T(8,128)(2,1)S(1)} %get-tuple-element.6, bf16[3,1,384,192]{2,3,1,0:T(8,128)(2,1)S(1)} %get-tuple-element.5), kind=kOutput, calls=%fused_computation.36 | convolution fusion | flops 684048384 | bytes 2949120 | tf_op jit(solution)/shard_map/qhpu,cpuw->chqw/dot_general | solution.py:213
  103.5 13.4 %all-gather.2.cloned.1.call-done = bf16[3,384,2,384]{1,3,2,0:T(8,128)(2,1)} async-done(((bf16[3,384,2,192]{1,3,2,0:T(8,128)(2,1)}), bf16[3,384,2,384]{1,3,2,0:T(8,128)(2,1)}) %all-gather.2.cloned.1.call-update) | async-done | bytes 1769488 | tf_op jit(solution)/shard_map/all_gather | solution.py:279
  116.9 2.0 %fusion.24 = bf16[3,384,192]{1,2,0:T(8,128)(2,1)S(1)} fusion(bf16[3,384,2,384]{1,3,2,0:T(8,128)(2,1)} %all-gather.2.cloned.1.call-done, bf16[1,384,192]{1,2,0:T(8,128)(2,1)S(1)} %copy-done.18, bf16[1,384,192]{1,2,0:T(8,128)(2,1)S(1)} %copy-done.17), kind=kOutput, calls=%fused_computation.39 | convolution fusion | flops 340770816 | bytes 2506752 | tf_op jit(solution)/shard_map/chqw,qwv->chv/dot_general | solution.py:280
  119.0 1.1 copy.27
  120.0 1.3 reshape.364
  121.3 0.8 copy.28
  122.2 1.2 copy.39.x_ref
  123.4 23.3 %shard_map.92 = bf16[128,16,128]{2,1,0:T(8,128)(2,1)} custom-call(bf16[128,16,128]{2,1,0:T(8,128)(2,1)} %copy.39.x_ref), custom_call_target="tpu_custom_call" | custom-call | tf_op jit(solution)/shard_map/pallas_call | solution.py:57
  146.6 1.2 copy.46
  147.9 2.1 %reshape.368 = f32[384,3,192]{2,1,0:T(4,128)} reshape(f32[128,1728]{1,0:T(8,128)S(1)} %slice_convert_fusion) | data formatting | bytes 1769472 | tf_op jit(solution)/shard_map/convert_element_type | solution.py:290
  150.0 1.7 %copy.30 = f32[384,3,192]{0,2,1:T(8,128)S(1)} copy(f32[384,3,192]{2,1,0:T(4,128)} %reshape.368) | data formatting | bytes 1769472 | tf_op jit(solution)/shard_map/convert_element_type | solution.py:290
  152.1 1.0 collective-permute-start.2
  153.1 1.2 collective-permute-done.2
  154.6 1.0 copy.31
  (77 shorter events, 6.3 us)
Async XLA Ops:
  6.5 7.7 %copy-start = (bf16[3,384,768]{2,1,0:T(8,128)(2,1)S(1)}, bf16[3,384,768]{2,1,0:T(8,128)(2,1)}, u32[]{:S(2)}) copy-start(bf16[3,384,768]{2,1,0:T(8,128)(2,1)} %param.9) | copy-start | bytes 5308420
  6.5 110.4 %all-gather.2.cloned.1.call-start = ((), (), s32[]{:S(2)}) async-start(), calls=%async_computation | async-start | bytes 2654208 | tf_op jit(solution)/shard_map/all_gather | solution.py:279
  23.6 8.6 %copy-start.7 = (bf16[3,3,192,384]{3,2,1,0:T(8,128)(2,1)S(1)}, bf16[3,3,192,384]{3,2,1,0:T(8,128)(2,1)}, u32[]{:S(2)}) copy-start(bf16[3,3,192,384]{3,2,1,0:T(8,128)(2,1)} %param.14) | copy-start | bytes 3981316
  24.2 16.9 %collective-permute-start = (bf16[3,1,768]{2,1,0:T(2,128)(2,1)}, bf16[3,1,768]{2,1,0:T(2,128)(2,1)S(1)}, u32[]{:S(2)}, u32[]{:S(2)}) collective-permute-start(bf16[3,1,768]{2,1,0:T(2,128)(2,1)} %slice.80), channel_id=1, source_target_pairs={{0,128},{1,129},{2,130},{3,131},{4,132},{5,133},{6,134},{7,135},{8... | collective-permute-start | bytes 13832 | tf_op jit(solution)/shard_map/ppermute | solution.py:77
  33.3 2.0 %copy-start.12 = (bf16[1,192,384]{2,1,0:T(8,128)(2,1)S(1)}, bf16[1,192,384]{2,1,0:T(8,128)(2,1)}, u32[]{:S(2)}) copy-start(bf16[1,192,384]{2,1,0:T(8,128)(2,1)} %get-tuple-element.9) | copy-start | bytes 442372
  33.3 2.0 %copy-start.13 = (bf16[1,192,384]{2,1,0:T(8,128)(2,1)S(1)}, bf16[1,192,384]{2,1,0:T(8,128)(2,1)}, u32[]{:S(2)}) copy-start(bf16[1,192,384]{2,1,0:T(8,128)(2,1)} %get-tuple-element.17) | copy-start | bytes 442372
  34.4 1.9 %copy-start.9 = (bf16[3,2,384,384]{3,2,1,0:T(8,128)(2,1)S(1)}, bf16[3,2,384,384]{3,2,1,0:T(8,128)(2,1)}, u32[]{:S(2)}) copy-start(bf16[3,2,384,384]{3,2,1,0:T(8,128)(2,1)} %param.17) | copy-start | bytes 5308420
  35.4 2.5 %copy-start.14 = (bf16[1,192,384]{2,1,0:T(8,128)(2,1)S(1)}, bf16[1,192,384]{2,1,0:T(8,128)(2,1)}, u32[]{:S(2)}) copy-start(bf16[1,192,384]{2,1,0:T(8,128)(2,1)} %get-tuple-element.10) | copy-start | bytes 442372
  35.4 2.5 %copy-start.15 = (bf16[1,192,384]{2,1,0:T(8,128)(2,1)S(1)}, bf16[1,192,384]{2,1,0:T(8,128)(2,1)}, u32[]{:S(2)}) copy-start(bf16[1,192,384]{2,1,0:T(8,128)(2,1)} %get-tuple-element.11) | copy-start | bytes 442372
  35.4 2.5 %copy-start.16 = (bf16[1,192,384]{2,1,0:T(8,128)(2,1)S(1)}, bf16[1,192,384]{2,1,0:T(8,128)(2,1)}, u32[]{:S(2)}) copy-start(bf16[1,192,384]{2,1,0:T(8,128)(2,1)} %get-tuple-element.16) | copy-start | bytes 442372
  36.3 1.6 %copy-start.8 = (bf16[384,1,384]{2,0,1:T(8,128)(2,1)S(1)}, bf16[384,1,384]{2,0,1:T(8,128)(2,1)}, u32[]{:S(2)}) copy-start(bf16[384,1,384]{2,0,1:T(8,128)(2,1)} %fusion.77) | copy-start | bytes 884740
  38.0 1.5 copy-start.2
  41.2 13.9 %collective-permute-start.1 = (bf16[1,193,768]{2,1,0:T(8,128)(2,1)S(1)}, bf16[1,193,768]{2,1,0:T(8,128)(2,1)S(1)}, u32[]{:S(2)}, u32[]{:S(2)}) collective-permute-start(bf16[1,193,768]{2,1,0:T(8,128)(2,1)S(1)} %pad_maximum_fusion.8), channel_id=1, source_target_pairs={{0,1},{1,2},{2,3},{3,4},{4,5},{5,6},{6,7},{7,8},{8,9},{9,10},{10,1... | collective-permute-start | bytes 889352 | tf_op jit(solution)/shard_map/ppermute | solution.py:77
  55.1 1.1 copy-start.4
  55.3 1.5 copy-start.1
  56.8 1.1 copy-start.3
  56.8 1.1 copy-start.21
  57.9 1.2 copy-start.22
  88.9 7.1 %copy-start.19 = (bf16[384,1,192]{0,2,1:T(8,128)(2,1)S(1)}, bf16[384,1,192]{0,2,1:T(8,128)(2,1)}, u32[]{:S(2)}) copy-start(bf16[384,1,192]{0,2,1:T(8,128)(2,1)} %get-tuple-element.19) | copy-start | bytes 442372
  88.9 7.1 %copy-start.20 = (bf16[384,1,192]{0,2,1:T(8,128)(2,1)S(1)}, bf16[384,1,192]{0,2,1:T(8,128)(2,1)}, u32[]{:S(2)}) copy-start(bf16[384,1,192]{0,2,1:T(8,128)(2,1)} %get-tuple-element.21) | copy-start | bytes 442372
  96.0 4.0 %copy-start.5 = (bf16[3,1,384,192]{2,3,1,0:T(8,128)(2,1)S(1)}, bf16[3,1,384,192]{2,3,1,0:T(8,128)(2,1)}, u32[]{:S(2)}) copy-start(bf16[3,1,384,192]{2,3,1,0:T(8,128)(2,1)} %copy.41) | copy-start | bytes 1327108
  96.0 4.0 %copy-start.6 = (bf16[3,1,384,192]{2,3,1,0:T(8,128)(2,1)S(1)}, bf16[3,1,384,192]{2,3,1,0:T(8,128)(2,1)}, u32[]{:S(2)}) copy-start(bf16[3,1,384,192]{2,3,1,0:T(8,128)(2,1)} %copy.42) | copy-start | bytes 1327108
  100.0 1.6 copy-start.10
  100.0 1.6 copy-start.11
  101.6 15.3 %copy-start.17 = (bf16[1,384,192]{1,2,0:T(8,128)(2,1)S(1)}, bf16[1,384,192]{1,2,0:T(8,128)(2,1)}, u32[]{:S(2)}) copy-start(bf16[1,384,192]{1,2,0:T(8,128)(2,1)} %get-tuple-element.18) | copy-start | bytes 442372
  101.6 15.3 %copy-start.18 = (bf16[1,384,192]{1,2,0:T(8,128)(2,1)S(1)}, bf16[1,384,192]{1,2,0:T(8,128)(2,1)}, u32[]{:S(2)}) copy-start(bf16[1,384,192]{1,2,0:T(8,128)(2,1)} %get-tuple-element.20) | copy-start | bytes 442372
  152.1 2.2 %collective-permute-start.2 = (bf16[192,3,192]{0,2,1:T(8,128)(2,1)S(1)}, bf16[192,3,192]{0,2,1:T(8,128)(2,1)S(1)}, u32[]{:S(2)}, u32[]{:S(2)}) collective-permute-start(bf16[192,3,192]{0,2,1:T(8,128)(2,1)S(1)} %get-tuple-element.27), channel_id=1, source_target_pairs={{0,128},{128,0},{1,129},{129,1},{2,130},{130,2},{3,131},{131,3},{4... | collective-permute-start | bytes 663560 | tf_op jit(solution)/shard_map/ppermute | solution.py:297
Sparse Core Ops, SparseCore 0:
  103.6 13.2 all-gather.1

commit v2 on v1

--- a/solution.py
+++ b/solution.py
@@ -251,7 +251,8 @@
         .transpose(1, 0, 2, 3)
         .reshape(group_width, tiles * tile_rows, cell_half)
     )
-    fields = lax.all_gather(fields, "section", axis=2, tiled=True)
+    swap = [(0, 1), (1, 0)]
+    other_fields = lax.ppermute(fields, "section", swap)
 
     cos_h, sin_h = fourier_tables(full_rows)
     if full_rows == field_cols:
@@ -272,13 +273,33 @@
     kernel_part = lax.dynamic_slice_in_dim(
         spectral_filter, section_index * cell_half, cell_half, 3
     )
+    own_start = section_index * cell_half
+    other_start = (1 - section_index) * cell_half
     frequency_rows = jnp.einsum(
-        "chx,xqw->chqw", fields, forward_table, preferred_element_type=jnp.float32
-    ).astype(jnp.bfloat16)
-    back_rows = filter_columns(frequency_rows, kernel_part, forward_h, inverse_h)
-    back_rows = lax.all_gather(back_rows, "section", axis=3, tiled=True)
+        "chx,xqw->chqw",
+        fields,
+        lax.dynamic_slice_in_dim(forward_table, own_start, cell_half, 0),
+        preferred_element_type=jnp.float32,
+    ) + jnp.einsum(
+        "chx,xqw->chqw",
+        other_fields,
+        lax.dynamic_slice_in_dim(forward_table, other_start, cell_half, 0),
+        preferred_element_type=jnp.float32,
+    )
+    back_rows = filter_columns(
+        frequency_rows.astype(jnp.bfloat16), kernel_part, forward_h, inverse_h
+    )
+    other_rows = lax.ppermute(back_rows, "section", swap)
     result = jnp.einsum(
-        "chqw,qwv->chv", back_rows, inverse_table, preferred_element_type=jnp.float32
+        "chqw,qwv->chv",
+        back_rows,
+        lax.dynamic_slice_in_dim(inverse_table, own_start, cell_half, 1),
+        preferred_element_type=jnp.float32,
+    ) + jnp.einsum(
+        "chqw,qwv->chv",
+        other_rows,
+        lax.dynamic_slice_in_dim(inverse_table, other_start, cell_half, 1),
+        preferred_element_type=jnp.float32,
     )
     filtered_fields = (result * norm_scale).astype(jnp.bfloat16)
     outgoing = (
@@ -294,7 +315,7 @@
     sent = lax.dynamic_slice_in_dim(
         summed, (1 - section_index) * half_channels, half_channels, 0
     )
-    received = lax.ppermute(sent, "section", [(0, 1), (1, 0)])
+    received = lax.ppermute(sent, "section", swap)
     return jnp.where(
         section_index == 0,
         jnp.concatenate([kept, received], axis=2),

time: 163 us -> 138 us (0.85)
  between operations: 13.8 us -> 0.44 us
  waiting for transfers between devices: 14.7 us -> 2.96 us
  blocking collectives: 4.49 us -> 0 us
  starting transfers between devices: 6.87 us -> 9.75 us
  Pallas kernels: 48.3 us -> 46.3 us
  local copies, waits for them, and re-layouts: 29.8 us -> 31.6 us
  other arithmetic: 17.5 us -> 19.2 us
    all_gather x1 -> x0, waiting for transfers between devices: 13.4 us -> none  [local(): back_rows = lax.all_gather(back_rows, 'section', axis=3, tiled=True)]
    all_gather x1 -> x0, blocking collectives: 4.49 us -> none  [local(): fields = lax.all_gather(fields, 'section', axis=2, tiled=True)]
    ppermute x1 -> x3, starting transfers between devices: 1.02 us -> 3.36 us  [the longest x1 2.06 us: local(): other_fields = lax.ppermute(fields, 'section', swap)]
    pallas_call x2, Pallas kernels: 48.3 us -> 46.3 us  [exchange(): pl.pallas_call(exchange_kernel, out_shape=jax.ShapeDtypeStruct(chunks.sha...]
    ppermute x1 -> x3, waiting for transfers between devices: 1.21 us -> 2.96 us  [the longest x1 1.75 us: local(): other_rows = lax.ppermute(back_rows, 'section', swap)]
    unnamed x51 -> x55, local copies, waits for them, and re-layouts: 7.57 us -> 7.6 us
  transfers between devices with their start and end apart: 4 -> 5, of which waited for: 2 -> 2; matrix products, arithmetic and copies ran while one was open for 15% -> 21% of each run, Pallas kernels for 0% -> 0%
where the time goes in v2:
time: 138 us; the launch traced here: 137 us
  Pallas kernels  46.3 us (34%)
  local copies, waits for them, and re-layouts  31.6 us (23%)
  matrix products  27.1 us (20%)
  other arithmetic  19.2 us (14%)
  starting transfers between devices  9.75 us (7%)
  waiting for transfers between devices  2.96 us (2%)
    pallas_call x2, Pallas kernels, exchange(): pl.pallas_call(exchange_kernel, out_shape=jax.ShapeDtypeStruct(chunks.sha...  46.3 us
    unnamed x55, local copies, waits for them, and re-layouts  7.6 us
    ppermute x2, starting transfers between devices, from_behind(): return lax.ppermute(block, axis, route)  6.39 us
    dot_general x1, matrix products, stem_layers(): jnp.einsum('zji,if->zjf', aerial_patch_grid, patch_kernel_matrix(patch_co...  5.07 us
    dot_general x1, matrix products, stem_layers(): jnp.einsum('zji,if->zjf', initial_layer, merging_kernel_matrix(merging_co...  4.26 us
    dot_general x1, matrix products, filter_columns(): jnp.einsum('puqh,chqw->cpuw', forward_h, row_spectrum, preferred_element_...  4.16 us
    convert_element_type x2, local copies, waits for them, and re-layouts, local(): rows_back.astype(jnp.float32)  3.82 us
    dot_general x1, matrix products, spread_kernel(): full = jnp.dot(picked, repeat, preferred_element_type=jnp.float32)  3.49 us
  transfers between devices with their start and end apart: 5, of which 2 were waited for; matrix products, arithmetic and copies ran while one was open for 21% of the time, Pallas kernels for 0%

profile of v2, /device:TPU:1, one launch (start us, length us, event | category | flops | bytes accessed | tf_op | source)
XLA Modules:
  0.0 137.3 jit_solution(14651710593333424066)
XLA Ops:
  0.1 0.8 tile.4
  1.7 2.5 %convolution_convert_fusion = bf16[1536,192]{0,1:T(8,128)(2,1)} fusion(bf16[384,192]{1,0:T(8,128)(2,1)} %bitcast.171, s32[1536]{0:T(1024)S(1)} %fusion.110), kind=kOutput, calls=%fused_computation.14 | convolution fusion | flops 227377152 | bytes 743424 | tf_op jit(solution)/shard_map/dot_general | solution.py:92
  4.2 3.5 %fusion.8 = bf16[768,1536,1]{1,0,2:T(8,128)(2,1)} fusion(s32[1536]{0:T(1024)S(1)} %get-tuple-element.45, s32[768]{0:T(1024)S(1)} %get-tuple-element.36, bf16[48,96]{1,0:T(8,128)(2,1)} %bitcast.172, s32[1536]{0:T(1024)S(1)} %get-tuple-element.44, s32[768]{0:T(1024)S(1)} %get-tuple-element.37), kind=kOutput, calls=%fused_computation.11 | convolution fusion | flops 237367296 | bytes 2386944 | tf_op jit(solution)/shard_map/dot_general | solution.py:98
  7.7 5.1 %fusion.7 = bf16[3,192,1536]{2,1,0:T(8,128)(2,1)} fusion(bf16[768,1536,1]{1,0,2:T(8,128)(2,1)} %fusion.8, f32[1536]{0:T(1024)S(1)} %add.332, bf16[3,384,768]{2,1,0:T(8,128)(2,1)S(1)} %copy-done, s32[]{:T(128)S(6)} %select_n.233), kind=kOutput, calls=%fused_computation.10 | convolution fusion | flops 1367801856 | bytes 5021700 | tf_op jit(solution)/shard_map/zji,if->zjf/dot_general | solution.py:148
  12.8 4.3 %fusion.17 = bf16[3,192,768]{2,1,0:T(8,128)(2,1)S(1)} fusion(bf16[3,192,1536]{2,1,0:T(8,128)(2,1)} %fusion.7, bf16[1536,192]{0,1:T(8,128)(2,1)} %convolution_convert_fusion, s32[768]{0:T(1024)S(1)} %get-tuple-element.35, s32[1536]{0:T(1024)S(1)} %fusion.103, f32[768]{0:T(1024)S(1)} %add.345, s32[768]{0:T(1024)S(1)} %get-tuple-element.34), kind=kOutput, calls=%fused_computation.23 | convolution fusion | flops 1820049408 | bytes 3259392 | tf_op jit(solution)/shard_map/zji,if->zjf/dot_general | solution.py:157
  17.7 1.3 collective-permute-start
  19.3 3.2 %sine_convert_fusion = (bf16[384,1,384]{2,0,1:T(8,128)(2,1)}, bf16[384,1,384]{2,0,1:T(8,128)(2,1)}) fusion(), kind=kLoop, calls=%fused_computation.96 | loop fusion | flops 1622016 | bytes 589824 | tf_op jit(solution)/shard_map/convert_element_type | solution.py:84
  22.6 2.2 %slice_bitcast_fusion.2 = (bf16[1,192,384]{2,1,0:T(8,128)(2,1)S(1)}, bf16[1,192,384]{2,1,0:T(8,128)(2,1)}, bf16[1,192,384]{2,1,0:T(8,128)(2,1)}, bf16[1,192,384]...) fusion(bf16[3,3,192,384]{3,2,1,0:T(8,128)(2,1)} %param.14), kind=kLoop, calls=%fused_computation.142 | loop fusion | bytes 2654208 | tf_op jit(solution)/shard_map/stack;squeeze | solution.py:135
  24.8 1.7 %fusion.89 = (bf16[1,384,192]{1,2,0:T(8,128)(2,1)}, bf16[384,1,192]{0,2,1:T(8,128)(2,1)}) fusion(f32[384,384]{0,1:T(8,128)S(1)} %fusion.54, s32[]{:T(128)S(6)} %select_n.233), kind=kLoop, calls=%fused_computation.152 | loop fusion | flops 294912 | bytes 589828 | tf_op jit(solution)/shard_map/stack | solution.py:265
  26.6 0.9 pad_maximum_fusion.6
  27.6 0.9 pad_maximum_fusion.7
  28.5 1.5 %constant_dynamic-slice_fusion = (bf16[3,1,384,192]{3,2,1,0:T(8,128)(2,1)}, bf16[3,1,384,192]{3,2,1,0:T(8,128)(2,1)}) fusion(bf16[3,2,384,384]{3,2,1,0:T(8,128)(2,1)S(1)} %copy-done.12, s32[]{:T(128)S(6)} %select_n.233, s32[]{:T(128)S(6)} %add.365), kind=kLoop, calls=%fused_computation.250 | loop fusion | bytes 1769480 | tf_op jit(solution)/shard_map/slice | solution.py:204
  30.1 1.7 %fusion.88 = (bf16[1,384,192]{1,2,0:T(8,128)(2,1)}, bf16[384,1,192]{0,2,1:T(8,128)(2,1)}) fusion(f32[384,384]{0,1:T(8,128)S(1)} %copy-done.4, s32[]{:T(128)S(6)} %select_n.233), kind=kLoop, calls=%fused_computation.151 | loop fusion | flops 73728 | bytes 589828 | tf_op jit(solution)/shard_map/stack | solution.py:265
  31.7 0.8 pad_maximum_fusion.8
  32.5 5.1 %collective-permute-start.1 = (bf16[1,193,768]{2,1,0:T(8,128)(2,1)}, bf16[1,193,768]{2,1,0:T(8,128)(2,1)}, u32[]{:S(2)}, u32[]{:S(2)}) collective-permute-start(bf16[1,193,768]{2,1,0:T(8,128)(2,1)} %pad_maximum_fusion.8), channel_id=1, source_target_pairs={{0,1},{1,2},{2,3},{3,4},{4,5},{5,6},{6,7},{7,8},{8,9},{9,10},{10,1... | collective-permute-start | bytes 889352 | tf_op jit(solution)/shard_map/ppermute | solution.py:77
  37.6 3.0 %fusion.86 = bf16[384,1,384]{2,0,1:T(8,128)(2,1)} fusion(), kind=kLoop, calls=%fused_computation.149 | loop fusion | flops 1916928 | bytes 294912 | tf_op jit(solution)/shard_map/neg | solution.py:267
  40.6 0.9 stack.117
  41.5 0.9 stack.125
  42.4 2.1 %copy.46 = bf16[3,1,384,192]{2,3,1,0:T(8,128)(2,1)} copy(bf16[3,1,384,192]{3,2,1,0:T(8,128)(2,1)} %get-tuple-element.7) | data formatting | bytes 884736
  44.4 2.1 %copy.47 = bf16[3,1,384,192]{2,3,1,0:T(8,128)(2,1)} copy(bf16[3,1,384,192]{3,2,1,0:T(8,128)(2,1)} %get-tuple-element.8) | data formatting | bytes 884736
  46.5 1.7 %fusion.151 = f32[384,3,192]{0,2,1:T(8,128)S(1)} fusion(bf16[768,384,1]{1,0,2:T(8,128)(2,1)} %bitcast.162, bf16[3,192,768]{2,1,0:T(8,128)(2,1)S(1)} %fusion.17), kind=kOutput, calls=%fused_computation.266 | convolution fusion | flops 339738624 | bytes 2359296 | tf_op jit(solution)/shard_map/rwk,kc->crw/dot_general | solution.py:173
  48.2 1.2 maximum_maximum_fusion
  52.6 0.9 copy.23
  54.1 0.9 copy.48
  55.0 24.5 %shard_map.91 = bf16[128,16,128]{2,1,0:T(8,128)(2,1)} custom-call(bf16[128,16,128]{2,1,0:T(8,128)(2,1)} %bitcast.165), custom_call_target="tpu_custom_call" | custom-call | tf_op jit(solution)/shard_map/pallas_call | solution.py:57
  79.5 1.5 %copy.41 = bf16[128,16,128]{0,2,1:T(8,128)(2,1)S(1)} copy(bf16[128,16,128]{2,1,0:T(8,128)(2,1)} %shard_map.91) | data formatting | bytes 1048576 | tf_op jit(solution)/shard_map/reshape | solution.py:71
  81.0 1.4 copy.25
  82.4 1.6 %reshape.363 = bf16[3,384,192]{2,1,0:T(8,128)(2,1)S(1)} reshape(bf16[3,128,3,192]{3,2,1,0:T(4,128)(2,1)} %copy.25) | data formatting | bytes 884736 | tf_op jit(solution)/shard_map/reshape | solution.py:252
  83.9 1.0 copy.27
  84.9 2.1 %collective-permute-start.2 = (bf16[3,384,192]{1,2,0:T(8,128)(2,1)}, bf16[3,384,192]{1,2,0:T(8,128)(2,1)S(1)}, u32[]{:S(2)}, u32[]{:S(2)}) collective-permute-start(bf16[3,384,192]{1,2,0:T(8,128)(2,1)} %copy.27), channel_id=1, source_target_pairs={{0,128},{128,0},{1,129},{129,1},{2,130},{130,2},{3,131},{131,3},{4... | collective-permute-start | bytes 1327112 | tf_op jit(solution)/shard_map/ppermute | solution.py:255
  87.0 2.6 %fusion.51 = (bf16[1,384,2,384]{3,1,2,0:T(8,128)(2,1)}, bf16[1,384,2,384]{3,1,2,0:T(8,128)(2,1)}, bf16[1,384,2,384]{3,1,2,0:T(8,128)(2,1)}, bf16[1,384,2,384]{3,1,2,0:T(8,128)(2,1)}) fusion(bf16[384,1,384]{2,0,1:T(8,128)(2,1)S(1)} %copy-done.11, bf16[384,1,384]{2,0,1:T(8,128)(2,1)S(1)} %copy-done.10, bf16[384,1,384]{2,0,1:T(8,128)(2,1)} %fusion.86), kind=kLoop, calls=%fused_computation.85 | loop fusion | flops 1179648 | bytes 3244032 | tf_op jit(solution)/shard_map/stack | solution.py:266
  89.6 1.7 %fusion.57 = f32[3,384,2,192]{1,3,2,0:T(8,128)} fusion(bf16[3,384,192]{2,1,0:T(8,128)(2,1)S(1)} %reshape.363, s32[]{:T(128)S(6)} %select_n.233, bf16[384,1,192]{0,2,1:T(8,128)(2,1)S(1)} %copy-done.17, bf16[384,1,192]{0,2,1:T(8,128)(2,1)S(1)} %copy-done.15), kind=kOutput, calls=%fused_computation.94 | convolution fusion | flops 170164224 | bytes 2506756 | tf_op jit(solution)/shard_map/chx,xqw->chqw/dot_general | solution.py:278
  91.4 0.8 copy-done.24
  92.2 4.2 %fusion.21 = bf16[3,2,384,192]{2,3,1,0:T(8,128)(2,1)} fusion(bf16[1,384,2,384]{3,1,2,0:T(8,128)(2,1)} %get-tuple-element.29, bf16[1,384,2,384]{3,1,2,0:T(8,128)(2,1)} %get-tuple-element.22, f32[3,384,2,192]{1,3,2,0:T(8,128)} %fusion.57, bf16[3,384,192]{1,2,0:T(8,128)(2,1)} %copy-done.24, s32[]{:T(128)S(6)} %select_n.255, ...), kind=kOutput, calls=%fused_computation.35 | convolution fusion | flops 853327872 | bytes 4571140 | tf_op jit(solution)/shard_map/puqh,chqw->cpuw/dot_general | solution.py:199
  96.3 1.6 %fusion.38 = (bf16[3,1,384,192]{2,3,1,0:T(8,128)(2,1)S(1)}, bf16[3,1,384,192]{2,3,1,0:T(8,128)(2,1)S(1)}) fusion(bf16[3,1,384,192]{2,3,1,0:T(8,128)(2,1)S(1)} %copy-done.6, bf16[3,1,384,192]{2,3,1,0:T(8,128)(2,1)S(1)} %copy-done.7, bf16[3,2,384,192]{2,3,1,0:T(8,128)(2,1)} %fusion.21), kind=kLoop, calls=%fused_computation.62 | loop fusion | flops 2654208 | bytes 2654208 | tf_op jit(solution)/shard_map/convert.1
  98.0 0.9 fusion.22
  99.8 1.7 %collective-permute-done.3 = bf16[3,384,2,192]{1,3,2,0:T(8,128)(2,1)S(1)} collective-permute-done((bf16[3,384,2,192]{1,3,2,0:T(8,128)(2,1)S(1)}, bf16[3,384,2,192]{1,3,2,0:T(8,128)(2,1)S(1)}, u32[]{:S(2)}, u32[]{:S(2)}) %collective-permute-start.3) | collective-permute-done | bytes 884768 | tf_op jit(solution)/shard_map/ppermute | solution.py:292
  102.2 1.1 copy.28
  103.3 1.3 reshape.364
  104.6 0.8 copy.29
  105.4 1.2 copy.44.x_ref
  106.6 21.8 %shard_map.92 = bf16[128,16,128]{2,1,0:T(8,128)(2,1)} custom-call(bf16[128,16,128]{2,1,0:T(8,128)(2,1)} %copy.44.x_ref), custom_call_target="tpu_custom_call" | custom-call | tf_op jit(solution)/shard_map/pallas_call | solution.py:57
  128.4 1.2 copy.51
  129.7 2.1 %reshape.368 = f32[384,3,192]{2,1,0:T(4,128)} reshape(f32[128,1728]{1,0:T(8,128)S(1)} %slice_convert_fusion) | data formatting | bytes 1769472 | tf_op jit(solution)/shard_map/convert_element_type | solution.py:311
  131.8 1.7 %copy.31 = f32[384,3,192]{0,2,1:T(8,128)S(1)} copy(f32[384,3,192]{2,1,0:T(4,128)} %reshape.368) | data formatting | bytes 1769472 | tf_op jit(solution)/shard_map/convert_element_type | solution.py:311
  133.9 1.0 collective-permute-start.4
  134.8 1.2 collective-permute-done.4
  136.3 1.0 copy.32
  (83 shorter events, 8.1 us)
Async XLA Ops:
  0.0 7.7 %copy-start = (bf16[3,384,768]{2,1,0:T(8,128)(2,1)S(1)}, bf16[3,384,768]{2,1,0:T(8,128)(2,1)}, u32[]{:S(2)}) copy-start(bf16[3,384,768]{2,1,0:T(8,128)(2,1)} %param.9) | copy-start | bytes 5308420
  17.7 14.1 %collective-permute-start = (bf16[3,1,768]{2,1,0:T(2,128)(2,1)}, bf16[3,1,768]{2,1,0:T(2,128)(2,1)S(1)}, u32[]{:S(2)}, u32[]{:S(2)}) collective-permute-start(bf16[3,1,768]{2,1,0:T(2,128)(2,1)} %slice.80), channel_id=1, source_target_pairs={{0,128},{1,129},{2,130},{3,131},{4,132},{5,133},{6,134},{7,135},{8... | collective-permute-start | bytes 13832 | tf_op jit(solution)/shard_map/ppermute | solution.py:77
  19.3 5.5 %copy-start.3 = (f32[384,384]{0,1:T(8,128)}, f32[384,384]{0,1:T(8,128)S(1)}, u32[]{:S(2)}) copy-start(f32[384,384]{0,1:T(8,128)S(1)} %fusion.54) | copy-start | bytes 1769476
  26.6 1.9 %copy-start.12 = (bf16[3,2,384,384]{3,2,1,0:T(8,128)(2,1)S(1)}, bf16[3,2,384,384]{3,2,1,0:T(8,128)(2,1)}, u32[]{:S(2)}) copy-start(bf16[3,2,384,384]{3,2,1,0:T(8,128)(2,1)} %param.17) | copy-start | bytes 5308420
  27.5 2.4 %copy-start.19 = (bf16[1,192,384]{2,1,0:T(8,128)(2,1)S(1)}, bf16[1,192,384]{2,1,0:T(8,128)(2,1)}, u32[]{:S(2)}) copy-start(bf16[1,192,384]{2,1,0:T(8,128)(2,1)} %get-tuple-element.10) | copy-start | bytes 442372
  27.6 2.4 %copy-start.20 = (bf16[1,192,384]{2,1,0:T(8,128)(2,1)S(1)}, bf16[1,192,384]{2,1,0:T(8,128)(2,1)}, u32[]{:S(2)}) copy-start(bf16[1,192,384]{2,1,0:T(8,128)(2,1)} %get-tuple-element.11) | copy-start | bytes 442372
  27.6 2.4 %copy-start.21 = (bf16[1,192,384]{2,1,0:T(8,128)(2,1)S(1)}, bf16[1,192,384]{2,1,0:T(8,128)(2,1)}, u32[]{:S(2)}) copy-start(bf16[1,192,384]{2,1,0:T(8,128)(2,1)} %get-tuple-element.16) | copy-start | bytes 442372
  28.5 1.6 %copy-start.4 = (f32[384,384]{0,1:T(8,128)S(1)}, f32[384,384]{0,1:T(8,128)}, u32[]{:S(2)}) copy-start(f32[384,384]{0,1:T(8,128)} %copy-done.3) | copy-start | bytes 1769476
  32.5 15.7 %collective-permute-start.1 = (bf16[1,193,768]{2,1,0:T(8,128)(2,1)}, bf16[1,193,768]{2,1,0:T(8,128)(2,1)}, u32[]{:S(2)}, u32[]{:S(2)}) collective-permute-start(bf16[1,193,768]{2,1,0:T(8,128)(2,1)} %pad_maximum_fusion.8), channel_id=1, source_target_pairs={{0,1},{1,2},{2,3},{3,4},{4,5},{5,6},{6,7},{7,8},{8,9},{9,10},{10,1... | collective-permute-start | bytes 889352 | tf_op jit(solution)/shard_map/ppermute | solution.py:77
  48.2 1.3 copy-start.5
  49.5 1.1 copy-start.1
  50.1 1.1 copy-start.2
  50.1 1.1 copy-start.22
  51.2 1.2 copy-start.23
  81.0 6.0 %copy-start.10 = (bf16[384,1,384]{2,0,1:T(8,128)(2,1)S(1)}, bf16[384,1,384]{2,0,1:T(8,128)(2,1)}, u32[]{:S(2)}) copy-start(bf16[384,1,384]{2,0,1:T(8,128)(2,1)} %get-tuple-element.32) | copy-start | bytes 884740
  82.4 4.6 %copy-start.11 = (bf16[384,1,384]{2,0,1:T(8,128)(2,1)S(1)}, bf16[384,1,384]{2,0,1:T(8,128)(2,1)}, u32[]{:S(2)}) copy-start(bf16[384,1,384]{2,0,1:T(8,128)(2,1)} %get-tuple-element.33) | copy-start | bytes 884740
  84.9 4.7 %copy-start.15 = (bf16[384,1,192]{0,2,1:T(8,128)(2,1)S(1)}, bf16[384,1,192]{0,2,1:T(8,128)(2,1)}, u32[]{:S(2)}) copy-start(bf16[384,1,192]{0,2,1:T(8,128)(2,1)} %get-tuple-element.19) | copy-start | bytes 442372
  84.9 4.7 %copy-start.17 = (bf16[384,1,192]{0,2,1:T(8,128)(2,1)S(1)}, bf16[384,1,192]{0,2,1:T(8,128)(2,1)}, u32[]{:S(2)}) copy-start(bf16[384,1,192]{0,2,1:T(8,128)(2,1)} %get-tuple-element.21) | copy-start | bytes 442372
  84.9 6.4 %collective-permute-start.2 = (bf16[3,384,192]{1,2,0:T(8,128)(2,1)}, bf16[3,384,192]{1,2,0:T(8,128)(2,1)S(1)}, u32[]{:S(2)}, u32[]{:S(2)}) collective-permute-start(bf16[3,384,192]{1,2,0:T(8,128)(2,1)} %copy.27), channel_id=1, source_target_pairs={{0,128},{128,0},{1,129},{129,1},{2,130},{130,2},{3,131},{131,3},{4... | collective-permute-start | bytes 1327112 | tf_op jit(solution)/shard_map/ppermute | solution.py:255
  89.6 2.5 %copy-start.16 = (bf16[384,1,192]{0,2,1:T(8,128)(2,1)S(1)}, bf16[384,1,192]{0,2,1:T(8,128)(2,1)}, u32[]{:S(2)}) copy-start(bf16[384,1,192]{0,2,1:T(8,128)(2,1)} %get-tuple-element.19) | copy-start | bytes 442372
  89.6 2.5 %copy-start.18 = (bf16[384,1,192]{0,2,1:T(8,128)(2,1)S(1)}, bf16[384,1,192]{0,2,1:T(8,128)(2,1)}, u32[]{:S(2)}) copy-start(bf16[384,1,192]{0,2,1:T(8,128)(2,1)} %get-tuple-element.21) | copy-start | bytes 442372
  91.4 0.8 copy-start.24
  92.1 4.2 %copy-start.6 = (bf16[3,1,384,192]{2,3,1,0:T(8,128)(2,1)S(1)}, bf16[3,1,384,192]{2,3,1,0:T(8,128)(2,1)}, u32[]{:S(2)}) copy-start(bf16[3,1,384,192]{2,3,1,0:T(8,128)(2,1)} %copy.46) | copy-start | bytes 1327108
  92.2 4.2 %copy-start.7 = (bf16[3,1,384,192]{2,3,1,0:T(8,128)(2,1)S(1)}, bf16[3,1,384,192]{2,3,1,0:T(8,128)(2,1)}, u32[]{:S(2)}) copy-start(bf16[3,1,384,192]{2,3,1,0:T(8,128)(2,1)} %copy.47) | copy-start | bytes 1327108
  96.3 1.6 %copy-start.13 = (bf16[1,384,2,384]{3,1,2,0:T(8,128)(2,1)S(1)}, bf16[1,384,2,384]{3,1,2,0:T(8,128)(2,1)}, u32[]{:S(2)}) copy-start(bf16[1,384,2,384]{3,1,2,0:T(8,128)(2,1)} %get-tuple-element.23) | copy-start | bytes 1769476
  96.3 1.6 %copy-start.14 = (bf16[1,384,2,384]{3,1,2,0:T(8,128)(2,1)S(1)}, bf16[1,384,2,384]{3,1,2,0:T(8,128)(2,1)}, u32[]{:S(2)}) copy-start(bf16[1,384,2,384]{3,1,2,0:T(8,128)(2,1)} %get-tuple-element.28) | copy-start | bytes 1769476
  97.9 1.3 copy-start.8
  97.9 1.3 copy-start.9
  98.9 2.7 %collective-permute-start.3 = (bf16[3,384,2,192]{1,3,2,0:T(8,128)(2,1)S(1)}, bf16[3,384,2,192]{1,3,2,0:T(8,128)(2,1)S(1)}, u32[]{:S(2)}, u32[]{:S(2)}) collective-permute-start(bf16[3,384,2,192]{1,3,2,0:T(8,128)(2,1)S(1)} %fusion.22), channel_id=1, source_target_pairs={{0,128},{128,0},{1,129},{129,1},{2,130},{130,2},{3,131},{131,3},{4... | collective-permute-start | bytes 2654216 | tf_op jit(solution)/shard_map/ppermute | solution.py:292
  133.9 2.2 %collective-permute-start.4 = (bf16[192,3,192]{0,2,1:T(8,128)(2,1)S(1)}, bf16[192,3,192]{0,2,1:T(8,128)(2,1)S(1)}, u32[]{:S(2)}, u32[]{:S(2)}) collective-permute-start(bf16[192,3,192]{0,2,1:T(8,128)(2,1)S(1)} %get-tuple-element.27), channel_id=1, source_target_pairs={{0,128},{128,0},{1,129},{129,1},{2,130},{130,2},{3,131},{131,3},{4... | collective-permute-start | bytes 663560 | tf_op jit(solution)/shard_map/ppermute | solution.py:318

commit v3 on v2

--- a/solution.py
+++ b/solution.py
@@ -81,7 +81,9 @@
     indices = jnp.arange(length, dtype=jnp.int32)
     product = indices[:, None] * indices[None, :] % length
     angles = product.astype(jnp.float32) * (2.0 * math.pi / length)
-    return (jnp.cos(angles).astype(jnp.bfloat16), jnp.sin(angles).astype(jnp.bfloat16))
+    return lax.optimization_barrier(
+        (jnp.cos(angles).astype(jnp.bfloat16), jnp.sin(angles).astype(jnp.bfloat16))
+    )
 
 
 def one_hot_rows(indices, width):
@@ -126,22 +128,14 @@
 
 
 def down_matrices(down_weight):
-    nothing = jnp.zeros_like(down_weight[0, 0])
     in_width = down_weight.shape[2]
     out_width = down_weight.shape[3]
-
-    def arrange(entries):
-        return jnp.stack(
-            [jnp.stack(entries[0], axis=0), jnp.stack(entries[1], axis=0)], axis=0
-        ).reshape(4 * in_width, out_width)
-
-    own_taps = arrange(
-        [[down_weight[1, 1], down_weight[1, 2]], [down_weight[2, 1], down_weight[2, 2]]]
-    )
-    upper_taps = arrange([[nothing, nothing], [down_weight[0, 1], down_weight[0, 2]]])
-    left_taps = arrange([[nothing, down_weight[1, 0]], [nothing, down_weight[2, 0]]])
-    corner_taps = arrange([[nothing, nothing], [nothing, down_weight[0, 0]]])
-    return (own_taps, upper_taps, left_taps, corner_taps)
+    padded = jnp.pad(down_weight, ((1, 0), (1, 0), (0, 0), (0, 0)))
+
+    def taps(first, second):
+        return padded[first : first + 2, second : second + 2].reshape(4 * in_width, out_width)
+
+    return (taps(2, 2), taps(0, 2), taps(2, 0), taps(0, 0))
 
 
 def stem_layers(aerial_patch_grid, patch_conv_weight, patch_bias, merging_conv_weight, merge_bias):
@@ -307,10 +301,10 @@
         .transpose(1, 0, 2, 3)
         .reshape(tiles, -1)
     )
-    rows_back = exchange_chunks(outgoing, 1).reshape(channels, tile_rows, cell_half)
-    summed = (feature_half.astype(jnp.float32) + rows_back.astype(jnp.float32)).astype(
-        jnp.bfloat16
-    )
+    rows_back = exchange_chunks(outgoing, 1)
+    summed = (
+        feature_half.reshape(tiles, -1).astype(jnp.float32) + rows_back.astype(jnp.float32)
+    ).astype(jnp.bfloat16).reshape(channels, tile_rows, cell_half)
     kept = lax.dynamic_slice_in_dim(summed, section_index * half_channels, half_channels, 0)
     sent = lax.dynamic_slice_in_dim(
         summed, (1 - section_index) * half_channels, half_channels, 0

time: 138 us -> 143 us (1.036)
  local copies, waits for them, and re-layouts: 31.6 us -> 36.6 us
  other arithmetic: 19.2 us -> 15 us
  matrix products: 27.1 us -> 30.3 us
  starting transfers between devices: 9.75 us -> 11.7 us
  waiting for transfers between devices: 2.96 us -> 1.36 us
    another operation x4 -> x0, local copies, waits for them, and re-layouts: 4.02 us -> none  [the longest x1 2.22 us: arrange(): jnp.stack(entries[0], axis=0)]
    neg x1 -> x0, other arithmetic: 2.97 us -> none  [local(): -sin_h]
    convert_element_type x2, other arithmetic: 0.15 us -> 3.03 us  [the longest x1 2.95 us: fourier_tables(): jnp.cos(angles).astype(jnp.bfloat16)]
    slice x0 -> x1, local copies, waits for them, and re-layouts: none -> 2.57 us  [taps(): padded[first:first + 2, second:second + 2].reshape(4 * in_width, out_width)]
    another operation x2 -> x1, other arithmetic: 3.37 us -> 0.85 us  [local(): inverse_table = jnp.stack([cos_part, -sin_part], axis=0)]
    ppermute x1, waiting for transfers between devices: 1.75 us -> 0.01 us  [local(): other_rows = lax.ppermute(back_rows, 'section', swap)]
    ppermute x1, starting transfers between devices: 2.06 us -> 3.69 us  [local(): other_fields = lax.ppermute(fields, 'section', swap)]
    another operation x5 -> x2, other arithmetic: 3.51 us -> 2.44 us  [the longest x4 1.93 us: arrange(): jnp.stack([jnp.stack(entries[0], axis=0), jnp.stack(entries[1], axis=0)],...]
  transfers between devices with their start and end apart: 5 -> 5, of which waited for: 2 -> 1; matrix products, arithmetic and copies ran while one was open for 21% -> 21% of each run, Pallas kernels for 0% -> 0%
where the time goes in v3:
time: 143 us; the launch traced here: 142 us
  Pallas kernels  46.5 us (33%)
  local copies, waits for them, and re-layouts  36.6 us (26%)
  matrix products  30.3 us (21%)
  other arithmetic  15 us (10%)
  starting transfers between devices  11.7 us (8%)
    pallas_call x2, Pallas kernels, exchange(): pl.pallas_call(exchange_kernel, out_shape=jax.ShapeDtypeStruct(chunks.sha...  46.5 us
    unnamed x37, local copies, waits for them, and re-layouts  7.6 us
    ppermute x2, starting transfers between devices, from_behind(): return lax.ppermute(block, axis, route)  6.37 us
    dot_general x1, matrix products, stem_layers(): jnp.einsum('zji,if->zjf', aerial_patch_grid, patch_kernel_matrix(patch_co...  5.05 us
    dot_general x1, matrix products, stem_layers(): jnp.einsum('zji,if->zjf', initial_layer, merging_kernel_matrix(merging_co...  4.15 us
    dot_general x1, matrix products, filter_columns(): jnp.einsum('puqh,chqw->cpuw', forward_h, row_spectrum, preferred_element_...  4.15 us
    ppermute x1, starting transfers between devices, local(): other_fields = lax.ppermute(fields, 'section', swap)  3.69 us
    convert_element_type x2, local copies, waits for them, and re-layouts, local(): feature_half.reshape(tiles, -1).astype(jnp.float32)  3.57 us
  transfers between devices with their start and end apart: 5, of which 1 were waited for; matrix products, arithmetic and copies ran while one was open for 21% of the time, Pallas kernels for 0%

profile of v3, /device:TPU:1, one launch (start us, length us, event | category | flops | bytes accessed | tf_op | source)
XLA Modules:
  0.0 141.8 jit_solution(12516306883633587641)
XLA Ops:
  1.7 1.7 %convolution_convert_fusion = bf16[1536,192]{0,1:T(8,128)(2,1)S(1)} fusion(bf16[384,192]{1,0:T(8,128)(2,1)} %bitcast.149, s32[1536]{0:T(1024)S(1)} %fusion.98), kind=kOutput, calls=%fused_computation.17 | convolution fusion | flops 227377152 | bytes 743424 | tf_op jit(solution)/shard_map/dot_general | solution.py:94
  3.4 3.5 %fusion.8 = bf16[768,1536,1]{1,0,2:T(8,128)(2,1)} fusion(s32[1536]{0:T(1024)S(1)} %get-tuple-element.36, s32[768]{0:T(1024)S(1)} %get-tuple-element.33, bf16[48,96]{1,0:T(8,128)(2,1)} %bitcast.150, s32[1536]{0:T(1024)S(1)} %get-tuple-element.35, s32[768]{0:T(1024)S(1)} %get-tuple-element.34), kind=kOutput, calls=%fused_computation.11 | convolution fusion | flops 237367296 | bytes 2386944 | tf_op jit(solution)/shard_map/dot_general | solution.py:100
  6.9 5.0 %fusion.7 = bf16[3,192,1536]{2,1,0:T(8,128)(2,1)} fusion(bf16[768,1536,1]{1,0,2:T(8,128)(2,1)} %fusion.8, f32[1536]{0:T(1024)S(1)} %add.293, bf16[3,384,768]{2,1,0:T(8,128)(2,1)S(1)} %copy-done, s32[]{:T(128)S(6)} %select_n.202), kind=kOutput, calls=%fused_computation.10 | convolution fusion | flops 1367801856 | bytes 5021700 | tf_op jit(solution)/shard_map/zji,if->zjf/dot_general | solution.py:142
  12.0 4.1 %fusion.17 = bf16[3,192,768]{2,1,0:T(8,128)(2,1)S(1)} fusion(bf16[3,192,1536]{2,1,0:T(8,128)(2,1)} %fusion.7, bf16[1536,192]{0,1:T(8,128)(2,1)S(1)} %convolution_convert_fusion, s32[768]{0:T(1024)S(1)} %get-tuple-element.32, s32[1536]{0:T(1024)S(1)} %fusion.91, f32[768]{0:T(1024)S(1)} %add.306, s32[768]{0:T(1024)S(1)} %get-tuple-element.31), kind=kOutput, calls=%fused_computation.26 | convolution fusion | flops 1820049408 | bytes 3259392 | tf_op jit(solution)/shard_map/zji,if->zjf/dot_general | solution.py:151
  16.8 1.3 collective-permute-start
  18.0 2.9 %cosine_convert_fusion = bf16[384,384]{0,1:T(8,128)(2,1)} fusion(), kind=kLoop, calls=%fused_computation.92 | loop fusion | flops 1474560 | bytes 294912 | tf_op jit(solution)/shard_map/convert_element_type | solution.py:85
  21.0 2.3 %sine_convert_fusion = bf16[384,384]{0,1:T(8,128)(2,1)S(1)} fusion(), kind=kLoop, calls=%fused_computation.91 | loop fusion | flops 1474560 | bytes 294912 | tf_op jit(solution)/shard_map/convert_element_type | solution.py:85
  23.3 2.6 %pad_slice_fusion.2 = (bf16[2,2,192,384]{3,2,1,0:T(8,128)(2,1)S(1)}, bf16[2,2,192,384]{3,2,1,0:T(8,128)(2,1)}, bf16[2,2,192,384]{3,2,1,0:T(8,128)(2,1)}, bf16[2,2,192,384]{3,2,1,0:T(8,128)(2,1)S(1)}) fusion(bf16[3,3,192,384]{3,2,1,0:T(8,128)(2,1)} %param.14), kind=kLoop, calls=%fused_computation.15 | loop fusion | bytes 4276224 | tf_op jit(solution)/shard_map/slice | solution.py:136
  25.9 1.6 %convolution_bitcast_fusion.2 = f32[384,3,192]{0,2,1:T(8,128)} fusion(bf16[3,192,768]{2,1,0:T(8,128)(2,1)S(1)} %fusion.17, bf16[768,384,1]{1,0,2:T(8,128)(2,1)S(1)} %bitcast.139), kind=kOutput, calls=%fused_computation.39 | convolution fusion | flops 339738624 | bytes 2359296 | tf_op jit(solution)/shard_map/rwk,kc->crw/dot_general | solution.py:167
  28.2 2.8 %constant_dynamic-slice_fusion = (bf16[3,1,384,192]{3,2,1,0:T(8,128)(2,1)}, bf16[3,1,384,192]{3,2,1,0:T(8,128)(2,1)}) fusion(bf16[3,2,384,384]{3,2,1,0:T(8,128)(2,1)} %param.17, s32[]{:T(128)S(6)} %select_n.202, s32[]{:T(128)S(6)} %add.325), kind=kLoop, calls=%fused_computation.223 | loop fusion | bytes 1769480 | tf_op jit(solution)/shard_map/slice | solution.py:198
  31.0 0.8 pad_maximum_fusion.6
  31.8 5.1 %collective-permute-start.1 = (bf16[1,193,768]{2,1,0:T(8,128)(2,1)}, bf16[1,193,768]{2,1,0:T(8,128)(2,1)}, u32[]{:S(2)}, u32[]{:S(2)}) collective-permute-start(bf16[1,193,768]{2,1,0:T(8,128)(2,1)} %pad_maximum_fusion.6), channel_id=1, source_target_pairs={{0,1},{1,2},{2,3},{3,4},{4,5},{5,6},{6,7},{7,8},{8,9},{9,10},{10,1... | collective-permute-start | bytes 889352 | tf_op jit(solution)/shard_map/ppermute | solution.py:77
  36.9 0.9 dynamic-slice_bitcast_fusion
  37.7 2.1 %copy.55 = bf16[3,1,384,192]{2,3,1,0:T(8,128)(2,1)} copy(bf16[3,1,384,192]{3,2,1,0:T(8,128)(2,1)} %get-tuple-element.11) | data formatting | bytes 884736
  39.8 2.1 %copy.56 = bf16[3,1,384,192]{2,3,1,0:T(8,128)(2,1)} copy(bf16[3,1,384,192]{3,2,1,0:T(8,128)(2,1)} %get-tuple-element.12) | data formatting | bytes 884736
  41.8 1.7 %fusion.40 = f32[384,3,192]{0,2,1:T(8,128)S(1)} fusion(bf16[768,384,1]{1,0,2:T(8,128)(2,1)} %bitcast.148, bf16[3,192,768]{2,1,0:T(8,128)(2,1)S(1)} %fusion.17, bf16[3,1,768]{2,1,0:T(2,128)(2,1)S(1)} %collective-permute-done), kind=kOutput, calls=%fused_computation.66 | convolution fusion | flops 341508096 | bytes 2363904 | tf_op jit(solution)/shard_map/rwk,kc->crw/dot_general | solution.py:173
  43.6 1.2 maximum_maximum_fusion
  46.0 0.8 fusion.139
  47.3 1.4 %copy.27 = bf16[384,3,192]{2,1,0:T(4,128)(2,1)} copy(bf16[384,3,192]{0,2,1:T(8,128)(2,1)S(1)} %multiply_convert_fusion) | data formatting | bytes 884736 | tf_op jit(solution)/shard_map/convert_element_type | solution.py:187
  48.8 1.7 %reshape.296 = bf16[128,1728]{1,0:T(8,128)(2,1)S(1)} reshape(bf16[384,3,192]{2,1,0:T(4,128)(2,1)} %copy.27) | data formatting | bytes 884736 | tf_op jit(solution)/shard_map/reshape | solution.py:242
  50.5 0.9 copy.57
  51.4 25.6 %shard_map.91 = bf16[128,16,128]{2,1,0:T(8,128)(2,1)} custom-call(bf16[128,16,128]{2,1,0:T(8,128)(2,1)} %bitcast.141), custom_call_target="tpu_custom_call" | custom-call | tf_op jit(solution)/shard_map/pallas_call | solution.py:57
  77.0 1.5 %copy.48 = bf16[128,16,128]{0,2,1:T(8,128)(2,1)S(1)} copy(bf16[128,16,128]{2,1,0:T(8,128)(2,1)} %shard_map.91) | data formatting | bytes 1048576 | tf_op jit(solution)/shard_map/reshape | solution.py:71
  78.5 0.8 slice.64
  79.3 2.2 %copy.29 = bf16[3,128,3,192]{3,2,1,0:T(4,128)(2,1)} copy(bf16[3,128,3,192]{1,3,2,0:T(8,128)(2,1)} %bitcast.147) | data formatting | bytes 884736 | tf_op jit(solution)/shard_map/transpose | solution.py:245
  81.5 1.5 %reshape.300 = bf16[3,384,192]{2,1,0:T(8,128)(2,1)S(1)} reshape(bf16[3,128,3,192]{3,2,1,0:T(4,128)(2,1)} %copy.29) | data formatting | bytes 884736 | tf_op jit(solution)/shard_map/reshape | solution.py:246
  83.1 1.0 copy.31
  84.1 3.7 %collective-permute-start.2 = (bf16[3,384,192]{1,2,0:T(8,128)(2,1)}, bf16[3,384,192]{1,2,0:T(8,128)(2,1)S(1)}, u32[]{:S(2)}, u32[]{:S(2)}) collective-permute-start(bf16[3,384,192]{1,2,0:T(8,128)(2,1)} %copy.31), channel_id=1, source_target_pairs={{0,128},{128,0},{1,129},{129,1},{2,130},{130,2},{3,131},{131,3},{4... | collective-permute-start | bytes 1327112 | tf_op jit(solution)/shard_map/ppermute | solution.py:249
  87.8 2.8 %fusion.48 = (bf16[1,384,2,384]{1,3,2,0:T(8,128)(2,1)}, bf16[1,384,2,384]{1,3,2,0:T(8,128)(2,1)}, bf16[1,384,2,384]{1,3,2,0:T(8,128)(2,1)}, bf16[1,384,2,384]{1,3,2,0:T(8,128)(2,1)}) fusion(bf16[384,1,384]{0,2,1:T(8,128)(2,1)} %bitcast.143, bf16[384,1,384]{0,2,1:T(8,128)(2,1)S(1)} %bitcast.135, bf16[384,1,384]{0,2,1:T(8,128)(2,1)} %negate_bitcast_fusion), kind=kLoop, calls=%fused_computation.84 | loop fusion | flops 1179648 | bytes 3244032 | tf_op jit(solution)/shard_map/stack | solution.py:260
  90.5 1.7 %fusion.52 = f32[3,384,2,192]{1,3,2,0:T(8,128)} fusion(bf16[3,384,192]{2,1,0:T(8,128)(2,1)S(1)} %reshape.300, s32[]{:T(128)S(6)} %select_n.202, bf16[384,1,192]{0,2,1:T(8,128)(2,1)S(1)} %copy-done.9, bf16[384,1,192]{0,2,1:T(8,128)(2,1)S(1)} %copy-done.11), kind=kOutput, calls=%fused_computation.89 | convolution fusion | flops 170164224 | bytes 2506756 | tf_op jit(solution)/shard_map/chx,xqw->chqw/dot_general | solution.py:272
  93.0 4.1 %fusion.22 = bf16[3,2,384,192]{2,3,1,0:T(8,128)(2,1)} fusion(bf16[1,384,2,384]{1,3,2,0:T(8,128)(2,1)} %get-tuple-element.28, bf16[1,384,2,384]{1,3,2,0:T(8,128)(2,1)} %get-tuple-element.19, f32[3,384,2,192]{1,3,2,0:T(8,128)} %fusion.52, bf16[3,384,192]{1,2,0:T(8,128)(2,1)} %copy-done.15, s32[]{:T(128)S(6)} %select_n.224, ...), kind=kOutput, calls=%fused_computation.35 | convolution fusion | flops 853327872 | bytes 4571140 | tf_op jit(solution)/shard_map/puqh,chqw->cpuw/dot_general | solution.py:193
  97.2 1.7 %fusion.35 = (bf16[3,1,384,192]{2,3,1,0:T(8,128)(2,1)S(1)}, bf16[3,1,384,192]{2,3,1,0:T(8,128)(2,1)S(1)}) fusion(bf16[3,1,384,192]{2,3,1,0:T(8,128)(2,1)S(1)} %copy-done.4, bf16[3,1,384,192]{2,3,1,0:T(8,128)(2,1)} %copy.56, bf16[3,2,384,192]{2,3,1,0:T(8,128)(2,1)} %fusion.22), kind=kLoop, calls=%fused_computation.60 | loop fusion | flops 2654208 | bytes 2654208 | tf_op jit(solution)/shard_map/convert.1
  98.9 1.8 %fusion.23 = bf16[3,384,2,192]{1,3,2,0:T(8,128)(2,1)} fusion(bf16[1,384,2,384]{1,3,2,0:T(8,128)(2,1)S(1)} %copy-done.7, bf16[1,384,2,384]{1,3,2,0:T(8,128)(2,1)S(1)} %copy-done.8, bf16[3,1,384,192]{2,3,1,0:T(8,128)(2,1)S(1)} %get-tuple-element.10, bf16[3,1,384,192]{2,3,1,0:T(8,128)(2,1)S(1)} %get-tuple-element.9), kind=kOutput, calls=%fused_computation.36 | convolution fusion | flops 684048384 | bytes 2949120 | tf_op jit(solution)/shard_map/qhpu,cpuw->chqw/dot_general | solution.py:207
  100.8 1.6 %copy.25 = f32[384,3,192]{2,1,0:T(4,128)} copy(f32[384,3,192]{0,2,1:T(8,128)S(1)} %get-tuple-element.30) | data formatting | bytes 1769472 | tf_op jit(solution)/shard_map/convert_element_type | solution.py:306
  102.3 2.0 %reshape.306 = f32[128,1728]{1,0:T(8,128)S(1)} reshape(f32[384,3,192]{2,1,0:T(4,128)} %copy.25) | data formatting | bytes 1769472 | tf_op jit(solution)/shard_map/convert_element_type | solution.py:306
  104.4 1.8 %convolution_bitcast_fusion.1 = f32[3,384,192]{1,2,0:T(8,128)S(1)} fusion(bf16[3,384,2,192]{1,3,2,0:T(8,128)(2,1)} %fusion.23, s32[]{:T(128)S(6)} %select_n.202, bf16[1,384,192]{1,2,0:T(8,128)(2,1)S(1)} %copy-done.5, bf16[1,384,192]{1,2,0:T(8,128)(2,1)S(1)} %copy-done.6), kind=kOutput, calls=%fused_computation.38 | convolution fusion | flops 170164224 | bytes 2064388 | tf_op jit(solution)/shard_map/chqw,qwv->chv/dot_general | solution.py:287
  106.2 1.8 %fusion.26 = bf16[3,384,192]{1,2,0:T(8,128)(2,1)S(1)} fusion(f32[3,384,192]{1,2,0:T(8,128)S(1)} %convolution_bitcast_fusion.1, bf16[3,384,2,192]{1,3,2,0:T(8,128)(2,1)} %collective-permute-done.3, s32[]{:T(128)S(6)} %select_n.224, bf16[1,384,192]{1,2,0:T(8,128)(2,1)S(1)} %copy-done.5, bf16[1,384,192]{1,2,0:T(8,128)(2,1)S(1)} %copy-done.6), kind=kOutput, calls=%fused_computation.42 | convolution fusion | flops 170827776 | bytes 2506756 | tf_op jit(solution)/shard_map/chqw,qwv->chv/dot_general | solution.py:292
  108.0 1.1 copy.34
  109.1 1.3 reshape.301
  110.4 1.3 copy.35
  111.7 1.1 pad.13
  112.8 1.2 copy.53.x_ref
  114.0 20.9 %shard_map.92 = bf16[128,16,128]{2,1,0:T(8,128)(2,1)} custom-call(bf16[128,16,128]{2,1,0:T(8,128)(2,1)} %copy.53.x_ref), custom_call_target="tpu_custom_call" | custom-call | tf_op jit(solution)/shard_map/pallas_call | solution.py:57
  134.9 1.2 copy.60
  137.1 1.6 %collective-permute-start.4 = (bf16[192,3,192]{2,1,0:T(4,128)(2,1)S(1)}, bf16[192,3,192]{2,1,0:T(4,128)(2,1)S(1)}, u32[]{:S(2)}, u32[]{:S(2)}) collective-permute-start(bf16[192,3,192]{2,1,0:T(4,128)(2,1)S(1)} %get-tuple-element.18), channel_id=1, source_target_pairs={{0,128},{128,0},{1,129},{129,1},{2,130},{130,2},{3,131},{131,3},{4... | collective-permute-start | bytes 663560 | tf_op jit(solution)/shard_map/ppermute | solution.py:312
  138.7 1.3 collective-permute-done.4
  140.1 1.0 maximum_select_fusion
  141.0 0.8 copy.37
  (57 shorter events, 6.6 us)
Async XLA Ops:
  0.0 6.9 %copy-start = (bf16[3,384,768]{2,1,0:T(8,128)(2,1)S(1)}, bf16[3,384,768]{2,1,0:T(8,128)(2,1)}, u32[]{:S(2)}) copy-start(bf16[3,384,768]{2,1,0:T(8,128)(2,1)} %param.9) | copy-start | bytes 5308420
  16.8 14.2 %collective-permute-start = (bf16[3,1,768]{2,1,0:T(2,128)(2,1)}, bf16[3,1,768]{2,1,0:T(2,128)(2,1)S(1)}, u32[]{:S(2)}, u32[]{:S(2)}) collective-permute-start(bf16[3,1,768]{2,1,0:T(2,128)(2,1)} %slice.61), channel_id=1, source_target_pairs={{0,128},{1,129},{2,130},{3,131},{4,132},{5,133},{6,134},{7,135},{8... | collective-permute-start | bytes 13832 | tf_op jit(solution)/shard_map/ppermute | solution.py:77
  28.2 8.7 %copy-start.3 = (bf16[384,384]{0,1:T(8,128)(2,1)S(1)}, bf16[384,384]{0,1:T(8,128)(2,1)}, u32[]{:S(2)}) copy-start(bf16[384,384]{0,1:T(8,128)(2,1)} %cosine_convert_fusion) | copy-start | bytes 884740
  31.8 11.8 %collective-permute-start.1 = (bf16[1,193,768]{2,1,0:T(8,128)(2,1)}, bf16[1,193,768]{2,1,0:T(8,128)(2,1)}, u32[]{:S(2)}, u32[]{:S(2)}) collective-permute-start(bf16[1,193,768]{2,1,0:T(8,128)(2,1)} %pad_maximum_fusion.6), channel_id=1, source_target_pairs={{0,1},{1,2},{2,3},{3,4},{4,5},{5,6},{6,7},{7,8},{8,9},{9,10},{10,1... | collective-permute-start | bytes 889352 | tf_op jit(solution)/shard_map/ppermute | solution.py:77
  43.5 1.3 copy-start.2
  44.8 1.2 copy-start.1
  44.8 1.2 copy-start.13
  46.0 1.1 copy-start.14
  84.1 6.5 %copy-start.9 = (bf16[384,1,192]{0,2,1:T(8,128)(2,1)S(1)}, bf16[384,1,192]{0,2,1:T(8,128)(2,1)}, u32[]{:S(2)}) copy-start(bf16[384,1,192]{0,2,1:T(8,128)(2,1)} %get-tuple-element.26) | copy-start | bytes 442372
  84.1 6.5 %copy-start.11 = (bf16[384,1,192]{0,2,1:T(8,128)(2,1)S(1)}, bf16[384,1,192]{0,2,1:T(8,128)(2,1)}, u32[]{:S(2)}) copy-start(bf16[384,1,192]{0,2,1:T(8,128)(2,1)} %get-tuple-element.37) | copy-start | bytes 442372
  84.1 8.2 %collective-permute-start.2 = (bf16[3,384,192]{1,2,0:T(8,128)(2,1)}, bf16[3,384,192]{1,2,0:T(8,128)(2,1)S(1)}, u32[]{:S(2)}, u32[]{:S(2)}) collective-permute-start(bf16[3,384,192]{1,2,0:T(8,128)(2,1)} %copy.31), channel_id=1, source_target_pairs={{0,128},{128,0},{1,129},{129,1},{2,130},{130,2},{3,131},{131,3},{4... | collective-permute-start | bytes 1327112 | tf_op jit(solution)/shard_map/ppermute | solution.py:249
  90.5 2.5 %copy-start.10 = (bf16[384,1,192]{0,2,1:T(8,128)(2,1)S(1)}, bf16[384,1,192]{0,2,1:T(8,128)(2,1)}, u32[]{:S(2)}) copy-start(bf16[384,1,192]{0,2,1:T(8,128)(2,1)} %get-tuple-element.26) | copy-start | bytes 442372
  90.5 2.5 %copy-start.12 = (bf16[384,1,192]{0,2,1:T(8,128)(2,1)S(1)}, bf16[384,1,192]{0,2,1:T(8,128)(2,1)}, u32[]{:S(2)}) copy-start(bf16[384,1,192]{0,2,1:T(8,128)(2,1)} %get-tuple-element.37) | copy-start | bytes 442372
  92.3 0.8 copy-start.15
  93.0 4.2 %copy-start.4 = (bf16[3,1,384,192]{2,3,1,0:T(8,128)(2,1)S(1)}, bf16[3,1,384,192]{2,3,1,0:T(8,128)(2,1)}, u32[]{:S(2)}) copy-start(bf16[3,1,384,192]{2,3,1,0:T(8,128)(2,1)} %copy.55) | copy-start | bytes 1327108
  97.2 1.7 %copy-start.7 = (bf16[1,384,2,384]{1,3,2,0:T(8,128)(2,1)S(1)}, bf16[1,384,2,384]{1,3,2,0:T(8,128)(2,1)}, u32[]{:S(2)}) copy-start(bf16[1,384,2,384]{1,3,2,0:T(8,128)(2,1)} %get-tuple-element.20) | copy-start | bytes 1769476
  97.2 1.7 %copy-start.8 = (bf16[1,384,2,384]{1,3,2,0:T(8,128)(2,1)S(1)}, bf16[1,384,2,384]{1,3,2,0:T(8,128)(2,1)}, u32[]{:S(2)}) copy-start(bf16[1,384,2,384]{1,3,2,0:T(8,128)(2,1)} %get-tuple-element.27) | copy-start | bytes 1769476
  100.7 5.4 %collective-permute-start.3 = (bf16[3,384,2,192]{1,3,2,0:T(8,128)(2,1)}, bf16[3,384,2,192]{1,3,2,0:T(8,128)(2,1)}, u32[]{:S(2)}, u32[]{:S(2)}) collective-permute-start(bf16[3,384,2,192]{1,3,2,0:T(8,128)(2,1)} %fusion.23), channel_id=1, source_target_pairs={{0,128},{128,0},{1,129},{129,1},{2,130},{130,2},{3,131},{131,3},{4... | collective-permute-start | bytes 2654216 | tf_op jit(solution)/shard_map/ppermute | solution.py:286
  102.3 2.0 %copy-start.5 = (bf16[1,384,192]{1,2,0:T(8,128)(2,1)S(1)}, bf16[1,384,192]{1,2,0:T(8,128)(2,1)}, u32[]{:S(2)}) copy-start(bf16[1,384,192]{1,2,0:T(8,128)(2,1)} %get-tuple-element.25) | copy-start | bytes 442372
  102.3 2.0 %copy-start.6 = (bf16[1,384,192]{1,2,0:T(8,128)(2,1)S(1)}, bf16[1,384,192]{1,2,0:T(8,128)(2,1)}, u32[]{:S(2)}) copy-start(bf16[1,384,192]{1,2,0:T(8,128)(2,1)} %get-tuple-element.38) | copy-start | bytes 442372
  137.1 3.0 %collective-permute-start.4 = (bf16[192,3,192]{2,1,0:T(4,128)(2,1)S(1)}, bf16[192,3,192]{2,1,0:T(4,128)(2,1)S(1)}, u32[]{:S(2)}, u32[]{:S(2)}) collective-permute-start(bf16[192,3,192]{2,1,0:T(4,128)(2,1)S(1)} %get-tuple-element.18), channel_id=1, source_target_pairs={{0,128},{128,0},{1,129},{129,1},{2,130},{130,2},{3,131},{131,3},{4... | collective-permute-start | bytes 663560 | tf_op jit(solution)/shard_map/ppermute | solution.py:312

commit v4 on v3

--- a/solution.py
+++ b/solution.py
@@ -81,9 +81,7 @@
     indices = jnp.arange(length, dtype=jnp.int32)
     product = indices[:, None] * indices[None, :] % length
     angles = product.astype(jnp.float32) * (2.0 * math.pi / length)
-    return lax.optimization_barrier(
-        (jnp.cos(angles).astype(jnp.bfloat16), jnp.sin(angles).astype(jnp.bfloat16))
-    )
+    return (jnp.cos(angles).astype(jnp.bfloat16), jnp.sin(angles).astype(jnp.bfloat16))
 
 
 def one_hot_rows(indices, width):

time: 143 us -> 145 us (1.014)
  other arithmetic: 15 us -> 18.8 us
  starting transfers between devices: 11.7 us -> 9.9 us
    neg x0 -> x1, other arithmetic: none -> 2.99 us  [local(): -sin_h]
    convert_element_type x1 -> x0, other arithmetic: 2.95 us -> none  [fourier_tables(): jnp.cos(angles).astype(jnp.bfloat16)]
    another operation x1 -> x2, other arithmetic: 0.85 us -> 3.36 us  [local(): inverse_table = jnp.stack([cos_part, -sin_part], axis=0)]
    ppermute x1, starting transfers between devices: 3.69 us -> 2.19 us  [local(): other_fields = lax.ppermute(fields, 'section', swap)]
    unnamed x37 -> x39, local copies, waits for them, and re-layouts: 7.6 us -> 8.54 us
  transfers between devices with their start and end apart: 5 -> 5, of which waited for: 1 -> 1; matrix products, arithmetic and copies ran while one was open for 21% -> 22% of each run, Pallas kernels for 0% -> 0%
where the time goes in v4:
time: 145 us; the launch traced here: 144 us
  Pallas kernels  46 us (32%)
  local copies, waits for them, and re-layouts  37.5 us (26%)
  matrix products  29.6 us (20%)
  other arithmetic  18.8 us (13%)
  starting transfers between devices  9.9 us (7%)
    pallas_call x2, Pallas kernels, exchange(): pl.pallas_call(exchange_kernel, out_shape=jax.ShapeDtypeStruct(chunks.sha...  46 us
    unnamed x39, local copies, waits for them, and re-layouts  8.54 us
    ppermute x2, starting transfers between devices, from_behind(): return lax.ppermute(block, axis, route)  6.35 us
    dot_general x1, matrix products, stem_layers(): jnp.einsum('zji,if->zjf', aerial_patch_grid, patch_kernel_matrix(patch_co...  5.05 us
    dot_general x1, matrix products, filter_columns(): jnp.einsum('puqh,chqw->cpuw', forward_h, row_spectrum, preferred_element_...  4.29 us
    dot_general x1, matrix products, stem_layers(): jnp.einsum('zji,if->zjf', initial_layer, merging_kernel_matrix(merging_co...  4.17 us
    convert_element_type x2, local copies, waits for them, and re-layouts, local(): feature_half.reshape(tiles, -1).astype(jnp.float32)  3.56 us
    dot_general x1, matrix products, spread_kernel(): full = jnp.dot(picked, repeat, preferred_element_type=jnp.float32)  3.51 us
  transfers between devices with their start and end apart: 5, of which 1 were waited for; matrix products, arithmetic and copies ran while one was open for 22% of the time, Pallas kernels for 0%

profile of v4, /device:TPU:1, one launch (start us, length us, event | category | flops | bytes accessed | tf_op | source)
XLA Modules:
  0.0 143.6 jit_solution(10295820833519470222)
XLA Ops:
  1.7 1.7 %convolution_convert_fusion = bf16[1536,192]{0,1:T(8,128)(2,1)S(1)} fusion(bf16[384,192]{1,0:T(8,128)(2,1)} %bitcast.143, s32[1536]{0:T(1024)S(1)} %fusion.107), kind=kOutput, calls=%fused_computation.17 | convolution fusion | flops 227377152 | bytes 743424 | tf_op jit(solution)/shard_map/dot_general | solution.py:92
  3.4 3.5 %fusion.8 = bf16[768,1536,1]{1,0,2:T(8,128)(2,1)} fusion(s32[1536]{0:T(1024)S(1)} %get-tuple-element.32, s32[768]{0:T(1024)S(1)} %get-tuple-element.29, bf16[48,96]{1,0:T(8,128)(2,1)} %bitcast.144, s32[1536]{0:T(1024)S(1)} %get-tuple-element.31, s32[768]{0:T(1024)S(1)} %get-tuple-element.30), kind=kOutput, calls=%fused_computation.11 | convolution fusion | flops 237367296 | bytes 2386944 | tf_op jit(solution)/shard_map/dot_general | solution.py:98
  6.9 5.0 %fusion.7 = bf16[3,192,1536]{2,1,0:T(8,128)(2,1)} fusion(bf16[768,1536,1]{1,0,2:T(8,128)(2,1)} %fusion.8, f32[1536]{0:T(1024)S(1)} %add.324, bf16[3,384,768]{2,1,0:T(8,128)(2,1)S(1)} %copy-done, s32[]{:T(128)S(6)} %select_n.233), kind=kOutput, calls=%fused_computation.10 | convolution fusion | flops 1367801856 | bytes 5021700 | tf_op jit(solution)/shard_map/zji,if->zjf/dot_general | solution.py:140
  12.0 4.2 %fusion.17 = bf16[3,192,768]{2,1,0:T(8,128)(2,1)S(1)} fusion(bf16[3,192,1536]{2,1,0:T(8,128)(2,1)} %fusion.7, bf16[1536,192]{0,1:T(8,128)(2,1)S(1)} %convolution_convert_fusion, s32[768]{0:T(1024)S(1)} %get-tuple-element.28, s32[1536]{0:T(1024)S(1)} %fusion.100, f32[768]{0:T(1024)S(1)} %add.337, s32[768]{0:T(1024)S(1)} %get-tuple-element.27), kind=kOutput, calls=%fused_computation.26 | convolution fusion | flops 1820049408 | bytes 3259392 | tf_op jit(solution)/shard_map/zji,if->zjf/dot_general | solution.py:149
  16.8 1.3 collective-permute-start
  18.4 3.3 %sine_convert_fusion = (bf16[384,1,384]{2,0,1:T(8,128)(2,1)}, bf16[384,1,384]{2,0,1:T(8,128)(2,1)}) fusion(), kind=kLoop, calls=%fused_computation.94 | loop fusion | flops 1622016 | bytes 589824 | tf_op jit(solution)/shard_map/convert_element_type | solution.py:84
  21.7 2.7 %pad_slice_fusion.2 = (bf16[2,2,192,384]{3,2,1,0:T(8,128)(2,1)}, bf16[2,2,192,384]{3,2,1,0:T(8,128)(2,1)}, bf16[2,2,192,384]{3,2,1,0:T(8,128)(2,1)}, bf16[2,2,192,384]{3,2,1,0:T(8,128)(2,1)S(1)}) fusion(bf16[3,3,192,384]{3,2,1,0:T(8,128)(2,1)} %param.14), kind=kLoop, calls=%fused_computation.15 | loop fusion | bytes 4276224 | tf_op jit(solution)/shard_map/slice | solution.py:134
  25.0 1.7 %fusion.86 = (bf16[1,384,192]{1,2,0:T(8,128)(2,1)}, bf16[384,1,192]{0,2,1:T(8,128)(2,1)}) fusion(f32[384,384]{0,1:T(8,128)S(1)} %fusion.51, s32[]{:T(128)S(6)} %select_n.233), kind=kLoop, calls=%fused_computation.134 | loop fusion | flops 294912 | bytes 589828 | tf_op jit(solution)/shard_map/stack | solution.py:257
  26.7 2.8 %constant_dynamic-slice_fusion = (bf16[3,1,384,192]{3,2,1,0:T(8,128)(2,1)}, bf16[3,1,384,192]{3,2,1,0:T(8,128)(2,1)}) fusion(bf16[3,2,384,384]{3,2,1,0:T(8,128)(2,1)} %param.17, s32[]{:T(128)S(6)} %select_n.233, s32[]{:T(128)S(6)} %add.357), kind=kLoop, calls=%fused_computation.232 | loop fusion | bytes 1769480 | tf_op jit(solution)/shard_map/slice | solution.py:196
  29.5 1.7 %fusion.85 = (bf16[1,384,192]{1,2,0:T(8,128)(2,1)}, bf16[384,1,192]{0,2,1:T(8,128)(2,1)}) fusion(f32[384,384]{0,1:T(8,128)S(1)} %copy-done.2, s32[]{:T(128)S(6)} %select_n.233), kind=kLoop, calls=%fused_computation.133 | loop fusion | flops 73728 | bytes 589828 | tf_op jit(solution)/shard_map/stack | solution.py:257
  32.0 5.1 %collective-permute-start.1 = (bf16[1,193,768]{2,1,0:T(8,128)(2,1)}, bf16[1,193,768]{2,1,0:T(8,128)(2,1)}, u32[]{:S(2)}, u32[]{:S(2)}) collective-permute-start(bf16[1,193,768]{2,1,0:T(8,128)(2,1)} %pad_maximum_fusion.6), channel_id=1, source_target_pairs={{0,1},{1,2},{2,3},{3,4},{4,5},{5,6},{6,7},{7,8},{8,9},{9,10},{10,1... | collective-permute-start | bytes 889352 | tf_op jit(solution)/shard_map/ppermute | solution.py:77
  37.1 3.0 %fusion.83 = bf16[384,1,384]{2,0,1:T(8,128)(2,1)} fusion(), kind=kLoop, calls=%fused_computation.131 | loop fusion | flops 1916928 | bytes 294912 | tf_op jit(solution)/shard_map/neg | solution.py:259
  40.1 2.1 %copy.45 = bf16[3,1,384,192]{2,3,1,0:T(8,128)(2,1)} copy(bf16[3,1,384,192]{3,2,1,0:T(8,128)(2,1)} %get-tuple-element.7) | data formatting | bytes 884736
  42.1 2.1 %copy.46 = bf16[3,1,384,192]{2,3,1,0:T(8,128)(2,1)} copy(bf16[3,1,384,192]{3,2,1,0:T(8,128)(2,1)} %get-tuple-element.8) | data formatting | bytes 884736
  44.2 1.7 %fusion.40 = f32[384,3,192]{0,2,1:T(8,128)S(1)} fusion(bf16[768,384,1]{1,0,2:T(8,128)(2,1)} %bitcast.142, bf16[3,192,768]{2,1,0:T(8,128)(2,1)S(1)} %fusion.17, bf16[3,1,768]{2,1,0:T(2,128)(2,1)S(1)} %collective-permute-done), kind=kOutput, calls=%fused_computation.66 | convolution fusion | flops 341508096 | bytes 2363904 | tf_op jit(solution)/shard_map/rwk,kc->crw/dot_general | solution.py:171
  45.9 1.2 maximum_maximum_fusion
  48.2 0.8 fusion.148
  49.4 1.0 multiply_convert_fusion
  50.4 1.6 %copy.23 = bf16[384,3,192]{2,1,0:T(4,128)(2,1)S(1)} copy(bf16[384,3,192]{0,2,1:T(8,128)(2,1)} %multiply_convert_fusion) | data formatting | bytes 884736 | tf_op jit(solution)/shard_map/convert_element_type | solution.py:185
  52.0 1.3 reshape.362
  53.3 1.1 pad_bitcast_fusion
  54.4 0.9 copy.47
  55.4 24.3 %shard_map.91 = bf16[128,16,128]{2,1,0:T(8,128)(2,1)} custom-call(bf16[128,16,128]{2,1,0:T(8,128)(2,1)} %bitcast.136), custom_call_target="tpu_custom_call" | custom-call | tf_op jit(solution)/shard_map/pallas_call | solution.py:57
  79.7 1.5 %copy.40 = bf16[128,16,128]{0,2,1:T(8,128)(2,1)S(1)} copy(bf16[128,16,128]{2,1,0:T(8,128)(2,1)} %shard_map.91) | data formatting | bytes 1048576 | tf_op jit(solution)/shard_map/reshape | solution.py:71
  81.9 2.3 %copy.25 = bf16[3,128,3,192]{3,2,1,0:T(4,128)(2,1)} copy(bf16[3,128,3,192]{1,3,2,0:T(8,128)(2,1)} %bitcast.141) | data formatting | bytes 884736 | tf_op jit(solution)/shard_map/transpose | solution.py:243
  84.2 1.5 %reshape.366 = bf16[3,384,192]{2,1,0:T(8,128)(2,1)S(1)} reshape(bf16[3,128,3,192]{3,2,1,0:T(4,128)(2,1)} %copy.25) | data formatting | bytes 884736 | tf_op jit(solution)/shard_map/reshape | solution.py:244
  85.7 1.0 copy.27
  86.7 2.2 %collective-permute-start.2 = (bf16[3,384,192]{1,2,0:T(8,128)(2,1)}, bf16[3,384,192]{1,2,0:T(8,128)(2,1)S(1)}, u32[]{:S(2)}, u32[]{:S(2)}) collective-permute-start(bf16[3,384,192]{1,2,0:T(8,128)(2,1)} %copy.27), channel_id=1, source_target_pairs={{0,128},{128,0},{1,129},{129,1},{2,130},{130,2},{3,131},{131,3},{4... | collective-permute-start | bytes 1327112 | tf_op jit(solution)/shard_map/ppermute | solution.py:247
  88.9 2.8 %fusion.48 = (bf16[1,384,2,384]{3,1,2,0:T(8,128)(2,1)}, bf16[1,384,2,384]{3,1,2,0:T(8,128)(2,1)}, bf16[1,384,2,384]{3,1,2,0:T(8,128)(2,1)}, bf16[1,384,2,384]{3,1,2,0:T(8,128)(2,1)}) fusion(bf16[384,1,384]{2,0,1:T(8,128)(2,1)} %get-tuple-element.34, bf16[384,1,384]{2,0,1:T(8,128)(2,1)S(1)} %copy-done.9, bf16[384,1,384]{2,0,1:T(8,128)(2,1)} %fusion.83), kind=kLoop, calls=%fused_computation.85 | loop fusion | flops 1179648 | bytes 3244032 | tf_op jit(solution)/shard_map/stack | solution.py:258
  91.7 1.7 %fusion.54 = f32[3,384,2,192]{1,3,2,0:T(8,128)} fusion(bf16[3,384,192]{2,1,0:T(8,128)(2,1)S(1)} %reshape.366, s32[]{:T(128)S(6)} %select_n.233, bf16[384,1,192]{0,2,1:T(8,128)(2,1)S(1)} %copy-done.13, bf16[384,1,192]{0,2,1:T(8,128)(2,1)S(1)} %copy-done.12), kind=kOutput, calls=%fused_computation.92 | convolution fusion | flops 170164224 | bytes 2506756 | tf_op jit(solution)/shard_map/chx,xqw->chqw/dot_general | solution.py:270
  94.2 4.3 %fusion.22 = bf16[3,2,384,192]{2,3,1,0:T(8,128)(2,1)} fusion(bf16[1,384,2,384]{3,1,2,0:T(8,128)(2,1)} %get-tuple-element.24, bf16[1,384,2,384]{3,1,2,0:T(8,128)(2,1)} %get-tuple-element.19, f32[3,384,2,192]{1,3,2,0:T(8,128)} %fusion.54, bf16[3,384,192]{1,2,0:T(8,128)(2,1)} %copy-done.16, s32[]{:T(128)S(6)} %select_n.255, ...), kind=kOutput, calls=%fused_computation.35 | convolution fusion | flops 853327872 | bytes 4571140 | tf_op jit(solution)/shard_map/puqh,chqw->cpuw/dot_general | solution.py:191
  98.5 1.6 %fusion.35 = (bf16[3,1,384,192]{2,3,1,0:T(8,128)(2,1)S(1)}, bf16[3,1,384,192]{2,3,1,0:T(8,128)(2,1)S(1)}) fusion(bf16[3,1,384,192]{2,3,1,0:T(8,128)(2,1)S(1)} %copy-done.5, bf16[3,1,384,192]{2,3,1,0:T(8,128)(2,1)S(1)} %copy-done.6, bf16[3,2,384,192]{2,3,1,0:T(8,128)(2,1)} %fusion.22), kind=kLoop, calls=%fused_computation.60 | loop fusion | flops 2654208 | bytes 2654208 | tf_op jit(solution)/shard_map/convert.1
  100.1 1.8 %fusion.23 = bf16[3,384,2,192]{1,3,2,0:T(8,128)(2,1)} fusion(bf16[1,384,2,384]{3,1,2,0:T(8,128)(2,1)S(1)} %copy-done.10, bf16[1,384,2,384]{3,1,2,0:T(8,128)(2,1)S(1)} %copy-done.11, bf16[3,1,384,192]{2,3,1,0:T(8,128)(2,1)S(1)} %get-tuple-element.6, bf16[3,1,384,192]{2,3,1,0:T(8,128)(2,1)S(1)} %get-tuple-element.5), kind=kOutput, calls=%fused_computation.36 | convolution fusion | flops 684048384 | bytes 2949120 | tf_op jit(solution)/shard_map/qhpu,cpuw->chqw/dot_general | solution.py:205
  101.9 1.6 %copy.21 = f32[384,3,192]{2,1,0:T(4,128)} copy(f32[384,3,192]{0,2,1:T(8,128)S(1)} %get-tuple-element.26) | data formatting | bytes 1769472 | tf_op jit(solution)/shard_map/convert_element_type | solution.py:304
  103.5 2.0 %reshape.372 = f32[128,1728]{1,0:T(8,128)S(1)} reshape(f32[384,3,192]{2,1,0:T(4,128)} %copy.21) | data formatting | bytes 1769472 | tf_op jit(solution)/shard_map/convert_element_type | solution.py:304
  105.5 1.8 %convolution_bitcast_fusion.1 = f32[3,384,192]{1,2,0:T(8,128)S(1)} fusion(bf16[3,384,2,192]{1,3,2,0:T(8,128)(2,1)} %fusion.23, s32[]{:T(128)S(6)} %select_n.233, bf16[1,384,192]{1,2,0:T(8,128)(2,1)S(1)} %copy-done.8, bf16[1,384,192]{1,2,0:T(8,128)(2,1)S(1)} %copy-done.7), kind=kOutput, calls=%fused_computation.38 | convolution fusion | flops 170164224 | bytes 2064388 | tf_op jit(solution)/shard_map/chqw,qwv->chv/dot_general | solution.py:285
  107.3 1.8 %fusion.26 = bf16[3,384,192]{1,2,0:T(8,128)(2,1)S(1)} fusion(f32[3,384,192]{1,2,0:T(8,128)S(1)} %convolution_bitcast_fusion.1, bf16[3,384,2,192]{1,3,2,0:T(8,128)(2,1)} %collective-permute-done.3, s32[]{:T(128)S(6)} %select_n.255, bf16[1,384,192]{1,2,0:T(8,128)(2,1)S(1)} %copy-done.8, bf16[1,384,192]{1,2,0:T(8,128)(2,1)S(1)} %copy-done.7), kind=kOutput, calls=%fused_computation.42 | convolution fusion | flops 170827776 | bytes 2506756 | tf_op jit(solution)/shard_map/chqw,qwv->chv/dot_general | solution.py:290
  109.2 1.1 copy.28
  110.2 1.3 reshape.367
  111.6 1.3 copy.29
  112.9 1.1 pad.13
  114.0 1.2 copy.43.x_ref
  115.2 21.7 %shard_map.92 = bf16[128,16,128]{2,1,0:T(8,128)(2,1)} custom-call(bf16[128,16,128]{2,1,0:T(8,128)(2,1)} %copy.43.x_ref), custom_call_target="tpu_custom_call" | custom-call | tf_op jit(solution)/shard_map/pallas_call | solution.py:57
  136.9 1.2 copy.50
  139.1 1.4 collective-permute-start.4
  140.4 1.3 collective-permute-done.4
  141.8 1.0 maximum_select_fusion
  142.8 0.8 copy.31
  (60 shorter events, 8.1 us)
Async XLA Ops:
  0.0 6.9 %copy-start = (bf16[3,384,768]{2,1,0:T(8,128)(2,1)S(1)}, bf16[3,384,768]{2,1,0:T(8,128)(2,1)}, u32[]{:S(2)}) copy-start(bf16[3,384,768]{2,1,0:T(8,128)(2,1)} %param.9) | copy-start | bytes 5308420
  16.8 14.4 %collective-permute-start = (bf16[3,1,768]{2,1,0:T(2,128)(2,1)}, bf16[3,1,768]{2,1,0:T(2,128)(2,1)S(1)}, u32[]{:S(2)}, u32[]{:S(2)}) collective-permute-start(bf16[3,1,768]{2,1,0:T(2,128)(2,1)} %slice.61), channel_id=1, source_target_pairs={{0,128},{1,129},{2,130},{3,131},{4,132},{5,133},{6,134},{7,135},{8... | collective-permute-start | bytes 13832 | tf_op jit(solution)/shard_map/ppermute | solution.py:77
  18.4 6.6 %copy-start.1 = (f32[384,384]{0,1:T(8,128)}, f32[384,384]{0,1:T(8,128)S(1)}, u32[]{:S(2)}) copy-start(f32[384,384]{0,1:T(8,128)S(1)} %fusion.51) | copy-start | bytes 1769476
  26.7 2.8 %copy-start.2 = (f32[384,384]{0,1:T(8,128)S(1)}, f32[384,384]{0,1:T(8,128)}, u32[]{:S(2)}) copy-start(f32[384,384]{0,1:T(8,128)} %copy-done.1) | copy-start | bytes 1769476
  32.0 13.9 %collective-permute-start.1 = (bf16[1,193,768]{2,1,0:T(8,128)(2,1)}, bf16[1,193,768]{2,1,0:T(8,128)(2,1)}, u32[]{:S(2)}, u32[]{:S(2)}) collective-permute-start(bf16[1,193,768]{2,1,0:T(8,128)(2,1)} %pad_maximum_fusion.6), channel_id=1, source_target_pairs={{0,1},{1,2},{2,3},{3,4},{4,5},{5,6},{6,7},{7,8},{8,9},{9,10},{10,1... | collective-permute-start | bytes 889352 | tf_op jit(solution)/shard_map/ppermute | solution.py:77
  45.9 1.3 copy-start.4
  47.2 1.1 copy-start.3
  47.2 1.1 copy-start.14
  48.2 1.1 copy-start.15
  81.9 7.0 %copy-start.9 = (bf16[384,1,384]{2,0,1:T(8,128)(2,1)S(1)}, bf16[384,1,384]{2,0,1:T(8,128)(2,1)}, u32[]{:S(2)}) copy-start(bf16[384,1,384]{2,0,1:T(8,128)(2,1)} %get-tuple-element.33) | copy-start | bytes 884740
  86.7 5.0 %copy-start.12 = (bf16[384,1,192]{0,2,1:T(8,128)(2,1)S(1)}, bf16[384,1,192]{0,2,1:T(8,128)(2,1)}, u32[]{:S(2)}) copy-start(bf16[384,1,192]{0,2,1:T(8,128)(2,1)} %get-tuple-element.16) | copy-start | bytes 442372
  86.7 5.0 %copy-start.13 = (bf16[384,1,192]{0,2,1:T(8,128)(2,1)S(1)}, bf16[384,1,192]{0,2,1:T(8,128)(2,1)}, u32[]{:S(2)}) copy-start(bf16[384,1,192]{0,2,1:T(8,128)(2,1)} %get-tuple-element.18) | copy-start | bytes 442372
  86.7 6.7 %collective-permute-start.2 = (bf16[3,384,192]{1,2,0:T(8,128)(2,1)}, bf16[3,384,192]{1,2,0:T(8,128)(2,1)S(1)}, u32[]{:S(2)}, u32[]{:S(2)}) collective-permute-start(bf16[3,384,192]{1,2,0:T(8,128)(2,1)} %copy.27), channel_id=1, source_target_pairs={{0,128},{128,0},{1,129},{129,1},{2,130},{130,2},{3,131},{131,3},{4... | collective-permute-start | bytes 1327112 | tf_op jit(solution)/shard_map/ppermute | solution.py:247
  93.4 0.8 copy-start.16
  94.2 4.3 %copy-start.5 = (bf16[3,1,384,192]{2,3,1,0:T(8,128)(2,1)S(1)}, bf16[3,1,384,192]{2,3,1,0:T(8,128)(2,1)}, u32[]{:S(2)}) copy-start(bf16[3,1,384,192]{2,3,1,0:T(8,128)(2,1)} %copy.45) | copy-start | bytes 1327108
  94.2 4.3 %copy-start.6 = (bf16[3,1,384,192]{2,3,1,0:T(8,128)(2,1)S(1)}, bf16[3,1,384,192]{2,3,1,0:T(8,128)(2,1)}, u32[]{:S(2)}) copy-start(bf16[3,1,384,192]{2,3,1,0:T(8,128)(2,1)} %copy.46) | copy-start | bytes 1327108
  98.5 1.6 %copy-start.10 = (bf16[1,384,2,384]{3,1,2,0:T(8,128)(2,1)S(1)}, bf16[1,384,2,384]{3,1,2,0:T(8,128)(2,1)}, u32[]{:S(2)}) copy-start(bf16[1,384,2,384]{3,1,2,0:T(8,128)(2,1)} %get-tuple-element.20) | copy-start | bytes 1769476
  98.5 1.6 %copy-start.11 = (bf16[1,384,2,384]{3,1,2,0:T(8,128)(2,1)S(1)}, bf16[1,384,2,384]{3,1,2,0:T(8,128)(2,1)}, u32[]{:S(2)}) copy-start(bf16[1,384,2,384]{3,1,2,0:T(8,128)(2,1)} %get-tuple-element.23) | copy-start | bytes 1769476
  101.9 5.4 %collective-permute-start.3 = (bf16[3,384,2,192]{1,3,2,0:T(8,128)(2,1)}, bf16[3,384,2,192]{1,3,2,0:T(8,128)(2,1)}, u32[]{:S(2)}, u32[]{:S(2)}) collective-permute-start(bf16[3,384,2,192]{1,3,2,0:T(8,128)(2,1)} %fusion.23), channel_id=1, source_target_pairs={{0,128},{128,0},{1,129},{129,1},{2,130},{130,2},{3,131},{131,3},{4... | collective-permute-start | bytes 2654216 | tf_op jit(solution)/shard_map/ppermute | solution.py:284
  103.5 2.0 %copy-start.7 = (bf16[1,384,192]{1,2,0:T(8,128)(2,1)S(1)}, bf16[1,384,192]{1,2,0:T(8,128)(2,1)}, u32[]{:S(2)}) copy-start(bf16[1,384,192]{1,2,0:T(8,128)(2,1)} %get-tuple-element.15) | copy-start | bytes 442372
  103.5 2.0 %copy-start.8 = (bf16[1,384,192]{1,2,0:T(8,128)(2,1)S(1)}, bf16[1,384,192]{1,2,0:T(8,128)(2,1)}, u32[]{:S(2)}) copy-start(bf16[1,384,192]{1,2,0:T(8,128)(2,1)} %get-tuple-element.17) | copy-start | bytes 442372
  139.1 2.7 %collective-permute-start.4 = (bf16[192,3,192]{2,1,0:T(4,128)(2,1)S(1)}, bf16[192,3,192]{2,1,0:T(4,128)(2,1)S(1)}, u32[]{:S(2)}, u32[]{:S(2)}) collective-permute-start(bf16[192,3,192]{2,1,0:T(4,128)(2,1)S(1)} %get-tuple-element.14), channel_id=1, source_target_pairs={{0,128},{128,0},{1,129},{129,1},{2,130},{130,2},{3,131},{131,3},{4... | collective-permute-start | bytes 663560 | tf_op jit(solution)/shard_map/ppermute | solution.py:310

commit v5 on v2

--- a/solution.py
+++ b/solution.py
@@ -11,7 +11,7 @@
 MESH_ID = pl.DeviceIdType.MESH
 
 
-def exchange_kernel(x_ref, o_ref, send_sem, recv_sem, own_sem):
+def start_exchange(x_ref, o_ref, send_sem, recv_sem, own_sem):
     count = x_ref.shape[0]
     me = lax.axis_index("tile")
     section = lax.axis_index("section")
@@ -48,9 +48,35 @@
         device_id=(section, lax.rem(me + 1, count)),
         device_id_type=MESH_ID,
     )
+    return every, own
+
+
+def finish_exchange(every, own):
     every.wait_send()
     every.wait_recv()
     own.wait()
+
+
+def exchange_kernel(x_ref, o_ref, send_sem, recv_sem, own_sem):
+    finish_exchange(*start_exchange(x_ref, o_ref, send_sem, recv_sem, own_sem))
+
+
+def exchange_tables_kernel(x_ref, o_ref, cos_ref, sin_ref, send_sem, recv_sem, own_sem):
+    pending = start_exchange(x_ref, o_ref, send_sem, recv_sem, own_sem)
+    length = cos_ref.shape[0]
+    block = 16
+
+    def rows(index, carry):
+        first = pl.multiple_of(index * block, block)
+        row = lax.broadcasted_iota(jnp.int32, (block, length), 0) + first
+        col = lax.broadcasted_iota(jnp.int32, (block, length), 1)
+        angles = lax.rem(row * col, length).astype(jnp.float32) * (2.0 * math.pi / length)
+        cos_ref[pl.ds(first, block), :] = jnp.cos(angles).astype(cos_ref.dtype)
+        sin_ref[pl.ds(first, block), :] = jnp.sin(angles).astype(sin_ref.dtype)
+        return carry
+
+    lax.fori_loop(0, length // block, rows, 0)
+    finish_exchange(*pending)
 
 
 def exchange(chunks, collective_id):
@@ -62,6 +88,33 @@
         scratch_shapes=[pltpu.SemaphoreType.DMA(())] * 3,
         compiler_params=pltpu.CompilerParams(collective_id=collective_id, has_side_effects=True),
     )(chunks)
+
+
+def exchange_with_tables(chunks, collective_id, length):
+    table = jax.ShapeDtypeStruct((length, length), jnp.bfloat16)
+    return pl.pallas_call(
+        exchange_tables_kernel,
+        out_shape=(jax.ShapeDtypeStruct(chunks.shape, chunks.dtype), table, table),
+        in_specs=[pl.BlockSpec(memory_space=pl.ANY)],
+        out_specs=(
+            pl.BlockSpec(memory_space=pl.ANY),
+            pl.BlockSpec(memory_space=pltpu.VMEM),
+            pl.BlockSpec(memory_space=pltpu.VMEM),
+        ),
+        scratch_shapes=[pltpu.SemaphoreType.DMA(())] * 3,
+        compiler_params=pltpu.CompilerParams(collective_id=collective_id, has_side_effects=True),
+    )(chunks)
+
+
+def pad_chunks(chunks):
+    count, length = chunks.shape
+    padded = -(-length // 2048) * 2048
+    slabs = jnp.pad(chunks, ((0, 0), (0, padded - length)))
+    return slabs.reshape(count, padded // 128, 128), length
+
+
+def unpad_chunks(slabs, length):
+    return slabs.reshape(slabs.shape[0], -1)[:, :length]
 
 
 def exchange_chunks(chunks, collective_id):
@@ -245,7 +298,9 @@
     normed_half = layer_norm(feature_half, norm_gain)
     tiles = lax.axis_size("tile")
     group_width, tile_rows = channels // tiles, normed_half.shape[1]
-    arrived = exchange_chunks(normed_half.reshape(tiles, -1), 0)
+    slabs, length = pad_chunks(normed_half.reshape(tiles, -1))
+    slabs, cos_h, sin_h = exchange_with_tables(slabs, 0, full_rows)
+    arrived = unpad_chunks(slabs, length)
     fields = (
         arrived.reshape(tiles, group_width, tile_rows, cell_half)
         .transpose(1, 0, 2, 3)
@@ -254,7 +309,6 @@
     swap = [(0, 1), (1, 0)]
     other_fields = lax.ppermute(fields, "section", swap)
 
-    cos_h, sin_h = fourier_tables(full_rows)
     if full_rows == field_cols:
         cos_w, sin_w = cos_h, sin_h
     else:

time: 138 us -> 137 us (level)
  other arithmetic: 19.2 us -> 12.8 us
  starting transfers between devices: 9.75 us -> 12.4 us
  local copies, waits for them, and re-layouts: 31.6 us -> 34 us
    pallas_call x2 -> x1, Pallas kernels: 46.3 us -> 20.6 us  [exchange(): pl.pallas_call(exchange_kernel, out_shape=jax.ShapeDtypeStruct(chunks.sha...]
    pallas_call x0 -> x1, Pallas kernels: none -> 25.6 us  [exchange_with_tables(): pl.pallas_call(exchange_tables_kernel, out_shape=(jax.ShapeDtypeStruct(ch...]
    convert_element_type x1 -> x0, other arithmetic: 3.23 us -> none  [fourier_tables(): jnp.sin(angles).astype(jnp.bfloat16)]
    neg x1 -> x0, other arithmetic: 2.97 us -> none  [local(): -sin_h]
    another operation x0 -> x1, local copies, waits for them, and re-layouts: none -> 1.81 us  [local(): inverse_table = jnp.stack([cos_part, -sin_part], axis=0)]
    another operation x1 -> x2, other arithmetic: 1.57 us -> 3.3 us  [the longest x1 1.72 us: local(): jnp.stack([-sin_h, cos_h], axis=1)]
    another operation x2 -> x1, other arithmetic: 3.37 us -> 1.74 us  [local(): inverse_table = jnp.stack([cos_part, -sin_part], axis=0)]
    ppermute x1, starting transfers between devices: 2.06 us -> 3.65 us  [local(): other_fields = lax.ppermute(fields, 'section', swap)]
  transfers between devices with their start and end apart: 5 -> 5, of which waited for: 2 -> 2; matrix products, arithmetic and copies ran while one was open for 21% -> 13% of each run, Pallas kernels for 0% -> 0%
where the time goes in v5:
time: 137 us; the launch traced here: 136 us
  Pallas kernels  46.2 us (34%)
  local copies, waits for them, and re-layouts  34 us (25%)
  matrix products  26.9 us (20%)
  other arithmetic  12.8 us (9%)
  starting transfers between devices  12.4 us (9%)
  waiting for transfers between devices  3.1 us (2%)
    pallas_call x1, Pallas kernels, exchange_with_tables(): pl.pallas_call(exchange_tables_kernel, out_shape=(jax.ShapeDtypeStruct(ch...  25.6 us
    pallas_call x1, Pallas kernels, exchange(): pl.pallas_call(exchange_kernel, out_shape=jax.ShapeDtypeStruct(chunks.sha...  20.6 us
    unnamed x43, local copies, waits for them, and re-layouts  8.22 us
    ppermute x2, starting transfers between devices, from_behind(): return lax.ppermute(block, axis, route)  6.37 us
    dot_general x1, matrix products, stem_layers(): jnp.einsum('zji,if->zjf', aerial_patch_grid, patch_kernel_matrix(patch_co...  5.05 us
    dot_general x1, matrix products, filter_columns(): jnp.einsum('puqh,chqw->cpuw', forward_h, row_spectrum, preferred_element_...  4.28 us
    dot_general x1, matrix products, stem_layers(): jnp.einsum('zji,if->zjf', initial_layer, merging_kernel_matrix(merging_co...  4.26 us
    convert_element_type x2, local copies, waits for them, and re-layouts, local(): rows_back.astype(jnp.float32)  3.81 us
  transfers between devices with their start and end apart: 5, of which 2 were waited for; matrix products, arithmetic and copies ran while one was open for 13% of the time, Pallas kernels for 0%

profile of v5, /device:TPU:1, one launch (start us, length us, event | category | flops | bytes accessed | tf_op | source)
XLA Modules:
  0.0 135.8 jit_solution(14570824947333231716)
XLA Ops:
  0.1 0.8 tile.4
  1.7 2.5 %convolution_convert_fusion = bf16[1536,192]{0,1:T(8,128)(2,1)} fusion(bf16[384,192]{1,0:T(8,128)(2,1)} %bitcast.177, s32[1536]{0:T(1024)S(1)} %fusion.96), kind=kOutput, calls=%fused_computation.14 | convolution fusion | flops 227377152 | bytes 743424 | tf_op jit(solution)/shard_map/dot_general | solution.py:145
  4.3 3.5 %fusion.8 = bf16[768,1536,1]{1,0,2:T(8,128)(2,1)} fusion(s32[1536]{0:T(1024)S(1)} %get-tuple-element.49, s32[768]{0:T(1024)S(1)} %get-tuple-element.46, bf16[48,96]{1,0:T(8,128)(2,1)} %bitcast.178, s32[1536]{0:T(1024)S(1)} %get-tuple-element.48, s32[768]{0:T(1024)S(1)} %get-tuple-element.47), kind=kOutput, calls=%fused_computation.11 | convolution fusion | flops 237367296 | bytes 2386944 | tf_op jit(solution)/shard_map/dot_general | solution.py:151
  7.7 5.0 %fusion.7 = bf16[3,192,1536]{2,1,0:T(8,128)(2,1)} fusion(bf16[768,1536,1]{1,0,2:T(8,128)(2,1)} %fusion.8, f32[1536]{0:T(1024)S(1)} %add.293, bf16[3,384,768]{2,1,0:T(8,128)(2,1)S(1)} %copy-done, s32[]{:T(128)S(6)} %select_n.194), kind=kOutput, calls=%fused_computation.10 | convolution fusion | flops 1367801856 | bytes 5021700 | tf_op jit(solution)/shard_map/zji,if->zjf/dot_general | solution.py:201
  12.8 4.3 %fusion.17 = bf16[3,192,768]{2,1,0:T(8,128)(2,1)S(1)} fusion(bf16[3,192,1536]{2,1,0:T(8,128)(2,1)} %fusion.7, bf16[1536,192]{0,1:T(8,128)(2,1)} %convolution_convert_fusion, s32[768]{0:T(1024)S(1)} %get-tuple-element.45, s32[1536]{0:T(1024)S(1)} %fusion.89, f32[768]{0:T(1024)S(1)} %add.306, s32[768]{0:T(1024)S(1)} %get-tuple-element.44), kind=kOutput, calls=%fused_computation.23 | convolution fusion | flops 1820049408 | bytes 3259392 | tf_op jit(solution)/shard_map/zji,if->zjf/dot_general | solution.py:210
  17.7 1.3 collective-permute-start
  18.9 2.2 %slice_bitcast_fusion.2 = (bf16[1,192,384]{2,1,0:T(8,128)(2,1)S(1)}, bf16[1,192,384]{2,1,0:T(8,128)(2,1)}, bf16[1,192,384]{2,1,0:T(8,128)(2,1)}, bf16[1,192,384]...) fusion(bf16[3,3,192,384]{3,2,1,0:T(8,128)(2,1)} %param.14), kind=kLoop, calls=%fused_computation.129 | loop fusion | bytes 2654208 | tf_op jit(solution)/shard_map/stack;squeeze | solution.py:188
  21.3 0.9 pad_maximum_fusion.6
  22.9 1.5 %constant_dynamic-slice_fusion = (bf16[3,1,384,192]{3,2,1,0:T(8,128)(2,1)}, bf16[3,1,384,192]{3,2,1,0:T(8,128)(2,1)}) fusion(bf16[3,2,384,384]{3,2,1,0:T(8,128)(2,1)S(1)} %copy-done.10, s32[]{:T(128)S(6)} %select_n.194, s32[]{:T(128)S(6)} %add.324), kind=kLoop, calls=%fused_computation.232 | loop fusion | bytes 1769480 | tf_op jit(solution)/shard_map/slice | solution.py:257
  24.4 0.9 pad_maximum_fusion.7
  25.3 0.8 pad_maximum_fusion.8
  26.0 5.1 %collective-permute-start.1 = (bf16[1,193,768]{2,1,0:T(8,128)(2,1)}, bf16[1,193,768]{2,1,0:T(8,128)(2,1)}, u32[]{:S(2)}, u32[]{:S(2)}) collective-permute-start(bf16[1,193,768]{2,1,0:T(8,128)(2,1)} %pad_maximum_fusion.8), channel_id=1, source_target_pairs={{0,1},{1,2},{2,3},{3,4},{4,5},{5,6},{6,7},{7,8},{8,9},{9,10},{10,1... | collective-permute-start | bytes 889352 | tf_op jit(solution)/shard_map/ppermute | solution.py:130
  31.2 0.9 stack.123
  32.1 0.9 stack.131
  32.9 2.1 %copy.62 = bf16[3,1,384,192]{2,3,1,0:T(8,128)(2,1)} copy(bf16[3,1,384,192]{3,2,1,0:T(8,128)(2,1)} %get-tuple-element.13) | data formatting | bytes 884736
  35.0 2.1 %copy.63 = bf16[3,1,384,192]{2,3,1,0:T(8,128)(2,1)} copy(bf16[3,1,384,192]{3,2,1,0:T(8,128)(2,1)} %get-tuple-element.14) | data formatting | bytes 884736
  37.1 1.7 %fusion.137 = f32[384,3,192]{0,2,1:T(8,128)S(1)} fusion(bf16[768,384,1]{1,0,2:T(8,128)(2,1)} %bitcast.166, bf16[3,192,768]{2,1,0:T(8,128)(2,1)S(1)} %fusion.17), kind=kOutput, calls=%fused_computation.248 | convolution fusion | flops 339738624 | bytes 2359296 | tf_op jit(solution)/shard_map/rwk,kc->crw/dot_general | solution.py:226
  38.8 1.2 maximum_maximum_fusion
  41.8 0.8 convert_reduce_fusion
  43.2 0.9 copy.27
  44.7 0.9 copy.64
  45.6 25.6 %shard_map.91 = (bf16[128,16,128]{2,1,0:T(8,128)(2,1)}, bf16[384,384]{1,0:T(8,128)(2,1)}, bf16[384,384]{1,0:T(8,128)(2,1)}) custom-call(bf16[128,16,128]{2,1,0:T(8,128)(2,1)} %bitcast.170), custom_call_target="tpu_custom_call" | custom-call | tf_op jit(solution)/shard_map/pallas_call | solution.py:95
  71.2 1.7 %fusion.75 = (bf16[1,384,192]{2,1,0:T(8,128)(2,1)S(1)}, bf16[384,1,192]{2,0,1:T(8,128)(2,1)}) fusion(bf16[384,384]{1,0:T(8,128)(2,1)} %get-tuple-element.10, s32[]{:T(128)S(6)} %select_n.194), kind=kLoop, calls=%fused_computation.125 | loop fusion | flops 221184 | bytes 442372 | tf_op jit(solution)/shard_map/stack | solution.py:319
  72.9 1.7 %negate_bitcast_fusion = bf16[384,1,384]{2,0,1:T(8,128)(2,1)} fusion(bf16[384,384]{1,0:T(8,128)(2,1)} %get-tuple-element.10), kind=kLoop, calls=%fused_computation.109 | loop fusion | flops 147456 | bytes 589824 | tf_op jit(solution)/shard_map/stack | solution.py:321
  74.7 1.5 %copy.53 = bf16[128,16,128]{0,2,1:T(8,128)(2,1)S(1)} copy(bf16[128,16,128]{2,1,0:T(8,128)(2,1)} %get-tuple-element.8) | data formatting | bytes 1048576 | tf_op jit(solution)/shard_map/reshape | solution.py:117
  76.2 1.4 %copy.29 = bf16[3,128,3,192]{3,2,1,0:T(4,128)(2,1)} copy(bf16[3,128,3,192]{1,3,2,0:T(8,128)(2,1)S(1)} %bitcast.175) | data formatting | bytes 884736 | tf_op jit(solution)/shard_map/transpose | solution.py:306
  77.6 1.6 %reshape.297 = bf16[3,384,192]{2,1,0:T(8,128)(2,1)S(1)} reshape(bf16[3,128,3,192]{3,2,1,0:T(4,128)(2,1)} %copy.29) | data formatting | bytes 884736 | tf_op jit(solution)/shard_map/reshape | solution.py:307
  79.1 1.8 %dynamic-slice_bitcast_fusion = (bf16[1,384,192]{2,1,0:T(8,128)(2,1)}, bf16[384,1,192]{2,0,1:T(8,128)(2,1)}) fusion(bf16[384,384]{1,0:T(8,128)(2,1)} %get-tuple-element.9, s32[]{:T(128)S(6)} %select_n.194), kind=kLoop, calls=%fused_computation.123 | loop fusion | bytes 442372 | tf_op jit(solution)/shard_map/stack | solution.py:319
  80.9 1.0 copy.32
  81.9 3.7 %collective-permute-start.2 = (bf16[3,384,192]{1,2,0:T(8,128)(2,1)}, bf16[3,384,192]{1,2,0:T(8,128)(2,1)S(1)}, u32[]{:S(2)}, u32[]{:S(2)}) collective-permute-start(bf16[3,384,192]{1,2,0:T(8,128)(2,1)} %copy.32), channel_id=1, source_target_pairs={{0,128},{128,0},{1,129},{129,1},{2,130},{130,2},{3,131},{131,3},{4... | collective-permute-start | bytes 1327112 | tf_op jit(solution)/shard_map/ppermute | solution.py:310
  85.6 2.8 %fusion.51 = (bf16[1,384,2,384]{3,1,2,0:T(8,128)(2,1)}, bf16[1,384,2,384]{3,1,2,0:T(8,128)(2,1)}, bf16[1,384,2,384]{3,1,2,0:T(8,128)(2,1)}, bf16[1,384,2,384]{3,1,2,0:T(8,128)(2,1)}) fusion(bf16[384,1,384]{2,0,1:T(8,128)(2,1)} %bitcast.176, bf16[384,1,384]{2,0,1:T(8,128)(2,1)S(1)} %bitcast.168, bf16[384,1,384]{2,0,1:T(8,128)(2,1)} %negate_bitcast_fusion), kind=kLoop, calls=%fused_computation.83 | loop fusion | flops 1179648 | bytes 3244032 | tf_op jit(solution)/shard_map/stack | solution.py:320
  88.4 1.7 %fusion.53 = f32[3,384,2,192]{1,3,2,0:T(8,128)} fusion(bf16[3,384,192]{2,1,0:T(8,128)(2,1)S(1)} %reshape.297, s32[]{:T(128)S(6)} %select_n.194, bf16[384,1,192]{2,0,1:T(8,128)(2,1)S(1)} %copy-done.9, bf16[384,1,192]{2,0,1:T(8,128)(2,1)S(1)} %copy-done.8), kind=kOutput, calls=%fused_computation.88 | convolution fusion | flops 170164224 | bytes 2506756 | tf_op jit(solution)/shard_map/chx,xqw->chqw/dot_general | solution.py:332
  90.1 0.8 copy-done.18
  90.9 4.3 %fusion.21 = bf16[3,2,384,192]{2,3,1,0:T(8,128)(2,1)} fusion(bf16[1,384,2,384]{3,1,2,0:T(8,128)(2,1)} %get-tuple-element.35, bf16[1,384,2,384]{3,1,2,0:T(8,128)(2,1)} %get-tuple-element.24, f32[3,384,2,192]{1,3,2,0:T(8,128)} %fusion.53, bf16[3,384,192]{1,2,0:T(8,128)(2,1)} %copy-done.18, s32[]{:T(128)S(6)} %select_n.215, ...), kind=kOutput, calls=%fused_computation.35 | convolution fusion | flops 853327872 | bytes 4571140 | tf_op jit(solution)/shard_map/puqh,chqw->cpuw/dot_general | solution.py:252
  95.2 1.6 %fusion.38 = (bf16[3,1,384,192]{2,3,1,0:T(8,128)(2,1)S(1)}, bf16[3,1,384,192]{2,3,1,0:T(8,128)(2,1)S(1)}) fusion(bf16[3,1,384,192]{2,3,1,0:T(8,128)(2,1)S(1)} %copy-done.6, bf16[3,1,384,192]{2,3,1,0:T(8,128)(2,1)S(1)} %copy-done.7, bf16[3,2,384,192]{2,3,1,0:T(8,128)(2,1)} %fusion.21), kind=kLoop, calls=%fused_computation.62 | loop fusion | flops 2654208 | bytes 2654208 | tf_op jit(solution)/shard_map/convert.1
  96.8 0.9 fusion.22
  98.5 1.9 %collective-permute-done.3 = bf16[3,384,2,192]{1,3,2,0:T(8,128)(2,1)S(1)} collective-permute-done((bf16[3,384,2,192]{1,3,2,0:T(8,128)(2,1)S(1)}, bf16[3,384,2,192]{1,3,2,0:T(8,128)(2,1)S(1)}, u32[]{:S(2)}, u32[]{:S(2)}) %collective-permute-start.3) | collective-permute-done | bytes 884768 | tf_op jit(solution)/shard_map/ppermute | solution.py:346
  100.9 1.1 copy.36
  102.0 1.3 reshape.298
  103.3 0.8 copy.37
  104.1 1.2 copy.60.x_ref
  105.3 20.6 %shard_map.92 = bf16[128,16,128]{2,1,0:T(8,128)(2,1)} custom-call(bf16[128,16,128]{2,1,0:T(8,128)(2,1)} %copy.60.x_ref), custom_call_target="tpu_custom_call" | custom-call | tf_op jit(solution)/shard_map/pallas_call | solution.py:83
  125.9 1.2 copy.67
  127.2 2.1 %reshape.302 = f32[384,3,192]{2,1,0:T(4,128)} reshape(f32[128,1728]{1,0:T(8,128)S(1)} %slice_convert_fusion) | data formatting | bytes 1769472 | tf_op jit(solution)/shard_map/convert_element_type | solution.py:365
  129.3 1.7 %copy.39 = f32[384,3,192]{0,2,1:T(8,128)S(1)} copy(f32[384,3,192]{2,1,0:T(4,128)} %reshape.302) | data formatting | bytes 1769472 | tf_op jit(solution)/shard_map/convert_element_type | solution.py:365
  131.3 2.0 %collective-permute-start.4 = (bf16[192,3,192]{0,2,1:T(8,128)(2,1)S(1)}, bf16[192,3,192]{0,2,1:T(8,128)(2,1)S(1)}, u32[]{:S(2)}, u32[]{:S(2)}) collective-permute-start(bf16[192,3,192]{0,2,1:T(8,128)(2,1)S(1)} %get-tuple-element.29), channel_id=1, source_target_pairs={{0,128},{128,0},{1,129},{129,1},{2,130},{130,2},{3,131},{131,3},{4... | collective-permute-start | bytes 663560 | tf_op jit(solution)/shard_map/ppermute | solution.py:372
  133.4 1.2 collective-permute-done.4
  134.8 1.0 copy.40
  (69 shorter events, 7.3 us)
Async XLA Ops:
  0.0 7.7 %copy-start = (bf16[3,384,768]{2,1,0:T(8,128)(2,1)S(1)}, bf16[3,384,768]{2,1,0:T(8,128)(2,1)}, u32[]{:S(2)}) copy-start(bf16[3,384,768]{2,1,0:T(8,128)(2,1)} %param.9) | copy-start | bytes 5308420
  17.7 7.6 %collective-permute-start = (bf16[3,1,768]{2,1,0:T(2,128)(2,1)}, bf16[3,1,768]{2,1,0:T(2,128)(2,1)S(1)}, u32[]{:S(2)}, u32[]{:S(2)}) collective-permute-start(bf16[3,1,768]{2,1,0:T(2,128)(2,1)} %slice.80), channel_id=1, source_target_pairs={{0,128},{1,129},{2,130},{3,131},{4,132},{5,133},{6,134},{7,135},{8... | collective-permute-start | bytes 13832 | tf_op jit(solution)/shard_map/ppermute | solution.py:130
  21.2 1.7 %copy-start.10 = (bf16[3,2,384,384]{3,2,1,0:T(8,128)(2,1)S(1)}, bf16[3,2,384,384]{3,2,1,0:T(8,128)(2,1)}, u32[]{:S(2)}) copy-start(bf16[3,2,384,384]{3,2,1,0:T(8,128)(2,1)} %param.17) | copy-start | bytes 5308420
  24.4 6.8 %copy-start.13 = (bf16[1,192,384]{2,1,0:T(8,128)(2,1)S(1)}, bf16[1,192,384]{2,1,0:T(8,128)(2,1)}, u32[]{:S(2)}) copy-start(bf16[1,192,384]{2,1,0:T(8,128)(2,1)} %get-tuple-element.16) | copy-start | bytes 442372
  24.4 6.8 %copy-start.14 = (bf16[1,192,384]{2,1,0:T(8,128)(2,1)S(1)}, bf16[1,192,384]{2,1,0:T(8,128)(2,1)}, u32[]{:S(2)}) copy-start(bf16[1,192,384]{2,1,0:T(8,128)(2,1)} %get-tuple-element.17) | copy-start | bytes 442372
  24.4 6.8 %copy-start.15 = (bf16[1,192,384]{2,1,0:T(8,128)(2,1)S(1)}, bf16[1,192,384]{2,1,0:T(8,128)(2,1)}, u32[]{:S(2)}) copy-start(bf16[1,192,384]{2,1,0:T(8,128)(2,1)} %get-tuple-element.22) | copy-start | bytes 442372
  26.0 12.7 %collective-permute-start.1 = (bf16[1,193,768]{2,1,0:T(8,128)(2,1)}, bf16[1,193,768]{2,1,0:T(8,128)(2,1)}, u32[]{:S(2)}, u32[]{:S(2)}) collective-permute-start(bf16[1,193,768]{2,1,0:T(8,128)(2,1)} %pad_maximum_fusion.8), channel_id=1, source_target_pairs={{0,1},{1,2},{2,3},{3,4},{4,5},{5,6},{6,7},{7,8},{8,9},{9,10},{10,1... | collective-permute-start | bytes 889352 | tf_op jit(solution)/shard_map/ppermute | solution.py:130
  38.8 1.3 copy-start.3
  40.0 1.1 copy-start.1
  40.7 1.1 copy-start.2
  40.7 1.1 copy-start.16
  41.8 1.2 copy-start.17
  77.6 8.0 %copy-start.4 = (bf16[384,384]{1,0:T(8,128)(2,1)S(1)}, bf16[384,384]{1,0:T(8,128)(2,1)}, u32[]{:S(2)}) copy-start(bf16[384,384]{1,0:T(8,128)(2,1)} %get-tuple-element.10) | copy-start | bytes 884740
  81.9 6.4 %copy-start.8 = (bf16[384,1,192]{2,0,1:T(8,128)(2,1)S(1)}, bf16[384,1,192]{2,0,1:T(8,128)(2,1)}, u32[]{:S(2)}) copy-start(bf16[384,1,192]{2,0,1:T(8,128)(2,1)} %get-tuple-element.31) | copy-start | bytes 442372
  81.9 6.4 %copy-start.9 = (bf16[384,1,192]{2,0,1:T(8,128)(2,1)S(1)}, bf16[384,1,192]{2,0,1:T(8,128)(2,1)}, u32[]{:S(2)}) copy-start(bf16[384,1,192]{2,0,1:T(8,128)(2,1)} %get-tuple-element.33) | copy-start | bytes 442372
  81.9 8.2 %collective-permute-start.2 = (bf16[3,384,192]{1,2,0:T(8,128)(2,1)}, bf16[3,384,192]{1,2,0:T(8,128)(2,1)S(1)}, u32[]{:S(2)}, u32[]{:S(2)}) collective-permute-start(bf16[3,384,192]{1,2,0:T(8,128)(2,1)} %copy.32), channel_id=1, source_target_pairs={{0,128},{128,0},{1,129},{129,1},{2,130},{130,2},{3,131},{131,3},{4... | collective-permute-start | bytes 1327112 | tf_op jit(solution)/shard_map/ppermute | solution.py:310
  90.1 0.8 copy-start.18
  90.9 4.3 %copy-start.6 = (bf16[3,1,384,192]{2,3,1,0:T(8,128)(2,1)S(1)}, bf16[3,1,384,192]{2,3,1,0:T(8,128)(2,1)}, u32[]{:S(2)}) copy-start(bf16[3,1,384,192]{2,3,1,0:T(8,128)(2,1)} %copy.62) | copy-start | bytes 1327108
  90.9 4.3 %copy-start.7 = (bf16[3,1,384,192]{2,3,1,0:T(8,128)(2,1)S(1)}, bf16[3,1,384,192]{2,3,1,0:T(8,128)(2,1)}, u32[]{:S(2)}) copy-start(bf16[3,1,384,192]{2,3,1,0:T(8,128)(2,1)} %copy.63) | copy-start | bytes 1327108
  95.2 1.6 %copy-start.11 = (bf16[1,384,2,384]{3,1,2,0:T(8,128)(2,1)S(1)}, bf16[1,384,2,384]{3,1,2,0:T(8,128)(2,1)}, u32[]{:S(2)}) copy-start(bf16[1,384,2,384]{3,1,2,0:T(8,128)(2,1)} %get-tuple-element.25) | copy-start | bytes 1769476
  95.2 1.6 %copy-start.12 = (bf16[1,384,2,384]{3,1,2,0:T(8,128)(2,1)S(1)}, bf16[1,384,2,384]{3,1,2,0:T(8,128)(2,1)}, u32[]{:S(2)}) copy-start(bf16[1,384,2,384]{3,1,2,0:T(8,128)(2,1)} %get-tuple-element.34) | copy-start | bytes 1769476
  96.8 1.3 copy-start.5
  97.7 2.7 %collective-permute-start.3 = (bf16[3,384,2,192]{1,3,2,0:T(8,128)(2,1)S(1)}, bf16[3,384,2,192]{1,3,2,0:T(8,128)(2,1)S(1)}, u32[]{:S(2)}, u32[]{:S(2)}) collective-permute-start(bf16[3,384,2,192]{1,3,2,0:T(8,128)(2,1)S(1)} %fusion.22), channel_id=1, source_target_pairs={{0,128},{128,0},{1,129},{129,1},{2,130},{130,2},{3,131},{131,3},{4... | collective-permute-start | bytes 2654216 | tf_op jit(solution)/shard_map/ppermute | solution.py:346
  131.3 3.2 %collective-permute-start.4 = (bf16[192,3,192]{0,2,1:T(8,128)(2,1)S(1)}, bf16[192,3,192]{0,2,1:T(8,128)(2,1)S(1)}, u32[]{:S(2)}, u32[]{:S(2)}) collective-permute-start(bf16[192,3,192]{0,2,1:T(8,128)(2,1)S(1)} %get-tuple-element.29), channel_id=1, source_target_pairs={{0,128},{128,0},{1,129},{129,1},{2,130},{130,2},{3,131},{131,3},{4... | collective-permute-start | bytes 663560 | tf_op jit(solution)/shard_map/ppermute | solution.py:372

commit v6 on v5

--- a/solution.py
+++ b/solution.py
@@ -216,12 +216,7 @@
     return jax.nn.gelu(layer_two + jnp.tile(merge_bias, 4), approximate=True).astype(jnp.bfloat16)
 
 
-def rim_above(extended):
-    return from_behind(extended[-1:], "tile", 1)
-
-
-def down_conv(upper_rim, extended, down_weight, down_bias):
-    stacked = jnp.concatenate([upper_rim, extended], axis=0)
+def down_conv(stacked, down_weight, down_bias):
     own_taps, upper_taps, left_taps, corner_taps = down_matrices(down_weight)
     summed = jnp.einsum(
         "rwk,kc->crw", stacked[1:, 1:], own_taps, preferred_element_type=jnp.float32
@@ -285,16 +280,17 @@
     full_rows = spectral_filter.shape[2]
     half_channels = channels // 2
     cell_half = field_cols // 2
-    image_part = lax.dynamic_slice_in_dim(
-        aerial_patch_grid, section_index * cell_half, cell_half, 1
-    )
+    tile_index = lax.axis_index("tile")
+    grid = jnp.pad(aerial_patch_grid, ((0, 0), (1, 0), (0, 0)))
+    own_part = lax.dynamic_slice_in_dim(grid, section_index * cell_half, cell_half + 1, 1)
+    image_part = jnp.concatenate([from_behind(own_part[-1:], "tile", 1), own_part], axis=0)
     layer_two = stem_layers(
         image_part, patch_conv_weight, patch_bias, merging_conv_weight, merge_bias
     )
-    left_column = from_behind(layer_two[:, -1:], "section", 1)
-    extended = jnp.concatenate([left_column, layer_two], axis=1)
-    upper_rim = rim_above(extended)
-    feature_half = down_conv(upper_rim, extended, down_weight, down_bias)
+    row_ok = (jnp.arange(layer_two.shape[0]) > 0) | (tile_index > 0)
+    col_ok = (jnp.arange(layer_two.shape[1]) > 0) | (section_index > 0)
+    stacked = jnp.where(row_ok[:, None, None] & col_ok[None, :, None], layer_two, 0)
+    feature_half = down_conv(stacked, down_weight, down_bias)
     normed_half = layer_norm(feature_half, norm_gain)
     tiles = lax.axis_size("tile")
     group_width, tile_rows = channels // tiles, normed_half.shape[1]

time: 137 us -> 116 us (0.85)
  local copies, waits for them, and re-layouts: 34 us -> 22.9 us
  starting transfers between devices: 12.4 us -> 7.86 us
  other arithmetic: 12.8 us -> 8.87 us
  matrix products: 26.9 us -> 24.4 us
    dot_general x2 -> x0, matrix products: 7.58 us -> none  [the longest x1 5.05 us: stem_layers(): jnp.einsum('zji,if->zjf', aerial_patch_grid, patch_kernel_matrix(patch_co...]
    dot_general x1, matrix products: 4.26 us -> 7.9 us  [stem_layers(): jnp.einsum('zji,if->zjf', initial_layer, merging_kernel_matrix(merging_co...]
    dot_general x1 -> x2, matrix products: 3.48 us -> 6.02 us  [spread_kernel(): full = jnp.dot(picked, repeat, preferred_element_type=jnp.float32)]
    another operation x1, local copies, waits for them, and re-layouts: 2.24 us -> 0.14 us  [arrange(): jnp.stack(entries[1], axis=0)]
    unnamed x43 -> x37, local copies, waits for them, and re-layouts: 8.22 us -> 6.13 us
    convert_element_type x2, local copies, waits for them, and re-layouts: 3.81 us -> 1.79 us  [local(): rows_back.astype(jnp.float32)]
    ppermute x1, starting transfers between devices: 3.65 us -> 1.73 us  [local(): other_fields = lax.ppermute(fields, 'section', swap)]
    ppermute x2 -> x1, starting transfers between devices: 6.37 us -> 5.08 us  [from_behind(): return lax.ppermute(block, axis, route)]
  transfers between devices with their start and end apart: 5 -> 4, of which waited for: 2 -> 2; matrix products, arithmetic and copies ran while one was open for 13% -> 14% of each run, Pallas kernels for 0% -> 0%
where the time goes in v6:
time: 116 us; the launch traced here: 115 us
  Pallas kernels  47.5 us (41%)
  matrix products  24.4 us (21%)
  local copies, waits for them, and re-layouts  22.9 us (20%)
  other arithmetic  8.87 us (8%)
  starting transfers between devices  7.86 us (7%)
  waiting for transfers between devices  3.14 us (3%)
    pallas_call x1, Pallas kernels, exchange_with_tables(): pl.pallas_call(exchange_tables_kernel, out_shape=(jax.ShapeDtypeStruct(ch...  25.6 us
    pallas_call x1, Pallas kernels, exchange(): pl.pallas_call(exchange_kernel, out_shape=jax.ShapeDtypeStruct(chunks.sha...  21.9 us
    dot_general x1, matrix products, stem_layers(): jnp.einsum('zji,if->zjf', initial_layer, merging_kernel_matrix(merging_co...  7.9 us
    unnamed x37, local copies, waits for them, and re-layouts  6.13 us
    dot_general x2, matrix products, spread_kernel(): full = jnp.dot(picked, repeat, preferred_element_type=jnp.float32)  6.02 us
    ppermute x1, starting transfers between devices, from_behind(): return lax.ppermute(block, axis, route)  5.08 us
    dot_general x1, matrix products, filter_columns(): jnp.einsum('puqh,chqw->cpuw', forward_h, row_spectrum, preferred_element_...  3.24 us
    another operation x1, other arithmetic, local(): jnp.stack([jnp.stack([cos_h, sin_h], axis=1), jnp.stack([-sin_h, cos_h],...  2.71 us
  transfers between devices with their start and end apart: 4, of which 2 were waited for; matrix products, arithmetic and copies ran while one was open for 14% of the time, Pallas kernels for 0%

profile of v6, /device:TPU:1, one launch (start us, length us, event | category | flops | bytes accessed | tf_op | source)
XLA Modules:
  0.0 115.1 jit_solution(13208668556328211923)
XLA Ops:
  0.0 1.9 %pad_dynamic-slice_fusion = bf16[1,193,768]{2,1,0:T(8,128)(2,1)} fusion(s32[]{:T(128)S(6)} %add.329, s32[]{:T(128)S(6)} %select_n.200, bf16[3,384,768]{2,1,0:T(8,128)(2,1)} %param.9), kind=kLoop, calls=%fused_computation.27 | loop fusion | bytes 2065928 | tf_op jit(solution)/shard_map/slice | solution.py:286
  1.9 5.1 %collective-permute-start = (bf16[1,193,768]{2,1,0:T(8,128)(2,1)}, bf16[1,193,768]{2,1,0:T(8,128)(2,1)}, u32[]{:S(2)}, u32[]{:S(2)}) collective-permute-start(bf16[1,193,768]{2,1,0:T(8,128)(2,1)} %pad_dynamic-slice_fusion), channel_id=1, source_target_pairs={{0,1},{1,2},{2,3},{3,4},{4,5},{5,6},{6,7},{7,8},{8,9},{9,10},{10,1... | collective-permute-start | bytes 889352 | tf_op jit(solution)/shard_map/ppermute | solution.py:130
  7.0 1.2 %pad_dynamic-slice_fusion.1 = bf16[3,193,768]{2,1,0:T(8,128)(2,1)} fusion(s32[]{:T(128)S(6)} %select_n.200, bf16[3,384,768]{2,1,0:T(8,128)(2,1)S(1)} %copy-done.1), kind=kLoop, calls=%fused_computation.28 | loop fusion | bytes 2658820 | tf_op jit(solution)/shard_map/dynamic_slice | solution.py:285
  8.6 0.9 pad_maximum_fusion.4
  9.7 0.6 copy-done.6
  10.3 0.5 constant_dynamic-slice_fusion
  10.8 2.8 %fusion.8 = bf16[768,1536,1]{1,0,2:T(8,128)(2,1)} fusion(s32[1536]{0:T(1024)S(1)} %get-tuple-element.51, s32[768]{0:T(1024)S(1)} %get-tuple-element.46, bf16[48,96]{1,0:T(8,128)(2,1)S(1)} %bitcast.174, s32[1536]{0:T(1024)S(1)} %get-tuple-element.50, s32[768]{0:T(1024)S(1)} %get-tuple-element.47), kind=kOutput, calls=%fused_computation.12 | convolution fusion | flops 237367296 | bytes 2386944 | tf_op jit(solution)/shard_map/dot_general | solution.py:151
  13.8 0.9 stack.131
  15.0 1.0 copy.63
  16.0 3.2 %fusion.9 = bf16[1536,768,1]{1,0,2:T(8,128)(2,1)} fusion(s32[768]{0:T(1024)S(1)} %get-tuple-element.45, s32[1536]{0:T(1024)S(1)} %get-tuple-element.48, bf16[384,192]{1,0:T(8,128)(2,1)S(1)} %bitcast.159, s32[1536]{0:T(1024)S(1)} %get-tuple-element.49, s32[768]{0:T(1024)S(1)} %get-tuple-element.44), kind=kOutput, calls=%fused_computation.13 | convolution fusion | flops 684048384 | bytes 2525184 | tf_op jit(solution)/shard_map/dot_general | solution.py:151
  19.2 7.9 %fusion.26 = bf16[4,193,768]{2,1,0:T(8,128)(2,1)S(1)} fusion(bf16[1536,768,1]{1,0,2:T(8,128)(2,1)} %fusion.9, f32[768]{0:T(1024)S(1)} %add.310, pred[4,193]{1,0:T(4,128)(4,1)S(1)} %broadcast_and_fusion, bf16[768,1536,1]{1,0,2:T(8,128)(2,1)} %fusion.8, f32[1536]{0:T(1024)S(1)} %add.297, bf16[3,193,768]{2,1,0:T(8,128)(2,1)} %pad_dynamic-slice_fusion.1, ...), kind=kOutput, calls=%fused_computation.45 | convolution fusion | flops 3661725696 | bytes 7100164 | tf_op jit(solution)/shard_map/zji,if->zjf/dot_general | solution.py:210
  27.1 1.7 %fusion.50 = f32[384,3,192]{0,2,1:T(8,128)S(1)} fusion(bf16[768,384,1]{1,0,2:T(8,128)(2,1)} %bitcast.172, bf16[4,193,768]{2,1,0:T(8,128)(2,1)S(1)} %fusion.26), kind=kOutput, calls=%fused_computation.74 | convolution fusion | flops 339738624 | bytes 2359296 | tf_op jit(solution)/shard_map/rwk,kc->crw/dot_general | solution.py:221
  28.8 0.6 convolution_add_fusion.2
  29.5 0.6 convolution_add_fusion.1
  30.1 0.4 copy-done.9
  30.5 0.7 convert_reduce_fusion
  31.3 0.4 fusion.41
  31.7 0.4 fusion.40
  32.1 0.9 copy.27
  33.0 0.5 reshape.335
  33.5 0.9 copy.64
  34.5 25.6 %shard_map.91 = (bf16[128,16,128]{2,1,0:T(8,128)(2,1)}, bf16[384,384]{1,0:T(8,128)(2,1)}, bf16[384,384]{1,0:T(8,128)(2,1)}) custom-call(bf16[128,16,128]{2,1,0:T(8,128)(2,1)} %bitcast.165), custom_call_target="tpu_custom_call" | custom-call | tf_op jit(solution)/shard_map/pallas_call | solution.py:95
  60.1 1.7 %fusion.79 = (bf16[1,384,192]{2,1,0:T(8,128)(2,1)S(1)}, bf16[384,1,192]{2,0,1:T(8,128)(2,1)}) fusion(bf16[384,384]{1,0:T(8,128)(2,1)} %get-tuple-element.10, s32[]{:T(128)S(6)} %select_n.222), kind=kLoop, calls=%fused_computation.128 | loop fusion | flops 221184 | bytes 442372 | tf_op jit(solution)/shard_map/stack | solution.py:315
  61.8 1.7 %negate_bitcast_fusion = bf16[384,1,384]{2,0,1:T(8,128)(2,1)} fusion(bf16[384,384]{1,0:T(8,128)(2,1)} %get-tuple-element.10), kind=kLoop, calls=%fused_computation.112 | loop fusion | flops 147456 | bytes 589824 | tf_op jit(solution)/shard_map/stack | solution.py:317
  63.5 1.5 %copy.53 = bf16[128,16,128]{0,2,1:T(8,128)(2,1)S(1)} copy(bf16[128,16,128]{2,1,0:T(8,128)(2,1)} %get-tuple-element.8) | data formatting | bytes 1048576 | tf_op jit(solution)/shard_map/reshape | solution.py:117
  65.0 0.7 copy.29
  65.8 0.5 reshape.339
  66.3 1.1 dynamic-slice_bitcast_fusion
  67.4 1.0 copy.32
  68.4 1.7 %collective-permute-start.1 = (bf16[3,384,192]{1,2,0:T(8,128)(2,1)}, bf16[3,384,192]{1,2,0:T(8,128)(2,1)S(1)}, u32[]{:S(2)}, u32[]{:S(2)}) collective-permute-start(bf16[3,384,192]{1,2,0:T(8,128)(2,1)} %copy.32), channel_id=1, source_target_pairs={{0,128},{128,0},{1,129},{129,1},{2,130},{130,2},{3,131},{131,3},{4... | collective-permute-start | bytes 1327112 | tf_op jit(solution)/shard_map/ppermute | solution.py:306
  70.2 2.7 %fusion.56 = (bf16[1,384,2,384]{3,1,2,0:T(8,128)(2,1)}, bf16[1,384,2,384]{3,1,2,0:T(8,128)(2,1)}, bf16[1,384,2,384]{3,1,2,0:T(8,128)(2,1)}, bf16[1,384,2,384]{3,1,2,0:T(8,128)(2,1)}) fusion(bf16[384,1,384]{2,0,1:T(8,128)(2,1)} %bitcast.171, bf16[384,1,384]{2,0,1:T(8,128)(2,1)S(1)} %bitcast.163, bf16[384,1,384]{2,0,1:T(8,128)(2,1)} %negate_bitcast_fusion), kind=kLoop, calls=%fused_computation.87 | loop fusion | flops 1179648 | bytes 3244032 | tf_op jit(solution)/shard_map/stack | solution.py:316
  72.9 1.7 %fusion.58 = f32[3,384,2,192]{1,3,2,0:T(8,128)} fusion(bf16[3,384,192]{2,1,0:T(8,128)(2,1)S(1)} %reshape.339, s32[]{:T(128)S(6)} %select_n.222, bf16[384,1,192]{2,0,1:T(8,128)(2,1)S(1)} %get-tuple-element.33, bf16[384,1,192]{2,0,1:T(8,128)(2,1)S(1)} %copy-done.5), kind=kOutput, calls=%fused_computation.92 | convolution fusion | flops 170164224 | bytes 2506756 | tf_op jit(solution)/shard_map/chx,xqw->chqw/dot_general | solution.py:328
  74.6 0.8 copy-done.13
  75.4 3.2 %fusion.20 = bf16[3,2,384,192]{2,3,1,0:T(8,128)(2,1)S(1)} fusion(bf16[1,384,2,384]{3,1,2,0:T(8,128)(2,1)} %get-tuple-element.35, bf16[1,384,2,384]{3,1,2,0:T(8,128)(2,1)} %get-tuple-element.24, f32[3,384,2,192]{1,3,2,0:T(8,128)} %fusion.58, bf16[3,384,192]{1,2,0:T(8,128)(2,1)} %copy-done.13, s32[]{:T(128)S(6)} %select_n.223, ...), kind=kOutput, calls=%fused_computation.37 | convolution fusion | flops 853327872 | bytes 4571140 | tf_op jit(solution)/shard_map/puqh,chqw->cpuw/dot_general | solution.py:247
  79.0 0.7 copy-done.7
  79.9 0.9 fusion.21
  80.9 0.5 convolution_bitcast_fusion.1
  81.4 1.9 %collective-permute-done.2 = bf16[3,384,2,192]{1,3,2,0:T(8,128)(2,1)S(1)} collective-permute-done((bf16[3,384,2,192]{1,3,2,0:T(8,128)(2,1)S(1)}, bf16[3,384,2,192]{1,3,2,0:T(8,128)(2,1)S(1)}, u32[]{:S(2)}, u32[]{:S(2)}) %collective-permute-start.2) | collective-permute-done | bytes 884768 | tf_op jit(solution)/shard_map/ppermute | solution.py:342
  83.3 0.5 fusion.24
  84.4 0.8 copy.37
  85.2 1.2 %copy.60.x_ref = bf16[128,16,128]{2,1,0:T(8,128)(2,1)} copy(bf16[128,16,128]{0,2,1:T(8,128)(2,1)S(1)} %bitcast.164) | data formatting | bytes 1048576 | tf_op jit(solution)/shard_map/reshape | solution.py:123
  86.5 21.9 %shard_map.92 = bf16[128,16,128]{2,1,0:T(8,128)(2,1)} custom-call(bf16[128,16,128]{2,1,0:T(8,128)(2,1)} %copy.60.x_ref), custom_call_target="tpu_custom_call" | custom-call | tf_op jit(solution)/shard_map/pallas_call | solution.py:83
  108.3 1.2 %copy.67 = bf16[16,8,16,128]{3,1,2,0:T(8,128)(2,1)S(1)} copy(bf16[16,8,16,128]{3,2,1,0:T(8,128)(2,1)} %bitcast.166) | data formatting | bytes 1048576
  109.6 0.9 reshape.344
  110.5 0.9 copy.39
  111.8 1.0 collective-permute-start.3
  112.7 1.2 %collective-permute-done.3 = bf16[192,3,192]{0,2,1:T(8,128)(2,1)S(1)} collective-permute-done((bf16[192,3,192]{0,2,1:T(8,128)(2,1)S(1)}, bf16[192,3,192]{0,2,1:T(8,128)(2,1)S(1)}, u32[]{:S(2)}, u32[]{:S(2)}) %collective-permute-start.3) | collective-permute-done | bytes 221216 | tf_op jit(solution)/shard_map/ppermute | solution.py:368
  114.2 1.0 copy.40
  (61 shorter events, 3.1 us)
Async XLA Ops:
  0.0 16.0 %copy-start = (bf16[2,2,96,192]{3,2,1,0:T(8,128)(2,1)S(1)}, bf16[2,2,96,192]{3,2,1,0:T(8,128)(2,1)}, u32[]{:S(2)}) copy-start(bf16[2,2,96,192]{3,2,1,0:T(8,128)(2,1)} %param.12) | copy-start | bytes 442372
  0.0 7.0 %copy-start.1 = (bf16[3,384,768]{2,1,0:T(8,128)(2,1)S(1)}, bf16[3,384,768]{2,1,0:T(8,128)(2,1)}, u32[]{:S(2)}) copy-start(bf16[3,384,768]{2,1,0:T(8,128)(2,1)} %param.9) | copy-start | bytes 5308420
  0.0 8.3 %copy-start.4 = (bf16[3,3,192,384]{3,2,1,0:T(8,128)(2,1)S(1)}, bf16[3,3,192,384]{3,2,1,0:T(8,128)(2,1)}, u32[]{:S(2)}) copy-start(bf16[3,3,192,384]{3,2,1,0:T(8,128)(2,1)} %param.14) | copy-start | bytes 3981316
  1.9 17.3 %collective-permute-start = (bf16[1,193,768]{2,1,0:T(8,128)(2,1)}, bf16[1,193,768]{2,1,0:T(8,128)(2,1)}, u32[]{:S(2)}, u32[]{:S(2)}) collective-permute-start(bf16[1,193,768]{2,1,0:T(8,128)(2,1)} %pad_dynamic-slice_fusion), channel_id=1, source_target_pairs={{0,1},{1,2},{2,3},{3,4},{4,5},{5,6},{6,7},{7,8},{8,9},{9,10},{10,1... | collective-permute-start | bytes 889352 | tf_op jit(solution)/shard_map/ppermute | solution.py:130
  8.6 1.7 %copy-start.6 = (bf16[3,2,384,384]{3,2,1,0:T(8,128)(2,1)S(1)}, bf16[3,2,384,384]{3,2,1,0:T(8,128)(2,1)}, u32[]{:S(2)}) copy-start(bf16[3,2,384,384]{3,2,1,0:T(8,128)(2,1)} %param.17) | copy-start | bytes 5308420
  9.5 1.3 %copy-start.14 = (bf16[3,4,4,96]{3,2,1,0:T(4,128)(2,1)S(1)}, bf16[3,4,4,96]{3,2,1,0:T(4,128)(2,1)}, u32[]{:S(2)}) copy-start(bf16[3,4,4,96]{3,2,1,0:T(4,128)(2,1)} %param.10) | copy-start | bytes 27652
  10.8 2.8 %copy-start.12 = (f32[96]{0:T(128)S(1)}, f32[96]{0:T(128)}, u32[]{:S(2)}) copy-start(f32[96]{0:T(128)} %param.11) | copy-start | bytes 1156
  10.8 2.9 %copy-start.11 = (f32[192]{0:T(256)S(1)}, f32[192]{0:T(256)}, u32[]{:S(2)}) copy-start(f32[192]{0:T(256)} %param.13) | copy-start | bytes 2308
  29.5 1.1 copy-start.9
  29.5 1.1 copy-start.15
  30.1 1.6 %copy-start.10 = (f32[384]{0:T(512)S(1)}, f32[384]{0:T(512)}, u32[]{:S(2)}) copy-start(f32[384]{0:T(512)} %param.16) | copy-start | bytes 4612
  65.0 5.2 %copy-start.2 = (bf16[384,384]{1,0:T(8,128)(2,1)S(1)}, bf16[384,384]{1,0:T(8,128)(2,1)}, u32[]{:S(2)}) copy-start(bf16[384,384]{1,0:T(8,128)(2,1)} %get-tuple-element.10) | copy-start | bytes 884740
  66.3 6.6 %copy-start.5 = (bf16[384,1,192]{2,0,1:T(8,128)(2,1)S(1)}, bf16[384,1,192]{2,0,1:T(8,128)(2,1)}, u32[]{:S(2)}) copy-start(bf16[384,1,192]{2,0,1:T(8,128)(2,1)} %get-tuple-element.31) | copy-start | bytes 442372
  68.4 6.2 %collective-permute-start.1 = (bf16[3,384,192]{1,2,0:T(8,128)(2,1)}, bf16[3,384,192]{1,2,0:T(8,128)(2,1)S(1)}, u32[]{:S(2)}, u32[]{:S(2)}) collective-permute-start(bf16[3,384,192]{1,2,0:T(8,128)(2,1)} %copy.32), channel_id=1, source_target_pairs={{0,128},{128,0},{1,129},{129,1},{2,130},{130,2},{3,131},{131,3},{4... | collective-permute-start | bytes 1327112 | tf_op jit(solution)/shard_map/ppermute | solution.py:306
  74.6 0.8 copy-start.13
  75.4 3.2 %copy-start.3 = (bf16[3,1,384,192]{2,3,1,0:T(8,128)(2,1)S(1)}, bf16[3,1,384,192]{2,3,1,0:T(8,128)(2,1)}, u32[]{:S(2)}) copy-start(bf16[3,1,384,192]{2,3,1,0:T(8,128)(2,1)} %copy.63) | copy-start | bytes 1327108
  78.6 1.1 copy-start.7
  78.7 1.2 %copy-start.8 = (bf16[1,384,2,384]{3,1,2,0:T(8,128)(2,1)S(1)}, bf16[1,384,2,384]{3,1,2,0:T(8,128)(2,1)}, u32[]{:S(2)}) copy-start(bf16[1,384,2,384]{3,1,2,0:T(8,128)(2,1)} %get-tuple-element.34) | copy-start | bytes 1769476
  80.8 2.5 %collective-permute-start.2 = (bf16[3,384,2,192]{1,3,2,0:T(8,128)(2,1)S(1)}, bf16[3,384,2,192]{1,3,2,0:T(8,128)(2,1)S(1)}, u32[]{:S(2)}, u32[]{:S(2)}) collective-permute-start(bf16[3,384,2,192]{1,3,2,0:T(8,128)(2,1)S(1)} %fusion.21), channel_id=1, source_target_pairs={{0,128},{128,0},{1,129},{129,1},{2,130},{130,2},{3,131},{131,3},{4... | collective-permute-start | bytes 2654216 | tf_op jit(solution)/shard_map/ppermute | solution.py:342
  111.8 2.2 %collective-permute-start.3 = (bf16[192,3,192]{0,2,1:T(8,128)(2,1)S(1)}, bf16[192,3,192]{0,2,1:T(8,128)(2,1)S(1)}, u32[]{:S(2)}, u32[]{:S(2)}) collective-permute-start(bf16[192,3,192]{0,2,1:T(8,128)(2,1)S(1)} %get-tuple-element.29), channel_id=1, source_target_pairs={{0,128},{128,0},{1,129},{129,1},{2,130},{130,2},{3,131},{131,3},{4... | collective-permute-start | bytes 663560 | tf_op jit(solution)/shard_map/ppermute | solution.py:368

commit v7 on v6

--- a/solution.py
+++ b/solution.py
@@ -283,7 +283,12 @@
     tile_index = lax.axis_index("tile")
     grid = jnp.pad(aerial_patch_grid, ((0, 0), (1, 0), (0, 0)))
     own_part = lax.dynamic_slice_in_dim(grid, section_index * cell_half, cell_half + 1, 1)
-    image_part = jnp.concatenate([from_behind(own_part[-1:], "tile", 1), own_part], axis=0)
+    band_count = patch_conv_weight.shape[0]
+    patch_halves = own_part[-1:].reshape(1, cell_half + 1, band_count, 2, -1)
+    lower_half = patch_halves[:, :, :, 1].reshape(1, cell_half + 1, -1)
+    lower_half = from_behind(lower_half, "tile", 1).reshape(patch_halves[:, :, :, 1:].shape)
+    rim = jnp.concatenate([jnp.zeros_like(lower_half), lower_half], axis=3)
+    image_part = jnp.concatenate([rim.reshape(own_part[-1:].shape), own_part], axis=0)
     layer_two = stem_layers(
         image_part, patch_conv_weight, patch_bias, merging_conv_weight, merge_bias
     )

time: 116 us -> 125 us (1.078)
  local copies, waits for them, and re-layouts: 22.9 us -> 31.6 us
    reshape x0 -> x3, local copies, waits for them, and re-layouts: none -> 2.06 us  [the longest x1 1.25 us: local(): from_behind(lower_half, 'tile', 1).reshape(patch_halves[:, :, :, 1:].shape)]
    unnamed x37 -> x43, local copies, waits for them, and re-layouts: 6.13 us -> 8.02 us
    another operation x1, other arithmetic: 0.33 us -> 1.71 us
  transfers between devices with their start and end apart: 4 -> 4, of which waited for: 2 -> 2; matrix products, arithmetic and copies ran while one was open for 14% -> 18% of each run, Pallas kernels for 0% -> 0%
where the time goes in v7:
time: 125 us
  Pallas kernels  47.5 us (38%)
  local copies, waits for them, and re-layouts  31.6 us (25%)
  matrix products  24.4 us (20%)
  other arithmetic  9.91 us (8%)
  starting transfers between devices  7.77 us (6%)
  waiting for transfers between devices  3.11 us (2%)
    pallas_call x1, Pallas kernels, exchange_with_tables(): pl.pallas_call(exchange_tables_kernel, out_shape=(jax.ShapeDtypeStruct(ch...  25.7 us
    pallas_call x1, Pallas kernels, exchange(): pl.pallas_call(exchange_kernel, out_shape=jax.ShapeDtypeStruct(chunks.sha...  21.9 us
    unnamed x43, local copies, waits for them, and re-layouts  8.02 us
    dot_general x1, matrix products, stem_layers(): jnp.einsum('zji,if->zjf', initial_layer, merging_kernel_matrix(merging_co...  7.79 us
    dot_general x2, matrix products, spread_kernel(): full = jnp.dot(picked, repeat, preferred_element_type=jnp.float32)  6.02 us
    ppermute x1, starting transfers between devices, from_behind(): return lax.ppermute(block, axis, route)  5.02 us
    dot_general x1, matrix products, filter_columns(): jnp.einsum('puqh,chqw->cpuw', forward_h, row_spectrum, preferred_element_...  3.72 us
    another operation x1, other arithmetic, local(): jnp.stack([jnp.stack([cos_h, sin_h], axis=1), jnp.stack([-sin_h, cos_h],...  2.55 us
  transfers between devices with their start and end apart: 4, of which 2 were waited for; matrix products, arithmetic and copies ran while one was open for 18% of the time, Pallas kernels for 0%

profile of v7, /device:TPU:1, one launch (start us, length us, event | category | flops | bytes accessed | tf_op | source)
XLA Modules:
  0.0 124.8 jit_solution(2736560554033768045)
XLA Ops:
  0.0 1.2 pad_dynamic-slice_fusion
  1.5 1.0 slice_reduce_fusion
  2.4 0.8 reshape_squeeze.3
  3.2 5.0 %collective-permute-start = (bf16[1,193,384]{2,1,0:T(8,128)(2,1)}, bf16[1,193,384]{2,1,0:T(8,128)(2,1)}, u32[]{:S(2)}, u32[]{:S(2)}) collective-permute-start(bf16[1,193,384]{2,1,0:T(8,128)(2,1)} %reshape_squeeze.3), channel_id=1, source_target_pairs={{0,1},{1,2},{2,3},{3,4},{4,5},{5,6},{6,7},{7,8},{8,9},{9,10},{10,1... | collective-permute-start | bytes 444680 | tf_op jit(solution)/shard_map/ppermute | solution.py:130
  8.4 0.9 slice_bitcast_fusion
  9.4 0.9 pad_maximum_fusion.4
  10.9 1.5 %constant_dynamic-slice_fusion = (bf16[3,1,384,192]{3,2,1,0:T(8,128)(2,1)}, bf16[3,1,384,192]{3,2,1,0:T(8,128)(2,1)}) fusion(bf16[3,2,384,384]{3,2,1,0:T(8,128)(2,1)S(1)} %copy-done.6, s32[]{:T(128)S(6)} %select_n.222, s32[]{:T(128)S(6)} %add.333), kind=kLoop, calls=%fused_computation.236 | loop fusion | bytes 1769480 | tf_op jit(solution)/shard_map/slice | solution.py:252
  12.4 2.8 %fusion.8 = bf16[768,1536,1]{1,0,2:T(8,128)(2,1)} fusion(s32[1536]{0:T(1024)S(1)} %get-tuple-element.51, s32[768]{0:T(1024)S(1)} %get-tuple-element.46, bf16[48,96]{1,0:T(8,128)(2,1)S(1)} %bitcast.174, s32[1536]{0:T(1024)S(1)} %get-tuple-element.50, s32[768]{0:T(1024)S(1)} %get-tuple-element.47), kind=kOutput, calls=%fused_computation.12 | convolution fusion | flops 237367296 | bytes 2386944 | tf_op jit(solution)/shard_map/dot_general | solution.py:151
  15.3 3.2 %fusion.9 = bf16[1536,768,1]{1,0,2:T(8,128)(2,1)} fusion(s32[768]{0:T(1024)S(1)} %get-tuple-element.45, s32[1536]{0:T(1024)S(1)} %get-tuple-element.48, bf16[384,192]{1,0:T(8,128)(2,1)S(1)} %bitcast.159, s32[1536]{0:T(1024)S(1)} %get-tuple-element.49, s32[768]{0:T(1024)S(1)} %get-tuple-element.44), kind=kOutput, calls=%fused_computation.13 | convolution fusion | flops 684048384 | bytes 2525184 | tf_op jit(solution)/shard_map/dot_general | solution.py:151
  18.5 0.8 maximum_bitcast_fusion.8
  19.4 1.0 stack.123
  20.5 0.9 stack.131
  21.3 2.1 %copy.67 = bf16[3,1,384,192]{2,3,1,0:T(8,128)(2,1)} copy(bf16[3,1,384,192]{3,2,1,0:T(8,128)(2,1)} %get-tuple-element.13) | data formatting | bytes 884736
  23.4 2.0 %copy.68 = bf16[3,1,384,192]{2,3,1,0:T(8,128)(2,1)} copy(bf16[3,1,384,192]{3,2,1,0:T(8,128)(2,1)} %get-tuple-element.14) | data formatting | bytes 884736
  25.5 1.2 pad_dynamic-slice_fusion.1
  26.6 1.3 %reshape.378 = bf16[1,193,3,1,128]{4,3,2,1,0:T(2,128)(2,1)S(1)} reshape(bf16[1,193,384]{2,1,0:T(8,128)(2,1)} %collective-permute-done) | data formatting | bytes 296448 | tf_op jit(solution)/shard_map/reshape | solution.py:289
  28.8 7.8 %fusion.26 = bf16[4,193,768]{2,1,0:T(8,128)(2,1)S(1)} fusion(bf16[1536,768,1]{1,0,2:T(8,128)(2,1)} %fusion.9, f32[768]{0:T(1024)S(1)} %add.312, pred[4,193]{1,0:T(4,128)(4,1)S(1)} %broadcast_and_fusion, bf16[768,1536,1]{1,0,2:T(8,128)(2,1)} %fusion.8, f32[1536]{0:T(1024)S(1)} %add.299, bf16[3,193,768]{2,1,0:T(8,128)(2,1)} %pad_dynamic-slice_fusion.1, ...), kind=kOutput, calls=%fused_computation.45 | convolution fusion | flops 3661725696 | bytes 7100164 | tf_op jit(solution)/shard_map/zji,if->zjf/dot_general | solution.py:210
  36.6 1.7 %fusion.50 = f32[384,3,192]{0,2,1:T(8,128)S(1)} fusion(bf16[768,384,1]{1,0,2:T(8,128)(2,1)} %bitcast.172, bf16[4,193,768]{2,1,0:T(8,128)(2,1)S(1)} %fusion.26), kind=kOutput, calls=%fused_computation.74 | convolution fusion | flops 339738624 | bytes 2359296 | tf_op jit(solution)/shard_map/rwk,kc->crw/dot_general | solution.py:221
  38.3 0.6 convolution_add_fusion.2
  39.0 0.6 convolution_add_fusion.1
  40.0 0.7 convert_reduce_fusion
  41.4 0.9 copy.31
  42.8 0.9 copy.70
  43.7 25.7 %shard_map.91 = (bf16[128,16,128]{2,1,0:T(8,128)(2,1)}, bf16[384,384]{1,0:T(8,128)(2,1)}, bf16[384,384]{1,0:T(8,128)(2,1)}) custom-call(bf16[128,16,128]{2,1,0:T(8,128)(2,1)} %bitcast.165), custom_call_target="tpu_custom_call" | custom-call | tf_op jit(solution)/shard_map/pallas_call | solution.py:95
  69.4 1.7 %fusion.79 = (bf16[1,384,192]{2,1,0:T(8,128)(2,1)S(1)}, bf16[384,1,192]{2,0,1:T(8,128)(2,1)}) fusion(bf16[384,384]{1,0:T(8,128)(2,1)} %get-tuple-element.10, s32[]{:T(128)S(6)} %select_n.222), kind=kLoop, calls=%fused_computation.129 | loop fusion | flops 221184 | bytes 442372 | tf_op jit(solution)/shard_map/stack | solution.py:320
  71.1 1.0 negate_bitcast_fusion
  72.1 1.5 %copy.57 = bf16[128,16,128]{0,2,1:T(8,128)(2,1)S(1)} copy(bf16[128,16,128]{2,1,0:T(8,128)(2,1)} %get-tuple-element.8) | data formatting | bytes 1048576 | tf_op jit(solution)/shard_map/reshape | solution.py:117
  73.6 0.7 copy.33
  74.4 0.5 reshape.351
  74.9 1.7 %dynamic-slice_bitcast_fusion = (bf16[1,384,192]{2,1,0:T(8,128)(2,1)S(1)}, bf16[384,1,192]{2,0,1:T(8,128)(2,1)}) fusion(bf16[384,384]{1,0:T(8,128)(2,1)} %get-tuple-element.9, s32[]{:T(128)S(6)} %select_n.222), kind=kLoop, calls=%fused_computation.127 | loop fusion | bytes 442372 | tf_op jit(solution)/shard_map/stack | solution.py:320
  76.7 1.0 copy.36
  77.7 1.7 %collective-permute-start.1 = (bf16[3,384,192]{1,2,0:T(8,128)(2,1)}, bf16[3,384,192]{1,2,0:T(8,128)(2,1)S(1)}, u32[]{:S(2)}, u32[]{:S(2)}) collective-permute-start(bf16[3,384,192]{1,2,0:T(8,128)(2,1)} %copy.36), channel_id=1, source_target_pairs={{0,128},{128,0},{1,129},{129,1},{2,130},{130,2},{3,131},{131,3},{4... | collective-permute-start | bytes 1327112 | tf_op jit(solution)/shard_map/ppermute | solution.py:311
  79.3 2.6 %fusion.56 = (bf16[1,384,2,384]{3,1,2,0:T(8,128)(2,1)}, bf16[1,384,2,384]{3,1,2,0:T(8,128)(2,1)}, bf16[1,384,2,384]{3,1,2,0:T(8,128)(2,1)}, bf16[1,384,2,384]{3,1,2,0:T(8,128)(2,1)}) fusion(bf16[384,1,384]{2,0,1:T(8,128)(2,1)} %bitcast.171, bf16[384,1,384]{2,0,1:T(8,128)(2,1)S(1)} %bitcast.163, bf16[384,1,384]{2,0,1:T(8,128)(2,1)S(1)} %negate_bitcast_fusion), kind=kLoop, calls=%fused_computation.87 | loop fusion | flops 1179648 | bytes 3244032 | tf_op jit(solution)/shard_map/stack | solution.py:321
  81.9 1.4 %fusion.58 = f32[3,384,2,192]{1,3,2,0:T(8,128)S(1)} fusion(bf16[3,384,192]{2,1,0:T(8,128)(2,1)S(1)} %reshape.351, s32[]{:T(128)S(6)} %select_n.222, bf16[384,1,192]{2,0,1:T(8,128)(2,1)S(1)} %copy-done.5, bf16[384,1,192]{2,0,1:T(8,128)(2,1)} %get-tuple-element.31), kind=kOutput, calls=%fused_computation.92 | convolution fusion | flops 170164224 | bytes 2506756 | tf_op jit(solution)/shard_map/chx,xqw->chqw/dot_general | solution.py:333
  83.3 0.8 copy-done.16
  84.1 3.7 %fusion.20 = bf16[3,2,384,192]{2,3,1,0:T(8,128)(2,1)} fusion(bf16[1,384,2,384]{3,1,2,0:T(8,128)(2,1)} %get-tuple-element.35, bf16[1,384,2,384]{3,1,2,0:T(8,128)(2,1)} %get-tuple-element.24, f32[3,384,2,192]{1,3,2,0:T(8,128)S(1)} %fusion.58, bf16[3,384,192]{1,2,0:T(8,128)(2,1)} %copy-done.16, s32[]{:T(128)S(6)} %select_n.223, ...), kind=kOutput, calls=%fused_computation.37 | convolution fusion | flops 853327872 | bytes 4571140 | tf_op jit(solution)/shard_map/puqh,chqw->cpuw/dot_general | solution.py:247
  87.8 1.7 %fusion.43 = (bf16[3,1,384,192]{2,3,1,0:T(8,128)(2,1)S(1)}, bf16[3,1,384,192]{2,3,1,0:T(8,128)(2,1)S(1)}) fusion(bf16[3,1,384,192]{2,3,1,0:T(8,128)(2,1)S(1)} %copy-done.3, bf16[3,1,384,192]{2,3,1,0:T(8,128)(2,1)} %copy.68, bf16[3,2,384,192]{2,3,1,0:T(8,128)(2,1)} %fusion.20), kind=kLoop, calls=%fused_computation.67 | loop fusion | flops 2654208 | bytes 2654208 | tf_op jit(solution)/shard_map/convert.1
  89.5 0.9 fusion.21
  91.1 1.9 %collective-permute-done.2 = bf16[3,384,2,192]{1,3,2,0:T(8,128)(2,1)S(1)} collective-permute-done((bf16[3,384,2,192]{1,3,2,0:T(8,128)(2,1)S(1)}, bf16[3,384,2,192]{1,3,2,0:T(8,128)(2,1)S(1)}, u32[]{:S(2)}, u32[]{:S(2)}) %collective-permute-start.2) | collective-permute-done | bytes 884768 | tf_op jit(solution)/shard_map/ppermute | solution.py:347
  94.0 0.8 copy.41
  94.9 1.2 copy.64.x_ref
  96.1 21.9 %shard_map.92 = bf16[128,16,128]{2,1,0:T(8,128)(2,1)} custom-call(bf16[128,16,128]{2,1,0:T(8,128)(2,1)} %copy.64.x_ref), custom_call_target="tpu_custom_call" | custom-call | tf_op jit(solution)/shard_map/pallas_call | solution.py:83
  118.0 1.2 copy.73
  119.2 0.9 reshape.356
  120.2 0.9 copy.43
  121.4 0.9 collective-permute-start.3
  122.4 1.2 collective-permute-done.3
  123.8 1.0 copy.44
  (73 shorter events, 6.3 us)
Async XLA Ops:
  0.0 15.3 %copy-start = (bf16[2,2,96,192]{3,2,1,0:T(8,128)(2,1)S(1)}, bf16[2,2,96,192]{3,2,1,0:T(8,128)(2,1)}, u32[]{:S(2)}) copy-start(bf16[2,2,96,192]{3,2,1,0:T(8,128)(2,1)} %param.12) | copy-start | bytes 442372
  0.0 8.4 %copy-start.4 = (bf16[3,3,192,384]{3,2,1,0:T(8,128)(2,1)S(1)}, bf16[3,3,192,384]{3,2,1,0:T(8,128)(2,1)}, u32[]{:S(2)}) copy-start(bf16[3,3,192,384]{3,2,1,0:T(8,128)(2,1)} %param.14) | copy-start | bytes 3981316
  3.2 23.4 %collective-permute-start = (bf16[1,193,384]{2,1,0:T(8,128)(2,1)}, bf16[1,193,384]{2,1,0:T(8,128)(2,1)}, u32[]{:S(2)}, u32[]{:S(2)}) collective-permute-start(bf16[1,193,384]{2,1,0:T(8,128)(2,1)} %reshape_squeeze.3), channel_id=1, source_target_pairs={{0,1},{1,2},{2,3},{3,4},{4,5},{5,6},{6,7},{7,8},{8,9},{9,10},{10,1... | collective-permute-start | bytes 444680 | tf_op jit(solution)/shard_map/ppermute | solution.py:130
  9.2 1.7 %copy-start.6 = (bf16[3,2,384,384]{3,2,1,0:T(8,128)(2,1)S(1)}, bf16[3,2,384,384]{3,2,1,0:T(8,128)(2,1)}, u32[]{:S(2)}) copy-start(bf16[3,2,384,384]{3,2,1,0:T(8,128)(2,1)} %param.17) | copy-start | bytes 5308420
  10.3 2.2 %copy-start.17 = (bf16[3,4,4,96]{3,2,1,0:T(4,128)(2,1)S(1)}, bf16[3,4,4,96]{3,2,1,0:T(4,128)(2,1)}, u32[]{:S(2)}) copy-start(bf16[3,4,4,96]{3,2,1,0:T(4,128)(2,1)} %param.10) | copy-start | bytes 27652
  15.3 3.2 %copy-start.10 = (bf16[1,192,384]{2,1,0:T(8,128)(2,1)S(1)}, bf16[1,192,384]{2,1,0:T(8,128)(2,1)}, u32[]{:S(2)}) copy-start(bf16[1,192,384]{2,1,0:T(8,128)(2,1)} %get-tuple-element.15) | copy-start | bytes 442372
  15.3 3.2 %copy-start.11 = (bf16[1,192,384]{2,1,0:T(8,128)(2,1)S(1)}, bf16[1,192,384]{2,1,0:T(8,128)(2,1)}, u32[]{:S(2)}) copy-start(bf16[1,192,384]{2,1,0:T(8,128)(2,1)} %get-tuple-element.17) | copy-start | bytes 442372
  15.3 3.2 %copy-start.12 = (bf16[1,192,384]{2,1,0:T(8,128)(2,1)S(1)}, bf16[1,192,384]{2,1,0:T(8,128)(2,1)}, u32[]{:S(2)}) copy-start(bf16[1,192,384]{2,1,0:T(8,128)(2,1)} %get-tuple-element.18) | copy-start | bytes 442372
  15.3 4.0 %copy-start.15 = (f32[96]{0:T(128)S(1)}, f32[96]{0:T(128)}, u32[]{:S(2)}) copy-start(f32[96]{0:T(128)} %param.11) | copy-start | bytes 1156
  15.3 4.1 %copy-start.14 = (f32[192]{0:T(256)S(1)}, f32[192]{0:T(256)}, u32[]{:S(2)}) copy-start(f32[192]{0:T(256)} %param.13) | copy-start | bytes 2308
  18.5 7.0 %copy-start.1 = (bf16[3,384,768]{2,1,0:T(8,128)(2,1)S(1)}, bf16[3,384,768]{2,1,0:T(8,128)(2,1)}, u32[]{:S(2)}) copy-start(bf16[3,384,768]{2,1,0:T(8,128)(2,1)} %param.9) | copy-start | bytes 5308420
  38.9 1.1 copy-start.9
  38.9 1.1 copy-start.18
  39.6 1.6 %copy-start.13 = (f32[384]{0:T(512)S(1)}, f32[384]{0:T(512)}, u32[]{:S(2)}) copy-start(f32[384]{0:T(512)} %param.16) | copy-start | bytes 4612
  73.6 5.8 %copy-start.2 = (bf16[384,384]{1,0:T(8,128)(2,1)S(1)}, bf16[384,384]{1,0:T(8,128)(2,1)}, u32[]{:S(2)}) copy-start(bf16[384,384]{1,0:T(8,128)(2,1)} %get-tuple-element.10) | copy-start | bytes 884740
  77.7 4.2 %copy-start.5 = (bf16[384,1,192]{2,0,1:T(8,128)(2,1)S(1)}, bf16[384,1,192]{2,0,1:T(8,128)(2,1)}, u32[]{:S(2)}) copy-start(bf16[384,1,192]{2,0,1:T(8,128)(2,1)} %get-tuple-element.33) | copy-start | bytes 442372
  77.7 5.6 %collective-permute-start.1 = (bf16[3,384,192]{1,2,0:T(8,128)(2,1)}, bf16[3,384,192]{1,2,0:T(8,128)(2,1)S(1)}, u32[]{:S(2)}, u32[]{:S(2)}) collective-permute-start(bf16[3,384,192]{1,2,0:T(8,128)(2,1)} %copy.36), channel_id=1, source_target_pairs={{0,128},{128,0},{1,129},{129,1},{2,130},{130,2},{3,131},{131,3},{4... | collective-permute-start | bytes 1327112 | tf_op jit(solution)/shard_map/ppermute | solution.py:311
  83.3 0.8 copy-start.16
  84.1 3.7 %copy-start.3 = (bf16[3,1,384,192]{2,3,1,0:T(8,128)(2,1)S(1)}, bf16[3,1,384,192]{2,3,1,0:T(8,128)(2,1)}, u32[]{:S(2)}) copy-start(bf16[3,1,384,192]{2,3,1,0:T(8,128)(2,1)} %copy.67) | copy-start | bytes 1327108
  87.8 1.7 %copy-start.7 = (bf16[1,384,2,384]{3,1,2,0:T(8,128)(2,1)S(1)}, bf16[1,384,2,384]{3,1,2,0:T(8,128)(2,1)}, u32[]{:S(2)}) copy-start(bf16[1,384,2,384]{3,1,2,0:T(8,128)(2,1)} %get-tuple-element.25) | copy-start | bytes 1769476
  87.8 1.7 %copy-start.8 = (bf16[1,384,2,384]{3,1,2,0:T(8,128)(2,1)S(1)}, bf16[1,384,2,384]{3,1,2,0:T(8,128)(2,1)}, u32[]{:S(2)}) copy-start(bf16[1,384,2,384]{3,1,2,0:T(8,128)(2,1)} %get-tuple-element.34) | copy-start | bytes 1769476
  90.4 2.5 %collective-permute-start.2 = (bf16[3,384,2,192]{1,3,2,0:T(8,128)(2,1)S(1)}, bf16[3,384,2,192]{1,3,2,0:T(8,128)(2,1)S(1)}, u32[]{:S(2)}, u32[]{:S(2)}) collective-permute-start(bf16[3,384,2,192]{1,3,2,0:T(8,128)(2,1)S(1)} %fusion.21), channel_id=1, source_target_pairs={{0,128},{128,0},{1,129},{129,1},{2,130},{130,2},{3,131},{131,3},{4... | collective-permute-start | bytes 2654216 | tf_op jit(solution)/shard_map/ppermute | solution.py:347
  121.4 2.2 %collective-permute-start.3 = (bf16[192,3,192]{0,2,1:T(8,128)(2,1)S(1)}, bf16[192,3,192]{0,2,1:T(8,128)(2,1)S(1)}, u32[]{:S(2)}, u32[]{:S(2)}) collective-permute-start(bf16[192,3,192]{0,2,1:T(8,128)(2,1)S(1)} %get-tuple-element.29), channel_id=1, source_target_pairs={{0,128},{128,0},{1,129},{129,1},{2,130},{130,2},{3,131},{131,3},{4... | collective-permute-start | bytes 663560 | tf_op jit(solution)/shard_map/ppermute | solution.py:373

commit v8 on v6

--- a/solution.py
+++ b/solution.py
@@ -197,11 +197,11 @@
     return (own_taps, upper_taps, left_taps, corner_taps)
 
 
-def stem_layers(aerial_patch_grid, patch_conv_weight, patch_bias, merging_conv_weight, merge_bias):
+def stem_layers(aerial_patch_grid, patch_matrix, patch_bias, merging_matrix, merge_bias):
     initial_layer = jnp.einsum(
         "zji,if->zjf",
         aerial_patch_grid,
-        patch_kernel_matrix(patch_conv_weight),
+        patch_matrix,
         preferred_element_type=jnp.float32,
     )
     initial_layer = jax.nn.gelu(initial_layer + jnp.tile(patch_bias, 16), approximate=True).astype(
@@ -210,7 +210,7 @@
     layer_two = jnp.einsum(
         "zji,if->zjf",
         initial_layer,
-        merging_kernel_matrix(merging_conv_weight),
+        merging_matrix,
         preferred_element_type=jnp.float32,
     )
     return jax.nn.gelu(layer_two + jnp.tile(merge_bias, 4), approximate=True).astype(jnp.bfloat16)
@@ -283,10 +283,14 @@
     tile_index = lax.axis_index("tile")
     grid = jnp.pad(aerial_patch_grid, ((0, 0), (1, 0), (0, 0)))
     own_part = lax.dynamic_slice_in_dim(grid, section_index * cell_half, cell_half + 1, 1)
-    image_part = jnp.concatenate([from_behind(own_part[-1:], "tile", 1), own_part], axis=0)
-    layer_two = stem_layers(
-        image_part, patch_conv_weight, patch_bias, merging_conv_weight, merge_bias
-    )
+    patch_matrix = patch_kernel_matrix(patch_conv_weight)
+    merging_matrix = merging_kernel_matrix(merging_conv_weight)
+    own_two = stem_layers(own_part, patch_matrix, patch_bias, merging_matrix, merge_bias)
+    last_row, own_two = lax.optimization_barrier((own_part[-1:], own_two))
+    rim_two = stem_layers(
+        from_behind(last_row, "tile", 1), patch_matrix, patch_bias, merging_matrix, merge_bias
+    )
+    layer_two = jnp.concatenate([rim_two, own_two], axis=0)
     row_ok = (jnp.arange(layer_two.shape[0]) > 0) | (tile_index > 0)
     col_ok = (jnp.arange(layer_two.shape[1]) > 0) | (section_index > 0)
     stacked = jnp.where(row_ok[:, None, None] & col_ok[None, :, None], layer_two, 0)

time: 116 us -> 120 us (1.034)
  local copies, waits for them, and re-layouts: 22.9 us -> 27.3 us
    another operation x1, local copies, waits for them, and re-layouts: 0.14 us -> 2.31 us  [arrange(): jnp.stack(entries[1], axis=0)]
    dot_general x1 -> x2, matrix products: 7.9 us -> 9.95 us  [stem_layers(): jnp.einsum('zji,if->zjf', initial_layer, merging_matrix, preferred_elemen...]
    another operation x1, other arithmetic: 0.33 us -> 1.71 us
    slice x1, local copies, waits for them, and re-layouts: 0.49 us -> 1.76 us  [filter_columns(): filter_real = kernel[:, 0].astype(jnp.float32)]
    dot_general x1, matrix products: 1.75 us -> 0.5 us  [local(): jnp.einsum('chx,xqw->chqw', fields, lax.dynamic_slice_in_dim(forward_tabl...]
    another operation x1, other arithmetic: 2.71 us -> 1.48 us  [local(): jnp.stack([jnp.stack([cos_h, sin_h], axis=1), jnp.stack([-sin_h, cos_h],...]
    unnamed x37 -> x33, local copies, waits for them, and re-layouts: 6.13 us -> 5.37 us
  transfers between devices with their start and end apart: 4 -> 4, of which waited for: 2 -> 2; matrix products, arithmetic and copies ran while one was open for 14% -> 10% of each run, Pallas kernels for 0% -> 0%
where the time goes in v8:
time: 120 us; the launch traced here: 119 us
  Pallas kernels  47.3 us (39%)
  local copies, waits for them, and re-layouts  27.3 us (23%)
  matrix products  24.7 us (21%)
  other arithmetic  8.49 us (7%)
  starting transfers between devices  8.16 us (7%)
  waiting for transfers between devices  3.13 us (3%)
    pallas_call x1, Pallas kernels, exchange_with_tables(): pl.pallas_call(exchange_tables_kernel, out_shape=(jax.ShapeDtypeStruct(ch...  25.6 us
    pallas_call x1, Pallas kernels, exchange(): pl.pallas_call(exchange_kernel, out_shape=jax.ShapeDtypeStruct(chunks.sha...  21.6 us
    dot_general x2, matrix products, stem_layers(): jnp.einsum('zji,if->zjf', initial_layer, merging_matrix, preferred_elemen...  9.95 us
    dot_general x2, matrix products, spread_kernel(): full = jnp.dot(picked, repeat, preferred_element_type=jnp.float32)  6.02 us
    unnamed x33, local copies, waits for them, and re-layouts  5.37 us
    ppermute x1, starting transfers between devices, from_behind(): return lax.ppermute(block, axis, route)  5.09 us
    dot_general x1, matrix products, filter_columns(): jnp.einsum('puqh,chqw->cpuw', forward_h, row_spectrum, preferred_element_...  3.72 us
  transfers between devices with their start and end apart: 4, of which 2 were waited for; matrix products, arithmetic and copies ran while one was open for 10% of the time, Pallas kernels for 0%

profile of v8, /device:TPU:1, one launch (start us, length us, event | category | flops | bytes accessed | tf_op | source)
XLA Modules:
  0.0 119.4 jit_solution(15019022384240094977)
XLA Ops:
  0.1 0.7 tile.4
  0.9 0.7 tile.5
  1.6 1.8 %pad_dynamic-slice_fusion = bf16[1,193,768]{2,1,0:T(8,128)(2,1)} fusion(s32[]{:T(128)S(6)} %add.379, s32[]{:T(128)S(6)} %select_n.200, bf16[3,384,768]{2,1,0:T(8,128)(2,1)} %param.9), kind=kLoop, calls=%fused_computation.30 | loop fusion | bytes 2065928 | tf_op jit(solution)/shard_map/slice | solution.py:289
  3.4 3.2 %select_convert_fusion = bf16[1536,768]{1,0:T(8,128)(2,1)} fusion(s32[768]{0:T(1024)S(1)} %get-tuple-element.49, s32[1536]{0:T(1024)S(1)} %get-tuple-element.52, bf16[384,192]{1,0:T(8,128)(2,1)S(1)} %bitcast.171, s32[1536]{0:T(1024)S(1)} %get-tuple-element.53, s32[768]{0:T(1024)S(1)} %get-tuple-element.48), kind=kOutput, calls=%fused_computation.1 | convolution fusion | flops 684048384 | bytes 2525184 | tf_op jit(solution)/shard_map/dot_general | solution.py:151
  6.6 2.8 %select_convert_fusion.1 = bf16[768,1536]{1,0:T(8,128)(2,1)} fusion(s32[1536]{0:T(1024)S(1)} %get-tuple-element.55, s32[768]{0:T(1024)S(1)} %get-tuple-element.50, bf16[48,96]{1,0:T(8,128)(2,1)S(1)} %bitcast.186, s32[1536]{0:T(1024)S(1)} %get-tuple-element.54, s32[768]{0:T(1024)S(1)} %get-tuple-element.51), kind=kOutput, calls=%fused_computation.2 | convolution fusion | flops 237367296 | bytes 2386944 | tf_op jit(solution)/shard_map/dot_general | solution.py:151
  9.4 6.1 %fusion.18 = bf16[3,193,768]{2,1,0:T(8,128)(2,1)S(1)} fusion(bf16[1536,768]{1,0:T(8,128)(2,1)} %select_convert_fusion, bf16[768,1536]{1,0:T(8,128)(2,1)} %select_convert_fusion.1, f32[1536]{0:T(1024)S(1)} %add.337, s32[]{:T(128)S(6)} %select_n.200, bf16[3,384,768]{2,1,0:T(8,128)(2,1)S(1)} %copy-done.2, f32[768]{0:T(1024)S(1)} %add.350), kind=kOutput, calls=%fused_computation.25 | convolution fusion | flops 2745404928 | bytes 7386628 | tf_op jit(solution)/shard_map/zji,if->zjf/dot_general | solution.py:210
  15.6 5.1 %collective-permute-start = (bf16[1,193,768]{2,1,0:T(8,128)(2,1)}, bf16[1,193,768]{2,1,0:T(8,128)(2,1)}, u32[]{:S(2)}, u32[]{:S(2)}) collective-permute-start(bf16[1,193,768]{2,1,0:T(8,128)(2,1)} %pad_dynamic-slice_fusion), channel_id=1, source_target_pairs={{0,1},{1,2},{2,3},{3,4},{4,5},{5,6},{6,7},{7,8},{8,9},{9,10},{10,1... | collective-permute-start | bytes 889352 | tf_op jit(solution)/shard_map/ppermute | solution.py:130
  20.7 2.3 %slice_bitcast_fusion = (bf16[1,192,384]{2,1,0:T(8,128)(2,1)S(1)}, bf16[1,192,384]{2,1,0:T(8,128)(2,1)}, bf16[1,192,384]{2,1,0:T(8,128)(2,1)S(1)}, bf16[1,192,38...) fusion(bf16[3,3,192,384]{3,2,1,0:T(8,128)(2,1)} %param.14), kind=kLoop, calls=%fused_computation.155 | loop fusion | bytes 2654208 | tf_op jit(solution)/shard_map/stack;squeeze | solution.py:188
  23.1 0.9 stack.131
  24.0 1.8 %constant_dynamic-slice_fusion = (bf16[3,1,384,192]{3,2,1,0:T(8,128)(2,1)S(1)}, bf16[3,1,384,192]{3,2,1,0:T(8,128)(2,1)S(1)}) fusion(bf16[3,2,384,384]{3,2,1,0:T(8,128)(2,1)} %param.17, s32[]{:T(128)S(6)} %select_n.222, s32[]{:T(128)S(6)} %add.380), kind=kLoop, calls=%fused_computation.260 | loop fusion | bytes 1769480 | tf_op jit(solution)/shard_map/slice | solution.py:252
  25.7 1.0 copy.62
  26.7 1.0 copy.63
  27.7 1.0 maximum_bitcast_fusion.6
  28.9 1.0 pad_bitcast_fusion.2
  30.1 3.8 %fusion.70 = bf16[1,193,768]{2,1,0:T(8,128)(2,1)S(1)} fusion(bf16[1536,768]{1,0:T(8,128)(2,1)} %select_convert_fusion, bf16[768,1536]{1,0:T(8,128)(2,1)} %select_convert_fusion.1, f32[1536]{0:T(1024)S(1)} %add.337, bf16[1,193,768]{2,1,0:T(8,128)(2,1)} %collective-permute-done, f32[768]{0:T(1024)S(1)} %add.350), kind=kOutput, calls=%fused_computation.103 | convolution fusion | flops 915134976 | bytes 5320704 | tf_op jit(solution)/shard_map/zji,if->zjf/dot_general | solution.py:210
  34.1 0.6 fusion.58
  34.7 0.6 convolution_add_fusion.3
  35.4 0.6 convolution_add_fusion.2
  36.4 0.7 convert_reduce_fusion
  37.8 0.9 copy.27
  38.7 0.5 reshape.371
  39.3 0.9 copy.64
  40.2 25.6 %shard_map.91 = (bf16[128,16,128]{2,1,0:T(8,128)(2,1)}, bf16[384,384]{1,0:T(8,128)(2,1)}, bf16[384,384]{1,0:T(8,128)(2,1)}) custom-call(bf16[128,16,128]{2,1,0:T(8,128)(2,1)} %bitcast.177), custom_call_target="tpu_custom_call" | custom-call | tf_op jit(solution)/shard_map/pallas_call | solution.py:95
  65.8 1.7 %fusion.103 = (bf16[1,384,192]{2,1,0:T(8,128)(2,1)S(1)}, bf16[384,1,192]{2,0,1:T(8,128)(2,1)}) fusion(bf16[384,384]{1,0:T(8,128)(2,1)} %get-tuple-element.14, s32[]{:T(128)S(6)} %select_n.222), kind=kLoop, calls=%fused_computation.153 | loop fusion | flops 221184 | bytes 442372 | tf_op jit(solution)/shard_map/stack | solution.py:319
  67.6 1.0 negate_bitcast_fusion
  68.6 1.5 %copy.53 = bf16[128,16,128]{0,2,1:T(8,128)(2,1)S(1)} copy(bf16[128,16,128]{2,1,0:T(8,128)(2,1)} %get-tuple-element.12) | data formatting | bytes 1048576 | tf_op jit(solution)/shard_map/reshape | solution.py:117
  70.1 0.7 copy.29
  70.8 0.5 reshape.375
  71.4 1.7 %dynamic-slice_bitcast_fusion = (bf16[1,384,192]{2,1,0:T(8,128)(2,1)S(1)}, bf16[384,1,192]{2,0,1:T(8,128)(2,1)}) fusion(bf16[384,384]{1,0:T(8,128)(2,1)} %get-tuple-element.13, s32[]{:T(128)S(6)} %select_n.222), kind=kLoop, calls=%fused_computation.151 | loop fusion | bytes 442372 | tf_op jit(solution)/shard_map/stack | solution.py:319
  73.1 1.0 copy.32
  74.1 2.0 %collective-permute-start.1 = (bf16[3,384,192]{1,2,0:T(8,128)(2,1)}, bf16[3,384,192]{1,2,0:T(8,128)(2,1)S(1)}, u32[]{:S(2)}, u32[]{:S(2)}) collective-permute-start(bf16[3,384,192]{1,2,0:T(8,128)(2,1)} %copy.32), channel_id=1, source_target_pairs={{0,128},{128,0},{1,129},{129,1},{2,130},{130,2},{3,131},{131,3},{4... | collective-permute-start | bytes 1327112 | tf_op jit(solution)/shard_map/ppermute | solution.py:310
  76.2 1.5 %fusion.78 = (bf16[1,384,2,384]{3,1,2,0:T(8,128)(2,1)}, bf16[1,384,2,384]{3,1,2,0:T(8,128)(2,1)}, bf16[1,384,2,384]{3,1,2,0:T(8,128)(2,1)}, bf16[1,384,2,384]{3,1,2,0:T(8,128)(2,1)}) fusion(bf16[384,1,384]{2,0,1:T(8,128)(2,1)S(1)} %bitcast.183, bf16[384,1,384]{2,0,1:T(8,128)(2,1)S(1)} %bitcast.175, bf16[384,1,384]{2,0,1:T(8,128)(2,1)S(1)} %negate_bitcast_fusion), kind=kLoop, calls=%fused_computation.111 | loop fusion | flops 1179648 | bytes 3244032 | tf_op jit(solution)/shard_map/stack | solution.py:320
  77.7 0.5 fusion.80
  78.2 0.8 copy-done.11
  79.0 3.7 %fusion.23 = bf16[3,2,384,192]{2,3,1,0:T(8,128)(2,1)} fusion(bf16[1,384,2,384]{3,1,2,0:T(8,128)(2,1)} %get-tuple-element.39, bf16[1,384,2,384]{3,1,2,0:T(8,128)(2,1)} %get-tuple-element.28, f32[3,384,2,192]{1,3,2,0:T(8,128)S(1)} %fusion.80, bf16[3,384,192]{1,2,0:T(8,128)(2,1)} %copy-done.11, s32[]{:T(128)S(6)} %select_n.223, ...), kind=kOutput, calls=%fused_computation.40 | convolution fusion | flops 853327872 | bytes 4571140 | tf_op jit(solution)/shard_map/puqh,chqw->cpuw/dot_general | solution.py:247
  82.7 1.7 %fusion.51 = (bf16[3,1,384,192]{2,3,1,0:T(8,128)(2,1)S(1)}, bf16[3,1,384,192]{2,3,1,0:T(8,128)(2,1)S(1)}) fusion(bf16[3,1,384,192]{2,3,1,0:T(8,128)(2,1)S(1)} %copy-done.3, bf16[3,1,384,192]{2,3,1,0:T(8,128)(2,1)} %copy.63, bf16[3,2,384,192]{2,3,1,0:T(8,128)(2,1)} %fusion.23), kind=kLoop, calls=%fused_computation.77 | loop fusion | flops 2654208 | bytes 2654208 | tf_op jit(solution)/shard_map/convert.1
  84.4 0.9 fusion.24
  85.4 0.5 convolution_bitcast_fusion.1
  85.9 1.9 %collective-permute-done.2 = bf16[3,384,2,192]{1,3,2,0:T(8,128)(2,1)S(1)} collective-permute-done((bf16[3,384,2,192]{1,3,2,0:T(8,128)(2,1)S(1)}, bf16[3,384,2,192]{1,3,2,0:T(8,128)(2,1)S(1)}, u32[]{:S(2)}, u32[]{:S(2)}) %collective-permute-start.2) | collective-permute-done | bytes 884768 | tf_op jit(solution)/shard_map/ppermute | solution.py:346
  88.9 0.8 copy.37
  89.8 1.2 %copy.60.x_ref = bf16[128,16,128]{2,1,0:T(8,128)(2,1)} copy(bf16[128,16,128]{0,2,1:T(8,128)(2,1)S(1)} %bitcast.176) | data formatting | bytes 1048576 | tf_op jit(solution)/shard_map/reshape | solution.py:123
  91.0 21.6 %shard_map.92 = bf16[128,16,128]{2,1,0:T(8,128)(2,1)} custom-call(bf16[128,16,128]{2,1,0:T(8,128)(2,1)} %copy.60.x_ref), custom_call_target="tpu_custom_call" | custom-call | tf_op jit(solution)/shard_map/pallas_call | solution.py:83
  112.6 1.2 copy.67
  113.9 0.9 reshape.380
  114.8 0.9 copy.39
  116.0 0.9 collective-permute-start.3
  117.0 1.2 %collective-permute-done.3 = bf16[192,3,192]{0,2,1:T(8,128)(2,1)S(1)} collective-permute-done((bf16[192,3,192]{0,2,1:T(8,128)(2,1)S(1)}, bf16[192,3,192]{0,2,1:T(8,128)(2,1)S(1)}, u32[]{:S(2)}, u32[]{:S(2)}) %collective-permute-start.3) | collective-permute-done | bytes 221216 | tf_op jit(solution)/shard_map/ppermute | solution.py:372
  118.4 1.0 copy.40
  (58 shorter events, 3.8 us)
Async XLA Ops:
  0.0 3.4 %copy-start = (bf16[2,2,96,192]{3,2,1,0:T(8,128)(2,1)S(1)}, bf16[2,2,96,192]{3,2,1,0:T(8,128)(2,1)}, u32[]{:S(2)}) copy-start(bf16[2,2,96,192]{3,2,1,0:T(8,128)(2,1)} %param.12) | copy-start | bytes 442372
  3.4 3.2 %copy-start.12 = (bf16[3,4,4,96]{3,2,1,0:T(4,128)(2,1)S(1)}, bf16[3,4,4,96]{3,2,1,0:T(4,128)(2,1)}, u32[]{:S(2)}) copy-start(bf16[3,4,4,96]{3,2,1,0:T(4,128)(2,1)} %param.10) | copy-start | bytes 27652
  6.6 2.8 %copy-start.2 = (bf16[3,384,768]{2,1,0:T(8,128)(2,1)S(1)}, bf16[3,384,768]{2,1,0:T(8,128)(2,1)}, u32[]{:S(2)}) copy-start(bf16[3,384,768]{2,1,0:T(8,128)(2,1)} %param.9) | copy-start | bytes 5308420
  15.6 14.5 %collective-permute-start = (bf16[1,193,768]{2,1,0:T(8,128)(2,1)}, bf16[1,193,768]{2,1,0:T(8,128)(2,1)}, u32[]{:S(2)}, u32[]{:S(2)}) collective-permute-start(bf16[1,193,768]{2,1,0:T(8,128)(2,1)} %pad_dynamic-slice_fusion), channel_id=1, source_target_pairs={{0,1},{1,2},{2,3},{3,4},{4,5},{5,6},{6,7},{7,8},{8,9},{9,10},{10,1... | collective-permute-start | bytes 889352 | tf_op jit(solution)/shard_map/ppermute | solution.py:130
  35.4 1.1 copy-start.9
  35.4 1.1 copy-start.13
  36.0 1.5 %copy-start.10 = (f32[384]{0:T(512)S(1)}, f32[384]{0:T(512)}, u32[]{:S(2)}) copy-start(f32[384]{0:T(512)} %param.16) | copy-start | bytes 4612
  70.1 6.1 %copy-start.1 = (bf16[384,384]{1,0:T(8,128)(2,1)S(1)}, bf16[384,384]{1,0:T(8,128)(2,1)}, u32[]{:S(2)}) copy-start(bf16[384,384]{1,0:T(8,128)(2,1)} %get-tuple-element.14) | copy-start | bytes 884740
  70.8 5.3 %copy-start.4 = (bf16[384,384]{1,0:T(8,128)(2,1)S(1)}, bf16[384,384]{1,0:T(8,128)(2,1)}, u32[]{:S(2)}) copy-start(bf16[384,384]{1,0:T(8,128)(2,1)} %get-tuple-element.13) | copy-start | bytes 884740
  74.1 3.5 %copy-start.5 = (bf16[384,1,192]{2,0,1:T(8,128)(2,1)S(1)}, bf16[384,1,192]{2,0,1:T(8,128)(2,1)}, u32[]{:S(2)}) copy-start(bf16[384,1,192]{2,0,1:T(8,128)(2,1)} %get-tuple-element.35) | copy-start | bytes 442372
  74.1 3.5 %copy-start.6 = (bf16[384,1,192]{2,0,1:T(8,128)(2,1)S(1)}, bf16[384,1,192]{2,0,1:T(8,128)(2,1)}, u32[]{:S(2)}) copy-start(bf16[384,1,192]{2,0,1:T(8,128)(2,1)} %get-tuple-element.37) | copy-start | bytes 442372
  74.1 4.0 %collective-permute-start.1 = (bf16[3,384,192]{1,2,0:T(8,128)(2,1)}, bf16[3,384,192]{1,2,0:T(8,128)(2,1)S(1)}, u32[]{:S(2)}, u32[]{:S(2)}) collective-permute-start(bf16[3,384,192]{1,2,0:T(8,128)(2,1)} %copy.32), channel_id=1, source_target_pairs={{0,128},{128,0},{1,129},{129,1},{2,130},{130,2},{3,131},{131,3},{4... | collective-permute-start | bytes 1327112 | tf_op jit(solution)/shard_map/ppermute | solution.py:310
  78.2 0.8 copy-start.11
  79.0 3.7 %copy-start.3 = (bf16[3,1,384,192]{2,3,1,0:T(8,128)(2,1)S(1)}, bf16[3,1,384,192]{2,3,1,0:T(8,128)(2,1)}, u32[]{:S(2)}) copy-start(bf16[3,1,384,192]{2,3,1,0:T(8,128)(2,1)} %copy.62) | copy-start | bytes 1327108
  82.7 1.7 %copy-start.7 = (bf16[1,384,2,384]{3,1,2,0:T(8,128)(2,1)S(1)}, bf16[1,384,2,384]{3,1,2,0:T(8,128)(2,1)}, u32[]{:S(2)}) copy-start(bf16[1,384,2,384]{3,1,2,0:T(8,128)(2,1)} %get-tuple-element.29) | copy-start | bytes 1769476
  82.7 1.7 %copy-start.8 = (bf16[1,384,2,384]{3,1,2,0:T(8,128)(2,1)S(1)}, bf16[1,384,2,384]{3,1,2,0:T(8,128)(2,1)}, u32[]{:S(2)}) copy-start(bf16[1,384,2,384]{3,1,2,0:T(8,128)(2,1)} %get-tuple-element.38) | copy-start | bytes 1769476
  85.3 2.5 %collective-permute-start.2 = (bf16[3,384,2,192]{1,3,2,0:T(8,128)(2,1)S(1)}, bf16[3,384,2,192]{1,3,2,0:T(8,128)(2,1)S(1)}, u32[]{:S(2)}, u32[]{:S(2)}) collective-permute-start(bf16[3,384,2,192]{1,3,2,0:T(8,128)(2,1)S(1)} %fusion.24), channel_id=1, source_target_pairs={{0,128},{128,0},{1,129},{129,1},{2,130},{130,2},{3,131},{131,3},{4... | collective-permute-start | bytes 2654216 | tf_op jit(solution)/shard_map/ppermute | solution.py:346
  116.0 2.1 %collective-permute-start.3 = (bf16[192,3,192]{0,2,1:T(8,128)(2,1)S(1)}, bf16[192,3,192]{0,2,1:T(8,128)(2,1)S(1)}, u32[]{:S(2)}, u32[]{:S(2)}) collective-permute-start(bf16[192,3,192]{0,2,1:T(8,128)(2,1)S(1)} %get-tuple-element.33), channel_id=1, source_target_pairs={{0,128},{128,0},{1,129},{129,1},{2,130},{130,2},{3,131},{131,3},{4... | collective-permute-start | bytes 663560 | tf_op jit(solution)/shard_map/ppermute | solution.py:372

commit v9 on v6

--- a/solution.py
+++ b/solution.py
@@ -156,26 +156,26 @@
 def patch_kernel_matrix(patch_conv_weight):
     band_count = patch_conv_weight.shape[0]
     width = patch_conv_weight.shape[3]
-    row = jnp.arange(band_count * 256, dtype=jnp.int32)
-    pick = (row // 256) * 16 + ((row // 16) % 4) * 4 + row % 4
-    row_cell = ((row // 64) % 4) * 4 + (row // 4) % 4
-    col = jnp.arange(16 * width, dtype=jnp.int32)
-    col_cell = col // width
+    row = jnp.arange(band_count * 128, dtype=jnp.int32)
+    pixel_row = (row % 128) // 16
+    pixel_col = row % 16
+    pick = (row // 128) * 16 + (pixel_row % 4) * 4 + pixel_col % 4
+    row_cell = (pixel_row // 4) * 4 + pixel_col // 4
+    col_cell = jnp.arange(8 * width, dtype=jnp.int32) // width
     weight_rows = patch_conv_weight.reshape(band_count * 16, width)
-    return spread_kernel(weight_rows, pick, row_cell, col_cell, width, 16 * width)
+    return spread_kernel(weight_rows, pick, row_cell, col_cell, width, 8 * width)
 
 
 def merging_kernel_matrix(merging_conv_weight):
     in_width = merging_conv_weight.shape[2]
     out_width = merging_conv_weight.shape[3]
-    row = jnp.arange(16 * in_width, dtype=jnp.int32)
-    pos = row // in_width
-    pick = ((pos // 4) % 2 * 2 + pos % 2) * in_width + row % in_width
-    row_cell = (pos // 8) * 2 + (pos // 2) % 2
-    col = jnp.arange(4 * out_width, dtype=jnp.int32)
-    col_cell = col // out_width
+    row = jnp.arange(8 * in_width, dtype=jnp.int32)
+    cell = row // in_width
+    pick = ((cell // 4) * 2 + cell % 2) * in_width + row % in_width
+    row_cell = (cell % 4) // 2
+    col_cell = jnp.arange(2 * out_width, dtype=jnp.int32) // out_width
     weight_rows = merging_conv_weight.reshape(4 * in_width, out_width)
-    return spread_kernel(weight_rows, pick, row_cell, col_cell, out_width, 4 * out_width)
+    return spread_kernel(weight_rows, pick, row_cell, col_cell, out_width, 2 * out_width)
 
 
 def down_matrices(down_weight):
@@ -198,22 +198,31 @@
 
 
 def stem_layers(aerial_patch_grid, patch_conv_weight, patch_bias, merging_conv_weight, merge_bias):
-    initial_layer = jnp.einsum(
-        "zji,if->zjf",
-        aerial_patch_grid,
-        patch_kernel_matrix(patch_conv_weight),
-        preferred_element_type=jnp.float32,
-    )
-    initial_layer = jax.nn.gelu(initial_layer + jnp.tile(patch_bias, 16), approximate=True).astype(
-        jnp.bfloat16
-    )
-    layer_two = jnp.einsum(
-        "zji,if->zjf",
-        initial_layer,
-        merging_kernel_matrix(merging_conv_weight),
-        preferred_element_type=jnp.float32,
-    )
-    return jax.nn.gelu(layer_two + jnp.tile(merge_bias, 4), approximate=True).astype(jnp.bfloat16)
+    band_count = patch_conv_weight.shape[0]
+    patch_matrix = patch_kernel_matrix(patch_conv_weight)
+    merging_matrix = merging_kernel_matrix(merging_conv_weight)
+    halves = []
+    for half in range(2):
+        pixels = jnp.concatenate(
+            [
+                aerial_patch_grid[..., band * 256 + half * 128 : band * 256 + half * 128 + 128]
+                for band in range(band_count)
+            ],
+            axis=-1,
+        )
+        initial_layer = jnp.einsum(
+            "zji,if->zjf", pixels, patch_matrix, preferred_element_type=jnp.float32
+        )
+        initial_layer = jax.nn.gelu(
+            initial_layer + jnp.tile(patch_bias, 8), approximate=True
+        ).astype(jnp.bfloat16)
+        layer_two = jnp.einsum(
+            "zji,if->zjf", initial_layer, merging_matrix, preferred_element_type=jnp.float32
+        )
+        halves.append(
+            jax.nn.gelu(layer_two + jnp.tile(merge_bias, 2), approximate=True).astype(jnp.bfloat16)
+        )
+    return jnp.concatenate(halves, axis=-1)
 
 
 def down_conv(stacked, down_weight, down_bias):

time: 116 us -> 112 us (0.966)
  matrix products: 24.4 us -> 18.3 us
  other arithmetic: 8.87 us -> 10.3 us
  local copies, waits for them, and re-layouts: 22.9 us -> 24.2 us
    dot_general x2, matrix products: 6.02 us -> 3.11 us  [spread_kernel(): full = jnp.dot(picked, repeat, preferred_element_type=jnp.float32)]
    another operation x1, local copies, waits for them, and re-layouts: 0.14 us -> 2.22 us  [arrange(): jnp.stack(entries[1], axis=0)]
    concatenate x0 -> x1, other arithmetic: none -> 1.76 us  [local(): jnp.concatenate([from_behind(own_part[-1:], 'tile', 1), own_part], axis=0)]
    dot_general x1 -> x2, matrix products: 7.9 us -> 6.5 us  [stem_layers(): jnp.einsum('zji,if->zjf', initial_layer, merging_matrix, preferred_elemen...]
    another operation x1, other arithmetic: 0.33 us -> 1.71 us
    slice x1, local copies, waits for them, and re-layouts: 0.49 us -> 1.76 us  [filter_columns(): filter_real = kernel[:, 0].astype(jnp.float32)]
    dot_general x1, matrix products: 1.75 us -> 0.5 us  [local(): jnp.einsum('chx,xqw->chqw', fields, lax.dynamic_slice_in_dim(forward_tabl...]
    another operation x1, other arithmetic: 2.71 us -> 1.47 us  [local(): jnp.stack([jnp.stack([cos_h, sin_h], axis=1), jnp.stack([-sin_h, cos_h],...]
  transfers between devices with their start and end apart: 4 -> 4, of which waited for: 2 -> 2; matrix products, arithmetic and copies ran while one was open for 14% -> 13% of each run, Pallas kernels for 0% -> 0%
where the time goes in v9:
time: 112 us
  Pallas kernels  47.2 us (42%)
  local copies, waits for them, and re-layouts  24.2 us (22%)
  matrix products  18.3 us (16%)
  other arithmetic  10.3 us (9%)
  starting transfers between devices  8.12 us (7%)
  waiting for transfers between devices  3.14 us (3%)
    pallas_call x1, Pallas kernels, exchange_with_tables(): pl.pallas_call(exchange_tables_kernel, out_shape=(jax.ShapeDtypeStruct(ch...  25.4 us
    pallas_call x1, Pallas kernels, exchange(): pl.pallas_call(exchange_kernel, out_shape=jax.ShapeDtypeStruct(chunks.sha...  21.8 us
    dot_general x2, matrix products, stem_layers(): jnp.einsum('zji,if->zjf', initial_layer, merging_matrix, preferred_elemen...  6.5 us
    unnamed x45, local copies, waits for them, and re-layouts  6.14 us
    ppermute x1, starting transfers between devices, from_behind(): return lax.ppermute(block, axis, route)  5.23 us
    dot_general x1, matrix products, filter_columns(): jnp.einsum('puqh,chqw->cpuw', forward_h, row_spectrum, preferred_element_...  3.7 us
    dot_general x2, matrix products, spread_kernel(): full = jnp.dot(picked, repeat, preferred_element_type=jnp.float32)  3.11 us
  transfers between devices with their start and end apart: 4, of which 2 were waited for; matrix products, arithmetic and copies ran while one was open for 13% of the time, Pallas kernels for 0%

profile of v9, /device:TPU:1, one launch (start us, length us, event | category | flops | bytes accessed | tf_op | source)
XLA Modules:
  0.0 111.7 jit_solution(14384157812858477483)
XLA Ops:
  0.0 1.9 %pad_dynamic-slice_fusion = bf16[1,193,768]{2,1,0:T(8,128)(2,1)} fusion(s32[]{:T(128)S(6)} %add.342, s32[]{:T(128)S(6)} %select_n.200, bf16[3,384,768]{2,1,0:T(8,128)(2,1)} %param.9), kind=kLoop, calls=%fused_computation.28 | loop fusion | bytes 2065928 | tf_op jit(solution)/shard_map/slice | solution.py:295
  1.9 5.2 %collective-permute-start = (bf16[1,193,768]{2,1,0:T(8,128)(2,1)}, bf16[1,193,768]{2,1,0:T(8,128)(2,1)}, u32[]{:S(2)}, u32[]{:S(2)}) collective-permute-start(bf16[1,193,768]{2,1,0:T(8,128)(2,1)} %pad_dynamic-slice_fusion), channel_id=1, source_target_pairs={{0,1},{1,2},{2,3},{3,4},{4,5},{5,6},{6,7},{7,8},{8,9},{9,10},{10,1... | collective-permute-start | bytes 889352 | tf_op jit(solution)/shard_map/ppermute | solution.py:130
  7.7 2.2 %slice_bitcast_fusion = (bf16[1,192,384]{2,1,0:T(8,128)(2,1)S(1)}, bf16[1,192,384]{2,1,0:T(8,128)(2,1)}, bf16[1,192,384]{2,1,0:T(8,128)(2,1)S(1)}, bf16[1,192,38...) fusion(bf16[3,3,192,384]{3,2,1,0:T(8,128)(2,1)} %param.14), kind=kLoop, calls=%fused_computation.180 | loop fusion | bytes 2654208 | tf_op jit(solution)/shard_map/stack;squeeze | solution.py:188
  10.0 0.9 stack.131
  10.9 1.8 %constant_dynamic-slice_fusion = (bf16[3,1,384,192]{3,2,1,0:T(8,128)(2,1)S(1)}, bf16[3,1,384,192]{3,2,1,0:T(8,128)(2,1)S(1)}) fusion(bf16[3,2,384,384]{3,2,1,0:T(8,128)(2,1)} %param.17, s32[]{:T(128)S(6)} %select_n.220, s32[]{:T(128)S(6)} %add.343), kind=kLoop, calls=%fused_computation.221 | loop fusion | bytes 1769480 | tf_op jit(solution)/shard_map/slice | solution.py:261
  12.6 1.0 copy.62
  13.6 1.0 copy.63
  14.7 0.9 pad_maximum_fusion.4
  15.8 1.7 %fusion.26 = bf16[768,384,1]{1,0,2:T(8,128)(2,1)} fusion(bf16[384,192]{1,0:T(8,128)(2,1)S(1)} %bitcast.161, s32[768]{0:T(1024)S(1)} %get-tuple-element.52, s32[384]{0:T(512)S(1)} %get-tuple-element.54, s32[768]{0:T(1024)S(1)} %get-tuple-element.50, s32[384]{0:T(512)S(1)} %get-tuple-element.53), kind=kOutput, calls=%fused_computation.57 | convolution fusion | flops 227893248 | bytes 746496 | tf_op jit(solution)/shard_map/dot_general | solution.py:151
  17.4 1.5 %fusion.27 = bf16[384,768,1]{1,0,2:T(8,128)(2,1)} fusion(bf16[48,96]{1,0:T(8,128)(2,1)S(1)} %bitcast.176, s32[768]{0:T(1024)S(1)} %get-tuple-element.51, s32[384]{0:T(512)S(1)} %get-tuple-element.55, s32[768]{0:T(1024)S(1)} %get-tuple-element.49, s32[384]{0:T(512)S(1)} %get-tuple-element.56), kind=kOutput, calls=%fused_computation.58 | convolution fusion | flops 61175808 | bytes 608256 | tf_op jit(solution)/shard_map/dot_general | solution.py:151
  19.0 1.8 %fusion.108 = (bf16[4,193,128]{2,1,0:T(8,128)(2,1)S(1)}, bf16[4,193,128]{2,1,0:T(8,128)(2,1)S(1)}, bf16[4,193,128]{2,1,0:T(8,128)(2,1)S(1)}, bf16[4,193,128]{2,1,0:T(8,128)(2,1)}, bf16[4,193,128]{2,1,0:T(8,128)(2,1)}) fusion(bf16[3,193,768]{2,1,0:T(8,128)(2,1)S(1)} %pad_dynamic-slice_fusion.1, bf16[1,193,768]{2,1,0:T(8,128)(2,1)} %collective-permute-done), kind=kLoop, calls=%fused_computation.160 | loop fusion | flops 494080 | bytes 2173952 | tf_op jit(solution)/shard_map/concatenate | solution.py:295
  20.7 3.1 %fusion.35 = bf16[4,193,384]{2,1,0:T(8,128)(2,1)S(1)} fusion(bf16[768,384,1]{1,0,2:T(8,128)(2,1)} %fusion.26, bf16[384,768,1]{1,0,2:T(8,128)(2,1)} %fusion.27, f32[768]{0:T(1024)S(1)} %add.308, bf16[4,193,128]{2,1,0:T(8,128)(2,1)S(1)} %get-tuple-element.26, bf16[4,193,128]{2,1,0:T(8,128)(2,1)S(1)} %get-tuple-element.25, ...), kind=kOutput, calls=%fused_computation.66 | convolution fusion | flops 921360384 | bytes 2370048 | tf_op jit(solution)/shard_map/zji,if->zjf/dot_general | solution.py:219
  23.9 3.4 %fusion.43 = bf16[4,193,384]{2,1,0:T(8,128)(2,1)S(1)} fusion(bf16[768,384,1]{1,0,2:T(8,128)(2,1)} %fusion.26, bf16[384,768,1]{1,0,2:T(8,128)(2,1)} %fusion.27, f32[768]{0:T(1024)S(1)} %add.308, bf16[3,193,768]{2,1,0:T(8,128)(2,1)S(1)} %pad_dynamic-slice_fusion.1, bf16[1,193,768]{2,1,0:T(8,128)(2,1)} %collective-permute-done, ...), kind=kOutput, calls=%fused_computation.74 | convolution fusion | flops 922842624 | bytes 3358208 | tf_op jit(solution)/shard_map/zji,if->zjf/dot_general | solution.py:219
  27.5 0.8 copy-done.10
  28.3 0.6 fusion.63
  28.9 0.6 convolution_add_fusion.4
  29.6 0.6 convolution_add_fusion.3
  30.6 0.8 convert_reduce_fusion
  32.0 1.0 copy.27
  33.1 0.5 reshape.334
  33.7 0.9 copy.64
  34.6 25.4 %shard_map.91 = (bf16[128,16,128]{2,1,0:T(8,128)(2,1)}, bf16[384,384]{1,0:T(8,128)(2,1)}, bf16[384,384]{1,0:T(8,128)(2,1)}) custom-call(bf16[128,16,128]{2,1,0:T(8,128)(2,1)} %bitcast.167), custom_call_target="tpu_custom_call" | custom-call | tf_op jit(solution)/shard_map/pallas_call | solution.py:95
  60.0 1.8 %fusion.127 = (bf16[1,384,192]{2,1,0:T(8,128)(2,1)S(1)}, bf16[384,1,192]{2,0,1:T(8,128)(2,1)}) fusion(bf16[384,384]{1,0:T(8,128)(2,1)} %get-tuple-element.10, s32[]{:T(128)S(6)} %select_n.220), kind=kLoop, calls=%fused_computation.178 | loop fusion | flops 221184 | bytes 442372 | tf_op jit(solution)/shard_map/stack | solution.py:324
  61.8 1.0 negate_bitcast_fusion
  62.8 0.5 copy.53
  63.3 0.7 copy.29
  64.1 0.5 reshape.338
  64.6 0.8 dynamic-slice_bitcast_fusion
  65.5 1.0 copy.32
  66.5 1.8 %collective-permute-start.1 = (bf16[3,384,192]{1,2,0:T(8,128)(2,1)}, bf16[3,384,192]{1,2,0:T(8,128)(2,1)S(1)}, u32[]{:S(2)}, u32[]{:S(2)}) collective-permute-start(bf16[3,384,192]{1,2,0:T(8,128)(2,1)} %copy.32), channel_id=1, source_target_pairs={{0,128},{128,0},{1,129},{129,1},{2,130},{130,2},{3,131},{131,3},{4... | collective-permute-start | bytes 1327112 | tf_op jit(solution)/shard_map/ppermute | solution.py:315
  68.3 1.5 %fusion.97 = (bf16[1,384,2,384]{3,1,2,0:T(8,128)(2,1)}, bf16[1,384,2,384]{3,1,2,0:T(8,128)(2,1)}, bf16[1,384,2,384]{3,1,2,0:T(8,128)(2,1)}, bf16[1,384,2,384]{3,1,2,0:T(8,128)(2,1)}) fusion(bf16[384,1,384]{2,0,1:T(8,128)(2,1)S(1)} %bitcast.173, bf16[384,1,384]{2,0,1:T(8,128)(2,1)S(1)} %bitcast.165, bf16[384,1,384]{2,0,1:T(8,128)(2,1)S(1)} %negate_bitcast_fusion), kind=kLoop, calls=%fused_computation.129 | loop fusion | flops 1179648 | bytes 3244032 | tf_op jit(solution)/shard_map/stack | solution.py:325
  69.8 0.5 fusion.99
  70.3 0.8 copy-done.17
  71.1 3.7 %fusion.20 = bf16[3,2,384,192]{2,3,1,0:T(8,128)(2,1)} fusion(bf16[1,384,2,384]{3,1,2,0:T(8,128)(2,1)} %get-tuple-element.40, bf16[1,384,2,384]{3,1,2,0:T(8,128)(2,1)} %get-tuple-element.29, f32[3,384,2,192]{1,3,2,0:T(8,128)S(1)} %fusion.99, bf16[3,384,192]{1,2,0:T(8,128)(2,1)} %copy-done.17, s32[]{:T(128)S(6)} %select_n.221, ...), kind=kOutput, calls=%fused_computation.44 | convolution fusion | flops 853327872 | bytes 4571140 | tf_op jit(solution)/shard_map/puqh,chqw->cpuw/dot_general | solution.py:256
  74.8 1.7 %fusion.56 = (bf16[3,1,384,192]{2,3,1,0:T(8,128)(2,1)S(1)}, bf16[3,1,384,192]{2,3,1,0:T(8,128)(2,1)S(1)}) fusion(bf16[3,1,384,192]{2,3,1,0:T(8,128)(2,1)S(1)} %copy-done.3, bf16[3,1,384,192]{2,3,1,0:T(8,128)(2,1)} %copy.63, bf16[3,2,384,192]{2,3,1,0:T(8,128)(2,1)} %fusion.20), kind=kLoop, calls=%fused_computation.98 | loop fusion | flops 2654208 | bytes 2654208 | tf_op jit(solution)/shard_map/convert.1
  76.5 0.9 fusion.21
  77.5 0.5 convolution_bitcast_fusion.1
  78.0 1.9 %collective-permute-done.2 = bf16[3,384,2,192]{1,3,2,0:T(8,128)(2,1)S(1)} collective-permute-done((bf16[3,384,2,192]{1,3,2,0:T(8,128)(2,1)S(1)}, bf16[3,384,2,192]{1,3,2,0:T(8,128)(2,1)S(1)}, u32[]{:S(2)}, u32[]{:S(2)}) %collective-permute-start.2) | collective-permute-done | bytes 884768 | tf_op jit(solution)/shard_map/ppermute | solution.py:351
  79.9 0.5 fusion.24
  81.0 0.8 copy.37
  81.8 1.2 %copy.60.x_ref = bf16[128,16,128]{2,1,0:T(8,128)(2,1)} copy(bf16[128,16,128]{0,2,1:T(8,128)(2,1)S(1)} %bitcast.166) | data formatting | bytes 1048576 | tf_op jit(solution)/shard_map/reshape | solution.py:123
  83.0 21.8 %shard_map.92 = bf16[128,16,128]{2,1,0:T(8,128)(2,1)} custom-call(bf16[128,16,128]{2,1,0:T(8,128)(2,1)} %copy.60.x_ref), custom_call_target="tpu_custom_call" | custom-call | tf_op jit(solution)/shard_map/pallas_call | solution.py:83
  104.9 1.2 %copy.67 = bf16[16,8,16,128]{3,1,2,0:T(8,128)(2,1)S(1)} copy(bf16[16,8,16,128]{3,2,1,0:T(8,128)(2,1)} %bitcast.168) | data formatting | bytes 1048576
  106.1 0.9 reshape.343
  107.0 0.9 copy.39
  108.3 1.0 collective-permute-start.3
  109.2 1.2 %collective-permute-done.3 = bf16[192,3,192]{0,2,1:T(8,128)(2,1)S(1)} collective-permute-done((bf16[192,3,192]{0,2,1:T(8,128)(2,1)S(1)}, bf16[192,3,192]{0,2,1:T(8,128)(2,1)S(1)}, u32[]{:S(2)}, u32[]{:S(2)}) %collective-permute-start.3) | collective-permute-done | bytes 221216 | tf_op jit(solution)/shard_map/ppermute | solution.py:377
  110.7 1.0 copy.40
  (72 shorter events, 3.7 us)
Async XLA Ops:
  0.0 15.8 %copy-start = (bf16[2,2,96,192]{3,2,1,0:T(8,128)(2,1)S(1)}, bf16[2,2,96,192]{3,2,1,0:T(8,128)(2,1)}, u32[]{:S(2)}) copy-start(bf16[2,2,96,192]{3,2,1,0:T(8,128)(2,1)} %param.12) | copy-start | bytes 442372
  0.0 7.1 %copy-start.1 = (bf16[3,384,768]{2,1,0:T(8,128)(2,1)S(1)}, bf16[3,384,768]{2,1,0:T(8,128)(2,1)}, u32[]{:S(2)}) copy-start(bf16[3,384,768]{2,1,0:T(8,128)(2,1)} %param.9) | copy-start | bytes 5308420
  1.9 5.6 %copy-start.16 = (f32[96]{0:T(128)S(1)}, f32[96]{0:T(128)}, u32[]{:S(2)}) copy-start(f32[96]{0:T(128)} %param.11) | copy-start | bytes 1156
  1.9 5.7 %copy-start.15 = (f32[192]{0:T(256)S(1)}, f32[192]{0:T(256)}, u32[]{:S(2)}) copy-start(f32[192]{0:T(256)} %param.13) | copy-start | bytes 2308
  1.9 17.1 %collective-permute-start = (bf16[1,193,768]{2,1,0:T(8,128)(2,1)}, bf16[1,193,768]{2,1,0:T(8,128)(2,1)}, u32[]{:S(2)}, u32[]{:S(2)}) collective-permute-start(bf16[1,193,768]{2,1,0:T(8,128)(2,1)} %pad_dynamic-slice_fusion), channel_id=1, source_target_pairs={{0,1},{1,2},{2,3},{3,4},{4,5},{5,6},{6,7},{7,8},{8,9},{9,10},{10,1... | collective-permute-start | bytes 889352 | tf_op jit(solution)/shard_map/ppermute | solution.py:130
  14.6 1.0 copy-start.11
  14.6 1.0 copy-start.12
  15.7 1.7 %copy-start.18 = (bf16[3,4,4,96]{3,2,1,0:T(4,128)(2,1)S(1)}, bf16[3,4,4,96]{3,2,1,0:T(4,128)(2,1)}, u32[]{:S(2)}) copy-start(bf16[3,4,4,96]{3,2,1,0:T(4,128)(2,1)} %param.10) | copy-start | bytes 27652
  27.2 1.1 copy-start.10
  29.6 1.1 copy-start.9
  29.6 1.1 copy-start.19
  30.6 1.2 %copy-start.14 = (f32[384]{0:T(512)S(1)}, f32[384]{0:T(512)}, u32[]{:S(2)}) copy-start(f32[384]{0:T(512)} %param.16) | copy-start | bytes 4612
  60.0 2.8 %copy-start.13 = (bf16[128,16,128]{2,1,0:T(8,128)(2,1)S(1)}, bf16[128,16,128]{2,1,0:T(8,128)(2,1)}, u32[]{:S(2)}) copy-start(bf16[128,16,128]{2,1,0:T(8,128)(2,1)} %get-tuple-element.8) | copy-start | bytes 1572868
  63.3 1.3 %copy-start.4 = (bf16[384,384]{1,0:T(8,128)(2,1)S(1)}, bf16[384,384]{1,0:T(8,128)(2,1)}, u32[]{:S(2)}) copy-start(bf16[384,384]{1,0:T(8,128)(2,1)} %get-tuple-element.9) | copy-start | bytes 884740
  64.1 4.2 %copy-start.2 = (bf16[384,384]{1,0:T(8,128)(2,1)S(1)}, bf16[384,384]{1,0:T(8,128)(2,1)}, u32[]{:S(2)}) copy-start(bf16[384,384]{1,0:T(8,128)(2,1)} %get-tuple-element.10) | copy-start | bytes 884740
  66.5 3.8 %collective-permute-start.1 = (bf16[3,384,192]{1,2,0:T(8,128)(2,1)}, bf16[3,384,192]{1,2,0:T(8,128)(2,1)S(1)}, u32[]{:S(2)}, u32[]{:S(2)}) collective-permute-start(bf16[3,384,192]{1,2,0:T(8,128)(2,1)} %copy.32), channel_id=1, source_target_pairs={{0,128},{128,0},{1,129},{129,1},{2,130},{130,2},{3,131},{131,3},{4... | collective-permute-start | bytes 1327112 | tf_op jit(solution)/shard_map/ppermute | solution.py:315
  68.3 1.5 %copy-start.5 = (bf16[384,1,192]{2,0,1:T(8,128)(2,1)S(1)}, bf16[384,1,192]{2,0,1:T(8,128)(2,1)}, u32[]{:S(2)}) copy-start(bf16[384,1,192]{2,0,1:T(8,128)(2,1)} %get-tuple-element.36) | copy-start | bytes 442372
  68.3 1.5 %copy-start.6 = (bf16[384,1,192]{2,0,1:T(8,128)(2,1)S(1)}, bf16[384,1,192]{2,0,1:T(8,128)(2,1)}, u32[]{:S(2)}) copy-start(bf16[384,1,192]{2,0,1:T(8,128)(2,1)} %get-tuple-element.38) | copy-start | bytes 442372
  70.3 0.8 copy-start.17
  71.1 3.7 %copy-start.3 = (bf16[3,1,384,192]{2,3,1,0:T(8,128)(2,1)S(1)}, bf16[3,1,384,192]{2,3,1,0:T(8,128)(2,1)}, u32[]{:S(2)}) copy-start(bf16[3,1,384,192]{2,3,1,0:T(8,128)(2,1)} %copy.62) | copy-start | bytes 1327108
  74.8 1.7 %copy-start.7 = (bf16[1,384,2,384]{3,1,2,0:T(8,128)(2,1)S(1)}, bf16[1,384,2,384]{3,1,2,0:T(8,128)(2,1)}, u32[]{:S(2)}) copy-start(bf16[1,384,2,384]{3,1,2,0:T(8,128)(2,1)} %get-tuple-element.30) | copy-start | bytes 1769476
  74.8 1.7 %copy-start.8 = (bf16[1,384,2,384]{3,1,2,0:T(8,128)(2,1)S(1)}, bf16[1,384,2,384]{3,1,2,0:T(8,128)(2,1)}, u32[]{:S(2)}) copy-start(bf16[1,384,2,384]{3,1,2,0:T(8,128)(2,1)} %get-tuple-element.39) | copy-start | bytes 1769476
  77.4 2.5 %collective-permute-start.2 = (bf16[3,384,2,192]{1,3,2,0:T(8,128)(2,1)S(1)}, bf16[3,384,2,192]{1,3,2,0:T(8,128)(2,1)S(1)}, u32[]{:S(2)}, u32[]{:S(2)}) collective-permute-start(bf16[3,384,2,192]{1,3,2,0:T(8,128)(2,1)S(1)} %fusion.21), channel_id=1, source_target_pairs={{0,128},{128,0},{1,129},{129,1},{2,130},{130,2},{3,131},{131,3},{4... | collective-permute-start | bytes 2654216 | tf_op jit(solution)/shard_map/ppermute | solution.py:351
  108.3 2.2 %collective-permute-start.3 = (bf16[192,3,192]{0,2,1:T(8,128)(2,1)S(1)}, bf16[192,3,192]{0,2,1:T(8,128)(2,1)S(1)}, u32[]{:S(2)}, u32[]{:S(2)}) collective-permute-start(bf16[192,3,192]{0,2,1:T(8,128)(2,1)S(1)} %get-tuple-element.34), channel_id=1, source_target_pairs={{0,128},{128,0},{1,129},{129,1},{2,130},{130,2},{3,131},{131,3},{4... | collective-permute-start | bytes 663560 | tf_op jit(solution)/shard_map/ppermute | solution.py:377

commit v10 on v9

--- a/solution.py
+++ b/solution.py
@@ -61,8 +61,27 @@
     finish_exchange(*start_exchange(x_ref, o_ref, send_sem, recv_sem, own_sem))
 
 
-def exchange_tables_kernel(x_ref, o_ref, cos_ref, sin_ref, send_sem, recv_sem, own_sem):
+def exchange_tables_kernel(
+    x_ref, filter_ref, o_ref, cos_ref, sin_ref, part_ref, send_sem, recv_sem, own_sem
+):
     pending = start_exchange(x_ref, o_ref, send_sem, recv_sem, own_sem)
+    section = lax.axis_index("section")
+    width = part_ref.shape[1]
+    step = 64
+
+    for half in range(filter_ref.shape[1] // width):
+
+        @pl.when(section == half)
+        def _():
+            def move(index, carry):
+                first = pl.multiple_of(index * step, step)
+                part_ref[pl.ds(first, step), :] = filter_ref[
+                    pl.ds(first, step), half * width : (half + 1) * width
+                ]
+                return carry
+
+            lax.fori_loop(0, part_ref.shape[0] // step, move, 0)
+
     length = cos_ref.shape[0]
     block = 16
 
@@ -90,20 +109,24 @@
     )(chunks)
 
 
-def exchange_with_tables(chunks, collective_id, length):
+def exchange_with_tables(chunks, filter_rows, collective_id, length):
     table = jax.ShapeDtypeStruct((length, length), jnp.bfloat16)
+    part = jax.ShapeDtypeStruct(
+        (filter_rows.shape[0], filter_rows.shape[1] // 2), filter_rows.dtype
+    )
     return pl.pallas_call(
         exchange_tables_kernel,
-        out_shape=(jax.ShapeDtypeStruct(chunks.shape, chunks.dtype), table, table),
-        in_specs=[pl.BlockSpec(memory_space=pl.ANY)],
+        out_shape=(jax.ShapeDtypeStruct(chunks.shape, chunks.dtype), table, table, part),
+        in_specs=[pl.BlockSpec(memory_space=pl.ANY), pl.BlockSpec(memory_space=pltpu.VMEM)],
         out_specs=(
             pl.BlockSpec(memory_space=pl.ANY),
+            pl.BlockSpec(memory_space=pltpu.VMEM),
             pl.BlockSpec(memory_space=pltpu.VMEM),
             pl.BlockSpec(memory_space=pltpu.VMEM),
         ),
         scratch_shapes=[pltpu.SemaphoreType.DMA(())] * 3,
         compiler_params=pltpu.CompilerParams(collective_id=collective_id, has_side_effects=True),
-    )(chunks)
+    )(chunks, filter_rows)
 
 
 def pad_chunks(chunks):
@@ -304,7 +327,9 @@
     tiles = lax.axis_size("tile")
     group_width, tile_rows = channels // tiles, normed_half.shape[1]
     slabs, length = pad_chunks(normed_half.reshape(tiles, -1))
-    slabs, cos_h, sin_h = exchange_with_tables(slabs, 0, full_rows)
+    filter_rows = spectral_filter.reshape(-1, field_cols)
+    slabs, cos_h, sin_h, kernel_part = exchange_with_tables(slabs, filter_rows, 0, full_rows)
+    kernel_part = kernel_part.reshape(spectral_filter.shape[:3] + (cell_half,))
     arrived = unpad_chunks(slabs, length)
     fields = (
         arrived.reshape(tiles, group_width, tile_rows, cell_half)
@@ -329,9 +354,6 @@
         [jnp.stack([cos_h, -sin_h], axis=1), jnp.stack([sin_h, cos_h], axis=1)], axis=0
     )
     norm_scale = 1.0 / (full_rows * field_cols)
-    kernel_part = lax.dynamic_slice_in_dim(
-        spectral_filter, section_index * cell_half, cell_half, 3
-    )
     own_start = section_index * cell_half
     other_start = (1 - section_index) * cell_half
     frequency_rows = jnp.einsum(

time: 112 us -> 112 us (level)
  other arithmetic: 10.3 us -> 6.89 us
  Pallas kernels: 47.2 us -> 49.6 us
  matrix products: 18.3 us -> 20 us
  local copies, waits for them, and re-layouts: 24.2 us -> 22.8 us
    pallas_call x1, Pallas kernels: 25.4 us -> 28.4 us  [exchange_with_tables(): pl.pallas_call(exchange_tables_kernel, out_shape=(jax.ShapeDtypeStruct(ch...]
    another operation x1, other arithmetic: 1.71 us -> 0.33 us
    dot_general x1, matrix products: 0.5 us -> 1.76 us  [local(): jnp.einsum('chx,xqw->chqw', fields, lax.dynamic_slice_in_dim(forward_tabl...]
  transfers between devices with their start and end apart: 4 -> 4, of which waited for: 2 -> 2; matrix products, arithmetic and copies ran while one was open for 13% -> 10% of each run, Pallas kernels for 0% -> 0%
where the time goes in v10:
time: 112 us
  Pallas kernels  49.6 us (44%)
  local copies, waits for them, and re-layouts  22.8 us (20%)
  matrix products  20 us (18%)
  starting transfers between devices  8.68 us (8%)
  other arithmetic  6.89 us (6%)
  waiting for transfers between devices  3.14 us (3%)
    pallas_call x1, Pallas kernels, exchange_with_tables(): pl.pallas_call(exchange_tables_kernel, out_shape=(jax.ShapeDtypeStruct(ch...  28.4 us
    pallas_call x1, Pallas kernels, exchange(): pl.pallas_call(exchange_kernel, out_shape=jax.ShapeDtypeStruct(chunks.sha...  21.2 us
    unnamed x45, local copies, waits for them, and re-layouts  6.71 us
    dot_general x2, matrix products, stem_layers(): jnp.einsum('zji,if->zjf', initial_layer, merging_matrix, preferred_elemen...  6.7 us
    ppermute x1, starting transfers between devices, from_behind(): return lax.ppermute(block, axis, route)  4.39 us
    dot_general x2, matrix products, spread_kernel(): full = jnp.dot(picked, repeat, preferred_element_type=jnp.float32)  3.82 us
    dot_general x1, matrix products, filter_columns(): jnp.einsum('puqh,chqw->cpuw', forward_h, row_spectrum, preferred_element_...  3.24 us
    ppermute x1, starting transfers between devices, local(): other_fields = lax.ppermute(fields, 'section', swap)  2.63 us
  transfers between devices with their start and end apart: 4, of which 2 were waited for; matrix products, arithmetic and copies ran while one was open for 10% of the time, Pallas kernels for 0%

profile of v10, /device:TPU:1, one launch (start us, length us, event | category | flops | bytes accessed | tf_op | source)
XLA Modules:
  0.0 111.5 jit_solution(17661278886478661824)
XLA Ops:
  0.0 1.2 %pad_dynamic-slice_fusion = bf16[1,193,768]{2,1,0:T(8,128)(2,1)S(1)} fusion(s32[]{:T(128)S(6)} %add.341, s32[]{:T(128)S(6)} %select_n.199, bf16[3,384,768]{2,1,0:T(8,128)(2,1)} %param.9), kind=kLoop, calls=%fused_computation.28 | loop fusion | bytes 2065928 | tf_op jit(solution)/shard_map/slice | solution.py:318
  1.2 4.4 %collective-permute-start = (bf16[1,193,768]{2,1,0:T(8,128)(2,1)S(1)}, bf16[1,193,768]{2,1,0:T(8,128)(2,1)S(1)}, u32[]{:S(2)}, u32[]{:S(2)}) collective-permute-start(bf16[1,193,768]{2,1,0:T(8,128)(2,1)S(1)} %pad_dynamic-slice_fusion), channel_id=1, source_target_pairs={{0,1},{1,2},{2,3},{3,4},{4,5},{5,6},{6,7},{7,8},{8,9},{9,10},{10,1... | collective-permute-start | bytes 889352 | tf_op jit(solution)/shard_map/ppermute | solution.py:153
  6.5 1.5 %slice_bitcast_fusion = (bf16[1,192,384]{2,1,0:T(8,128)(2,1)S(1)}, bf16[1,192,384]{2,1,0:T(8,128)(2,1)S(1)}, bf16[1,192,384]{2,1,0:T(8,128)(2,1)S(1)}, bf16[1,19...) fusion(bf16[3,3,192,384]{3,2,1,0:T(8,128)(2,1)} %param.14), kind=kLoop, calls=%fused_computation.180 | loop fusion | bytes 2654208 | tf_op jit(solution)/shard_map/stack;squeeze | solution.py:211
  8.2 0.9 stack.131
  9.3 0.9 pad_maximum_fusion.4
  10.2 2.2 %fusion.27 = bf16[384,768,1]{1,0,2:T(8,128)(2,1)} fusion(bf16[48,96]{1,0:T(8,128)(2,1)} %bitcast.180, s32[768]{0:T(1024)S(1)} %get-tuple-element.53, s32[384]{0:T(512)S(1)} %get-tuple-element.57, s32[768]{0:T(1024)S(1)} %get-tuple-element.51, s32[384]{0:T(512)S(1)} %get-tuple-element.58), kind=kOutput, calls=%fused_computation.58 | convolution fusion | flops 61175808 | bytes 608256 | tf_op jit(solution)/shard_map/dot_general | solution.py:174
  12.3 1.7 %fusion.26 = bf16[768,384,1]{1,0,2:T(8,128)(2,1)} fusion(bf16[384,192]{1,0:T(8,128)(2,1)S(1)} %bitcast.163, s32[768]{0:T(1024)S(1)} %get-tuple-element.54, s32[384]{0:T(512)S(1)} %get-tuple-element.56, s32[768]{0:T(1024)S(1)} %get-tuple-element.52, s32[384]{0:T(512)S(1)} %get-tuple-element.55), kind=kOutput, calls=%fused_computation.57 | convolution fusion | flops 227893248 | bytes 746496 | tf_op jit(solution)/shard_map/dot_general | solution.py:174
  14.1 1.0 fusion.108
  15.1 3.3 %fusion.35 = bf16[4,193,384]{2,1,0:T(8,128)(2,1)S(1)} fusion(bf16[768,384,1]{1,0,2:T(8,128)(2,1)} %fusion.26, bf16[384,768,1]{1,0,2:T(8,128)(2,1)} %fusion.27, f32[768]{0:T(1024)S(1)} %add.307, bf16[4,193,128]{2,1,0:T(8,128)(2,1)} %get-tuple-element.26, bf16[4,193,128]{2,1,0:T(8,128)(2,1)} %get-tuple-element.25, ...), kind=kOutput, calls=%fused_computation.66 | convolution fusion | flops 921360384 | bytes 2370048 | tf_op jit(solution)/shard_map/zji,if->zjf/dot_general | solution.py:242
  18.4 3.4 %fusion.43 = bf16[4,193,384]{2,1,0:T(8,128)(2,1)S(1)} fusion(bf16[768,384,1]{1,0,2:T(8,128)(2,1)} %fusion.26, bf16[384,768,1]{1,0,2:T(8,128)(2,1)} %fusion.27, f32[768]{0:T(1024)S(1)} %add.307, bf16[3,193,768]{2,1,0:T(8,128)(2,1)S(1)} %pad_dynamic-slice_fusion.1, bf16[1,193,768]{2,1,0:T(8,128)(2,1)} %copy-done.14, ...), kind=kOutput, calls=%fused_computation.74 | convolution fusion | flops 922842624 | bytes 3358208 | tf_op jit(solution)/shard_map/zji,if->zjf/dot_general | solution.py:242
  22.1 0.8 copy-done.12
  22.9 0.6 fusion.63
  23.5 0.6 convolution_add_fusion.4
  24.2 0.6 convolution_add_fusion.3
  24.8 0.4 copy-done.11
  25.2 0.8 convert_reduce_fusion
  26.6 0.9 copy.28
  27.5 0.5 reshape.340
  28.1 0.9 copy.66
  29.0 28.4 %shard_map.91 = (bf16[128,16,128]{2,1,0:T(8,128)(2,1)}, bf16[384,384]{1,0:T(8,128)(2,1)}, bf16[384,384]{1,0:T(8,128)(2,1)}, bf16[2304,192]{1,0:T(8,128)(2,1)}) custom-call(bf16[128,16,128]{2,1,0:T(8,128)(2,1)} %bitcast.170, bf16[2304,384]{1,0:T(8,128)(2,1)} %bitcast.175), custom_call_target="tpu_custom_call" | custom-call | tf_op jit(solution)/shard_map/pallas_call | solution.py:117
  57.4 1.4 %fusion.198 = (bf16[3,1,384,192]{3,2,1,0:T(8,128)(2,1)S(1)}, bf16[3,1,384,192]{3,2,1,0:T(8,128)(2,1)S(1)}) fusion(bf16[3,2,384,192]{3,2,1,0:T(8,128)(2,1)} %bitcast.176), kind=kLoop, calls=%fused_computation.304 | loop fusion | bytes 1769472 | tf_op jit(solution)/shard_map/slice | solution.py:284
  59.0 0.7 negate_bitcast_fusion
  59.8 0.8 fusion.127
  60.6 0.8 dynamic-slice_bitcast_fusion
  61.4 1.0 copy.65
  62.4 0.5 copy.56
  62.9 0.7 copy.31
  63.6 0.5 reshape.346
  64.2 1.0 copy.34
  65.2 2.6 %collective-permute-start.1 = (bf16[3,384,192]{1,2,0:T(8,128)(2,1)}, bf16[3,384,192]{1,2,0:T(8,128)(2,1)S(1)}, u32[]{:S(2)}, u32[]{:S(2)}) collective-permute-start(bf16[3,384,192]{1,2,0:T(8,128)(2,1)} %copy.34), channel_id=1, source_target_pairs={{0,128},{128,0},{1,129},{129,1},{2,130},{130,2},{3,131},{131,3},{4... | collective-permute-start | bytes 1327112 | tf_op jit(solution)/shard_map/ppermute | solution.py:340
  67.8 1.5 %fusion.97 = (bf16[1,384,2,384]{3,1,2,0:T(8,128)(2,1)}, bf16[1,384,2,384]{3,1,2,0:T(8,128)(2,1)}, bf16[1,384,2,384]{3,1,2,0:T(8,128)(2,1)}, bf16[1,384,2,384]{3,1,2,0:T(8,128)(2,1)}) fusion(bf16[384,1,384]{2,0,1:T(8,128)(2,1)S(1)} %bitcast.177, bf16[384,1,384]{2,0,1:T(8,128)(2,1)S(1)} %bitcast.167, bf16[384,1,384]{2,0,1:T(8,128)(2,1)S(1)} %copy-done.4), kind=kLoop, calls=%fused_computation.129 | loop fusion | flops 1179648 | bytes 3244032 | tf_op jit(solution)/shard_map/stack | solution.py:350
  69.3 1.8 %fusion.99 = f32[3,384,2,192]{1,3,2,0:T(8,128)} fusion(bf16[3,384,192]{2,1,0:T(8,128)(2,1)S(1)} %reshape.346, s32[]{:T(128)S(6)} %select_n.219, bf16[384,1,192]{2,0,1:T(8,128)(2,1)S(1)} %copy-done.8, bf16[384,1,192]{2,0,1:T(8,128)(2,1)S(1)} %copy-done.7), kind=kOutput, calls=%fused_computation.134 | convolution fusion | flops 170164224 | bytes 2506756 | tf_op jit(solution)/shard_map/chx,xqw->chqw/dot_general | solution.py:359
  71.1 0.8 copy-done.18
  71.9 3.2 %fusion.20 = bf16[3,2,384,192]{2,3,1,0:T(8,128)(2,1)S(1)} fusion(bf16[1,384,2,384]{3,1,2,0:T(8,128)(2,1)} %get-tuple-element.42, bf16[1,384,2,384]{3,1,2,0:T(8,128)(2,1)} %get-tuple-element.31, f32[3,384,2,192]{1,3,2,0:T(8,128)} %fusion.99, bf16[3,384,192]{1,2,0:T(8,128)(2,1)} %copy-done.18, s32[]{:T(128)S(6)} %select_n.220, ...), kind=kOutput, calls=%fused_computation.44 | convolution fusion | flops 853327872 | bytes 4571140 | tf_op jit(solution)/shard_map/puqh,chqw->cpuw/dot_general | solution.py:279
  75.5 0.7 copy-done.9
  76.4 0.9 fusion.21
  77.4 0.5 convolution_bitcast_fusion.1
  77.8 1.9 %collective-permute-done.2 = bf16[3,384,2,192]{1,3,2,0:T(8,128)(2,1)S(1)} collective-permute-done((bf16[3,384,2,192]{1,3,2,0:T(8,128)(2,1)S(1)}, bf16[3,384,2,192]{1,3,2,0:T(8,128)(2,1)S(1)}, u32[]{:S(2)}, u32[]{:S(2)}) %collective-permute-start.2) | collective-permute-done | bytes 884768 | tf_op jit(solution)/shard_map/ppermute | solution.py:373
  79.8 0.5 fusion.24
  80.9 0.8 copy.40
  81.7 1.2 %copy.63.x_ref = bf16[128,16,128]{2,1,0:T(8,128)(2,1)} copy(bf16[128,16,128]{0,2,1:T(8,128)(2,1)S(1)} %bitcast.168) | data formatting | bytes 1048576 | tf_op jit(solution)/shard_map/reshape | solution.py:146
  82.9 21.2 %shard_map.92 = bf16[128,16,128]{2,1,0:T(8,128)(2,1)} custom-call(bf16[128,16,128]{2,1,0:T(8,128)(2,1)} %copy.63.x_ref), custom_call_target="tpu_custom_call" | custom-call | tf_op jit(solution)/shard_map/pallas_call | solution.py:102
  104.1 1.2 %copy.69 = bf16[16,8,16,128]{3,1,2,0:T(8,128)(2,1)S(1)} copy(bf16[16,8,16,128]{3,2,1,0:T(8,128)(2,1)} %bitcast.169) | data formatting | bytes 1048576
  105.4 0.9 reshape.351
  106.3 0.9 copy.42
  107.5 1.6 %collective-permute-start.3 = (bf16[192,3,192]{0,2,1:T(8,128)(2,1)S(1)}, bf16[192,3,192]{0,2,1:T(8,128)(2,1)S(1)}, u32[]{:S(2)}, u32[]{:S(2)}) collective-permute-start(bf16[192,3,192]{0,2,1:T(8,128)(2,1)S(1)} %get-tuple-element.36), channel_id=1, source_target_pairs={{0,128},{128,0},{1,129},{129,1},{2,130},{130,2},{3,131},{131,3},{4... | collective-permute-start | bytes 663560 | tf_op jit(solution)/shard_map/ppermute | solution.py:399
  109.1 1.2 %collective-permute-done.3 = bf16[192,3,192]{0,2,1:T(8,128)(2,1)S(1)} collective-permute-done((bf16[192,3,192]{0,2,1:T(8,128)(2,1)S(1)}, bf16[192,3,192]{0,2,1:T(8,128)(2,1)S(1)}, u32[]{:S(2)}, u32[]{:S(2)}) %collective-permute-start.3) | collective-permute-done | bytes 221216 | tf_op jit(solution)/shard_map/ppermute | solution.py:399
  110.5 1.0 copy.43
  (72 shorter events, 4.5 us)
Async XLA Ops:
  0.0 12.3 %copy-start = (bf16[2,2,96,192]{3,2,1,0:T(8,128)(2,1)S(1)}, bf16[2,2,96,192]{3,2,1,0:T(8,128)(2,1)}, u32[]{:S(2)}) copy-start(bf16[2,2,96,192]{3,2,1,0:T(8,128)(2,1)} %param.12) | copy-start | bytes 442372
  0.0 5.7 %copy-start.1 = (bf16[3,384,768]{2,1,0:T(8,128)(2,1)S(1)}, bf16[3,384,768]{2,1,0:T(8,128)(2,1)}, u32[]{:S(2)}) copy-start(bf16[3,384,768]{2,1,0:T(8,128)(2,1)} %param.9) | copy-start | bytes 5308420
  1.2 12.9 %collective-permute-start = (bf16[1,193,768]{2,1,0:T(8,128)(2,1)S(1)}, bf16[1,193,768]{2,1,0:T(8,128)(2,1)S(1)}, u32[]{:S(2)}, u32[]{:S(2)}) collective-permute-start(bf16[1,193,768]{2,1,0:T(8,128)(2,1)S(1)} %pad_dynamic-slice_fusion), channel_id=1, source_target_pairs={{0,1},{1,2},{2,3},{3,4},{4,5},{5,6},{6,7},{7,8},{8,9},{9,10},{10,1... | collective-permute-start | bytes 889352 | tf_op jit(solution)/shard_map/ppermute | solution.py:153
  5.7 0.7 copy-start.16
  5.7 0.8 copy-start.17
  14.1 1.0 copy-start.14
  21.8 1.1 copy-start.12
  24.1 1.1 copy-start.11
  24.2 1.1 copy-start.19
  25.2 1.2 %copy-start.15 = (f32[384]{0:T(512)S(1)}, f32[384]{0:T(512)}, u32[]{:S(2)}) copy-start(f32[384]{0:T(512)} %param.16) | copy-start | bytes 4612
  57.4 1.7 %copy-start.2 = (bf16[384,384]{1,0:T(8,128)(2,1)S(1)}, bf16[384,384]{1,0:T(8,128)(2,1)}, u32[]{:S(2)}) copy-start(bf16[384,384]{1,0:T(8,128)(2,1)} %get-tuple-element.12) | copy-start | bytes 884740
  58.7 1.8 %copy-start.5 = (bf16[384,384]{1,0:T(8,128)(2,1)S(1)}, bf16[384,384]{1,0:T(8,128)(2,1)}, u32[]{:S(2)}) copy-start(bf16[384,384]{1,0:T(8,128)(2,1)} %get-tuple-element.11) | copy-start | bytes 884740
  59.8 2.6 %copy-start.13 = (bf16[128,16,128]{2,1,0:T(8,128)(2,1)S(1)}, bf16[128,16,128]{2,1,0:T(8,128)(2,1)}, u32[]{:S(2)}) copy-start(bf16[128,16,128]{2,1,0:T(8,128)(2,1)} %get-tuple-element.10) | copy-start | bytes 1572868
  63.6 4.2 %copy-start.4 = (bf16[384,1,384]{2,0,1:T(8,128)(2,1)S(1)}, bf16[384,1,384]{2,0,1:T(8,128)(2,1)}, u32[]{:S(2)}) copy-start(bf16[384,1,384]{2,0,1:T(8,128)(2,1)} %negate_bitcast_fusion) | copy-start | bytes 884740
  64.2 3.6 %copy-start.6 = (bf16[384,384]{1,0:T(8,128)(2,1)S(1)}, bf16[384,384]{1,0:T(8,128)(2,1)}, u32[]{:S(2)}) copy-start(bf16[384,384]{1,0:T(8,128)(2,1)} %get-tuple-element.11) | copy-start | bytes 884740
  65.2 5.9 %collective-permute-start.1 = (bf16[3,384,192]{1,2,0:T(8,128)(2,1)}, bf16[3,384,192]{1,2,0:T(8,128)(2,1)S(1)}, u32[]{:S(2)}, u32[]{:S(2)}) collective-permute-start(bf16[3,384,192]{1,2,0:T(8,128)(2,1)} %copy.34), channel_id=1, source_target_pairs={{0,128},{128,0},{1,129},{129,1},{2,130},{130,2},{3,131},{131,3},{4... | collective-permute-start | bytes 1327112 | tf_op jit(solution)/shard_map/ppermute | solution.py:340
  67.8 1.5 %copy-start.7 = (bf16[384,1,192]{2,0,1:T(8,128)(2,1)S(1)}, bf16[384,1,192]{2,0,1:T(8,128)(2,1)}, u32[]{:S(2)}) copy-start(bf16[384,1,192]{2,0,1:T(8,128)(2,1)} %get-tuple-element.38) | copy-start | bytes 442372
  67.8 1.5 %copy-start.8 = (bf16[384,1,192]{2,0,1:T(8,128)(2,1)S(1)}, bf16[384,1,192]{2,0,1:T(8,128)(2,1)}, u32[]{:S(2)}) copy-start(bf16[384,1,192]{2,0,1:T(8,128)(2,1)} %get-tuple-element.40) | copy-start | bytes 442372
  71.1 0.8 copy-start.18
  71.9 3.3 %copy-start.3 = (bf16[3,1,384,192]{2,3,1,0:T(8,128)(2,1)S(1)}, bf16[3,1,384,192]{2,3,1,0:T(8,128)(2,1)}, u32[]{:S(2)}) copy-start(bf16[3,1,384,192]{2,3,1,0:T(8,128)(2,1)} %copy.65) | copy-start | bytes 1327108
  75.1 1.1 copy-start.9
  75.1 1.2 %copy-start.10 = (bf16[1,384,2,384]{3,1,2,0:T(8,128)(2,1)S(1)}, bf16[1,384,2,384]{3,1,2,0:T(8,128)(2,1)}, u32[]{:S(2)}) copy-start(bf16[1,384,2,384]{3,1,2,0:T(8,128)(2,1)} %get-tuple-element.41) | copy-start | bytes 1769476
  77.3 2.5 %collective-permute-start.2 = (bf16[3,384,2,192]{1,3,2,0:T(8,128)(2,1)S(1)}, bf16[3,384,2,192]{1,3,2,0:T(8,128)(2,1)S(1)}, u32[]{:S(2)}, u32[]{:S(2)}) collective-permute-start(bf16[3,384,2,192]{1,3,2,0:T(8,128)(2,1)S(1)} %fusion.21), channel_id=1, source_target_pairs={{0,128},{128,0},{1,129},{129,1},{2,130},{130,2},{3,131},{131,3},{4... | collective-permute-start | bytes 2654216 | tf_op jit(solution)/shard_map/ppermute | solution.py:373
  107.5 2.8 %collective-permute-start.3 = (bf16[192,3,192]{0,2,1:T(8,128)(2,1)S(1)}, bf16[192,3,192]{0,2,1:T(8,128)(2,1)S(1)}, u32[]{:S(2)}, u32[]{:S(2)}) collective-permute-start(bf16[192,3,192]{0,2,1:T(8,128)(2,1)S(1)} %get-tuple-element.36), channel_id=1, source_target_pairs={{0,128},{128,0},{1,129},{129,1},{2,130},{130,2},{3,131},{131,3},{4... | collective-permute-start | bytes 663560 | tf_op jit(solution)/shard_map/ppermute | solution.py:399

commit v11 on v10

--- a/solution.py
+++ b/solution.py
@@ -62,7 +62,17 @@
 
 
 def exchange_tables_kernel(
-    x_ref, filter_ref, o_ref, cos_ref, sin_ref, part_ref, send_sem, recv_sem, own_sem
+    x_ref,
+    filter_ref,
+    o_ref,
+    cos_ref,
+    sin_ref,
+    part_ref,
+    cos_part_ref,
+    sin_part_ref,
+    send_sem,
+    recv_sem,
+    own_sem,
 ):
     pending = start_exchange(x_ref, o_ref, send_sem, recv_sem, own_sem)
     section = lax.axis_index("section")
@@ -95,6 +105,18 @@
         return carry
 
     lax.fori_loop(0, length // block, rows, 0)
+    cols, half = cos_part_ref.shape
+
+    def part_rows(index, carry):
+        first = pl.multiple_of(index * block, block)
+        row = lax.broadcasted_iota(jnp.int32, (block, half), 0) + first
+        col = lax.broadcasted_iota(jnp.int32, (block, half), 1) + section * half
+        angles = lax.rem(row * col, cols).astype(jnp.float32) * (2.0 * math.pi / cols)
+        cos_part_ref[pl.ds(first, block), :] = jnp.cos(angles).astype(cos_part_ref.dtype)
+        sin_part_ref[pl.ds(first, block), :] = jnp.sin(angles).astype(sin_part_ref.dtype)
+        return carry
+
+    lax.fori_loop(0, cols // block, part_rows, 0)
     finish_exchange(*pending)
 
 
@@ -116,10 +138,13 @@
     )
     return pl.pallas_call(
         exchange_tables_kernel,
-        out_shape=(jax.ShapeDtypeStruct(chunks.shape, chunks.dtype), table, table, part),
+        out_shape=(jax.ShapeDtypeStruct(chunks.shape, chunks.dtype), table, table, part)
+        + (jax.ShapeDtypeStruct((filter_rows.shape[1], part.shape[1]), jnp.bfloat16),) * 2,
         in_specs=[pl.BlockSpec(memory_space=pl.ANY), pl.BlockSpec(memory_space=pltpu.VMEM)],
         out_specs=(
             pl.BlockSpec(memory_space=pl.ANY),
+            pl.BlockSpec(memory_space=pltpu.VMEM),
+            pl.BlockSpec(memory_space=pltpu.VMEM),
             pl.BlockSpec(memory_space=pltpu.VMEM),
             pl.BlockSpec(memory_space=pltpu.VMEM),
             pl.BlockSpec(memory_space=pltpu.VMEM),
@@ -328,7 +353,9 @@
     group_width, tile_rows = channels // tiles, normed_half.shape[1]
     slabs, length = pad_chunks(normed_half.reshape(tiles, -1))
     filter_rows = spectral_filter.reshape(-1, field_cols)
-    slabs, cos_h, sin_h, kernel_part = exchange_with_tables(slabs, filter_rows, 0, full_rows)
+    slabs, cos_h, sin_h, kernel_part, cos_part, sin_part = exchange_with_tables(
+        slabs, filter_rows, 0, full_rows
+    )
     kernel_part = kernel_part.reshape(spectral_filter.shape[:3] + (cell_half,))
     arrived = unpad_chunks(slabs, length)
     fields = (
@@ -339,12 +366,6 @@
     swap = [(0, 1), (1, 0)]
     other_fields = lax.ppermute(fields, "section", swap)
 
-    if full_rows == field_cols:
-        cos_w, sin_w = cos_h, sin_h
-    else:
-        cos_w, sin_w = fourier_tables(field_cols)
-    cos_part = lax.dynamic_slice_in_dim(cos_w, section_index * cell_half, cell_half, 1)
-    sin_part = lax.dynamic_slice_in_dim(sin_w, section_index * cell_half, cell_half, 1)
     forward_table = jnp.stack([cos_part, -sin_part], axis=1)
     inverse_table = jnp.stack([cos_part, -sin_part], axis=0)
     forward_h = jnp.stack(

time: 112 us -> 111 us (level)
    another operation x1, other arithmetic: 0.33 us -> 1.71 us
    dot_general x1, matrix products: 1.76 us -> 0.5 us  [local(): jnp.einsum('chx,xqw->chqw', fields, lax.dynamic_slice_in_dim(forward_tabl...]
    unnamed x45 -> x43, local copies, waits for them, and re-layouts: 6.71 us -> 6.52 us
  transfers between devices with their start and end apart: 4 -> 4, of which waited for: 2 -> 2; matrix products, arithmetic and copies ran while one was open for 10% -> 9% of each run, Pallas kernels for 0% -> 0%
where the time goes in v11:
time: 111 us; the launch traced here: 110 us
  Pallas kernels  49.7 us (45%)
  local copies, waits for them, and re-layouts  21.8 us (20%)
  matrix products  19.2 us (17%)
  starting transfers between devices  8.69 us (8%)
  other arithmetic  7.47 us (7%)
  waiting for transfers between devices  3.14 us (3%)
    pallas_call x1, Pallas kernels, exchange_with_tables(): pl.pallas_call(exchange_tables_kernel, out_shape=(jax.ShapeDtypeStruct(ch...  28.5 us
    pallas_call x1, Pallas kernels, exchange(): pl.pallas_call(exchange_kernel, out_shape=jax.ShapeDtypeStruct(chunks.sha...  21.2 us
    dot_general x2, matrix products, stem_layers(): jnp.einsum('zji,if->zjf', initial_layer, merging_matrix, preferred_elemen...  6.71 us
    unnamed x43, local copies, waits for them, and re-layouts  6.52 us
    ppermute x1, starting transfers between devices, from_behind(): return lax.ppermute(block, axis, route)  4.39 us
    dot_general x2, matrix products, spread_kernel(): full = jnp.dot(picked, repeat, preferred_element_type=jnp.float32)  3.82 us
    dot_general x1, matrix products, filter_columns(): jnp.einsum('puqh,chqw->cpuw', forward_h, row_spectrum, preferred_element_...  3.67 us
    ppermute x1, starting transfers between devices, local(): other_fields = lax.ppermute(fields, 'section', swap)  2.61 us
  transfers between devices with their start and end apart: 4, of which 2 were waited for; matrix products, arithmetic and copies ran while one was open for 9% of the time, Pallas kernels for 0%

profile of v11, /device:TPU:1, one launch (start us, length us, event | category | flops | bytes accessed | tf_op | source)
XLA Modules:
  0.0 110.4 jit_solution(5638613431224677194)
XLA Ops:
  0.0 1.2 %pad_dynamic-slice_fusion = bf16[1,193,768]{2,1,0:T(8,128)(2,1)S(1)} fusion(s32[]{:T(128)S(6)} %add.339, s32[]{:T(128)S(6)} %select_n.197, bf16[3,384,768]{2,1,0:T(8,128)(2,1)} %param.9), kind=kLoop, calls=%fused_computation.28 | loop fusion | bytes 2065928 | tf_op jit(solution)/shard_map/slice | solution.py:343
  1.2 4.4 %collective-permute-start = (bf16[1,193,768]{2,1,0:T(8,128)(2,1)S(1)}, bf16[1,193,768]{2,1,0:T(8,128)(2,1)S(1)}, u32[]{:S(2)}, u32[]{:S(2)}) collective-permute-start(bf16[1,193,768]{2,1,0:T(8,128)(2,1)S(1)} %pad_dynamic-slice_fusion), channel_id=1, source_target_pairs={{0,1},{1,2},{2,3},{3,4},{4,5},{5,6},{6,7},{7,8},{8,9},{9,10},{10,1... | collective-permute-start | bytes 889352 | tf_op jit(solution)/shard_map/ppermute | solution.py:178
  6.0 0.4 copy-done.15
  6.5 1.5 %slice_bitcast_fusion = (bf16[1,192,384]{2,1,0:T(8,128)(2,1)S(1)}, bf16[1,192,384]{2,1,0:T(8,128)(2,1)S(1)}, bf16[1,192,384]{2,1,0:T(8,128)(2,1)S(1)}, bf16[1,19...) fusion(bf16[3,3,192,384]{3,2,1,0:T(8,128)(2,1)} %param.14), kind=kLoop, calls=%fused_computation.177 | loop fusion | bytes 2654208 | tf_op jit(solution)/shard_map/stack;squeeze | solution.py:236
  8.2 0.9 stack.131
  9.3 0.9 pad_maximum_fusion.4
  10.2 2.2 %fusion.27 = bf16[384,768,1]{1,0,2:T(8,128)(2,1)} fusion(bf16[48,96]{1,0:T(8,128)(2,1)} %bitcast.182, s32[768]{0:T(1024)S(1)} %get-tuple-element.55, s32[384]{0:T(512)S(1)} %get-tuple-element.59, s32[768]{0:T(1024)S(1)} %get-tuple-element.53, s32[384]{0:T(512)S(1)} %get-tuple-element.60), kind=kOutput, calls=%fused_computation.58 | convolution fusion | flops 61175808 | bytes 608256 | tf_op jit(solution)/shard_map/dot_general | solution.py:199
  12.4 1.7 %fusion.26 = bf16[768,384,1]{1,0,2:T(8,128)(2,1)} fusion(bf16[384,192]{1,0:T(8,128)(2,1)S(1)} %bitcast.161, s32[768]{0:T(1024)S(1)} %get-tuple-element.56, s32[384]{0:T(512)S(1)} %get-tuple-element.58, s32[768]{0:T(1024)S(1)} %get-tuple-element.54, s32[384]{0:T(512)S(1)} %get-tuple-element.57), kind=kOutput, calls=%fused_computation.57 | convolution fusion | flops 227893248 | bytes 746496 | tf_op jit(solution)/shard_map/dot_general | solution.py:199
  14.1 1.0 fusion.108
  15.1 3.3 %fusion.35 = bf16[4,193,384]{2,1,0:T(8,128)(2,1)S(1)} fusion(bf16[768,384,1]{1,0,2:T(8,128)(2,1)} %fusion.26, bf16[384,768,1]{1,0,2:T(8,128)(2,1)} %fusion.27, f32[768]{0:T(1024)S(1)} %add.305, bf16[4,193,128]{2,1,0:T(8,128)(2,1)} %get-tuple-element.30, bf16[4,193,128]{2,1,0:T(8,128)(2,1)} %get-tuple-element.29, ...), kind=kOutput, calls=%fused_computation.66 | convolution fusion | flops 921360384 | bytes 2370048 | tf_op jit(solution)/shard_map/zji,if->zjf/dot_general | solution.py:267
  18.4 3.4 %fusion.43 = bf16[4,193,384]{2,1,0:T(8,128)(2,1)S(1)} fusion(bf16[768,384,1]{1,0,2:T(8,128)(2,1)} %fusion.26, bf16[384,768,1]{1,0,2:T(8,128)(2,1)} %fusion.27, f32[768]{0:T(1024)S(1)} %add.305, bf16[3,193,768]{2,1,0:T(8,128)(2,1)S(1)} %pad_dynamic-slice_fusion.1, bf16[1,193,768]{2,1,0:T(8,128)(2,1)} %copy-done.11, ...), kind=kOutput, calls=%fused_computation.74 | convolution fusion | flops 922842624 | bytes 3358208 | tf_op jit(solution)/shard_map/zji,if->zjf/dot_general | solution.py:267
  22.1 0.8 copy-done.9
  22.9 0.6 fusion.63
  23.5 0.6 convolution_add_fusion.4
  24.2 0.6 convolution_add_fusion.3
  24.8 0.4 copy-done.8
  25.2 0.8 convert_reduce_fusion
  26.6 0.9 copy.28
  27.5 0.5 reshape.340
  28.0 0.9 copy.66
  29.0 28.5 %shard_map.91 = (bf16[128,16,128]{2,1,0:T(8,128)(2,1)}, bf16[384,384]{1,0:T(8,128)(2,1)}, bf16[384,384]{1,0:T(8,128)(2,1)}, bf16[2304,192]{1,0:T(8,128)(2,1)}, b...) custom-call(bf16[128,16,128]{2,1,0:T(8,128)(2,1)} %bitcast.167, bf16[2304,384]{1,0:T(8,128)(2,1)} %bitcast.176), custom_call_target="tpu_custom_call" | custom-call | tf_op jit(solution)/shard_map/pallas_call | solution.py:139
  57.5 1.4 %fusion.196 = (bf16[3,1,384,192]{3,2,1,0:T(8,128)(2,1)S(1)}, bf16[3,1,384,192]{3,2,1,0:T(8,128)(2,1)S(1)}) fusion(bf16[3,2,384,192]{3,2,1,0:T(8,128)(2,1)} %bitcast.178), kind=kLoop, calls=%fused_computation.301 | loop fusion | bytes 1769472 | tf_op jit(solution)/shard_map/slice | solution.py:309
  58.9 1.0 copy.64
  59.9 0.7 negate_bitcast_fusion.1
  60.6 1.0 copy.65
  61.6 0.5 copy.56
  62.1 0.7 copy.31
  62.9 0.5 reshape.346
  63.4 1.0 copy.34
  64.4 2.6 %collective-permute-start.1 = (bf16[3,384,192]{1,2,0:T(8,128)(2,1)}, bf16[3,384,192]{1,2,0:T(8,128)(2,1)S(1)}, u32[]{:S(2)}, u32[]{:S(2)}) collective-permute-start(bf16[3,384,192]{1,2,0:T(8,128)(2,1)} %copy.34), channel_id=1, source_target_pairs={{0,128},{128,0},{1,129},{129,1},{2,130},{130,2},{3,131},{131,3},{4... | collective-permute-start | bytes 1327112 | tf_op jit(solution)/shard_map/ppermute | solution.py:367
  67.0 1.5 %fusion.97 = (bf16[1,384,2,384]{3,1,2,0:T(8,128)(2,1)}, bf16[1,384,2,384]{3,1,2,0:T(8,128)(2,1)}, bf16[1,384,2,384]{3,1,2,0:T(8,128)(2,1)}, bf16[1,384,2,384]{3,1,2,0:T(8,128)(2,1)}) fusion(bf16[384,1,384]{2,0,1:T(8,128)(2,1)S(1)} %bitcast.181, bf16[384,1,384]{2,0,1:T(8,128)(2,1)S(1)} %bitcast.177, bf16[384,1,384]{2,0,1:T(8,128)(2,1)S(1)} %negate_bitcast_fusion), kind=kLoop, calls=%fused_computation.129 | loop fusion | flops 1179648 | bytes 3244032 | tf_op jit(solution)/shard_map/stack | solution.py:371
  68.5 0.5 fusion.99
  69.1 0.7 copy-done.17
  69.8 3.7 %fusion.20 = bf16[3,2,384,192]{2,3,1,0:T(8,128)(2,1)} fusion(bf16[1,384,2,384]{3,1,2,0:T(8,128)(2,1)} %get-tuple-element.42, bf16[1,384,2,384]{3,1,2,0:T(8,128)(2,1)} %get-tuple-element.35, f32[3,384,2,192]{1,3,2,0:T(8,128)S(1)} %fusion.99, bf16[3,384,192]{1,2,0:T(8,128)(2,1)} %copy-done.17, s32[]{:T(128)S(6)} %select_n.218, ...), kind=kOutput, calls=%fused_computation.44 | convolution fusion | flops 853327872 | bytes 4571140 | tf_op jit(solution)/shard_map/puqh,chqw->cpuw/dot_general | solution.py:304
  73.5 1.7 %fusion.56 = (bf16[3,1,384,192]{2,3,1,0:T(8,128)(2,1)S(1)}, bf16[3,1,384,192]{2,3,1,0:T(8,128)(2,1)S(1)}) fusion(bf16[3,1,384,192]{2,3,1,0:T(8,128)(2,1)S(1)} %copy-done.3, bf16[3,1,384,192]{2,3,1,0:T(8,128)(2,1)} %copy.65, bf16[3,2,384,192]{2,3,1,0:T(8,128)(2,1)} %fusion.20), kind=kLoop, calls=%fused_computation.98 | loop fusion | flops 2654208 | bytes 2654208 | tf_op jit(solution)/shard_map/convert.1
  75.2 0.9 fusion.21
  76.2 0.5 convolution_bitcast_fusion.1
  76.7 1.9 %collective-permute-done.2 = bf16[3,384,2,192]{1,3,2,0:T(8,128)(2,1)S(1)} collective-permute-done((bf16[3,384,2,192]{1,3,2,0:T(8,128)(2,1)S(1)}, bf16[3,384,2,192]{1,3,2,0:T(8,128)(2,1)S(1)}, u32[]{:S(2)}, u32[]{:S(2)}) %collective-permute-start.2) | collective-permute-done | bytes 884768 | tf_op jit(solution)/shard_map/ppermute | solution.py:394
  78.6 0.5 fusion.24
  79.7 0.8 copy.40
  80.6 1.2 %copy.63.x_ref = bf16[128,16,128]{2,1,0:T(8,128)(2,1)} copy(bf16[128,16,128]{0,2,1:T(8,128)(2,1)S(1)} %bitcast.165) | data formatting | bytes 1048576 | tf_op jit(solution)/shard_map/reshape | solution.py:171
  81.8 21.2 %shard_map.92 = bf16[128,16,128]{2,1,0:T(8,128)(2,1)} custom-call(bf16[128,16,128]{2,1,0:T(8,128)(2,1)} %copy.63.x_ref), custom_call_target="tpu_custom_call" | custom-call | tf_op jit(solution)/shard_map/pallas_call | solution.py:124
  103.0 1.2 %copy.69 = bf16[16,8,16,128]{3,1,2,0:T(8,128)(2,1)S(1)} copy(bf16[16,8,16,128]{3,2,1,0:T(8,128)(2,1)} %bitcast.166) | data formatting | bytes 1048576
  104.2 0.9 reshape.351
  105.2 0.9 copy.42
  106.4 1.6 %collective-permute-start.3 = (bf16[192,3,192]{0,2,1:T(8,128)(2,1)S(1)}, bf16[192,3,192]{0,2,1:T(8,128)(2,1)S(1)}, u32[]{:S(2)}, u32[]{:S(2)}) collective-permute-start(bf16[192,3,192]{0,2,1:T(8,128)(2,1)S(1)} %get-tuple-element.40), channel_id=1, source_target_pairs={{0,128},{128,0},{1,129},{129,1},{2,130},{130,2},{3,131},{131,3},{4... | collective-permute-start | bytes 663560 | tf_op jit(solution)/shard_map/ppermute | solution.py:420
  108.0 1.2 %collective-permute-done.3 = bf16[192,3,192]{0,2,1:T(8,128)(2,1)S(1)} collective-permute-done((bf16[192,3,192]{0,2,1:T(8,128)(2,1)S(1)}, bf16[192,3,192]{0,2,1:T(8,128)(2,1)S(1)}, u32[]{:S(2)}, u32[]{:S(2)}) %collective-permute-start.3) | collective-permute-done | bytes 221216 | tf_op jit(solution)/shard_map/ppermute | solution.py:420
  109.4 1.0 copy.43
  (69 shorter events, 3.3 us)
Async XLA Ops:
  0.0 12.4 %copy-start = (bf16[2,2,96,192]{3,2,1,0:T(8,128)(2,1)S(1)}, bf16[2,2,96,192]{3,2,1,0:T(8,128)(2,1)}, u32[]{:S(2)}) copy-start(bf16[2,2,96,192]{3,2,1,0:T(8,128)(2,1)} %param.12) | copy-start | bytes 442372
  0.0 5.7 %copy-start.1 = (bf16[3,384,768]{2,1,0:T(8,128)(2,1)S(1)}, bf16[3,384,768]{2,1,0:T(8,128)(2,1)}, u32[]{:S(2)}) copy-start(bf16[3,384,768]{2,1,0:T(8,128)(2,1)} %param.9) | copy-start | bytes 5308420
  1.2 12.9 %collective-permute-start = (bf16[1,193,768]{2,1,0:T(8,128)(2,1)S(1)}, bf16[1,193,768]{2,1,0:T(8,128)(2,1)S(1)}, u32[]{:S(2)}, u32[]{:S(2)}) collective-permute-start(bf16[1,193,768]{2,1,0:T(8,128)(2,1)S(1)} %pad_dynamic-slice_fusion), channel_id=1, source_target_pairs={{0,1},{1,2},{2,3},{3,4},{4,5},{5,6},{6,7},{7,8},{8,9},{9,10},{10,1... | collective-permute-start | bytes 889352 | tf_op jit(solution)/shard_map/ppermute | solution.py:178
  5.7 0.7 copy-start.15
  5.7 0.8 copy-start.16
  14.1 1.0 copy-start.11
  21.8 1.1 copy-start.9
  24.1 1.1 copy-start.8
  24.1 1.1 copy-start.18
  25.2 1.2 %copy-start.14 = (f32[384]{0:T(512)S(1)}, f32[384]{0:T(512)}, u32[]{:S(2)}) copy-start(f32[384]{0:T(512)} %param.16) | copy-start | bytes 4612
  57.5 2.4 %copy-start.4 = (bf16[384,384]{1,0:T(8,128)(2,1)S(1)}, bf16[384,384]{1,0:T(8,128)(2,1)}, u32[]{:S(2)}) copy-start(bf16[384,384]{1,0:T(8,128)(2,1)} %get-tuple-element.16) | copy-start | bytes 884740
  58.9 1.0 copy-start.13
  59.9 1.8 %copy-start.10 = (bf16[128,16,128]{2,1,0:T(8,128)(2,1)S(1)}, bf16[128,16,128]{2,1,0:T(8,128)(2,1)}, u32[]{:S(2)}) copy-start(bf16[128,16,128]{2,1,0:T(8,128)(2,1)} %get-tuple-element.12) | copy-start | bytes 1572868
  62.9 4.2 %copy-start.12 = (bf16[384,384]{1,0:T(8,128)(2,1)S(1)}, bf16[384,384]{1,0:T(8,128)(2,1)}, u32[]{:S(2)}) copy-start(bf16[384,384]{1,0:T(8,128)(2,1)} %get-tuple-element.15) | copy-start | bytes 884740
  64.4 4.6 %collective-permute-start.1 = (bf16[3,384,192]{1,2,0:T(8,128)(2,1)}, bf16[3,384,192]{1,2,0:T(8,128)(2,1)S(1)}, u32[]{:S(2)}, u32[]{:S(2)}) collective-permute-start(bf16[3,384,192]{1,2,0:T(8,128)(2,1)} %copy.34), channel_id=1, source_target_pairs={{0,128},{128,0},{1,129},{129,1},{2,130},{130,2},{3,131},{131,3},{4... | collective-permute-start | bytes 1327112 | tf_op jit(solution)/shard_map/ppermute | solution.py:367
  67.0 1.5 %copy-start.2 = (bf16[384,192]{1,0:T(8,128)(2,1)S(1)}, bf16[384,192]{1,0:T(8,128)(2,1)}, u32[]{:S(2)}) copy-start(bf16[384,192]{1,0:T(8,128)(2,1)} %get-tuple-element.13) | copy-start | bytes 442372
  67.0 1.5 %copy-start.5 = (bf16[384,1,192]{2,0,1:T(8,128)(2,1)S(1)}, bf16[384,1,192]{2,0,1:T(8,128)(2,1)}, u32[]{:S(2)}) copy-start(bf16[384,1,192]{2,0,1:T(8,128)(2,1)} %get-tuple-element.44) | copy-start | bytes 442372
  69.0 0.8 copy-start.17
  69.8 3.7 %copy-start.3 = (bf16[3,1,384,192]{2,3,1,0:T(8,128)(2,1)S(1)}, bf16[3,1,384,192]{2,3,1,0:T(8,128)(2,1)}, u32[]{:S(2)}) copy-start(bf16[3,1,384,192]{2,3,1,0:T(8,128)(2,1)} %copy.64) | copy-start | bytes 1327108
  73.5 1.7 %copy-start.6 = (bf16[1,384,2,384]{3,1,2,0:T(8,128)(2,1)S(1)}, bf16[1,384,2,384]{3,1,2,0:T(8,128)(2,1)}, u32[]{:S(2)}) copy-start(bf16[1,384,2,384]{3,1,2,0:T(8,128)(2,1)} %get-tuple-element.36) | copy-start | bytes 1769476
  73.5 1.7 %copy-start.7 = (bf16[1,384,2,384]{3,1,2,0:T(8,128)(2,1)S(1)}, bf16[1,384,2,384]{3,1,2,0:T(8,128)(2,1)}, u32[]{:S(2)}) copy-start(bf16[1,384,2,384]{3,1,2,0:T(8,128)(2,1)} %get-tuple-element.41) | copy-start | bytes 1769476
  76.1 2.5 %collective-permute-start.2 = (bf16[3,384,2,192]{1,3,2,0:T(8,128)(2,1)S(1)}, bf16[3,384,2,192]{1,3,2,0:T(8,128)(2,1)S(1)}, u32[]{:S(2)}, u32[]{:S(2)}) collective-permute-start(bf16[3,384,2,192]{1,3,2,0:T(8,128)(2,1)S(1)} %fusion.21), channel_id=1, source_target_pairs={{0,128},{128,0},{1,129},{129,1},{2,130},{130,2},{3,131},{131,3},{4... | collective-permute-start | bytes 2654216 | tf_op jit(solution)/shard_map/ppermute | solution.py:394
  106.4 2.8 %collective-permute-start.3 = (bf16[192,3,192]{0,2,1:T(8,128)(2,1)S(1)}, bf16[192,3,192]{0,2,1:T(8,128)(2,1)S(1)}, u32[]{:S(2)}, u32[]{:S(2)}) collective-permute-start(bf16[192,3,192]{0,2,1:T(8,128)(2,1)S(1)} %get-tuple-element.40), channel_id=1, source_target_pairs={{0,128},{128,0},{1,129},{129,1},{2,130},{130,2},{3,131},{131,3},{4... | collective-permute-start | bytes 663560 | tf_op jit(solution)/shard_map/ppermute | solution.py:420

commit v12 on v11

--- a/solution.py
+++ b/solution.py
@@ -67,9 +67,10 @@
     o_ref,
     cos_ref,
     sin_ref,
+    negated_ref,
     part_ref,
     cos_part_ref,
-    sin_part_ref,
+    negated_part_ref,
     send_sem,
     recv_sem,
     own_sem,
@@ -101,7 +102,9 @@
         col = lax.broadcasted_iota(jnp.int32, (block, length), 1)
         angles = lax.rem(row * col, length).astype(jnp.float32) * (2.0 * math.pi / length)
         cos_ref[pl.ds(first, block), :] = jnp.cos(angles).astype(cos_ref.dtype)
-        sin_ref[pl.ds(first, block), :] = jnp.sin(angles).astype(sin_ref.dtype)
+        sines = jnp.sin(angles)
+        sin_ref[pl.ds(first, block), :] = sines.astype(sin_ref.dtype)
+        negated_ref[pl.ds(first, block), :] = (-sines).astype(negated_ref.dtype)
         return carry
 
     lax.fori_loop(0, length // block, rows, 0)
@@ -113,7 +116,7 @@
         col = lax.broadcasted_iota(jnp.int32, (block, half), 1) + section * half
         angles = lax.rem(row * col, cols).astype(jnp.float32) * (2.0 * math.pi / cols)
         cos_part_ref[pl.ds(first, block), :] = jnp.cos(angles).astype(cos_part_ref.dtype)
-        sin_part_ref[pl.ds(first, block), :] = jnp.sin(angles).astype(sin_part_ref.dtype)
+        negated_part_ref[pl.ds(first, block), :] = (-jnp.sin(angles)).astype(negated_part_ref.dtype)
         return carry
 
     lax.fori_loop(0, cols // block, part_rows, 0)
@@ -138,11 +141,12 @@
     )
     return pl.pallas_call(
         exchange_tables_kernel,
-        out_shape=(jax.ShapeDtypeStruct(chunks.shape, chunks.dtype), table, table, part)
+        out_shape=(jax.ShapeDtypeStruct(chunks.shape, chunks.dtype), table, table, table, part)
         + (jax.ShapeDtypeStruct((filter_rows.shape[1], part.shape[1]), jnp.bfloat16),) * 2,
         in_specs=[pl.BlockSpec(memory_space=pl.ANY), pl.BlockSpec(memory_space=pltpu.VMEM)],
         out_specs=(
             pl.BlockSpec(memory_space=pl.ANY),
+            pl.BlockSpec(memory_space=pltpu.VMEM),
             pl.BlockSpec(memory_space=pltpu.VMEM),
             pl.BlockSpec(memory_space=pltpu.VMEM),
             pl.BlockSpec(memory_space=pltpu.VMEM),
@@ -353,7 +357,7 @@
     group_width, tile_rows = channels // tiles, normed_half.shape[1]
     slabs, length = pad_chunks(normed_half.reshape(tiles, -1))
     filter_rows = spectral_filter.reshape(-1, field_cols)
-    slabs, cos_h, sin_h, kernel_part, cos_part, sin_part = exchange_with_tables(
+    slabs, cos_h, sin_h, negated_h, kernel_part, cos_part, negated_part = exchange_with_tables(
         slabs, filter_rows, 0, full_rows
     )
     kernel_part = kernel_part.reshape(spectral_filter.shape[:3] + (cell_half,))
@@ -366,13 +370,13 @@
     swap = [(0, 1), (1, 0)]
     other_fields = lax.ppermute(fields, "section", swap)
 
-    forward_table = jnp.stack([cos_part, -sin_part], axis=1)
-    inverse_table = jnp.stack([cos_part, -sin_part], axis=0)
+    forward_table = jnp.stack([cos_part, negated_part], axis=1)
+    inverse_table = jnp.stack([cos_part, negated_part], axis=0)
     forward_h = jnp.stack(
-        [jnp.stack([cos_h, sin_h], axis=1), jnp.stack([-sin_h, cos_h], axis=1)], axis=0
+        [jnp.stack([cos_h, sin_h], axis=1), jnp.stack([negated_h, cos_h], axis=1)], axis=0
     )
     inverse_h = jnp.stack(
-        [jnp.stack([cos_h, -sin_h], axis=1), jnp.stack([sin_h, cos_h], axis=1)], axis=0
+        [jnp.stack([cos_h, negated_h], axis=1), jnp.stack([sin_h, cos_h], axis=1)], axis=0
     )
     norm_scale = 1.0 / (full_rows * field_cols)
     own_start = section_index * cell_half

time: 111 us -> 110 us (level)
    another operation x4 -> x2, other arithmetic: 3.94 us -> 3.19 us
    unnamed x43 -> x45, local copies, waits for them, and re-layouts: 6.52 us -> 6.13 us
where the time goes in v12:
time: 110 us
  Pallas kernels  50.6 us (46%)
  local copies, waits for them, and re-layouts  21.3 us (19%)
  matrix products  18.4 us (17%)
  starting transfers between devices  8.87 us (8%)
  other arithmetic  6.72 us (6%)
  waiting for transfers between devices  3.13 us (3%)
    pallas_call x1, Pallas kernels, exchange_with_tables(): pl.pallas_call(exchange_tables_kernel, out_shape=(jax.ShapeDtypeStruct(ch...  29.5 us
    pallas_call x1, Pallas kernels, exchange(): pl.pallas_call(exchange_kernel, out_shape=jax.ShapeDtypeStruct(chunks.sha...  21.1 us
    dot_general x2, matrix products, stem_layers(): jnp.einsum('zji,if->zjf', initial_layer, merging_matrix, preferred_elemen...  6.71 us
    unnamed x45, local copies, waits for them, and re-layouts  6.13 us
    ppermute x1, starting transfers between devices, from_behind(): return lax.ppermute(block, axis, route)  4.39 us
    dot_general x1, matrix products, filter_columns(): jnp.einsum('puqh,chqw->cpuw', forward_h, row_spectrum, preferred_element_...  3.63 us
    ppermute x1, starting transfers between devices, local(): other_fields = lax.ppermute(fields, 'section', swap)  3.12 us
    dot_general x2, matrix products, spread_kernel(): full = jnp.dot(picked, repeat, preferred_element_type=jnp.float32)  3.12 us
  transfers between devices with their start and end apart: 4, of which 2 were waited for; matrix products, arithmetic and copies ran while one was open for 9% of the time, Pallas kernels for 0%

profile of v12, /device:TPU:1, one launch (start us, length us, event | category | flops | bytes accessed | tf_op | source)
XLA Modules:
  0.0 109.5 jit_solution(11396788779013456554)
XLA Ops:
  0.0 1.2 %pad_dynamic-slice_fusion = bf16[1,193,768]{2,1,0:T(8,128)(2,1)S(1)} fusion(s32[]{:T(128)S(6)} %add.339, s32[]{:T(128)S(6)} %select_n.197, bf16[3,384,768]{2,1,0:T(8,128)(2,1)} %param.9), kind=kLoop, calls=%fused_computation.28 | loop fusion | bytes 2065928 | tf_op jit(solution)/shard_map/slice | solution.py:347
  1.2 4.4 %collective-permute-start = (bf16[1,193,768]{2,1,0:T(8,128)(2,1)S(1)}, bf16[1,193,768]{2,1,0:T(8,128)(2,1)S(1)}, u32[]{:S(2)}, u32[]{:S(2)}) collective-permute-start(bf16[1,193,768]{2,1,0:T(8,128)(2,1)S(1)} %pad_dynamic-slice_fusion), channel_id=1, source_target_pairs={{0,1},{1,2},{2,3},{3,4},{4,5},{5,6},{6,7},{7,8},{8,9},{9,10},{10,1... | collective-permute-start | bytes 889352 | tf_op jit(solution)/shard_map/ppermute | solution.py:182
  6.0 1.5 %slice_bitcast_fusion = (bf16[1,192,384]{2,1,0:T(8,128)(2,1)S(1)}, bf16[1,192,384]{2,1,0:T(8,128)(2,1)S(1)}, bf16[1,192,384]{2,1,0:T(8,128)(2,1)S(1)}, bf16[1,19...) fusion(bf16[3,3,192,384]{3,2,1,0:T(8,128)(2,1)} %param.14), kind=kLoop, calls=%fused_computation.174 | loop fusion | bytes 2654208 | tf_op jit(solution)/shard_map/stack;squeeze | solution.py:240
  7.8 0.9 stack.131
  8.7 0.9 pad_maximum_fusion.4
  9.8 1.7 %fusion.26 = bf16[768,384,1]{1,0,2:T(8,128)(2,1)} fusion(bf16[384,192]{1,0:T(8,128)(2,1)S(1)} %bitcast.158, s32[768]{0:T(1024)S(1)} %get-tuple-element.56, s32[384]{0:T(512)S(1)} %get-tuple-element.58, s32[768]{0:T(1024)S(1)} %get-tuple-element.54, s32[384]{0:T(512)S(1)} %get-tuple-element.57), kind=kOutput, calls=%fused_computation.57 | convolution fusion | flops 227893248 | bytes 746496 | tf_op jit(solution)/shard_map/dot_general | solution.py:203
  11.5 1.5 %fusion.27 = bf16[384,768,1]{1,0,2:T(8,128)(2,1)} fusion(bf16[48,96]{1,0:T(8,128)(2,1)S(1)} %bitcast.184, s32[768]{0:T(1024)S(1)} %get-tuple-element.55, s32[384]{0:T(512)S(1)} %get-tuple-element.59, s32[768]{0:T(1024)S(1)} %get-tuple-element.53, s32[384]{0:T(512)S(1)} %get-tuple-element.60), kind=kOutput, calls=%fused_computation.58 | convolution fusion | flops 61175808 | bytes 608256 | tf_op jit(solution)/shard_map/dot_general | solution.py:203
  13.0 1.0 fusion.108
  14.0 3.3 %fusion.35 = bf16[4,193,384]{2,1,0:T(8,128)(2,1)S(1)} fusion(bf16[768,384,1]{1,0,2:T(8,128)(2,1)} %fusion.26, bf16[384,768,1]{1,0,2:T(8,128)(2,1)} %fusion.27, f32[768]{0:T(1024)S(1)} %add.305, bf16[4,193,128]{2,1,0:T(8,128)(2,1)} %get-tuple-element.32, bf16[4,193,128]{2,1,0:T(8,128)(2,1)} %get-tuple-element.31, ...), kind=kOutput, calls=%fused_computation.66 | convolution fusion | flops 921360384 | bytes 2370048 | tf_op jit(solution)/shard_map/zji,if->zjf/dot_general | solution.py:271
  17.4 3.4 %fusion.43 = bf16[4,193,384]{2,1,0:T(8,128)(2,1)S(1)} fusion(bf16[768,384,1]{1,0,2:T(8,128)(2,1)} %fusion.26, bf16[384,768,1]{1,0,2:T(8,128)(2,1)} %fusion.27, f32[768]{0:T(1024)S(1)} %add.305, bf16[3,193,768]{2,1,0:T(8,128)(2,1)S(1)} %pad_dynamic-slice_fusion.1, bf16[1,193,768]{2,1,0:T(8,128)(2,1)} %copy-done.10, ...), kind=kOutput, calls=%fused_computation.74 | convolution fusion | flops 922842624 | bytes 3358208 | tf_op jit(solution)/shard_map/zji,if->zjf/dot_general | solution.py:271
  21.0 0.8 copy-done.8
  21.8 0.6 fusion.63
  22.4 0.6 convolution_add_fusion.4
  23.1 0.6 convolution_add_fusion.3
  23.7 0.4 copy-done.7
  24.1 0.8 convert_reduce_fusion
  24.9 0.4 fusion.54
  25.5 0.9 copy.28
  26.4 0.5 reshape.340
  27.0 0.9 copy.66
  27.9 29.5 %shard_map.91 = (bf16[128,16,128]{2,1,0:T(8,128)(2,1)}, bf16[384,384]{1,0:T(8,128)(2,1)}, bf16[384,384]{1,0:T(8,128)(2,1)}, bf16[384,384]{1,0:T(8,128)(2,1)}, bf...) custom-call(bf16[128,16,128]{2,1,0:T(8,128)(2,1)} %bitcast.164, ...), custom_call_target="tpu_custom_call" | custom-call | tf_op jit(solution)/shard_map/pallas_call | solution.py:142
  57.3 1.3 %fusion.196 = (bf16[3,1,384,192]{3,2,1,0:T(8,128)(2,1)S(1)}, bf16[3,1,384,192]{3,2,1,0:T(8,128)(2,1)S(1)}) fusion(bf16[3,2,384,192]{3,2,1,0:T(8,128)(2,1)} %bitcast.178), kind=kLoop, calls=%fused_computation.298 | loop fusion | bytes 1769472 | tf_op jit(solution)/shard_map/slice | solution.py:313
  58.7 1.0 copy.64
  59.7 1.0 copy.65
  60.7 0.5 copy.56
  61.2 0.7 copy.31
  62.0 0.5 reshape.346
  62.5 1.0 copy.34
  63.5 3.1 %collective-permute-start.1 = (bf16[3,384,192]{1,2,0:T(8,128)(2,1)}, bf16[3,384,192]{1,2,0:T(8,128)(2,1)S(1)}, u32[]{:S(2)}, u32[]{:S(2)}) collective-permute-start(bf16[3,384,192]{1,2,0:T(8,128)(2,1)} %copy.34), channel_id=1, source_target_pairs={{0,128},{128,0},{1,129},{129,1},{2,130},{130,2},{3,131},{131,3},{4... | collective-permute-start | bytes 1327112 | tf_op jit(solution)/shard_map/ppermute | solution.py:371
  66.6 1.5 %fusion.97 = (bf16[1,384,2,384]{3,1,2,0:T(8,128)(2,1)}, bf16[1,384,2,384]{3,1,2,0:T(8,128)(2,1)}, bf16[1,384,2,384]{3,1,2,0:T(8,128)(2,1)}, bf16[1,384,2,384]{3,1,2,0:T(8,128)(2,1)}) fusion(bf16[384,1,384]{2,0,1:T(8,128)(2,1)S(1)} %bitcast.181, bf16[384,1,384]{2,0,1:T(8,128)(2,1)S(1)} %bitcast.182, bf16[384,1,384]{2,0,1:T(8,128)(2,1)S(1)} %bitcast.183), kind=kLoop, calls=%fused_computation.129 | loop fusion | flops 1179648 | bytes 3244032 | tf_op jit(solution)/shard_map/stack | solution.py:375
  68.1 0.5 fusion.99
  68.7 0.7 copy-done.17
  69.4 3.6 %fusion.20 = bf16[3,2,384,192]{2,3,1,0:T(8,128)(2,1)} fusion(bf16[1,384,2,384]{3,1,2,0:T(8,128)(2,1)} %get-tuple-element.44, bf16[1,384,2,384]{3,1,2,0:T(8,128)(2,1)} %get-tuple-element.37, f32[3,384,2,192]{1,3,2,0:T(8,128)S(1)} %fusion.99, bf16[3,384,192]{1,2,0:T(8,128)(2,1)} %copy-done.17, s32[]{:T(128)S(6)} %select_n.218, ...), kind=kOutput, calls=%fused_computation.44 | convolution fusion | flops 853327872 | bytes 4571140 | tf_op jit(solution)/shard_map/puqh,chqw->cpuw/dot_general | solution.py:308
  73.0 1.7 %fusion.56 = (bf16[3,1,384,192]{2,3,1,0:T(8,128)(2,1)S(1)}, bf16[3,1,384,192]{2,3,1,0:T(8,128)(2,1)S(1)}) fusion(bf16[3,1,384,192]{2,3,1,0:T(8,128)(2,1)S(1)} %copy-done.4, bf16[3,1,384,192]{2,3,1,0:T(8,128)(2,1)} %copy.65, bf16[3,2,384,192]{2,3,1,0:T(8,128)(2,1)} %fusion.20), kind=kLoop, calls=%fused_computation.98 | loop fusion | flops 2654208 | bytes 2654208 | tf_op jit(solution)/shard_map/convert.1
  74.8 0.9 fusion.21
  75.8 0.5 convolution_bitcast_fusion.1
  76.2 1.9 %collective-permute-done.2 = bf16[3,384,2,192]{1,3,2,0:T(8,128)(2,1)S(1)} collective-permute-done((bf16[3,384,2,192]{1,3,2,0:T(8,128)(2,1)S(1)}, bf16[3,384,2,192]{1,3,2,0:T(8,128)(2,1)S(1)}, u32[]{:S(2)}, u32[]{:S(2)}) %collective-permute-start.2) | collective-permute-done | bytes 884768 | tf_op jit(solution)/shard_map/ppermute | solution.py:398
  78.2 0.5 fusion.24
  78.9 0.4 reshape.347
  79.3 0.8 copy.40
  80.1 1.2 %copy.63.x_ref = bf16[128,16,128]{2,1,0:T(8,128)(2,1)} copy(bf16[128,16,128]{0,2,1:T(8,128)(2,1)S(1)} %bitcast.162) | data formatting | bytes 1048576 | tf_op jit(solution)/shard_map/reshape | solution.py:175
  81.3 21.1 %shard_map.92 = bf16[128,16,128]{2,1,0:T(8,128)(2,1)} custom-call(bf16[128,16,128]{2,1,0:T(8,128)(2,1)} %copy.63.x_ref), custom_call_target="tpu_custom_call" | custom-call | tf_op jit(solution)/shard_map/pallas_call | solution.py:127
  102.4 1.2 %copy.69 = bf16[16,8,16,128]{3,1,2,0:T(8,128)(2,1)S(1)} copy(bf16[16,8,16,128]{3,2,1,0:T(8,128)(2,1)} %bitcast.163) | data formatting | bytes 1048576
  103.7 0.9 reshape.351
  104.6 0.9 copy.42
  105.8 1.2 %collective-permute-start.3 = (bf16[192,3,192]{0,2,1:T(8,128)(2,1)S(1)}, bf16[192,3,192]{0,2,1:T(8,128)(2,1)S(1)}, u32[]{:S(2)}, u32[]{:S(2)}) collective-permute-start(bf16[192,3,192]{0,2,1:T(8,128)(2,1)S(1)} %get-tuple-element.42), channel_id=1, source_target_pairs={{0,128},{128,0},{1,129},{129,1},{2,130},{130,2},{3,131},{131,3},{4... | collective-permute-start | bytes 663560 | tf_op jit(solution)/shard_map/ppermute | solution.py:424
  107.1 1.2 %collective-permute-done.3 = bf16[192,3,192]{0,2,1:T(8,128)(2,1)S(1)} collective-permute-done((bf16[192,3,192]{0,2,1:T(8,128)(2,1)S(1)}, bf16[192,3,192]{0,2,1:T(8,128)(2,1)S(1)}, u32[]{:S(2)}, u32[]{:S(2)}) %collective-permute-start.3) | collective-permute-done | bytes 221216 | tf_op jit(solution)/shard_map/ppermute | solution.py:424
  108.5 1.0 copy.43
  (69 shorter events, 2.6 us)
Async XLA Ops:
  0.0 9.8 %copy-start = (bf16[2,2,96,192]{3,2,1,0:T(8,128)(2,1)S(1)}, bf16[2,2,96,192]{3,2,1,0:T(8,128)(2,1)}, u32[]{:S(2)}) copy-start(bf16[2,2,96,192]{3,2,1,0:T(8,128)(2,1)} %param.12) | copy-start | bytes 442372
  0.0 5.7 %copy-start.1 = (bf16[3,384,768]{2,1,0:T(8,128)(2,1)S(1)}, bf16[3,384,768]{2,1,0:T(8,128)(2,1)}, u32[]{:S(2)}) copy-start(bf16[3,384,768]{2,1,0:T(8,128)(2,1)} %param.9) | copy-start | bytes 5308420
  1.2 11.8 %collective-permute-start = (bf16[1,193,768]{2,1,0:T(8,128)(2,1)S(1)}, bf16[1,193,768]{2,1,0:T(8,128)(2,1)S(1)}, u32[]{:S(2)}, u32[]{:S(2)}) collective-permute-start(bf16[1,193,768]{2,1,0:T(8,128)(2,1)S(1)} %pad_dynamic-slice_fusion), channel_id=1, source_target_pairs={{0,1},{1,2},{2,3},{3,4},{4,5},{5,6},{6,7},{7,8},{8,9},{9,10},{10,1... | collective-permute-start | bytes 889352 | tf_op jit(solution)/shard_map/ppermute | solution.py:182
  5.9 1.6 %copy-start.16 = (f32[96]{0:T(128)S(1)}, f32[96]{0:T(128)}, u32[]{:S(2)}) copy-start(f32[96]{0:T(128)} %param.11) | copy-start | bytes 1156
  5.9 1.6 %copy-start.15 = (f32[192]{0:T(256)S(1)}, f32[192]{0:T(256)}, u32[]{:S(2)}) copy-start(f32[192]{0:T(256)} %param.13) | copy-start | bytes 2308
  9.8 1.7 %copy-start.18 = (bf16[3,4,4,96]{3,2,1,0:T(4,128)(2,1)S(1)}, bf16[3,4,4,96]{3,2,1,0:T(4,128)(2,1)}, u32[]{:S(2)}) copy-start(bf16[3,4,4,96]{3,2,1,0:T(4,128)(2,1)} %param.10) | copy-start | bytes 27652
  13.0 1.0 copy-start.10
  20.7 1.1 copy-start.8
  23.1 1.1 copy-start.7
  23.1 1.1 copy-start.19
  24.1 1.2 %copy-start.14 = (f32[384]{0:T(512)S(1)}, f32[384]{0:T(512)}, u32[]{:S(2)}) copy-start(f32[384]{0:T(512)} %param.16) | copy-start | bytes 4612
  58.7 2.0 %copy-start.9 = (bf16[128,16,128]{2,1,0:T(8,128)(2,1)S(1)}, bf16[128,16,128]{2,1,0:T(8,128)(2,1)}, u32[]{:S(2)}) copy-start(bf16[128,16,128]{2,1,0:T(8,128)(2,1)} %get-tuple-element.13) | copy-start | bytes 1572868
  61.9 4.7 %copy-start.11 = (bf16[384,384]{1,0:T(8,128)(2,1)S(1)}, bf16[384,384]{1,0:T(8,128)(2,1)}, u32[]{:S(2)}) copy-start(bf16[384,384]{1,0:T(8,128)(2,1)} %get-tuple-element.16) | copy-start | bytes 884740
  61.9 4.7 %copy-start.12 = (bf16[384,384]{1,0:T(8,128)(2,1)S(1)}, bf16[384,384]{1,0:T(8,128)(2,1)}, u32[]{:S(2)}) copy-start(bf16[384,384]{1,0:T(8,128)(2,1)} %get-tuple-element.17) | copy-start | bytes 884740
  61.9 4.7 %copy-start.13 = (bf16[384,384]{1,0:T(8,128)(2,1)S(1)}, bf16[384,384]{1,0:T(8,128)(2,1)}, u32[]{:S(2)}) copy-start(bf16[384,384]{1,0:T(8,128)(2,1)} %get-tuple-element.18) | copy-start | bytes 884740
  63.5 5.2 %collective-permute-start.1 = (bf16[3,384,192]{1,2,0:T(8,128)(2,1)}, bf16[3,384,192]{1,2,0:T(8,128)(2,1)S(1)}, u32[]{:S(2)}, u32[]{:S(2)}) collective-permute-start(bf16[3,384,192]{1,2,0:T(8,128)(2,1)} %copy.34), channel_id=1, source_target_pairs={{0,128},{128,0},{1,129},{129,1},{2,130},{130,2},{3,131},{131,3},{4... | collective-permute-start | bytes 1327112 | tf_op jit(solution)/shard_map/ppermute | solution.py:371
  66.6 1.5 %copy-start.2 = (bf16[384,192]{1,0:T(8,128)(2,1)S(1)}, bf16[384,192]{1,0:T(8,128)(2,1)}, u32[]{:S(2)}) copy-start(bf16[384,192]{1,0:T(8,128)(2,1)} %get-tuple-element.14) | copy-start | bytes 442372
  66.6 1.5 %copy-start.3 = (bf16[384,192]{1,0:T(8,128)(2,1)S(1)}, bf16[384,192]{1,0:T(8,128)(2,1)}, u32[]{:S(2)}) copy-start(bf16[384,192]{1,0:T(8,128)(2,1)} %get-tuple-element.15) | copy-start | bytes 442372
  68.6 0.8 copy-start.17
  69.4 3.6 %copy-start.4 = (bf16[3,1,384,192]{2,3,1,0:T(8,128)(2,1)S(1)}, bf16[3,1,384,192]{2,3,1,0:T(8,128)(2,1)}, u32[]{:S(2)}) copy-start(bf16[3,1,384,192]{2,3,1,0:T(8,128)(2,1)} %copy.64) | copy-start | bytes 1327108
  73.0 1.7 %copy-start.5 = (bf16[1,384,2,384]{3,1,2,0:T(8,128)(2,1)S(1)}, bf16[1,384,2,384]{3,1,2,0:T(8,128)(2,1)}, u32[]{:S(2)}) copy-start(bf16[1,384,2,384]{3,1,2,0:T(8,128)(2,1)} %get-tuple-element.38) | copy-start | bytes 1769476
  73.0 1.7 %copy-start.6 = (bf16[1,384,2,384]{3,1,2,0:T(8,128)(2,1)S(1)}, bf16[1,384,2,384]{3,1,2,0:T(8,128)(2,1)}, u32[]{:S(2)}) copy-start(bf16[1,384,2,384]{3,1,2,0:T(8,128)(2,1)} %get-tuple-element.43) | copy-start | bytes 1769476
  75.7 2.5 %collective-permute-start.2 = (bf16[3,384,2,192]{1,3,2,0:T(8,128)(2,1)S(1)}, bf16[3,384,2,192]{1,3,2,0:T(8,128)(2,1)S(1)}, u32[]{:S(2)}, u32[]{:S(2)}) collective-permute-start(bf16[3,384,2,192]{1,3,2,0:T(8,128)(2,1)S(1)} %fusion.21), channel_id=1, source_target_pairs={{0,128},{128,0},{1,129},{129,1},{2,130},{130,2},{3,131},{131,3},{4... | collective-permute-start | bytes 2654216 | tf_op jit(solution)/shard_map/ppermute | solution.py:398
  105.8 2.5 %collective-permute-start.3 = (bf16[192,3,192]{0,2,1:T(8,128)(2,1)S(1)}, bf16[192,3,192]{0,2,1:T(8,128)(2,1)S(1)}, u32[]{:S(2)}, u32[]{:S(2)}) collective-permute-start(bf16[192,3,192]{0,2,1:T(8,128)(2,1)S(1)} %get-tuple-element.42), channel_id=1, source_target_pairs={{0,128},{128,0},{1,129},{129,1},{2,130},{130,2},{3,131},{131,3},{4... | collective-permute-start | bytes 663560 | tf_op jit(solution)/shard_map/ppermute | solution.py:424

commit v13 on v12

--- a/solution.py
+++ b/solution.py
@@ -77,21 +77,22 @@
 ):
     pending = start_exchange(x_ref, o_ref, send_sem, recv_sem, own_sem)
     section = lax.axis_index("section")
-    width = part_ref.shape[1]
-    step = 64
-
+    width = filter_ref.shape[1] // 2
+
+    span = part_ref.shape[1]
     for half in range(filter_ref.shape[1] // width):
 
         @pl.when(section == half)
         def _():
             def move(index, carry):
-                first = pl.multiple_of(index * step, step)
-                part_ref[pl.ds(first, step), :] = filter_ref[
-                    pl.ds(first, step), half * width : (half + 1) * width
-                ]
+                first = pl.multiple_of(index * span, 8)
+                flipped = filter_ref[pl.ds(first, span), :].astype(jnp.float32).T
+                part_ref[pl.ds(pl.multiple_of(index * width, 8), width), :] = flipped[
+                    half * width : (half + 1) * width
+                ].astype(part_ref.dtype)
                 return carry
 
-            lax.fori_loop(0, part_ref.shape[0] // step, move, 0)
+            lax.fori_loop(0, filter_ref.shape[0] // span, move, 0)
 
     length = cos_ref.shape[0]
     block = 16
@@ -137,12 +138,12 @@
 def exchange_with_tables(chunks, filter_rows, collective_id, length):
     table = jax.ShapeDtypeStruct((length, length), jnp.bfloat16)
     part = jax.ShapeDtypeStruct(
-        (filter_rows.shape[0], filter_rows.shape[1] // 2), filter_rows.dtype
+        (filter_rows.shape[0] // length * (filter_rows.shape[1] // 2), length), filter_rows.dtype
     )
     return pl.pallas_call(
         exchange_tables_kernel,
         out_shape=(jax.ShapeDtypeStruct(chunks.shape, chunks.dtype), table, table, table, part)
-        + (jax.ShapeDtypeStruct((filter_rows.shape[1], part.shape[1]), jnp.bfloat16),) * 2,
+        + (jax.ShapeDtypeStruct((filter_rows.shape[1], filter_rows.shape[1] // 2), jnp.bfloat16),) * 2,
         in_specs=[pl.BlockSpec(memory_space=pl.ANY), pl.BlockSpec(memory_space=pltpu.VMEM)],
         out_specs=(
             pl.BlockSpec(memory_space=pl.ANY),
@@ -360,7 +361,9 @@
     slabs, cos_h, sin_h, negated_h, kernel_part, cos_part, negated_part = exchange_with_tables(
         slabs, filter_rows, 0, full_rows
     )
-    kernel_part = kernel_part.reshape(spectral_filter.shape[:3] + (cell_half,))
+    kernel_part = jnp.swapaxes(
+        kernel_part.reshape(spectral_filter.shape[:2] + (cell_half, full_rows)), 2, 3
+    )
     arrived = unpad_chunks(slabs, length)
     fields = (
         arrived.reshape(tiles, group_width, tile_rows, cell_half)

time: 110 us -> 107 us (0.973)
  local copies, waits for them, and re-layouts: 21.3 us -> 18.7 us
    unnamed x45 -> x35, local copies, waits for them, and re-layouts: 6.13 us -> 3.8 us
    slice x1 -> x0, local copies, waits for them, and re-layouts: 1.33 us -> none  [filter_columns(): filter_real = kernel[:, 0].astype(jnp.float32)]
  transfers between devices with their start and end apart: 4 -> 4, of which waited for: 2 -> 2; matrix products, arithmetic and copies ran while one was open for 9% -> 10% of each run, Pallas kernels for 0% -> 0%
where the time goes in v13:
time: 107 us
  Pallas kernels  49.8 us (47%)
  matrix products  19.1 us (18%)
  local copies, waits for them, and re-layouts  18.7 us (17%)
  starting transfers between devices  8.72 us (8%)
  other arithmetic  6.86 us (6%)
  waiting for transfers between devices  3.08 us (3%)
    pallas_call x1, Pallas kernels, exchange_with_tables(): pl.pallas_call(exchange_tables_kernel, out_shape=(jax.ShapeDtypeStruct(ch...  28.5 us
    pallas_call x1, Pallas kernels, exchange(): pl.pallas_call(exchange_kernel, out_shape=jax.ShapeDtypeStruct(chunks.sha...  21.2 us
    dot_general x2, matrix products, stem_layers(): jnp.einsum('zji,if->zjf', initial_layer, merging_matrix, preferred_elemen...  6.71 us
    ppermute x1, starting transfers between devices, from_behind(): return lax.ppermute(block, axis, route)  4.39 us
    unnamed x35, local copies, waits for them, and re-layouts  3.8 us
    dot_general x2, matrix products, spread_kernel(): full = jnp.dot(picked, repeat, preferred_element_type=jnp.float32)  3.8 us
    dot_general x1, matrix products, filter_columns(): jnp.einsum('puqh,chqw->cpuw', forward_h, row_spectrum, preferred_element_...  3.63 us
    ppermute x1, starting transfers between devices, local(): other_fields = lax.ppermute(fields, 'section', swap)  2.62 us
  transfers between devices with their start and end apart: 4, of which 2 were waited for; matrix products, arithmetic and copies ran while one was open for 10% of the time, Pallas kernels for 0%

profile of v13, /device:TPU:1, one launch (start us, length us, event | category | flops | bytes accessed | tf_op | source)
XLA Modules:
  0.0 106.7 jit_solution(12242544676495352237)
XLA Ops:
  0.0 1.2 %pad_dynamic-slice_fusion = bf16[1,193,768]{2,1,0:T(8,128)(2,1)S(1)} fusion(s32[]{:T(128)S(6)} %add.339, s32[]{:T(128)S(6)} %select_n.197, bf16[3,384,768]{2,1,0:T(8,128)(2,1)} %param.9), kind=kLoop, calls=%fused_computation.28 | loop fusion | bytes 2065928 | tf_op jit(solution)/shard_map/slice | solution.py:348
  1.2 4.4 %collective-permute-start = (bf16[1,193,768]{2,1,0:T(8,128)(2,1)S(1)}, bf16[1,193,768]{2,1,0:T(8,128)(2,1)S(1)}, u32[]{:S(2)}, u32[]{:S(2)}) collective-permute-start(bf16[1,193,768]{2,1,0:T(8,128)(2,1)S(1)} %pad_dynamic-slice_fusion), channel_id=1, source_target_pairs={{0,1},{1,2},{2,3},{3,4},{4,5},{5,6},{6,7},{7,8},{8,9},{9,10},{10,1... | collective-permute-start | bytes 889352 | tf_op jit(solution)/shard_map/ppermute | solution.py:183
  6.0 0.4 copy-done.13
  6.5 1.5 %slice_bitcast_fusion = (bf16[1,192,384]{2,1,0:T(8,128)(2,1)S(1)}, bf16[1,192,384]{2,1,0:T(8,128)(2,1)S(1)}, bf16[1,192,384]{2,1,0:T(8,128)(2,1)S(1)}, bf16[1,19...) fusion(bf16[3,3,192,384]{3,2,1,0:T(8,128)(2,1)} %param.14), kind=kLoop, calls=%fused_computation.174 | loop fusion | bytes 2654208 | tf_op jit(solution)/shard_map/stack;squeeze | solution.py:241
  8.2 0.9 stack.131
  9.3 0.9 pad_maximum_fusion.4
  10.2 2.2 %fusion.27 = bf16[384,768,1]{1,0,2:T(8,128)(2,1)} fusion(bf16[48,96]{1,0:T(8,128)(2,1)} %bitcast.186, s32[768]{0:T(1024)S(1)} %get-tuple-element.53, s32[384]{0:T(512)S(1)} %get-tuple-element.57, s32[768]{0:T(1024)S(1)} %get-tuple-element.51, s32[384]{0:T(512)S(1)} %get-tuple-element.58), kind=kOutput, calls=%fused_computation.58 | convolution fusion | flops 61175808 | bytes 608256 | tf_op jit(solution)/shard_map/dot_general | solution.py:204
  12.4 1.6 %fusion.26 = bf16[768,384,1]{1,0,2:T(8,128)(2,1)} fusion(bf16[384,192]{1,0:T(8,128)(2,1)S(1)} %bitcast.160, s32[768]{0:T(1024)S(1)} %get-tuple-element.54, s32[384]{0:T(512)S(1)} %get-tuple-element.56, s32[768]{0:T(1024)S(1)} %get-tuple-element.52, s32[384]{0:T(512)S(1)} %get-tuple-element.55), kind=kOutput, calls=%fused_computation.57 | convolution fusion | flops 227893248 | bytes 746496 | tf_op jit(solution)/shard_map/dot_general | solution.py:204
  14.1 1.0 fusion.108
  15.1 3.3 %fusion.35 = bf16[4,193,384]{2,1,0:T(8,128)(2,1)S(1)} fusion(bf16[768,384,1]{1,0,2:T(8,128)(2,1)} %fusion.26, bf16[384,768,1]{1,0,2:T(8,128)(2,1)} %fusion.27, f32[768]{0:T(1024)S(1)} %add.305, bf16[4,193,128]{2,1,0:T(8,128)(2,1)} %get-tuple-element.32, bf16[4,193,128]{2,1,0:T(8,128)(2,1)} %get-tuple-element.31, ...), kind=kOutput, calls=%fused_computation.66 | convolution fusion | flops 921360384 | bytes 2370048 | tf_op jit(solution)/shard_map/zji,if->zjf/dot_general | solution.py:272
  18.4 3.4 %fusion.43 = bf16[4,193,384]{2,1,0:T(8,128)(2,1)S(1)} fusion(bf16[768,384,1]{1,0,2:T(8,128)(2,1)} %fusion.26, bf16[384,768,1]{1,0,2:T(8,128)(2,1)} %fusion.27, f32[768]{0:T(1024)S(1)} %add.305, bf16[3,193,768]{2,1,0:T(8,128)(2,1)S(1)} %pad_dynamic-slice_fusion.1, bf16[1,193,768]{2,1,0:T(8,128)(2,1)} %copy-done.8, ...), kind=kOutput, calls=%fused_computation.74 | convolution fusion | flops 922842624 | bytes 3358208 | tf_op jit(solution)/shard_map/zji,if->zjf/dot_general | solution.py:272
  21.8 0.3 maximum_select_fusion
  22.1 0.8 copy-done.7
  22.9 0.6 fusion.63
  23.5 0.6 convolution_add_fusion.4
  24.2 0.6 convolution_add_fusion.3
  24.8 0.4 copy-done.6
  25.2 0.8 convert_reduce_fusion
  26.0 0.4 fusion.54
  26.6 0.9 copy.24
  27.5 0.5 reshape.340
  28.1 0.9 copy.58
  29.0 28.5 %shard_map.91 = (bf16[128,16,128]{2,1,0:T(8,128)(2,1)}, bf16[384,384]{1,0:T(8,128)(2,1)}, bf16[384,384]{1,0:T(8,128)(2,1)}, bf16[384,384]{1,0:T(8,128)(2,1)}, bf...) custom-call(bf16[128,16,128]{2,1,0:T(8,128)(2,1)} %bitcast.166, ...), custom_call_target="tpu_custom_call" | custom-call | tf_op jit(solution)/shard_map/pallas_call | solution.py:143
  57.5 1.5 %copy.50 = bf16[128,16,128]{0,2,1:T(8,128)(2,1)S(1)} copy(bf16[128,16,128]{2,1,0:T(8,128)(2,1)} %get-tuple-element.13) | data formatting | bytes 1048576 | tf_op jit(solution)/shard_map/reshape | solution.py:170
  59.0 0.7 copy.26
  59.8 0.5 reshape.346
  60.3 1.0 copy.29
  61.3 2.6 %collective-permute-start.1 = (bf16[3,384,192]{1,2,0:T(8,128)(2,1)}, bf16[3,384,192]{1,2,0:T(8,128)(2,1)}, u32[]{:S(2)}, u32[]{:S(2)}) collective-permute-start(bf16[3,384,192]{1,2,0:T(8,128)(2,1)} %copy.29), channel_id=1, source_target_pairs={{0,128},{128,0},{1,129},{129,1},{2,130},{130,2},{3,131},{131,3},{4... | collective-permute-start | bytes 1327112 | tf_op jit(solution)/shard_map/ppermute | solution.py:374
  64.0 1.5 %fusion.97 = (bf16[1,384,2,384]{3,1,2,0:T(8,128)(2,1)}, bf16[1,384,2,384]{3,1,2,0:T(8,128)(2,1)}, bf16[1,384,2,384]{3,1,2,0:T(8,128)(2,1)}, bf16[1,384,2,384]{3,1,2,0:T(8,128)(2,1)}) fusion(bf16[384,1,384]{2,0,1:T(8,128)(2,1)S(1)} %bitcast.183, bf16[384,1,384]{2,0,1:T(8,128)(2,1)S(1)} %bitcast.184, bf16[384,1,384]{2,0,1:T(8,128)(2,1)S(1)} %bitcast.185), kind=kLoop, calls=%fused_computation.129 | loop fusion | flops 1179648 | bytes 3244032 | tf_op jit(solution)/shard_map/stack | solution.py:378
  65.5 0.5 fusion.99
  66.0 3.6 %fusion.20 = bf16[3,2,384,192]{2,3,1,0:T(8,128)(2,1)} fusion(bf16[1,384,2,384]{3,1,2,0:T(8,128)(2,1)} %get-tuple-element.42, bf16[1,384,2,384]{3,1,2,0:T(8,128)(2,1)} %get-tuple-element.35, f32[3,384,2,192]{1,3,2,0:T(8,128)S(1)} %fusion.99, bf16[3,384,192]{1,2,0:T(8,128)(2,1)} %collective-permute-done.1, s32[]{:T(128)S(6)} %select_n.218, ...), kind=kOutput, calls=%fused_computation.44 | convolution fusion | flops 853327872 | bytes 4571140 | tf_op jit(solution)/shard_map/puqh,chqw->cpuw/dot_general | solution.py:309
  69.6 1.8 %fusion.56 = (bf16[3,1,384,192]{2,3,1,0:T(8,128)(2,1)S(1)}, bf16[3,1,384,192]{2,3,1,0:T(8,128)(2,1)S(1)}) fusion(bf16[3,2,384,192]{2,3,1,0:T(8,128)(2,1)} %fusion.20, bf16[3,2,384,192]{2,3,1,0:T(8,128)(2,1)} %bitcast.180), kind=kLoop, calls=%fused_computation.98 | loop fusion | flops 2654208 | bytes 2654208 | tf_op jit(solution)/shard_map/convert.1
  71.5 0.9 fusion.21
  72.5 0.5 convolution_bitcast_fusion.1
  73.0 1.9 %collective-permute-done.2 = bf16[3,384,2,192]{1,3,2,0:T(8,128)(2,1)S(1)} collective-permute-done((bf16[3,384,2,192]{1,3,2,0:T(8,128)(2,1)S(1)}, bf16[3,384,2,192]{1,3,2,0:T(8,128)(2,1)S(1)}, u32[]{:S(2)}, u32[]{:S(2)}) %collective-permute-start.2) | collective-permute-done | bytes 884768 | tf_op jit(solution)/shard_map/ppermute | solution.py:401
  74.9 0.5 fusion.24
  75.4 0.2 copy.33
  75.6 0.4 reshape.347
  76.0 0.8 copy.34
  76.8 1.2 %copy.57.x_ref = bf16[128,16,128]{2,1,0:T(8,128)(2,1)} copy(bf16[128,16,128]{0,2,1:T(8,128)(2,1)S(1)} %bitcast.164) | data formatting | bytes 1048576 | tf_op jit(solution)/shard_map/reshape | solution.py:176
  78.0 21.2 %shard_map.92 = bf16[128,16,128]{2,1,0:T(8,128)(2,1)} custom-call(bf16[128,16,128]{2,1,0:T(8,128)(2,1)} %copy.57.x_ref), custom_call_target="tpu_custom_call" | custom-call | tf_op jit(solution)/shard_map/pallas_call | solution.py:128
  99.3 1.2 %copy.61 = bf16[16,8,16,128]{3,1,2,0:T(8,128)(2,1)S(1)} copy(bf16[16,8,16,128]{3,2,1,0:T(8,128)(2,1)} %bitcast.165) | data formatting | bytes 1048576
  100.6 0.9 reshape.351
  101.5 0.9 copy.36
  102.4 0.3 constant_dynamic-slice_fusion.1
  102.7 1.5 %collective-permute-start.3 = (bf16[192,3,192]{0,2,1:T(8,128)(2,1)S(1)}, bf16[192,3,192]{0,2,1:T(8,128)(2,1)S(1)}, u32[]{:S(2)}, u32[]{:S(2)}) collective-permute-start(bf16[192,3,192]{0,2,1:T(8,128)(2,1)S(1)} %get-tuple-element.40), channel_id=1, source_target_pairs={{0,128},{128,0},{1,129},{129,1},{2,130},{130,2},{3,131},{131,3},{4... | collective-permute-start | bytes 663560 | tf_op jit(solution)/shard_map/ppermute | solution.py:427
  104.3 1.2 %collective-permute-done.3 = bf16[192,3,192]{0,2,1:T(8,128)(2,1)S(1)} collective-permute-done((bf16[192,3,192]{0,2,1:T(8,128)(2,1)S(1)}, bf16[192,3,192]{0,2,1:T(8,128)(2,1)S(1)}, u32[]{:S(2)}, u32[]{:S(2)}) %collective-permute-start.3) | collective-permute-done | bytes 221216 | tf_op jit(solution)/shard_map/ppermute | solution.py:427
  105.7 1.0 copy.37
  (58 shorter events, 1.8 us)
Async XLA Ops:
  0.0 12.4 %copy-start = (bf16[2,2,96,192]{3,2,1,0:T(8,128)(2,1)S(1)}, bf16[2,2,96,192]{3,2,1,0:T(8,128)(2,1)}, u32[]{:S(2)}) copy-start(bf16[2,2,96,192]{3,2,1,0:T(8,128)(2,1)} %param.12) | copy-start | bytes 442372
  0.0 5.7 %copy-start.1 = (bf16[3,384,768]{2,1,0:T(8,128)(2,1)S(1)}, bf16[3,384,768]{2,1,0:T(8,128)(2,1)}, u32[]{:S(2)}) copy-start(bf16[3,384,768]{2,1,0:T(8,128)(2,1)} %param.9) | copy-start | bytes 5308420
  1.2 12.9 %collective-permute-start = (bf16[1,193,768]{2,1,0:T(8,128)(2,1)S(1)}, bf16[1,193,768]{2,1,0:T(8,128)(2,1)S(1)}, u32[]{:S(2)}, u32[]{:S(2)}) collective-permute-start(bf16[1,193,768]{2,1,0:T(8,128)(2,1)S(1)} %pad_dynamic-slice_fusion), channel_id=1, source_target_pairs={{0,1},{1,2},{2,3},{3,4},{4,5},{5,6},{6,7},{7,8},{8,9},{9,10},{10,1... | collective-permute-start | bytes 889352 | tf_op jit(solution)/shard_map/ppermute | solution.py:183
  5.7 0.7 copy-start.13
  5.7 0.8 copy-start.14
  14.1 1.0 copy-start.8
  21.8 1.1 copy-start.7
  24.1 1.1 copy-start.6
  24.2 1.1 copy-start.15
  25.2 1.2 %copy-start.12 = (f32[384]{0:T(512)S(1)}, f32[384]{0:T(512)}, u32[]{:S(2)}) copy-start(f32[384]{0:T(512)} %param.16) | copy-start | bytes 4612
  59.8 4.2 %copy-start.9 = (bf16[384,384]{1,0:T(8,128)(2,1)S(1)}, bf16[384,384]{1,0:T(8,128)(2,1)}, u32[]{:S(2)}) copy-start(bf16[384,384]{1,0:T(8,128)(2,1)} %get-tuple-element.16) | copy-start | bytes 884740
  59.8 4.2 %copy-start.10 = (bf16[384,384]{1,0:T(8,128)(2,1)S(1)}, bf16[384,384]{1,0:T(8,128)(2,1)}, u32[]{:S(2)}) copy-start(bf16[384,384]{1,0:T(8,128)(2,1)} %get-tuple-element.17) | copy-start | bytes 884740
  59.8 4.2 %copy-start.11 = (bf16[384,384]{1,0:T(8,128)(2,1)S(1)}, bf16[384,384]{1,0:T(8,128)(2,1)}, u32[]{:S(2)}) copy-start(bf16[384,384]{1,0:T(8,128)(2,1)} %get-tuple-element.18) | copy-start | bytes 884740
  61.3 4.7 %collective-permute-start.1 = (bf16[3,384,192]{1,2,0:T(8,128)(2,1)}, bf16[3,384,192]{1,2,0:T(8,128)(2,1)}, u32[]{:S(2)}, u32[]{:S(2)}) collective-permute-start(bf16[3,384,192]{1,2,0:T(8,128)(2,1)} %copy.29), channel_id=1, source_target_pairs={{0,128},{128,0},{1,129},{129,1},{2,130},{130,2},{3,131},{131,3},{4... | collective-permute-start | bytes 1327112 | tf_op jit(solution)/shard_map/ppermute | solution.py:374
  64.0 1.5 %copy-start.2 = (bf16[384,192]{1,0:T(8,128)(2,1)S(1)}, bf16[384,192]{1,0:T(8,128)(2,1)}, u32[]{:S(2)}) copy-start(bf16[384,192]{1,0:T(8,128)(2,1)} %get-tuple-element.14) | copy-start | bytes 442372
  64.0 1.5 %copy-start.3 = (bf16[384,192]{1,0:T(8,128)(2,1)S(1)}, bf16[384,192]{1,0:T(8,128)(2,1)}, u32[]{:S(2)}) copy-start(bf16[384,192]{1,0:T(8,128)(2,1)} %get-tuple-element.15) | copy-start | bytes 442372
  69.6 1.8 %copy-start.4 = (bf16[1,384,2,384]{3,1,2,0:T(8,128)(2,1)S(1)}, bf16[1,384,2,384]{3,1,2,0:T(8,128)(2,1)}, u32[]{:S(2)}) copy-start(bf16[1,384,2,384]{3,1,2,0:T(8,128)(2,1)} %get-tuple-element.36) | copy-start | bytes 1769476
  69.6 1.9 %copy-start.5 = (bf16[1,384,2,384]{3,1,2,0:T(8,128)(2,1)S(1)}, bf16[1,384,2,384]{3,1,2,0:T(8,128)(2,1)}, u32[]{:S(2)}) copy-start(bf16[1,384,2,384]{3,1,2,0:T(8,128)(2,1)} %get-tuple-element.41) | copy-start | bytes 1769476
  72.4 2.5 %collective-permute-start.2 = (bf16[3,384,2,192]{1,3,2,0:T(8,128)(2,1)S(1)}, bf16[3,384,2,192]{1,3,2,0:T(8,128)(2,1)S(1)}, u32[]{:S(2)}, u32[]{:S(2)}) collective-permute-start(bf16[3,384,2,192]{1,3,2,0:T(8,128)(2,1)S(1)} %fusion.21), channel_id=1, source_target_pairs={{0,128},{128,0},{1,129},{129,1},{2,130},{130,2},{3,131},{131,3},{4... | collective-permute-start | bytes 2654216 | tf_op jit(solution)/shard_map/ppermute | solution.py:401
  102.7 2.8 %collective-permute-start.3 = (bf16[192,3,192]{0,2,1:T(8,128)(2,1)S(1)}, bf16[192,3,192]{0,2,1:T(8,128)(2,1)S(1)}, u32[]{:S(2)}, u32[]{:S(2)}) collective-permute-start(bf16[192,3,192]{0,2,1:T(8,128)(2,1)S(1)} %get-tuple-element.40), channel_id=1, source_target_pairs={{0,128},{128,0},{1,129},{129,1},{2,130},{130,2},{3,131},{131,3},{4... | collective-permute-start | bytes 663560 | tf_op jit(solution)/shard_map/ppermute | solution.py:427

commit v14 on v13

--- a/solution.py
+++ b/solution.py
@@ -425,10 +425,9 @@
         summed, (1 - section_index) * half_channels, half_channels, 0
     )
     received = lax.ppermute(sent, "section", swap)
-    return jnp.where(
-        section_index == 0,
-        jnp.concatenate([kept, received], axis=2),
-        jnp.concatenate([received, kept], axis=2),
+    first_section = section_index == 0
+    return jnp.concatenate(
+        [jnp.where(first_section, kept, received), jnp.where(first_section, received, kept)], axis=2
     )
 
 

time: 107 us -> 107 us (level)
  no operation moved by 1% of the time
where the time goes in v14:
time: 107 us
  Pallas kernels  49.8 us (47%)
  matrix products  19.1 us (18%)
  local copies, waits for them, and re-layouts  18.6 us (17%)
  starting transfers between devices  8.72 us (8%)
  other arithmetic  7.01 us (7%)
  waiting for transfers between devices  3.08 us (3%)
    pallas_call x1, Pallas kernels, exchange_with_tables(): pl.pallas_call(exchange_tables_kernel, out_shape=(jax.ShapeDtypeStruct(ch...  28.5 us
    pallas_call x1, Pallas kernels, exchange(): pl.pallas_call(exchange_kernel, out_shape=jax.ShapeDtypeStruct(chunks.sha...  21.2 us
    dot_general x2, matrix products, stem_layers(): jnp.einsum('zji,if->zjf', initial_layer, merging_matrix, preferred_elemen...  6.71 us
    ppermute x1, starting transfers between devices, from_behind(): return lax.ppermute(block, axis, route)  4.39 us
    unnamed x35, local copies, waits for them, and re-layouts  3.8 us
    dot_general x2, matrix products, spread_kernel(): full = jnp.dot(picked, repeat, preferred_element_type=jnp.float32)  3.8 us
    dot_general x1, matrix products, filter_columns(): jnp.einsum('puqh,chqw->cpuw', forward_h, row_spectrum, preferred_element_...  3.63 us
    ppermute x1, starting transfers between devices, local(): other_fields = lax.ppermute(fields, 'section', swap)  2.62 us
  transfers between devices with their start and end apart: 4, of which 2 were waited for; matrix products, arithmetic and copies ran while one was open for 10% of the time, Pallas kernels for 0%

profile of v14, /device:TPU:1, one launch (start us, length us, event | category | flops | bytes accessed | tf_op | source)
XLA Modules:
  0.0 106.7 jit_solution(5757101424520013695)
XLA Ops:
  0.0 1.2 %pad_dynamic-slice_fusion = bf16[1,193,768]{2,1,0:T(8,128)(2,1)S(1)} fusion(s32[]{:T(128)S(6)} %add.339, s32[]{:T(128)S(6)} %select_n.201, bf16[3,384,768]{2,1,0:T(8,128)(2,1)} %param.9), kind=kLoop, calls=%fused_computation.28 | loop fusion | bytes 2065928 | tf_op jit(solution)/shard_map/slice | solution.py:348
  1.2 4.4 %collective-permute-start = (bf16[1,193,768]{2,1,0:T(8,128)(2,1)S(1)}, bf16[1,193,768]{2,1,0:T(8,128)(2,1)S(1)}, u32[]{:S(2)}, u32[]{:S(2)}) collective-permute-start(bf16[1,193,768]{2,1,0:T(8,128)(2,1)S(1)} %pad_dynamic-slice_fusion), channel_id=1, source_target_pairs={{0,1},{1,2},{2,3},{3,4},{4,5},{5,6},{6,7},{7,8},{8,9},{9,10},{10,1... | collective-permute-start | bytes 889352 | tf_op jit(solution)/shard_map/ppermute | solution.py:183
  6.0 0.4 copy-done.13
  6.5 1.5 %slice_bitcast_fusion = (bf16[1,192,384]{2,1,0:T(8,128)(2,1)S(1)}, bf16[1,192,384]{2,1,0:T(8,128)(2,1)S(1)}, bf16[1,192,384]{2,1,0:T(8,128)(2,1)S(1)}, bf16[1,19...) fusion(bf16[3,3,192,384]{3,2,1,0:T(8,128)(2,1)} %param.14), kind=kLoop, calls=%fused_computation.176 | loop fusion | bytes 2654208 | tf_op jit(solution)/shard_map/stack;squeeze | solution.py:241
  8.2 0.9 stack.131
  9.3 0.9 pad_maximum_fusion.4
  10.2 2.2 %fusion.27 = bf16[384,768,1]{1,0,2:T(8,128)(2,1)} fusion(bf16[48,96]{1,0:T(8,128)(2,1)} %bitcast.186, s32[768]{0:T(1024)S(1)} %get-tuple-element.53, s32[384]{0:T(512)S(1)} %get-tuple-element.57, s32[768]{0:T(1024)S(1)} %get-tuple-element.51, s32[384]{0:T(512)S(1)} %get-tuple-element.58), kind=kOutput, calls=%fused_computation.58 | convolution fusion | flops 61175808 | bytes 608256 | tf_op jit(solution)/shard_map/dot_general | solution.py:204
  12.4 1.6 %fusion.26 = bf16[768,384,1]{1,0,2:T(8,128)(2,1)} fusion(bf16[384,192]{1,0:T(8,128)(2,1)S(1)} %bitcast.160, s32[768]{0:T(1024)S(1)} %get-tuple-element.54, s32[384]{0:T(512)S(1)} %get-tuple-element.56, s32[768]{0:T(1024)S(1)} %get-tuple-element.52, s32[384]{0:T(512)S(1)} %get-tuple-element.55), kind=kOutput, calls=%fused_computation.57 | convolution fusion | flops 227893248 | bytes 746496 | tf_op jit(solution)/shard_map/dot_general | solution.py:204
  14.1 1.0 fusion.108
  15.1 3.3 %fusion.35 = bf16[4,193,384]{2,1,0:T(8,128)(2,1)S(1)} fusion(bf16[768,384,1]{1,0,2:T(8,128)(2,1)} %fusion.26, bf16[384,768,1]{1,0,2:T(8,128)(2,1)} %fusion.27, f32[768]{0:T(1024)S(1)} %add.305, bf16[4,193,128]{2,1,0:T(8,128)(2,1)} %get-tuple-element.32, bf16[4,193,128]{2,1,0:T(8,128)(2,1)} %get-tuple-element.31, ...), kind=kOutput, calls=%fused_computation.66 | convolution fusion | flops 921360384 | bytes 2370048 | tf_op jit(solution)/shard_map/zji,if->zjf/dot_general | solution.py:272
  18.4 3.4 %fusion.43 = bf16[4,193,384]{2,1,0:T(8,128)(2,1)S(1)} fusion(bf16[768,384,1]{1,0,2:T(8,128)(2,1)} %fusion.26, bf16[384,768,1]{1,0,2:T(8,128)(2,1)} %fusion.27, f32[768]{0:T(1024)S(1)} %add.305, bf16[3,193,768]{2,1,0:T(8,128)(2,1)S(1)} %pad_dynamic-slice_fusion.1, bf16[1,193,768]{2,1,0:T(8,128)(2,1)} %copy-done.8, ...), kind=kOutput, calls=%fused_computation.74 | convolution fusion | flops 922842624 | bytes 3358208 | tf_op jit(solution)/shard_map/zji,if->zjf/dot_general | solution.py:272
  21.8 0.3 maximum_select_fusion
  22.1 0.8 copy-done.7
  22.9 0.6 fusion.63
  23.5 0.6 convolution_add_fusion.4
  24.2 0.6 convolution_add_fusion.3
  24.8 0.4 copy-done.6
  25.2 0.8 convert_reduce_fusion
  26.0 0.4 fusion.54
  26.6 0.9 copy.24
  27.5 0.5 reshape.340
  28.1 0.9 copy.58
  29.0 28.5 %shard_map.91 = (bf16[128,16,128]{2,1,0:T(8,128)(2,1)}, bf16[384,384]{1,0:T(8,128)(2,1)}, bf16[384,384]{1,0:T(8,128)(2,1)}, bf16[384,384]{1,0:T(8,128)(2,1)}, bf...) custom-call(bf16[128,16,128]{2,1,0:T(8,128)(2,1)} %bitcast.166, ...), custom_call_target="tpu_custom_call" | custom-call | tf_op jit(solution)/shard_map/pallas_call | solution.py:143
  57.5 1.5 %copy.50 = bf16[128,16,128]{0,2,1:T(8,128)(2,1)S(1)} copy(bf16[128,16,128]{2,1,0:T(8,128)(2,1)} %get-tuple-element.13) | data formatting | bytes 1048576 | tf_op jit(solution)/shard_map/reshape | solution.py:170
  59.0 0.7 copy.26
  59.8 0.5 reshape.346
  60.3 1.0 copy.29
  61.3 2.6 %collective-permute-start.1 = (bf16[3,384,192]{1,2,0:T(8,128)(2,1)}, bf16[3,384,192]{1,2,0:T(8,128)(2,1)}, u32[]{:S(2)}, u32[]{:S(2)}) collective-permute-start(bf16[3,384,192]{1,2,0:T(8,128)(2,1)} %copy.29), channel_id=1, source_target_pairs={{0,128},{128,0},{1,129},{129,1},{2,130},{130,2},{3,131},{131,3},{4... | collective-permute-start | bytes 1327112 | tf_op jit(solution)/shard_map/ppermute | solution.py:374
  64.0 1.5 %fusion.97 = (bf16[1,384,2,384]{3,1,2,0:T(8,128)(2,1)}, bf16[1,384,2,384]{3,1,2,0:T(8,128)(2,1)}, bf16[1,384,2,384]{3,1,2,0:T(8,128)(2,1)}, bf16[1,384,2,384]{3,1,2,0:T(8,128)(2,1)}) fusion(bf16[384,1,384]{2,0,1:T(8,128)(2,1)S(1)} %bitcast.183, bf16[384,1,384]{2,0,1:T(8,128)(2,1)S(1)} %bitcast.184, bf16[384,1,384]{2,0,1:T(8,128)(2,1)S(1)} %bitcast.185), kind=kLoop, calls=%fused_computation.129 | loop fusion | flops 1179648 | bytes 3244032 | tf_op jit(solution)/shard_map/stack | solution.py:378
  65.5 0.5 fusion.99
  66.0 3.6 %fusion.20 = bf16[3,2,384,192]{2,3,1,0:T(8,128)(2,1)} fusion(bf16[1,384,2,384]{3,1,2,0:T(8,128)(2,1)} %get-tuple-element.42, bf16[1,384,2,384]{3,1,2,0:T(8,128)(2,1)} %get-tuple-element.37, f32[3,384,2,192]{1,3,2,0:T(8,128)S(1)} %fusion.99, bf16[3,384,192]{1,2,0:T(8,128)(2,1)} %collective-permute-done.1, s32[]{:T(128)S(6)} %select_n.222, ...), kind=kOutput, calls=%fused_computation.44 | convolution fusion | flops 853327872 | bytes 4571140 | tf_op jit(solution)/shard_map/puqh,chqw->cpuw/dot_general | solution.py:309
  69.6 1.8 %fusion.56 = (bf16[3,1,384,192]{2,3,1,0:T(8,128)(2,1)S(1)}, bf16[3,1,384,192]{2,3,1,0:T(8,128)(2,1)S(1)}) fusion(bf16[3,2,384,192]{2,3,1,0:T(8,128)(2,1)} %fusion.20, bf16[3,2,384,192]{2,3,1,0:T(8,128)(2,1)} %bitcast.180), kind=kLoop, calls=%fused_computation.98 | loop fusion | flops 2654208 | bytes 2654208 | tf_op jit(solution)/shard_map/convert.1
  71.5 0.9 fusion.21
  72.5 0.5 convolution_bitcast_fusion.1
  73.0 1.9 %collective-permute-done.2 = bf16[3,384,2,192]{1,3,2,0:T(8,128)(2,1)S(1)} collective-permute-done((bf16[3,384,2,192]{1,3,2,0:T(8,128)(2,1)S(1)}, bf16[3,384,2,192]{1,3,2,0:T(8,128)(2,1)S(1)}, u32[]{:S(2)}, u32[]{:S(2)}) %collective-permute-start.2) | collective-permute-done | bytes 884768 | tf_op jit(solution)/shard_map/ppermute | solution.py:401
  74.9 0.5 fusion.24
  75.4 0.2 copy.33
  75.6 0.4 reshape.347
  76.0 0.8 copy.34
  76.8 1.2 %copy.57.x_ref = bf16[128,16,128]{2,1,0:T(8,128)(2,1)} copy(bf16[128,16,128]{0,2,1:T(8,128)(2,1)S(1)} %bitcast.164) | data formatting | bytes 1048576 | tf_op jit(solution)/shard_map/reshape | solution.py:176
  78.0 21.2 %shard_map.92 = bf16[128,16,128]{2,1,0:T(8,128)(2,1)} custom-call(bf16[128,16,128]{2,1,0:T(8,128)(2,1)} %copy.57.x_ref), custom_call_target="tpu_custom_call" | custom-call | tf_op jit(solution)/shard_map/pallas_call | solution.py:128
  99.3 1.2 %copy.61 = bf16[16,8,16,128]{3,1,2,0:T(8,128)(2,1)S(1)} copy(bf16[16,8,16,128]{3,2,1,0:T(8,128)(2,1)} %bitcast.165) | data formatting | bytes 1048576
  100.6 0.9 reshape.351
  101.5 0.9 copy.36
  102.6 1.5 %collective-permute-start.3 = (bf16[192,3,192]{0,2,1:T(8,128)(2,1)S(1)}, bf16[192,3,192]{0,2,1:T(8,128)(2,1)S(1)}, u32[]{:S(2)}, u32[]{:S(2)}) collective-permute-start(bf16[192,3,192]{0,2,1:T(8,128)(2,1)S(1)} %constant_dynamic-slice_fusion), channel_id=1, source_target_pairs={{0,128},{128,0},{1,129},{129,1},{2,130},{130,2},{3,131},{131,3},{4... | collective-permute-start | bytes 663560 | tf_op jit(solution)/shard_map/ppermute | solution.py:427
  104.2 1.2 %collective-permute-done.3 = bf16[192,3,192]{0,2,1:T(8,128)(2,1)S(1)} collective-permute-done((bf16[192,3,192]{0,2,1:T(8,128)(2,1)S(1)}, bf16[192,3,192]{0,2,1:T(8,128)(2,1)S(1)}, u32[]{:S(2)}, u32[]{:S(2)}) %collective-permute-start.3) | collective-permute-done | bytes 221216 | tf_op jit(solution)/shard_map/ppermute | solution.py:427
  105.4 0.3 broadcast_select_fusion.1
  105.8 1.0 copy.37
  (59 shorter events, 1.9 us)
Async XLA Ops:
  0.0 12.4 %copy-start = (bf16[2,2,96,192]{3,2,1,0:T(8,128)(2,1)S(1)}, bf16[2,2,96,192]{3,2,1,0:T(8,128)(2,1)}, u32[]{:S(2)}) copy-start(bf16[2,2,96,192]{3,2,1,0:T(8,128)(2,1)} %param.12) | copy-start | bytes 442372
  0.0 5.7 %copy-start.1 = (bf16[3,384,768]{2,1,0:T(8,128)(2,1)S(1)}, bf16[3,384,768]{2,1,0:T(8,128)(2,1)}, u32[]{:S(2)}) copy-start(bf16[3,384,768]{2,1,0:T(8,128)(2,1)} %param.9) | copy-start | bytes 5308420
  1.2 12.9 %collective-permute-start = (bf16[1,193,768]{2,1,0:T(8,128)(2,1)S(1)}, bf16[1,193,768]{2,1,0:T(8,128)(2,1)S(1)}, u32[]{:S(2)}, u32[]{:S(2)}) collective-permute-start(bf16[1,193,768]{2,1,0:T(8,128)(2,1)S(1)} %pad_dynamic-slice_fusion), channel_id=1, source_target_pairs={{0,1},{1,2},{2,3},{3,4},{4,5},{5,6},{6,7},{7,8},{8,9},{9,10},{10,1... | collective-permute-start | bytes 889352 | tf_op jit(solution)/shard_map/ppermute | solution.py:183
  5.7 0.7 copy-start.13
  5.7 0.8 copy-start.14
  14.1 1.0 copy-start.8
  21.8 1.1 copy-start.7
  24.1 1.1 copy-start.6
  24.2 1.1 copy-start.15
  25.2 1.2 %copy-start.12 = (f32[384]{0:T(512)S(1)}, f32[384]{0:T(512)}, u32[]{:S(2)}) copy-start(f32[384]{0:T(512)} %param.16) | copy-start | bytes 4612
  59.8 4.2 %copy-start.9 = (bf16[384,384]{1,0:T(8,128)(2,1)S(1)}, bf16[384,384]{1,0:T(8,128)(2,1)}, u32[]{:S(2)}) copy-start(bf16[384,384]{1,0:T(8,128)(2,1)} %get-tuple-element.16) | copy-start | bytes 884740
  59.8 4.2 %copy-start.10 = (bf16[384,384]{1,0:T(8,128)(2,1)S(1)}, bf16[384,384]{1,0:T(8,128)(2,1)}, u32[]{:S(2)}) copy-start(bf16[384,384]{1,0:T(8,128)(2,1)} %get-tuple-element.17) | copy-start | bytes 884740
  59.8 4.2 %copy-start.11 = (bf16[384,384]{1,0:T(8,128)(2,1)S(1)}, bf16[384,384]{1,0:T(8,128)(2,1)}, u32[]{:S(2)}) copy-start(bf16[384,384]{1,0:T(8,128)(2,1)} %get-tuple-element.18) | copy-start | bytes 884740
  61.3 4.7 %collective-permute-start.1 = (bf16[3,384,192]{1,2,0:T(8,128)(2,1)}, bf16[3,384,192]{1,2,0:T(8,128)(2,1)}, u32[]{:S(2)}, u32[]{:S(2)}) collective-permute-start(bf16[3,384,192]{1,2,0:T(8,128)(2,1)} %copy.29), channel_id=1, source_target_pairs={{0,128},{128,0},{1,129},{129,1},{2,130},{130,2},{3,131},{131,3},{4... | collective-permute-start | bytes 1327112 | tf_op jit(solution)/shard_map/ppermute | solution.py:374
  64.0 1.5 %copy-start.2 = (bf16[384,192]{1,0:T(8,128)(2,1)S(1)}, bf16[384,192]{1,0:T(8,128)(2,1)}, u32[]{:S(2)}) copy-start(bf16[384,192]{1,0:T(8,128)(2,1)} %get-tuple-element.14) | copy-start | bytes 442372
  64.0 1.5 %copy-start.3 = (bf16[384,192]{1,0:T(8,128)(2,1)S(1)}, bf16[384,192]{1,0:T(8,128)(2,1)}, u32[]{:S(2)}) copy-start(bf16[384,192]{1,0:T(8,128)(2,1)} %get-tuple-element.15) | copy-start | bytes 442372
  69.6 1.8 %copy-start.4 = (bf16[1,384,2,384]{3,1,2,0:T(8,128)(2,1)S(1)}, bf16[1,384,2,384]{3,1,2,0:T(8,128)(2,1)}, u32[]{:S(2)}) copy-start(bf16[1,384,2,384]{3,1,2,0:T(8,128)(2,1)} %get-tuple-element.38) | copy-start | bytes 1769476
  69.6 1.9 %copy-start.5 = (bf16[1,384,2,384]{3,1,2,0:T(8,128)(2,1)S(1)}, bf16[1,384,2,384]{3,1,2,0:T(8,128)(2,1)}, u32[]{:S(2)}) copy-start(bf16[1,384,2,384]{3,1,2,0:T(8,128)(2,1)} %get-tuple-element.41) | copy-start | bytes 1769476
  72.4 2.5 %collective-permute-start.2 = (bf16[3,384,2,192]{1,3,2,0:T(8,128)(2,1)S(1)}, bf16[3,384,2,192]{1,3,2,0:T(8,128)(2,1)S(1)}, u32[]{:S(2)}, u32[]{:S(2)}) collective-permute-start(bf16[3,384,2,192]{1,3,2,0:T(8,128)(2,1)S(1)} %fusion.21), channel_id=1, source_target_pairs={{0,128},{128,0},{1,129},{129,1},{2,130},{130,2},{3,131},{131,3},{4... | collective-permute-start | bytes 2654216 | tf_op jit(solution)/shard_map/ppermute | solution.py:401
  102.6 2.8 %collective-permute-start.3 = (bf16[192,3,192]{0,2,1:T(8,128)(2,1)S(1)}, bf16[192,3,192]{0,2,1:T(8,128)(2,1)S(1)}, u32[]{:S(2)}, u32[]{:S(2)}) collective-permute-start(bf16[192,3,192]{0,2,1:T(8,128)(2,1)S(1)} %constant_dynamic-slice_fusion), channel_id=1, source_target_pairs={{0,128},{128,0},{1,129},{129,1},{2,130},{130,2},{3,131},{131,3},{4... | collective-permute-start | bytes 663560 | tf_op jit(solution)/shard_map/ppermute | solution.py:427

commit v15 on v13

--- a/solution.py
+++ b/solution.py
@@ -28,7 +28,8 @@
     own.start()
 
     def send(step, carry):
-        peer = lax.rem(me + step, count)
+        offset = jnp.where(step % 2 == 1, (step + 1) // 2, count - step // 2)
+        peer = lax.rem(me + offset, count)
         pltpu.make_async_remote_copy(
             src_ref=x_ref.at[pl.ds(peer, 1)],
             dst_ref=o_ref.at[pl.ds(me, 1)],

time: 107 us -> 108 us (level)
  Pallas kernels: 49.8 us -> 52.2 us
  starting transfers between devices: 8.72 us -> 7.35 us
    pallas_call x1, Pallas kernels: 28.5 us -> 30 us  [exchange_with_tables(): pl.pallas_call(exchange_tables_kernel, out_shape=(jax.ShapeDtypeStruct(ch...]
where the time goes in v15:
time: 108 us
  Pallas kernels  52.2 us (48%)
  matrix products  19.1 us (18%)
  local copies, waits for them, and re-layouts  18.7 us (17%)
  starting transfers between devices  7.35 us (7%)
  other arithmetic  6.86 us (6%)
  waiting for transfers between devices  3.07 us (3%)
    pallas_call x1, Pallas kernels, exchange_with_tables(): pl.pallas_call(exchange_tables_kernel, out_shape=(jax.ShapeDtypeStruct(ch...  30 us
    pallas_call x1, Pallas kernels, exchange(): pl.pallas_call(exchange_kernel, out_shape=jax.ShapeDtypeStruct(chunks.sha...  22.2 us
    dot_general x2, matrix products, stem_layers(): jnp.einsum('zji,if->zjf', initial_layer, merging_matrix, preferred_elemen...  6.71 us
    ppermute x1, starting transfers between devices, from_behind(): return lax.ppermute(block, axis, route)  4.39 us
    unnamed x35, local copies, waits for them, and re-layouts  3.8 us
    dot_general x2, matrix products, spread_kernel(): full = jnp.dot(picked, repeat, preferred_element_type=jnp.float32)  3.8 us
    dot_general x1, matrix products, filter_columns(): jnp.einsum('puqh,chqw->cpuw', forward_h, row_spectrum, preferred_element_...  3.63 us
  transfers between devices with their start and end apart: 4, of which 2 were waited for; matrix products, arithmetic and copies ran while one was open for 10% of the time, Pallas kernels for 0%

profile of v15, /device:TPU:1, one launch (start us, length us, event | category | flops | bytes accessed | tf_op | source)
XLA Modules:
  0.0 107.7 jit_solution(5636467910953480278)
XLA Ops:
  0.0 1.2 %pad_dynamic-slice_fusion = bf16[1,193,768]{2,1,0:T(8,128)(2,1)S(1)} fusion(s32[]{:T(128)S(6)} %add.339, s32[]{:T(128)S(6)} %select_n.197, bf16[3,384,768]{2,1,0:T(8,128)(2,1)} %param.9), kind=kLoop, calls=%fused_computation.28 | loop fusion | bytes 2065928 | tf_op jit(solution)/shard_map/slice | solution.py:349
  1.2 4.4 %collective-permute-start = (bf16[1,193,768]{2,1,0:T(8,128)(2,1)S(1)}, bf16[1,193,768]{2,1,0:T(8,128)(2,1)S(1)}, u32[]{:S(2)}, u32[]{:S(2)}) collective-permute-start(bf16[1,193,768]{2,1,0:T(8,128)(2,1)S(1)} %pad_dynamic-slice_fusion), channel_id=1, source_target_pairs={{0,1},{1,2},{2,3},{3,4},{4,5},{5,6},{6,7},{7,8},{8,9},{9,10},{10,1... | collective-permute-start | bytes 889352 | tf_op jit(solution)/shard_map/ppermute | solution.py:184
  6.0 0.4 copy-done.13
  6.5 1.5 %slice_bitcast_fusion = (bf16[1,192,384]{2,1,0:T(8,128)(2,1)S(1)}, bf16[1,192,384]{2,1,0:T(8,128)(2,1)S(1)}, bf16[1,192,384]{2,1,0:T(8,128)(2,1)S(1)}, bf16[1,19...) fusion(bf16[3,3,192,384]{3,2,1,0:T(8,128)(2,1)} %param.14), kind=kLoop, calls=%fused_computation.174 | loop fusion | bytes 2654208 | tf_op jit(solution)/shard_map/stack;squeeze | solution.py:242
  8.2 0.9 stack.131
  9.3 0.9 pad_maximum_fusion.4
  10.2 2.2 %fusion.27 = bf16[384,768,1]{1,0,2:T(8,128)(2,1)} fusion(bf16[48,96]{1,0:T(8,128)(2,1)} %bitcast.186, s32[768]{0:T(1024)S(1)} %get-tuple-element.53, s32[384]{0:T(512)S(1)} %get-tuple-element.57, s32[768]{0:T(1024)S(1)} %get-tuple-element.51, s32[384]{0:T(512)S(1)} %get-tuple-element.58), kind=kOutput, calls=%fused_computation.58 | convolution fusion | flops 61175808 | bytes 608256 | tf_op jit(solution)/shard_map/dot_general | solution.py:205
  12.4 1.6 %fusion.26 = bf16[768,384,1]{1,0,2:T(8,128)(2,1)} fusion(bf16[384,192]{1,0:T(8,128)(2,1)S(1)} %bitcast.160, s32[768]{0:T(1024)S(1)} %get-tuple-element.54, s32[384]{0:T(512)S(1)} %get-tuple-element.56, s32[768]{0:T(1024)S(1)} %get-tuple-element.52, s32[384]{0:T(512)S(1)} %get-tuple-element.55), kind=kOutput, calls=%fused_computation.57 | convolution fusion | flops 227893248 | bytes 746496 | tf_op jit(solution)/shard_map/dot_general | solution.py:205
  14.1 1.0 fusion.108
  15.1 3.3 %fusion.35 = bf16[4,193,384]{2,1,0:T(8,128)(2,1)S(1)} fusion(bf16[768,384,1]{1,0,2:T(8,128)(2,1)} %fusion.26, bf16[384,768,1]{1,0,2:T(8,128)(2,1)} %fusion.27, f32[768]{0:T(1024)S(1)} %add.305, bf16[4,193,128]{2,1,0:T(8,128)(2,1)} %get-tuple-element.32, bf16[4,193,128]{2,1,0:T(8,128)(2,1)} %get-tuple-element.31, ...), kind=kOutput, calls=%fused_computation.66 | convolution fusion | flops 921360384 | bytes 2370048 | tf_op jit(solution)/shard_map/zji,if->zjf/dot_general | solution.py:273
  18.4 3.4 %fusion.43 = bf16[4,193,384]{2,1,0:T(8,128)(2,1)S(1)} fusion(bf16[768,384,1]{1,0,2:T(8,128)(2,1)} %fusion.26, bf16[384,768,1]{1,0,2:T(8,128)(2,1)} %fusion.27, f32[768]{0:T(1024)S(1)} %add.305, bf16[3,193,768]{2,1,0:T(8,128)(2,1)S(1)} %pad_dynamic-slice_fusion.1, bf16[1,193,768]{2,1,0:T(8,128)(2,1)} %copy-done.8, ...), kind=kOutput, calls=%fused_computation.74 | convolution fusion | flops 922842624 | bytes 3358208 | tf_op jit(solution)/shard_map/zji,if->zjf/dot_general | solution.py:273
  21.8 0.3 maximum_select_fusion
  22.1 0.8 copy-done.7
  22.9 0.6 fusion.63
  23.5 0.6 convolution_add_fusion.4
  24.2 0.6 convolution_add_fusion.3
  24.8 0.4 copy-done.6
  25.2 0.8 convert_reduce_fusion
  26.0 0.4 fusion.54
  26.6 0.9 copy.24
  27.5 0.5 reshape.340
  28.1 0.9 copy.58
  29.0 30.0 %shard_map.91 = (bf16[128,16,128]{2,1,0:T(8,128)(2,1)}, bf16[384,384]{1,0:T(8,128)(2,1)}, bf16[384,384]{1,0:T(8,128)(2,1)}, bf16[384,384]{1,0:T(8,128)(2,1)}, bf...) custom-call(bf16[128,16,128]{2,1,0:T(8,128)(2,1)} %bitcast.166, ...), custom_call_target="tpu_custom_call" | custom-call | tf_op jit(solution)/shard_map/pallas_call | solution.py:144
  59.0 1.5 %copy.50 = bf16[128,16,128]{0,2,1:T(8,128)(2,1)S(1)} copy(bf16[128,16,128]{2,1,0:T(8,128)(2,1)} %get-tuple-element.13) | data formatting | bytes 1048576 | tf_op jit(solution)/shard_map/reshape | solution.py:171
  60.5 0.7 copy.26
  61.3 0.5 reshape.346
  61.8 1.0 copy.29
  62.8 1.7 %collective-permute-start.1 = (bf16[3,384,192]{1,2,0:T(8,128)(2,1)}, bf16[3,384,192]{1,2,0:T(8,128)(2,1)}, u32[]{:S(2)}, u32[]{:S(2)}) collective-permute-start(bf16[3,384,192]{1,2,0:T(8,128)(2,1)} %copy.29), channel_id=1, source_target_pairs={{0,128},{128,0},{1,129},{129,1},{2,130},{130,2},{3,131},{131,3},{4... | collective-permute-start | bytes 1327112 | tf_op jit(solution)/shard_map/ppermute | solution.py:375
  64.5 1.5 %fusion.97 = (bf16[1,384,2,384]{3,1,2,0:T(8,128)(2,1)}, bf16[1,384,2,384]{3,1,2,0:T(8,128)(2,1)}, bf16[1,384,2,384]{3,1,2,0:T(8,128)(2,1)}, bf16[1,384,2,384]{3,1,2,0:T(8,128)(2,1)}) fusion(bf16[384,1,384]{2,0,1:T(8,128)(2,1)S(1)} %bitcast.183, bf16[384,1,384]{2,0,1:T(8,128)(2,1)S(1)} %bitcast.184, bf16[384,1,384]{2,0,1:T(8,128)(2,1)S(1)} %bitcast.185), kind=kLoop, calls=%fused_computation.129 | loop fusion | flops 1179648 | bytes 3244032 | tf_op jit(solution)/shard_map/stack | solution.py:379
  66.0 0.5 fusion.99
  66.5 3.6 %fusion.20 = bf16[3,2,384,192]{2,3,1,0:T(8,128)(2,1)} fusion(bf16[1,384,2,384]{3,1,2,0:T(8,128)(2,1)} %get-tuple-element.42, bf16[1,384,2,384]{3,1,2,0:T(8,128)(2,1)} %get-tuple-element.35, f32[3,384,2,192]{1,3,2,0:T(8,128)S(1)} %fusion.99, bf16[3,384,192]{1,2,0:T(8,128)(2,1)} %collective-permute-done.1, s32[]{:T(128)S(6)} %select_n.218, ...), kind=kOutput, calls=%fused_computation.44 | convolution fusion | flops 853327872 | bytes 4571140 | tf_op jit(solution)/shard_map/puqh,chqw->cpuw/dot_general | solution.py:310
  70.2 1.8 %fusion.56 = (bf16[3,1,384,192]{2,3,1,0:T(8,128)(2,1)S(1)}, bf16[3,1,384,192]{2,3,1,0:T(8,128)(2,1)S(1)}) fusion(bf16[3,2,384,192]{2,3,1,0:T(8,128)(2,1)} %fusion.20, bf16[3,2,384,192]{2,3,1,0:T(8,128)(2,1)} %bitcast.180), kind=kLoop, calls=%fused_computation.98 | loop fusion | flops 2654208 | bytes 2654208 | tf_op jit(solution)/shard_map/convert.1
  72.0 0.9 fusion.21
  73.1 0.5 convolution_bitcast_fusion.1
  73.6 1.9 %collective-permute-done.2 = bf16[3,384,2,192]{1,3,2,0:T(8,128)(2,1)S(1)} collective-permute-done((bf16[3,384,2,192]{1,3,2,0:T(8,128)(2,1)S(1)}, bf16[3,384,2,192]{1,3,2,0:T(8,128)(2,1)S(1)}, u32[]{:S(2)}, u32[]{:S(2)}) %collective-permute-start.2) | collective-permute-done | bytes 884768 | tf_op jit(solution)/shard_map/ppermute | solution.py:402
  75.4 0.5 fusion.24
  75.9 0.2 copy.33
  76.2 0.4 reshape.347
  76.5 0.8 copy.34
  77.4 1.2 %copy.57.x_ref = bf16[128,16,128]{2,1,0:T(8,128)(2,1)} copy(bf16[128,16,128]{0,2,1:T(8,128)(2,1)S(1)} %bitcast.164) | data formatting | bytes 1048576 | tf_op jit(solution)/shard_map/reshape | solution.py:177
  78.6 22.2 %shard_map.92 = bf16[128,16,128]{2,1,0:T(8,128)(2,1)} custom-call(bf16[128,16,128]{2,1,0:T(8,128)(2,1)} %copy.57.x_ref), custom_call_target="tpu_custom_call" | custom-call | tf_op jit(solution)/shard_map/pallas_call | solution.py:129
  100.8 1.2 %copy.61 = bf16[16,8,16,128]{3,1,2,0:T(8,128)(2,1)S(1)} copy(bf16[16,8,16,128]{3,2,1,0:T(8,128)(2,1)} %bitcast.165) | data formatting | bytes 1048576
  102.0 0.9 reshape.351
  103.0 0.9 copy.36
  103.9 0.3 constant_dynamic-slice_fusion.1
  104.2 1.1 %collective-permute-start.3 = (bf16[192,3,192]{0,2,1:T(8,128)(2,1)S(1)}, bf16[192,3,192]{0,2,1:T(8,128)(2,1)S(1)}, u32[]{:S(2)}, u32[]{:S(2)}) collective-permute-start(bf16[192,3,192]{0,2,1:T(8,128)(2,1)S(1)} %get-tuple-element.40), channel_id=1, source_target_pairs={{0,128},{128,0},{1,129},{129,1},{2,130},{130,2},{3,131},{131,3},{4... | collective-permute-start | bytes 663560 | tf_op jit(solution)/shard_map/ppermute | solution.py:428
  105.3 1.2 %collective-permute-done.3 = bf16[192,3,192]{0,2,1:T(8,128)(2,1)S(1)} collective-permute-done((bf16[192,3,192]{0,2,1:T(8,128)(2,1)S(1)}, bf16[192,3,192]{0,2,1:T(8,128)(2,1)S(1)}, u32[]{:S(2)}, u32[]{:S(2)}) %collective-permute-start.3) | collective-permute-done | bytes 221216 | tf_op jit(solution)/shard_map/ppermute | solution.py:428
  106.7 1.0 copy.37
  (58 shorter events, 1.9 us)
Async XLA Ops:
  0.0 12.4 %copy-start = (bf16[2,2,96,192]{3,2,1,0:T(8,128)(2,1)S(1)}, bf16[2,2,96,192]{3,2,1,0:T(8,128)(2,1)}, u32[]{:S(2)}) copy-start(bf16[2,2,96,192]{3,2,1,0:T(8,128)(2,1)} %param.12) | copy-start | bytes 442372
  0.0 5.7 %copy-start.1 = (bf16[3,384,768]{2,1,0:T(8,128)(2,1)S(1)}, bf16[3,384,768]{2,1,0:T(8,128)(2,1)}, u32[]{:S(2)}) copy-start(bf16[3,384,768]{2,1,0:T(8,128)(2,1)} %param.9) | copy-start | bytes 5308420
  1.2 12.9 %collective-permute-start = (bf16[1,193,768]{2,1,0:T(8,128)(2,1)S(1)}, bf16[1,193,768]{2,1,0:T(8,128)(2,1)S(1)}, u32[]{:S(2)}, u32[]{:S(2)}) collective-permute-start(bf16[1,193,768]{2,1,0:T(8,128)(2,1)S(1)} %pad_dynamic-slice_fusion), channel_id=1, source_target_pairs={{0,1},{1,2},{2,3},{3,4},{4,5},{5,6},{6,7},{7,8},{8,9},{9,10},{10,1... | collective-permute-start | bytes 889352 | tf_op jit(solution)/shard_map/ppermute | solution.py:184
  5.7 0.7 copy-start.13
  5.7 0.8 copy-start.14
  14.1 1.0 copy-start.8
  21.8 1.1 copy-start.7
  24.1 1.1 copy-start.6
  24.2 1.1 copy-start.15
  25.2 1.2 %copy-start.12 = (f32[384]{0:T(512)S(1)}, f32[384]{0:T(512)}, u32[]{:S(2)}) copy-start(f32[384]{0:T(512)} %param.16) | copy-start | bytes 4612
  61.2 3.2 %copy-start.9 = (bf16[384,384]{1,0:T(8,128)(2,1)S(1)}, bf16[384,384]{1,0:T(8,128)(2,1)}, u32[]{:S(2)}) copy-start(bf16[384,384]{1,0:T(8,128)(2,1)} %get-tuple-element.16) | copy-start | bytes 884740
  61.3 3.2 %copy-start.10 = (bf16[384,384]{1,0:T(8,128)(2,1)S(1)}, bf16[384,384]{1,0:T(8,128)(2,1)}, u32[]{:S(2)}) copy-start(bf16[384,384]{1,0:T(8,128)(2,1)} %get-tuple-element.17) | copy-start | bytes 884740
  61.3 3.2 %copy-start.11 = (bf16[384,384]{1,0:T(8,128)(2,1)S(1)}, bf16[384,384]{1,0:T(8,128)(2,1)}, u32[]{:S(2)}) copy-start(bf16[384,384]{1,0:T(8,128)(2,1)} %get-tuple-element.18) | copy-start | bytes 884740
  62.8 3.7 %collective-permute-start.1 = (bf16[3,384,192]{1,2,0:T(8,128)(2,1)}, bf16[3,384,192]{1,2,0:T(8,128)(2,1)}, u32[]{:S(2)}, u32[]{:S(2)}) collective-permute-start(bf16[3,384,192]{1,2,0:T(8,128)(2,1)} %copy.29), channel_id=1, source_target_pairs={{0,128},{128,0},{1,129},{129,1},{2,130},{130,2},{3,131},{131,3},{4... | collective-permute-start | bytes 1327112 | tf_op jit(solution)/shard_map/ppermute | solution.py:375
  64.5 1.5 %copy-start.2 = (bf16[384,192]{1,0:T(8,128)(2,1)S(1)}, bf16[384,192]{1,0:T(8,128)(2,1)}, u32[]{:S(2)}) copy-start(bf16[384,192]{1,0:T(8,128)(2,1)} %get-tuple-element.14) | copy-start | bytes 442372
  64.5 1.5 %copy-start.3 = (bf16[384,192]{1,0:T(8,128)(2,1)S(1)}, bf16[384,192]{1,0:T(8,128)(2,1)}, u32[]{:S(2)}) copy-start(bf16[384,192]{1,0:T(8,128)(2,1)} %get-tuple-element.15) | copy-start | bytes 442372
  70.2 1.8 %copy-start.4 = (bf16[1,384,2,384]{3,1,2,0:T(8,128)(2,1)S(1)}, bf16[1,384,2,384]{3,1,2,0:T(8,128)(2,1)}, u32[]{:S(2)}) copy-start(bf16[1,384,2,384]{3,1,2,0:T(8,128)(2,1)} %get-tuple-element.36) | copy-start | bytes 1769476
  70.2 1.9 %copy-start.5 = (bf16[1,384,2,384]{3,1,2,0:T(8,128)(2,1)S(1)}, bf16[1,384,2,384]{3,1,2,0:T(8,128)(2,1)}, u32[]{:S(2)}) copy-start(bf16[1,384,2,384]{3,1,2,0:T(8,128)(2,1)} %get-tuple-element.41) | copy-start | bytes 1769476
  72.9 2.5 %collective-permute-start.2 = (bf16[3,384,2,192]{1,3,2,0:T(8,128)(2,1)S(1)}, bf16[3,384,2,192]{1,3,2,0:T(8,128)(2,1)S(1)}, u32[]{:S(2)}, u32[]{:S(2)}) collective-permute-start(bf16[3,384,2,192]{1,3,2,0:T(8,128)(2,1)S(1)} %fusion.21), channel_id=1, source_target_pairs={{0,128},{128,0},{1,129},{129,1},{2,130},{130,2},{3,131},{131,3},{4... | collective-permute-start | bytes 2654216 | tf_op jit(solution)/shard_map/ppermute | solution.py:402
  104.2 2.3 %collective-permute-start.3 = (bf16[192,3,192]{0,2,1:T(8,128)(2,1)S(1)}, bf16[192,3,192]{0,2,1:T(8,128)(2,1)S(1)}, u32[]{:S(2)}, u32[]{:S(2)}) collective-permute-start(bf16[192,3,192]{0,2,1:T(8,128)(2,1)S(1)} %get-tuple-element.40), channel_id=1, source_target_pairs={{0,128},{128,0},{1,129},{129,1},{2,130},{130,2},{3,131},{131,3},{4... | collective-permute-start | bytes 663560 | tf_op jit(solution)/shard_map/ppermute | solution.py:428
